TPU v7x, 128 devices: a whole 4x4x4 slice. The times are simulated.
128 devices in a mesh: ctx: 64 (over y, x, z), head: 2 (over core).
Axes of the slice: x: 4, y: 4, z: 4, core: 2. Of those that a mesh axis runs over, the one named last changes fastest.
Arguments:
- queries: float32 [16384, 2048], P('ctx', 'head')
- keys: float32 [16384, 512], P(('ctx', 'head'))
- values: float32 [16384, 512], P(('ctx', 'head')), may hold values from -6 to 6
- cotangent: float32 [16384, 2048], P('ctx', 'head'), may hold values from -6 to 6
- selected: int32 [16, 3], replicated, may hold values from -1 to 15, as said below
Outputs:
- attended: float32 [16384, 2048], P('ctx', 'head')
- grad_queries: float32 [16384, 2048], P('ctx', 'head')
- grad_keys: float32 [16384, 512], P(('ctx', 'head'))
- grad_values: float32 [16384, 512], P(('ctx', 'head'))
Inputs may be any that keep to these rules, and one draw needn't show every extreme that they name: selected[b, 0] = b; entries 1 and 2 of row b are different blocks before b, except that an entry is -1 when no further block before b is left: row 0 is [0, -1, -1] and row 1 is [1, 0, -1].
All inputs are finite; a program needn't handle non-finite values.
Results may differ from a plain program's by a relative error of at most 0.0003.
Values sent between devices are 32-bit elements; how exact they have to be, the bound alone decides.
No kernel may reach another device: no remote copies, remote signals or barrier semaphores. Data moves between devices by JAX's collectives and lax.ppermute only.
A program may use at most 192 MiB of HBM per device.

v0:
```python
import math

import jax
import jax.numpy as jnp
from jax import lax
from jax.sharding import PartitionSpec as P

QUERY_HEADS = 16
KEY_VALUE_HEADS = 4
HEAD_WIDTH = 128
BLOCK_TOKENS = 1024
TOPK = 3


def block_masks(selected, block_index, query_pos):
    masks = []
    for slot_index in range(TOPK):
        chosen = selected[block_index, slot_index]
        if slot_index == 0:
            key_pos = block_index * BLOCK_TOKENS + jnp.arange(BLOCK_TOKENS, dtype=jnp.int32)
            masks.append(key_pos[None, :] <= query_pos[:, None])
        else:
            masks.append(jnp.broadcast_to(chosen >= 0, (query_pos.shape[0], BLOCK_TOKENS)))
    return jnp.concatenate(masks, 1)


def pick_blocks(whole_keys, whole_values, selected, block_index, kv_heads):
    key_parts, value_parts, offsets = ([], [], [])
    for slot_index in range(TOPK):
        chosen = selected[block_index, slot_index]
        offset = jnp.maximum(chosen, 0) * BLOCK_TOKENS
        offsets.append(offset)
        key_parts.append(lax.dynamic_slice_in_dim(whole_keys, offset, BLOCK_TOKENS, 0))
        value_parts.append(lax.dynamic_slice_in_dim(whole_values, offset, BLOCK_TOKENS, 0))
    picked_keys = jnp.concatenate(key_parts, 0).reshape(TOPK * BLOCK_TOKENS, kv_heads, HEAD_WIDTH)
    picked_values = jnp.concatenate(value_parts, 0).reshape(
        TOPK * BLOCK_TOKENS, kv_heads, HEAD_WIDTH
    )
    return (picked_keys, picked_values, offsets)


def shards(queries, keys, values, cotangent, selected):
    highest = lax.Precision.HIGHEST
    scaling = 1.0 / math.sqrt(HEAD_WIDTH)
    group_width = QUERY_HEADS // KEY_VALUE_HEADS
    local_keys, local_values = (
        lax.all_to_all(keys, "head", split_axis=1, concat_axis=0, tiled=True),
        lax.all_to_all(values, "head", split_axis=1, concat_axis=0, tiled=True),
    )
    tokens_here = local_keys.shape[0]
    width = local_keys.shape[1]
    kv_heads = width // HEAD_WIDTH
    first_position = lax.axis_index("ctx") * tokens_here
    block_index = first_position // BLOCK_TOKENS
    query_pos = first_position + jnp.arange(tokens_here, dtype=jnp.int32)
    allowed = block_masks(selected, block_index, query_pos)
    whole_keys, whole_values = (
        lax.all_gather(local_keys, "ctx", axis=0, tiled=True),
        lax.all_gather(local_values, "ctx", axis=0, tiled=True),
    )
    picked_keys, picked_values, offsets = pick_blocks(
        whole_keys, whole_values, selected, block_index, kv_heads
    )
    block_of_queries = queries.reshape(tokens_here, kv_heads, group_width, HEAD_WIDTH)
    cotangent_block = cotangent.reshape(tokens_here, kv_heads, group_width, HEAD_WIDTH)
    scores = scaling * jnp.einsum(
        "thgd,shd->hgts", block_of_queries, picked_keys, precision=highest
    )
    scores = jnp.where(allowed[None, None], scores, -jnp.inf)
    maximum = jnp.max(scores, axis=-1, keepdims=True)
    probs = jnp.exp(scores - maximum)
    probs = probs / jnp.sum(probs, axis=-1, keepdims=True)
    attended = jnp.einsum("hgts,shd->thgd", probs, picked_values, precision=highest)
    row_dots = jnp.transpose(jnp.sum(cotangent_block * attended, axis=-1), (1, 2, 0))
    grad_probs = jnp.einsum("thgd,shd->hgts", cotangent_block, picked_values, precision=highest)
    grad_scores = probs * (grad_probs - row_dots[..., None])
    query_gradient = scaling * jnp.einsum(
        "hgts,shd->thgd", grad_scores, picked_keys, precision=highest
    )
    grad_k_sel = scaling * jnp.einsum(
        "hgts,thgd->shd", grad_scores, block_of_queries, precision=highest
    )
    grad_v_sel = jnp.einsum("hgts,thgd->shd", probs, cotangent_block, precision=highest)
    seq_rows = whole_keys.shape[0]
    key_gradient_total = jnp.zeros((seq_rows, kv_heads, HEAD_WIDTH), jnp.float32)
    value_gradient_total = jnp.zeros((seq_rows, kv_heads, HEAD_WIDTH), jnp.float32)
    for slot_index in range(TOPK):
        offset = offsets[slot_index]
        piece_k = grad_k_sel[slot_index * BLOCK_TOKENS : (slot_index + 1) * BLOCK_TOKENS]
        piece_v = grad_v_sel[slot_index * BLOCK_TOKENS : (slot_index + 1) * BLOCK_TOKENS]
        key_gradient_total = lax.dynamic_update_slice_in_dim(
            key_gradient_total,
            lax.dynamic_slice_in_dim(key_gradient_total, offset, BLOCK_TOKENS, 0) + piece_k,
            offset,
            0,
        )
        value_gradient_total = lax.dynamic_update_slice_in_dim(
            value_gradient_total,
            lax.dynamic_slice_in_dim(value_gradient_total, offset, BLOCK_TOKENS, 0) + piece_v,
            offset,
            0,
        )
    owned_k, owned_v = (
        lax.psum_scatter(
            key_gradient_total.reshape(seq_rows, width), "ctx", scatter_dimension=0, tiled=True
        ),
        lax.psum_scatter(
            value_gradient_total.reshape(seq_rows, width), "ctx", scatter_dimension=0, tiled=True
        ),
    )
    grad_keys, grad_values = (
        lax.all_to_all(owned_k, "head", split_axis=0, concat_axis=1, tiled=True),
        lax.all_to_all(owned_v, "head", split_axis=0, concat_axis=1, tiled=True),
    )
    return (
        attended.reshape(tokens_here, -1),
        query_gradient.reshape(tokens_here, -1),
        grad_keys,
        grad_values,
    )


def solution(mesh):
    placed = (
        P("ctx", "head"),
        P(("ctx", "head"), None),
        P(("ctx", "head"), None),
        P("ctx", "head"),
        P(),
    )
    return jax.shard_map(
        shards,
        mesh=mesh,
        in_specs=placed,
        out_specs=(
            P("ctx", "head"),
            P("ctx", "head"),
            P(("ctx", "head"), None),
            P(("ctx", "head"), None),
        ),
        check_vma=False,
    )
```

profile of v0, /device:TPU:1, one launch (start us, length us, event | category | flops | bytes accessed | tf_op | source)
XLA Modules:
  0.0 1183.4 jit_solution(17859586762684518673)
XLA Ops:
  8.3 5.0 all_to_all.76
  15.4 3.9 all_to_all.77
  24.8 2.5 copy.85
  27.3 2.6 copy.115
  30.1 3.9 add_add_fusion
  34.1 86.8 %all-gather.5.cloned.1.call-done = f32[16384,256]{1,0:T(8,128)} async-done(((f32[256,256]{1,0:T(8,128)}), f32[16384,256]{1,0:T(8,128)}) %all-gather.5.cloned.1.call-update) | async-done | bytes 16777232 | tf_op jit(solution)/shard_map/all_gather | solution.py:58
  127.3 24.6 %fusion.3 = (f32[2,4,256]{2,1,0:T(4,128)S(1)}, f32[2,3072,256,4]{2,1,3,0:T(8,128)S(1)}) fusion(pred[256,3072]{0,1:T(8,128)(4,1)} %add_add_fusion, f32[3072,2,128,1]{0,2,3,1:T(8,128)S(1)} %bitcast.93, f32[256,2,4,128]{0,3,2,1:T(8,128)} %bitcast.95), kind=kOutput, calls=%fused_computation.6 | convolution fusion | flops 9682548736 | bytes 30154752 | tf_op jit(solution)/shard_map/thgd,shd->hgts/dot_general | solution.py:66
  151.9 8.6 copy-done
  160.6 5.3 fusion.2
  165.8 77.2 %all-gather.3.cloned.1.call-done = f32[16384,256]{0,1:T(8,128)} async-done(((f32[256,256]{0,1:T(8,128)}), f32[16384,256]{0,1:T(8,128)}) %all-gather.3.cloned.1.call-update) | async-done | bytes 16777232 | tf_op jit(solution)/shard_map/all_gather | solution.py:59
  247.3 25.6 %fusion.10 = (f32[256,2,4]{0,2,1:T(4,128)S(1)}, f32[2,128,4,256]{3,1,2,0:T(8,128)}) fusion(f32[256,1024]{0,1:T(8,128)S(1)} %copy-done.7, f32[3072,2,128,1]{0,2,3,1:T(8,128)} %bitcast.98, f32[2,3072,256,4]{2,1,3,0:T(8,128)} %copy-done, f32[2,4,256]{2,1,0:T(4,128)S(1)} %fusion.2, f32[2,4,256]{2,1,0:T(4,128)S(1)} %get-tuple-element.33, ...), kind=kOutput, calls=%fused_computation.26 | convolution fusion | flops 9689364480 | bytes 31219712 | tf_op jit(solution)/shard_map/hgts,shd->thgd/dot_general | solution.py:73
  272.9 34.7 %convolution_bitcast_fusion = f32[3072,2,128]{0,2,1:T(8,128)S(1)} fusion(f32[256,2,4,128]{0,3,2,1:T(8,128)S(1)} %bitcast.100, f32[2,3072,256,4]{2,1,3,0:T(8,128)} %copy-done, f32[2,4,256]{2,1,0:T(4,128)S(1)} %fusion.2, f32[2,4,256]{2,1,0:T(4,128)S(1)} %get-tuple-element.33, pred[256,3072]{0,1:T(8,128)(4,1)S(1)} %copy-done.5), kind=kOutput, calls=%fused_computation.7 | convolution fusion | flops 9688842240 | bytes 30162944 | tf_op jit(solution)/shard_map/hgts,thgd->shd/dot_general | solution.py:83
  307.7 34.6 %fusion = f32[2,4,256,3072]{2,3,1,0:T(8,128)} fusion(f32[2,4,256]{2,1,0:T(4,128)S(1)} %bitcast.112, f32[3072,2,128,1]{0,2,3,1:T(8,128)} %bitcast.99, f32[256,2,4,128]{0,3,2,1:T(8,128)S(1)} %bitcast.101, f32[2,4,256]{2,1,0:T(4,128)S(1)} %fusion.2, f32[2,4,256]{2,1,0:T(4,128)S(1)} %get-tuple-element.33, f32[2,3072,256,4]{2,1,3,0:T(8,128)} %copy-done, ...), kind=kOutput, calls=%fused_computation.1 | convolution fusion | flops 9701425152 | bytes 55336960 | tf_op jit(solution)/shard_map/thgd,shd->hgts/dot_general | solution.py:75
  342.2 29.3 %fusion.5 = f32[3072,2,128]{0,2,1:T(8,128)S(1)} fusion(f32[2,4,256,3072]{2,3,1,0:T(8,128)} %fusion, f32[256,2,4,128]{0,3,2,1:T(8,128)S(1)} %bitcast.96), kind=kOutput, calls=%fused_computation.10 | convolution fusion | flops 9664462848 | bytes 29360128 | tf_op jit(solution)/shard_map/hgts,thgd->shd/dot_general | solution.py:80
  371.5 7.7 broadcast.22.clone
  380.2 7.7 broadcast.22.clone.1
  389.0 3.4 fusion.7
  394.8 2.8 fusion.6
  397.7 2.5 copy.96
  400.2 18.0 %convolution_multiply_fusion = f32[2,128,4,256]{3,1,2,0:T(8,128)} fusion(f32[3072,2,128,1]{0,2,3,1:T(8,128)S(1)} %bitcast.94, f32[2,4,256,3072]{2,3,1,0:T(8,128)} %fusion), kind=kOutput, calls=%fused_computation.14 | convolution fusion | flops 9663938560 | bytes 29360128 | tf_op jit(solution)/shard_map/hgts,shd->thgd/dot_general | solution.py:77
  420.7 313.4 %reduce-scatter.3.cloned.1.call-done = f32[256,256]{0,1:T(8,128)} async-done(((f32[16384,256]{0,1:T(8,128)}), f32[256,256]{0,1:T(8,128)}) %reduce-scatter.3.cloned.1.call-update) | async-done | bytes 262160 | tf_op jit(solution)/shard_map/reduce_scatter | solution.py:104
  735.2 54.7 %all_to_all.78 = f32[2,128,256]{2,1,0:T(8,128)S(1)} all-to-all(f32[2,128,256]{2,1,0:T(8,128)S(1)} %bitcast.106), channel_id=1, replica_groups=mesh['ctx'=64,'head'=2] {'head'}, dimensions={0} | all-to-all | bytes 524288 | tf_op jit(solution)/shard_map/all_to_all | solution.py:112
  790.8 332.1 %reduce-scatter.5.cloned.1.call-done = f32[256,256]{0,1:T(8,128)} async-done(((f32[16384,256]{0,1:T(8,128)}), f32[256,256]{0,1:T(8,128)}) %reduce-scatter.5.cloned.1.call-update) | async-done | bytes 262160 | tf_op jit(solution)/shard_map/reduce_scatter | solution.py:107
  1124.0 51.7 %all_to_all.79 = f32[2,128,256]{2,1,0:T(8,128)S(1)} all-to-all(f32[2,128,256]{2,1,0:T(8,128)S(1)} %bitcast.108), channel_id=1, replica_groups=mesh['ctx'=64,'head'=2] {'head'}, dimensions={0} | all-to-all | bytes 524288 | tf_op jit(solution)/shard_map/all_to_all | solution.py:113
  (51 shorter events, 27.6 us)
Async XLA Ops:
  7.2 113.7 %all-gather.5.cloned.1.call-start = ((), (), s32[]{:S(2)}) async-start(), calls=%async_computation.7 | async-start | bytes 17039360 | tf_op jit(solution)/shard_map/all_gather | solution.py:58
  14.2 228.9 %all-gather.3.cloned.1.call-start = ((), (), s32[]{:S(2)}) async-start(), calls=%async_computation.6 | async-start | bytes 17039360 | tf_op jit(solution)/shard_map/all_gather | solution.py:59
  20.2 713.9 %reduce-scatter.3.cloned.1.call-start = ((), (), s32[]{:S(2)}) async-start(), calls=%async_computation.8 | async-start | bytes 17039360 | tf_op jit(solution)/shard_map/reduce_scatter | solution.py:104
  127.3 24.6 %copy-start.1 = (f32[3072,256]{0,1:T(8,128)}, f32[3072,256]{0,1:T(8,128)S(1)}, u32[]{:S(2)}) copy-start(f32[3072,256]{0,1:T(8,128)S(1)} %copy.81) | copy-start | bytes 9437188
  127.3 33.3 %copy-start.4 = (pred[256,3072]{0,1:T(8,128)(4,1)S(1)}, pred[256,3072]{0,1:T(8,128)(4,1)}, u32[]{:S(2)}) copy-start(pred[256,3072]{0,1:T(8,128)(4,1)} %add_add_fusion) | copy-start | bytes 2359300
  151.9 8.7 copy-start
  160.6 86.7 %copy-start.5 = (pred[256,3072]{0,1:T(8,128)(4,1)S(1)}, pred[256,3072]{0,1:T(8,128)(4,1)}, u32[]{:S(2)}) copy-start(pred[256,3072]{0,1:T(8,128)(4,1)} %add_add_fusion) | copy-start | bytes 2359300
  160.6 86.7 %copy-start.7 = (f32[256,1024]{0,1:T(8,128)S(1)}, f32[256,1024]{0,1:T(8,128)}, u32[]{:S(2)}) copy-start(f32[256,1024]{0,1:T(8,128)} %copy.85) | copy-start | bytes 3145732
  307.6 81.3 %copy-start.6 = (f32[3072,2,128]{0,2,1:T(8,128)}, f32[3072,2,128]{0,2,1:T(8,128)S(1)}, u32[]{:S(2)}) copy-start(f32[3072,2,128]{0,2,1:T(8,128)S(1)} %convolution_bitcast_fusion) | copy-start | bytes 9437188
  307.7 34.6 %copy-start.3 = (f32[256,1024]{0,1:T(8,128)S(1)}, f32[256,1024]{0,1:T(8,128)}, u32[]{:S(2)}) copy-start(f32[256,1024]{0,1:T(8,128)} %copy.115) | copy-start | bytes 3145732
  394.7 5.5 copy-start.2
  394.7 728.2 %reduce-scatter.5.cloned.1.call-start = ((), (), s32[]{:S(2)}) async-start(), calls=%async_computation.9 | async-start | bytes 17039360 | tf_op jit(solution)/shard_map/reduce_scatter | solution.py:107
Sparse Core Ops, SparseCore 0:
  14.3 106.5 all-gather.4
  124.1 118.8 all-gather.2
  394.9 339.1 reduce-scatter.2
  736.4 386.5 reduce-scatter.4
where the time goes:
time: 1190 us; the launch traced here: 1180 us
  waiting for transfers between devices  810 us (68%)
  matrix products  167 us (14%)
  blocking collectives  115 us (10%)
  local copies, waits for them, and re-layouts  52.6 us (4%)
  other arithmetic  21.8 us (2%)
  between operations  17.2 us (1%)
    reduce_scatter x1, waiting for transfers between devices, shards(): lax.psum_scatter(value_gradient_total.reshape(seq_rows, width), 'ctx', sc...  332 us
    reduce_scatter x1, waiting for transfers between devices, shards(): lax.psum_scatter(key_gradient_total.reshape(seq_rows, width), 'ctx', scat...  313 us
    all_gather x1, waiting for transfers between devices, shards(): lax.all_gather(local_keys, 'ctx', axis=0, tiled=True)  86.8 us
    all_gather x1, waiting for transfers between devices, shards(): lax.all_gather(local_values, 'ctx', axis=0, tiled=True)  77.2 us
    all_to_all x1, blocking collectives, shards(): lax.all_to_all(owned_k, 'head', split_axis=0, concat_axis=1, tiled=True)  54.7 us
    all_to_all x1, blocking collectives, shards(): lax.all_to_all(owned_v, 'head', split_axis=0, concat_axis=1, tiled=True)  51.7 us
    dot_general x1, matrix products, shards(): jnp.einsum('hgts,thgd->shd', probs, cotangent_block, precision=highest)  34.7 us
    dot_general x1, matrix products, shards(): jnp.einsum('thgd,shd->hgts', cotangent_block, picked_values, precision=hi...  34.6 us
  transfers between devices with their start and end apart: 4, of which 4 were waited for; matrix products, arithmetic and copies ran while one was open for 7% of the time, Pallas kernels for 0%

commit v1 on v0

v1 whole, which is shorter than its diff:
```python
import math
import jax
import jax.numpy as jnp
from jax import lax
from jax.sharding import Mesh, PartitionSpec as P
from jax.experimental import pallas as pl
from jax.experimental.pallas import tpu as pltpu

W = 128
T = 256
BLK = 1024
NK = 3 * BLK
CH = 512
SCALE = 1.0 / math.sqrt(W)
LOG2E = math.log2(math.e)
LN2 = math.log(2.0)
BF = jnp.bfloat16
F32 = jnp.float32

def split(x):
    hi = x.astype(BF)
    return hi, (x - hi.astype(F32)).astype(BF)

def nn(a, b):
    return lax.dot_general(a, b, (((1,), (0,)), ((), ())), preferred_element_type=F32)

def nt(a, b):
    return lax.dot_general(a, b, (((1,), (1,)), ((), ())), preferred_element_type=F32)

def attn_kernel(info, q_ref, do_ref, kvs_ref, kvo_ref, o_ref, dq_ref, dkvs_ref, dkvo_ref,
                kc, vc, kt, vt, s_sc, phi, plo, oacc, oacc2):
    g = pl.program_id(0)
    qh = pl.program_id(1)
    kcol = pl.ds(pl.multiple_of(g * W, W), W)
    vcol = pl.ds(pl.multiple_of(2 * W + g * W, W), W)
    pieces = [(kvs_ref, (z, j), j * BLK + z * T) for j in range(2) for z in range(4)]
    pieces += [(kvo_ref, (z,), 2 * BLK + z * T) for z in range(4)]

    @pl.when(qh == 0)
    def _():
        for ref, idx, row in pieces:
            for col, cat, tr in ((kcol, kc, kt), (vcol, vc, vt)):
                x = ref[idx + (slice(None), col)]
                hi, lo = split(x)
                cat[row:row + T, 0:W] = hi
                cat[row:row + T, W:2 * W] = lo
                hit, lot = split(x.T)
                tr[0:W, row:row + T] = hit
                tr[W:2 * W, row:row + T] = lot

    qs = q_ref[...] * (SCALE * LOG2E)
    qhi, qlo = split(qs)
    qcat = jnp.concatenate([qhi, qhi, qlo, qlo], axis=1)

    def scores(c):
        k = kc[pl.ds(pl.multiple_of(c * CH, CH), CH), :]
        return nt(jnp.concatenate([k, k], axis=1), qcat)

    per = BLK // CH
    def sel_chunk(c, m):
        ok = info[2 + c // per] > 0
        s = jnp.where(ok, scores(c), -jnp.inf)
        s_sc[pl.ds(pl.multiple_of(c * CH, CH), CH), :] = s
        return jnp.maximum(m, jnp.max(s, axis=0, keepdims=True))

    def own_chunk(c, m):
        off = info[1] * T - (c - 2 * per) * CH
        d = lax.broadcasted_iota(jnp.int32, (CH, T), 0) - lax.broadcasted_iota(jnp.int32, (CH, T), 1)
        s = jnp.where(d <= off, scores(c), -jnp.inf)
        s_sc[pl.ds(pl.multiple_of(c * CH, CH), CH), :] = s
        return jnp.maximum(m, jnp.max(s, axis=0, keepdims=True))

    m = jnp.full((1, T), -jnp.inf, F32)
    m = lax.fori_loop(0, 2 * per, sel_chunk, m)
    m = lax.fori_loop(2 * per, 3 * per, own_chunk, m)

    oacc[...] = jnp.zeros_like(oacc)
    oacc2[...] = jnp.zeros_like(oacc2)

    def out_chunk(c, l):
        rows = pl.ds(pl.multiple_of(c * CH, CH), CH)
        p = jnp.exp2(s_sc[rows, :] - m)
        s_sc[rows, :] = p
        hi, lo = split(p)
        phi[rows, :] = hi
        plo[rows, :] = lo
        v = vt[:, rows]
        oacc[...] += nn(v, hi)
        oacc2[...] += nn(v[0:W], lo)
        return l + jnp.sum(p, axis=0, keepdims=True)

    l = lax.fori_loop(0, NK // CH, out_chunk, jnp.zeros((1, T), F32))
    inv = 1.0 / l
    ot = (oacc[0:W, :] + oacc[W:2 * W, :] + oacc2[...]) * inv
    o_ref[...] = ot.T
    dot = do_ref[...].T * inv
    rd = jnp.sum(dot * ot, axis=0, keepdims=True)
    dhi, dlo = split(dot.T)
    dcat = jnp.concatenate([dhi, dhi, dlo, dlo], axis=1)
    dc = jnp.concatenate([dhi, dlo], axis=1)
    dc2 = jnp.concatenate([dc, dc], axis=0)
    qc = jnp.concatenate([qhi, qlo], axis=1)
    qc2 = jnp.concatenate([qc, qc], axis=0)
    oacc[...] = jnp.zeros_like(oacc)
    oacc2[...] = jnp.zeros_like(oacc2)

    def grad_chunk(blk, sub):
        start = blk * BLK + sub * CH
        rows = pl.ds(pl.multiple_of(start, CH), CH)
        v = vc[rows, :]
        dp = nt(jnp.concatenate([v, v], axis=1), dcat)
        ds = s_sc[rows, :] * (dp - rd)
        hi, lo = split(ds)
        k = kt[:, rows]
        oacc[...] += nn(k, hi)
        oacc2[...] += nn(k[0:W], lo)
        dv = nn(jnp.concatenate([phi[rows, :], plo[rows, :]], axis=1), dc2)
        dk = nn(jnp.concatenate([hi, lo], axis=1), qc2)
        dv = dv[:, 0:W] + dv[:, W:2 * W]
        dk = (dk[:, 0:W] + dk[:, W:2 * W]) * LN2
        for u in range(CH // T):
            z = sub * (CH // T) + u
            piece = slice(u * T, (u + 1) * T)
            ref, idx = (dkvs_ref, (z, blk)) if blk < 2 else (dkvo_ref, (z,))
            for col, d in ((kcol, dk), (vcol, dv)):
                at = idx + (slice(None), col)

                @pl.when(qh == 0)
                def _(ref=ref, at=at, d=d, piece=piece):
                    ref[at] = d[piece]

                @pl.when(qh > 0)
                def _(ref=ref, at=at, d=d, piece=piece):
                    ref[at] += d[piece]

    for blk in range(3):
        @pl.loop(0, per)
        def _(sub, blk=blk):
            grad_chunk(blk, sub)
    dq_ref[...] = (oacc[0:W, :] + oacc[W:2 * W, :] + oacc2[...]).T * SCALE


def attention(info, q, do, kvs, kvo):
    heads = pl.BlockSpec((T, W), lambda g, h, *_: (0, g * 4 + h))
    whole = lambda a: pl.BlockSpec(a.shape, lambda g, h, *_: (0,) * a.ndim)
    return pl.pallas_call(
        attn_kernel,
        out_shape=(
            jax.ShapeDtypeStruct(q.shape, F32),
            jax.ShapeDtypeStruct(q.shape, F32),
            jax.ShapeDtypeStruct(kvs.shape, F32),
            jax.ShapeDtypeStruct(kvo.shape, F32),
        ),
        grid_spec=pltpu.PrefetchScalarGridSpec(
            num_scalar_prefetch=1,
            grid=(2, 4),
            in_specs=[heads, heads, whole(kvs), whole(kvo)],
            out_specs=(heads, heads, whole(kvs), whole(kvo)),
            scratch_shapes=[
                pltpu.VMEM((NK, 2 * W), BF),
                pltpu.VMEM((NK, 2 * W), BF),
                pltpu.VMEM((2 * W, NK), BF),
                pltpu.VMEM((2 * W, NK), BF),
                pltpu.VMEM((NK, T), F32),
                pltpu.VMEM((NK, T), BF),
                pltpu.VMEM((NK, T), BF),
                pltpu.VMEM((2 * W, T), F32),
                pltpu.VMEM((W, T), F32),
            ],
        ),
        compiler_params=pltpu.CompilerParams(
            dimension_semantics=("arbitrary", "arbitrary"), vmem_limit_bytes=60 << 20),
        cost_estimate=pl.CostEstimate(flops=5 * 2 * 2048 * NK * W * 3, transcendentals=2048 * NK, bytes_accessed=20 << 20),
    )(info, q, do, kvs, kvo)


GRID = ("y", "x")


def shards(queries, keys, values, cotangent, selected):
    core = lax.axis_index("head")
    block = lax.axis_index("y") * 4 + lax.axis_index("x")
    chosen = lax.dynamic_slice_in_dim(selected, block, 1, 0)[0, 1:]
    info = jnp.concatenate(
        [jnp.stack([block, lax.axis_index("z")]), (chosen >= 0).astype(jnp.int32)]
    )
    chosen = jnp.maximum(chosen, 0)
    swap = [(0, 1), (1, 0)]

    def columns(h):
        return jnp.concatenate(
            [lax.dynamic_slice_in_dim(a, h * 2 * W, 2 * W, 1) for a in (keys, values)], 1
        )

    mine, theirs = columns(core), lax.ppermute(columns(1 - core), "head", swap)
    kv = jnp.where(
        core == 0, jnp.concatenate([mine, theirs], 0), jnp.concatenate([theirs, mine], 0)
    )
    own = lax.all_gather(kv, "z", axis=0)
    every = lax.all_gather(kv, GRID, axis=0)
    quarter = jnp.stack(
        [lax.dynamic_index_in_dim(every, chosen[j], 0, keepdims=False) for j in range(2)]
    )
    picked = lax.all_gather(quarter, "z", axis=0)
    attended, grad_queries, grad_picked, grad_own = attention(
        info, queries, cotangent, picked, own
    )
    grad_picked = lax.psum_scatter(grad_picked, "z", scatter_dimension=0)
    grad_own = lax.psum_scatter(grad_own, "z", scatter_dimension=0)
    at = jnp.arange(16, dtype=jnp.int32)[:, None, None]
    spread = sum(jnp.where(at == chosen[j], grad_picked[j][None], 0.0) for j in range(2))
    grad_kv = lax.psum_scatter(spread, GRID, scatter_dimension=0) + grad_own
    half = T // 2
    keep = lax.dynamic_slice_in_dim(grad_kv, core * half, half, 0)
    back = lax.ppermute(
        lax.dynamic_slice_in_dim(grad_kv, (1 - core) * half, half, 0), "head", swap
    )

    def joined(cols):
        a, b = keep[:, cols], back[:, cols]
        return jnp.where(core == 0, jnp.concatenate([a, b], 1), jnp.concatenate([b, a], 1))

    return attended, grad_queries, joined(slice(0, 2 * W)), joined(slice(2 * W, 4 * W))


def solution(mesh):
    grid = Mesh(mesh.devices.reshape(4, 4, 4, 2), ("y", "x", "z", "head"))
    tokens = ("y", "x", "z")
    wide, narrow = P(tokens, "head"), P(tokens + ("head",), None)
    return jax.shard_map(
        shards,
        mesh=grid,
        in_specs=(wide, narrow, narrow, wide, P()),
        out_specs=(wide, wide, narrow, narrow),
        check_vma=False,
    )
```

time: 1190 us -> 445 us (0.37)
  waiting for transfers between devices: 810 us -> 310 us
  matrix products: 167 us -> 0 us
  blocking collectives: 115 us -> 0 us
  Pallas kernels: 0 us -> 97.5 us
  local copies, waits for them, and re-layouts: 52.6 us -> 4.44 us
    reduce_scatter x2, waiting for transfers between devices: 646 us -> 71.6 us  [the longest x1 45.5 us: shards(): grad_picked = lax.psum_scatter(grad_picked, 'z', scatter_dimension=0)]
    dot_general x6 -> x0, matrix products: 167 us -> none  [the longest x1 34.7 us: shards(): jnp.einsum('hgts,thgd->shd', probs, cotangent_block, precision=highest)]
    all_to_all x4 -> x0, blocking collectives: 115 us -> none  [the longest x1 54.7 us: shards(): lax.all_to_all(owned_k, 'head', split_axis=0, concat_axis=1, tiled=True)]
    pallas_call x0 -> x1, Pallas kernels: none -> 97.5 us  [attention(): pl.pallas_call(attn_kernel, out_shape=(jax.ShapeDtypeStruct(q.shape, F32)...]
    unnamed x4 -> x7, waiting for transfers between devices: 0.07 us -> 88 us
    unnamed x23 -> x2, local copies, waits for them, and re-layouts: 20.1 us -> 0.01 us
    all_gather x2 -> x3, waiting for transfers between devices: 164 us -> 148 us  [the longest x1 67.5 us: shards(): every = lax.all_gather(kv, GRID, axis=0)]
    another operation x2 -> x0, local copies, waits for them, and re-layouts: 15.3 us -> none
  transfers between devices with their start and end apart: 4 -> 8, of which waited for: 4 -> 8; matrix products, arithmetic and copies ran while one was open for 7% -> 2% of each run, Pallas kernels for 0% -> 0%
where the time goes in v1:
time: 445 us
  waiting for transfers between devices  310 us (70%)
  Pallas kernels  97.5 us (22%)
  between operations  18 us (4%)
  other arithmetic  11.2 us (3%)
    pallas_call x1, Pallas kernels, attention(): pl.pallas_call(attn_kernel, out_shape=(jax.ShapeDtypeStruct(q.shape, F32)...  97.5 us
    unnamed x7, waiting for transfers between devices  88 us
    all_gather x1, waiting for transfers between devices, shards(): every = lax.all_gather(kv, GRID, axis=0)  67.5 us
    all_gather x1, waiting for transfers between devices, shards(): picked = lax.all_gather(quarter, 'z', axis=0)  50.6 us
    reduce_scatter x1, waiting for transfers between devices, shards(): grad_picked = lax.psum_scatter(grad_picked, 'z', scatter_dimension=0)  45.5 us
    all_gather x1, waiting for transfers between devices, shards(): own = lax.all_gather(kv, 'z', axis=0)  30 us
    reduce_scatter x1, waiting for transfers between devices, shards(): grad_own = lax.psum_scatter(grad_own, 'z', scatter_dimension=0)  26.1 us
  transfers between devices with their start and end apart: 8, of which 8 were waited for; matrix products, arithmetic and copies ran while one was open for 2% of the time, Pallas kernels for 0%

profile of v1, /device:TPU:1, one launch (start us, length us, event | category | flops | bytes accessed | tf_op | source)
XLA Modules:
  0.0 444.9 jit_solution(7284374173078399711)
XLA Ops:
  7.2 1.1 constant_dynamic-slice_fusion.4
  8.4 1.5 collective-permute-start
  9.9 1.1 collective-permute-done
  11.1 0.8 maximum_select_fusion
  12.0 0.7 all-gather.7.cloned.1.call-update
  12.9 0.6 fusion.3
  17.3 67.5 %all-gather.5.cloned.1.call-done = f32[16,256,512]{2,1,0:T(8,128)} async-done(((f32[1,256,512]{2,1,0:T(8,128)}), f32[16,256,512]{2,1,0:T(8,128)}) %all-gather.5.cloned.1.call-update) | async-done | bytes 8388624 | tf_op jit(solution)/shard_map/all_gather | solution.py:200
  84.9 1.3 constant_dynamic-slice_fusion.1
  86.1 1.0 pad_maximum_fusion
  87.3 0.6 pad_add_fusion.info
  87.9 30.0 %all-gather.7.cloned.1.call-done.kvo_ref = f32[4,256,512]{2,1,0:T(8,128)} async-done(((f32[1,256,512]{2,1,0:T(8,128)}), f32[4,256,512]{2,1,0:T(8,128)}) %all-gather.7.cloned.1.call-update) | async-done | bytes 2097168 | tf_op jit(solution)/shard_map/all_gather | solution.py:199
  117.9 50.6 %all-gather.9.cloned.1.call-done = f32[8,256,512]{2,1,0:T(8,128)} async-done(((f32[2,256,512]{2,1,0:T(8,128)}), f32[8,256,512]{2,1,0:T(8,128)}) %all-gather.9.cloned.1.call-update) | async-done | bytes 4194320 | tf_op jit(solution)/shard_map/all_gather | solution.py:204
  168.5 97.5 %shard_map.84 = (f32[256,1024]{1,0:T(8,128)}, f32[256,1024]{1,0:T(8,128)}, f32[4,2,256,512]{3,2,1,0:T(8,128)}, f32[4,256,512]{2,1,0:T(8,128)}) custom-call(s32[4]{0:T(128)} %pad_add_fusion.info, f32[256,1024]{1,0:T(8,128)} %q_ref.1, f32[256,1024]{1,0:T(8,128)} %do_ref.1, f32[4,2,256,512]{3,2,1,0:T(8,128)} %bitcast.18, ...), custom_call_target="tpu_custom_call" | custom-call | flops 24159191040 | bytes 20971520 | tf_op jit(solution)/shard_map/pallas_call | solution.py:146
  266.7 1.3 iota_compare_fusion
  268.0 45.5 %reduce-scatter.6.cloned.1.call-done = f32[1,2,256,512]{3,2,1,0:T(8,128)} async-done(((f32[4,2,256,512]{3,2,1,0:T(8,128)}), f32[1,2,256,512]{3,2,1,0:T(8,128)}) %reduce-scatter.6.cloned.1.call-update) | async-done | bytes 1048592 | tf_op jit(solution)/shard_map/reduce_scatter | solution.py:208
  313.5 1.3 slice_bitcast_fusion.1
  314.8 4.5 %select_add_fusion = f32[16,256,512]{2,1,0:T(8,128)} fusion(f32[256,512]{1,0:T(8,128)S(1)} %get-tuple-element.15, f32[256,512]{1,0:T(8,128)S(1)} %get-tuple-element.14, pred[16]{0:T(512)(128)(4,1)S(1)} %get-tuple-element.32, pred[16]{0:T(512)(128)(4,1)S(1)} %get-tuple-element.33), kind=kLoop, calls=%fused_computation | loop fusion | flops 6291456 | bytes 9437216 | tf_op jit(solution)/shard_map/add | solution.py:211
  319.3 26.1 %reduce-scatter.8.cloned.1.call-done = f32[1,256,512]{2,1,0:T(8,128)} async-done(((f32[4,256,512]{2,1,0:T(8,128)}), f32[1,256,512]{2,1,0:T(8,128)}) %reduce-scatter.8.cloned.1.call-update) | async-done | bytes 524304 | tf_op jit(solution)/shard_map/reduce_scatter | solution.py:209
  345.4 86.7 %reduce-scatter.10.cloned.1.call-done = f32[1,256,512]{2,1,0:T(8,128)} async-done(((f32[16,256,512]{2,1,0:T(8,128)}), f32[1,256,512]{2,1,0:T(8,128)}) %reduce-scatter.10.cloned.1.call-update) | async-done | bytes 524304
  432.1 1.3 add.47
  433.5 2.0 collective-permute-start.1
  435.5 1.1 collective-permute-done.1
  436.6 0.7 maximum_select_fusion.2
  437.4 0.7 maximum_select_fusion.1
  (20 shorter events, 1.2 us)
Async XLA Ops:
  7.2 5.6 %copy-start = (s32[16,3]{0,1:T(4,128)S(1)}, s32[16,3]{0,1:T(4,128)}, u32[]{:S(2)}) copy-start(s32[16,3]{0,1:T(4,128)} %param.9) | copy-start | bytes 580
  7.2 77.7 %all-gather.5.cloned.1.call-start = ((), (), s32[]{:S(2)}) async-start(), calls=%async_computation.3 | async-start | bytes 8912896 | tf_op jit(solution)/shard_map/all_gather | solution.py:200
  8.4 2.7 collective-permute-start
  11.9 106.0 %all-gather.7.cloned.1.call-start = ((), (), s32[]{:S(2)}) async-start(), calls=%async_computation.4 | async-start | bytes 2621440 | tf_op jit(solution)/shard_map/all_gather | solution.py:199
  12.7 155.9 %all-gather.9.cloned.1.call-start = ((), (), s32[]{:S(2)}) async-start(), calls=%async_computation.7 | async-start | bytes 5242880 | tf_op jit(solution)/shard_map/all_gather | solution.py:204
  87.2 226.3 %reduce-scatter.6.cloned.1.call-start = ((), (), s32[]{:S(2)}) async-start(), calls=%async_computation.5 | async-start | bytes 5242880 | tf_op jit(solution)/shard_map/reduce_scatter | solution.py:208
  266.1 79.3 %reduce-scatter.8.cloned.1.call-start = ((), (), s32[]{:S(2)}) async-start(), calls=%async_computation.6 | async-start | bytes 2621440 | tf_op jit(solution)/shard_map/reduce_scatter | solution.py:209
  266.7 165.4 %reduce-scatter.10.cloned.1.call-start = ((), (), s32[]{:S(2)}) async-start(), calls=%async_computation.8 | async-start | bytes 8912896
  433.5 3.1 collective-permute-start.1
Sparse Core Ops, SparseCore 0:
  12.1 72.7 all-gather.4
  87.1 30.7 all-gather.6
  120.1 48.3 all-gather.8
  266.2 47.2 reduce-scatter.5
  315.9 29.4 reduce-scatter.7
  348.7 83.4 reduce-scatter.9

commit v2 on v1

v2 whole, which is shorter than its diff:
```python
import math

import jax
import jax.numpy as jnp
from jax import lax
from jax.experimental import pallas as pl
from jax.experimental.pallas import tpu as pltpu
from jax.sharding import Mesh, PartitionSpec as P

W = 128
T = 256
SEL = 8 * T
NK = 12 * T
CH = 512
SCALE = 1.0 / math.sqrt(W)
LOG2E = math.log2(math.e)
LN2 = math.log(2.0)
BF = jnp.bfloat16
F32 = jnp.float32


def split(x):
    hi = x.astype(BF)
    return hi, (x - hi.astype(F32)).astype(BF)


def nn(a, b):
    return lax.dot_general(a, b, (((1,), (0,)), ((), ())), preferred_element_type=F32)


def nt(a, b):
    return lax.dot_general(a, b, (((1,), (1,)), ((), ())), preferred_element_type=F32)


def attn_kernel(info, ql_ref, qr_ref, dl_ref, dr_ref, s0, s1, s2, s3, own_ref,
                ol_ref, or_ref, gl_ref, gr_ref, g0, g1, g2, g3, h0, h1, h2, h3,
                kc, vc, kt, vt, s_sc, phi, plo, oacc, oacc2, dk_acc, dv_acc):
    u = pl.program_id(0)
    qh = pl.program_id(1)
    z = info[0]
    head = info[1]
    quarter = jnp.where(u == 0, z, 3 - z)

    @pl.when((u == 0) & (qh == 0))
    def _():
        pieces = []
        for j in range(2):
            for x, ref in enumerate((s0, s1, s2, s3)):
                pieces.append((ref.at[0, j], ref.at[1, j], (j * 4 + x) * T))
        for c in range(4):
            cols = [pl.ds(pl.multiple_of(k + head * W, W), W) for k in (0, 2 * W)]
            pieces.append((own_ref.at[c, :, cols[0]], own_ref.at[c, :, cols[1]], SEL + c * T))
        for kref, vref, row in pieces:
            for ref, cat, tr in ((kref, kc, kt), (vref, vc, vt)):
                x = ref[...]
                hi, lo = split(x)
                cat[row:row + T, 0:W] = hi
                cat[row:row + T, W:2 * W] = lo
                hit, lot = split(x.T)
                tr[0:W, row:row + T] = hit
                tr[W:2 * W, row:row + T] = lot
        dk_acc[...] = jnp.zeros_like(dk_acc)
        dv_acc[...] = jnp.zeros_like(dv_acc)

    q = jnp.where(u == 0, ql_ref[...], qr_ref[...])
    do = jnp.where(u == 0, dl_ref[...], dr_ref[...])
    qhi, qlo = split(q * (SCALE * LOG2E))
    qcat = jnp.concatenate([qhi, qhi, qlo, qlo], axis=1)

    def sel_rows(c):
        return pl.ds(pl.multiple_of(c * CH, CH), CH)

    def own_rows(c):
        return pl.ds(pl.multiple_of(SEL + c * T, T), T)

    def scores(rows):
        k = kc[rows, :]
        return nt(jnp.concatenate([k, k], axis=1), qcat)

    def sel_scores(c, m):
        rows = sel_rows(c)
        s = jnp.where(info[2 + c // 2] > 0, scores(rows), -jnp.inf)
        s_sc[rows, :] = s
        return jnp.maximum(m, jnp.max(s, axis=0, keepdims=True))

    def own_scores(c, m):
        rows = own_rows(c)
        ahead = lax.broadcasted_iota(jnp.int32, (T, T), 0) - lax.broadcasted_iota(
            jnp.int32, (T, T), 1)
        s = jnp.where(ahead <= (quarter - c) * T, scores(rows), -jnp.inf)
        s_sc[rows, :] = s
        return jnp.maximum(m, jnp.max(s, axis=0, keepdims=True))

    m = jnp.full((1, T), -jnp.inf, F32)
    m = lax.fori_loop(0, SEL // CH, sel_scores, m)
    m = lax.fori_loop(0, quarter + 1, own_scores, m)

    oacc[...] = jnp.zeros_like(oacc)
    oacc2[...] = jnp.zeros_like(oacc2)

    def out(rows, l):
        p = jnp.exp2(s_sc[rows, :] - m)
        s_sc[rows, :] = p
        hi, lo = split(p)
        phi[rows, :] = hi
        plo[rows, :] = lo
        v = vt[:, rows]
        oacc[...] += nn(v, hi)
        oacc2[...] += nn(v[0:W], lo)
        return l + jnp.sum(p, axis=0, keepdims=True)

    l = jnp.zeros((1, T), F32)
    l = lax.fori_loop(0, SEL // CH, lambda c, l: out(sel_rows(c), l), l)
    l = lax.fori_loop(0, quarter + 1, lambda c, l: out(own_rows(c), l), l)
    inv = 1.0 / l
    ot = (oacc[0:W, :] + oacc[W:2 * W, :] + oacc2[...]) * inv
    dot = do.T * inv
    rd = jnp.sum(dot * ot, axis=0, keepdims=True)
    dhi, dlo = split(dot.T)
    dcat = jnp.concatenate([dhi, dhi, dlo, dlo], axis=1)
    dc = jnp.concatenate([dhi, dlo], axis=1)
    dc2 = jnp.concatenate([dc, dc], axis=0)
    qc = jnp.concatenate([qhi, qlo], axis=1)
    qc2 = jnp.concatenate([qc, qc], axis=0)
    oacc[...] = jnp.zeros_like(oacc)
    oacc2[...] = jnp.zeros_like(oacc2)

    def grads(rows):
        v = vc[rows, :]
        dp = nt(jnp.concatenate([v, v], axis=1), dcat)
        ds = s_sc[rows, :] * (dp - rd)
        hi, lo = split(ds)
        k = kt[:, rows]
        oacc[...] += nn(k, hi)
        oacc2[...] += nn(k[0:W], lo)
        dv = nn(jnp.concatenate([phi[rows, :], plo[rows, :]], axis=1), dc2)
        dk = nn(jnp.concatenate([hi, lo], axis=1), qc2)
        dv_acc[rows, :] += dv[:, 0:W] + dv[:, W:2 * W]
        dk_acc[rows, :] += dk[:, 0:W] + dk[:, W:2 * W]

    @pl.loop(0, SEL // CH)
    def _(c):
        grads(sel_rows(c))

    @pl.loop(0, quarter + 1)
    def _(c):
        grads(own_rows(c))

    dq = (oacc[0:W, :] + oacc[W:2 * W, :] + oacc2[...]).T * SCALE
    o = ot.T

    @pl.when(u == 0)
    def _():
        ol_ref[...] = o
        gl_ref[...] = dq

    @pl.when(u == 1)
    def _():
        or_ref[...] = o
        gr_ref[...] = dq

    @pl.when((u == 1) & (qh == 3))
    def _():
        for acc, k, mul in ((dk_acc, 0, LN2), (dv_acc, 1, 1.0)):
            for x, (ref, own) in enumerate(((g0, h0), (g1, h1), (g2, h2), (g3, h3))):
                for j in range(2):
                    row = (j * 4 + x) * T
                    ref[k, j] = acc[row:row + T, :] * mul
                own[k] = acc[own_rows(z ^ x), :] * mul


def attention(info, q, q_far, do, do_far, pieces, own):
    near = pl.BlockSpec((T, W), lambda u, h, i: (0, i[1] * 4 + h))
    far = pl.BlockSpec((T, W), lambda u, h, i: (0, h))
    first = pl.BlockSpec((T, W), lambda u, h, i: (0, jnp.where(u == 0, h, 3)))
    second = pl.BlockSpec((T, W), lambda u, h, i: (0, jnp.where(u == 0, 0, h)))
    whole = lambda shape: pl.BlockSpec(shape, lambda u, h, i: (0,) * len(shape))
    half = jax.ShapeDtypeStruct((T, 4 * W), F32)
    picked = (2, 2, T, W)
    grads = [jax.ShapeDtypeStruct(picked, F32)] * 4 + [jax.ShapeDtypeStruct((2, T, W), F32)] * 4
    return pl.pallas_call(
        attn_kernel,
        out_shape=[half] * 4 + grads,
        grid_spec=pltpu.PrefetchScalarGridSpec(
            num_scalar_prefetch=1,
            grid=(2, 4),
            in_specs=[near, far, near, far] + [whole(picked)] * 4 + [whole(own.shape)],
            out_specs=[first, second, first, second] + [whole(g.shape) for g in grads],
            scratch_shapes=[
                pltpu.VMEM((NK, 2 * W), BF),
                pltpu.VMEM((NK, 2 * W), BF),
                pltpu.VMEM((2 * W, NK), BF),
                pltpu.VMEM((2 * W, NK), BF),
                pltpu.VMEM((NK, T), F32),
                pltpu.VMEM((NK, T), BF),
                pltpu.VMEM((NK, T), BF),
                pltpu.VMEM((2 * W, T), F32),
                pltpu.VMEM((W, T), F32),
                pltpu.VMEM((NK, W), F32),
                pltpu.VMEM((NK, W), F32),
            ],
        ),
        compiler_params=pltpu.CompilerParams(
            dimension_semantics=("arbitrary", "arbitrary"), vmem_limit_bytes=40 << 20),
        cost_estimate=pl.CostEstimate(
            flops=30 * 2048 * NK * W, transcendentals=2048 * NK, bytes_accessed=20 << 20),
    )(info, q, q_far, do, do_far, *pieces, own)


def ring(axis, array):
    return [array] + [
        lax.ppermute(array, axis, [(i, (i + step) % 4) for i in range(4)]) for step in (1, 2, 3)
    ]


def mirror(array, flip):
    return lax.ppermute(array, "z", [(i, i ^ flip) for i in range(4)])


def choose(index, arrays):
    out = arrays[0]
    for i in range(1, len(arrays)):
        out = jnp.where(index == i, arrays[i], out)
    return out


def route(array, first, second, rows, columns):
    along = ring(first, array)
    here, there = lax.axis_index(first), lax.axis_index(second)

    def to(step):
        target = (there + step) % 4
        return jnp.stack(
            [choose((here - rows[target, j]) % 4, along) for j in range(2)]
        )

    arrived = [to(0)] + [
        lax.ppermute(to(step), second, [(i, (i + step) % 4) for i in range(4)])
        for step in (1, 2, 3)
    ]
    return [choose((there - columns[there, j]) % 4, [a[j] for a in arrived]) for j in range(2)]


def unroute(array, first, second, rows, columns):
    here, there = lax.axis_index(first), lax.axis_index(second)
    arrived = ring(second, array)
    parts = []
    for off in range(4):
        total = 0.0
        for step in range(4):
            source = (there - step) % 4
            for j in range(2):
                hit = (columns[source, j] == there) & ((here - rows[source, j]) % 4 == off)
                total = total + jnp.where(hit, arrived[step][j], 0.0)
        parts.append(total)
    out = parts[0]
    for off in range(1, 4):
        out = out + lax.ppermute(parts[off], first, [(i, (i - off) % 4) for i in range(4)])
    return out


def shards(queries, keys, values, cotangent, selected):
    core, z = lax.axis_index("head"), lax.axis_index("z")
    y, x = lax.axis_index("y"), lax.axis_index("x")
    head = z // 2
    table = selected[:, 1:]
    mine = lax.dynamic_index_in_dim(table, y * 4 + x, 0, keepdims=False)
    info = jnp.concatenate([jnp.stack([z, head]), (mine >= 0).astype(jnp.int32)])
    table = jnp.maximum(table, 0).reshape(4, 4, 2)
    by_row = lax.dynamic_index_in_dim(table, y, 0, keepdims=False)
    by_column = lax.dynamic_index_in_dim(table, x, 1, keepdims=False)
    swap = [(0, 1), (1, 0)]

    far = 1 - head
    q_far, do_far = (
        mirror(lax.dynamic_slice_in_dim(a, far * 4 * W, 4 * W, 1), 3)
        for a in (queries, cotangent)
    )

    def columns(h):
        return jnp.concatenate(
            [lax.dynamic_slice_in_dim(a, h * 2 * W, 2 * W, 1) for a in (keys, values)], 1
        )

    near, other = columns(core), lax.ppermute(columns(1 - core), "head", swap)
    kv = jnp.where(
        core == 0, jnp.concatenate([near, other], 0), jnp.concatenate([other, near], 0)
    )
    own = lax.all_gather(kv, "z", axis=0)
    k, v = (jnp.stack([kv[:, a:a + W], kv[:, a + W:a + 2 * W]]) for a in (0, 2 * W))
    k_args = ("y", "x", by_row // 4, by_row % 4)
    v_args = ("x", "y", by_column % 4, by_column // 4)
    got_k = route(k, *k_args)
    got_v = route(v, *v_args)

    def picked(h):
        return jnp.stack(
            [jnp.stack([lax.dynamic_index_in_dim(a, h, 0, keepdims=False) for a in got])
             for got in (got_k, got_v)]
        )

    same, cross = picked(head), picked(far)
    p1 = mirror(same, 1)
    p3 = mirror(cross, 3)
    p2 = mirror(p3, 1)
    out = attention(info, queries, q_far, cotangent, do_far, (same, p1, p2, p3), own)
    o_near, o_far, dq_near, dq_far = out[:4]
    o_far, dq_far = mirror(o_far, 3), mirror(dq_far, 3)

    def sides(a, b):
        return jnp.where(head == 0, jnp.concatenate([a, b], 1), jnp.concatenate([b, a], 1))

    def reduced(g):
        passed = mirror(g[3] + mirror(g[2], 1), 3)
        kept = g[0] + mirror(g[1], 1)
        return kept, passed

    def heads(kept, passed):
        return jnp.where(head == 0, jnp.stack([kept, passed]), jnp.stack([passed, kept]))

    kept, passed = reduced(out[4:8])
    grad_k = unroute(jnp.stack([heads(kept[0, j], passed[0, j]) for j in range(2)]), *k_args)
    grad_v = unroute(jnp.stack([heads(kept[1, j], passed[1, j]) for j in range(2)]), *v_args)
    kept, passed = reduced(out[8:12])
    grad_k = grad_k + heads(kept[0], passed[0])
    grad_v = grad_v + heads(kept[1], passed[1])
    grad_kv = jnp.concatenate([grad_k[0], grad_k[1], grad_v[0], grad_v[1]], 1)
    half = T // 2
    keep = lax.dynamic_slice_in_dim(grad_kv, core * half, half, 0)
    back = lax.ppermute(
        lax.dynamic_slice_in_dim(grad_kv, (1 - core) * half, half, 0), "head", swap
    )

    def joined(cols):
        a, b = keep[:, cols], back[:, cols]
        return jnp.where(core == 0, jnp.concatenate([a, b], 1), jnp.concatenate([b, a], 1))

    return (
        sides(o_near, o_far),
        sides(dq_near, dq_far),
        joined(slice(0, 2 * W)),
        joined(slice(2 * W, 4 * W)),
    )


def solution(mesh):
    grid = Mesh(mesh.devices.reshape(4, 4, 4, 2), ("y", "x", "z", "head"))
    tokens = ("y", "x", "z")
    wide, narrow = P(tokens, "head"), P(tokens + ("head",), None)
    return jax.shard_map(
        shards,
        mesh=grid,
        in_specs=(wide, narrow, narrow, wide, P()),
        out_specs=(wide, wide, narrow, narrow),
        check_vma=False,
    )
```

time: 445 us -> 345 us (0.78)
  waiting for transfers between devices: 310 us -> 104 us
  starting transfers between devices: 3.72 us -> 77.7 us
  between operations: 18 us -> 46.1 us
  local copies, waits for them, and re-layouts: 4.44 us -> 19.5 us
  Pallas kernels: 97.5 us -> 86.1 us
    all_gather x2 -> x0, waiting for transfers between devices: 118 us -> none  [the longest x1 67.5 us: shards(): every = lax.all_gather(kv, GRID, axis=0)]
    ppermute x1 -> x38, waiting for transfers between devices: 1.14 us -> 104 us  [the longest x13 53.1 us: mirror(): return lax.ppermute(array, 'z', [(i, i ^ flip) for i in range(4)])]
    unnamed x7 -> x1, waiting for transfers between devices: 88 us -> 0.02 us
    ppermute x1 -> x38, starting transfers between devices: 1.5 us -> 73.6 us  [the longest x6 26.7 us: route(): lax.ppermute(to(step), second, [(i, (i + step) % 4) for i in range(4)])]
    reduce_scatter x2 -> x0, waiting for transfers between devices: 71.6 us -> none  [the longest x1 45.5 us: shards(): grad_picked = lax.psum_scatter(grad_picked, 'z', scatter_dimension=0)]
    all_gather x1, waiting for transfers between devices: 30 us -> 0.01 us  [shards(): own = lax.all_gather(kv, 'z', axis=0)]
    unnamed x2 -> x32, local copies, waits for them, and re-layouts: 0.01 us -> 13.3 us
    pallas_call x1, Pallas kernels: 97.5 us -> 86.1 us  [attention(): pl.pallas_call(attn_kernel, out_shape=[half] * 4 + grads, grid_spec=pltpu...]
  transfers between devices with their start and end apart: 8 -> 40, of which waited for: 8 -> 15; matrix products, arithmetic and copies ran while one was open for 2% -> 4% of each run, Pallas kernels for 0% -> 0%
where the time goes in v2:
time: 345 us; the launch traced here: 344 us
  waiting for transfers between devices  104 us (30%)
  Pallas kernels  86.1 us (25%)
  starting transfers between devices  77.7 us (23%)
  between operations  46.1 us (13%)
  local copies, waits for them, and re-layouts  19.5 us (6%)
  other arithmetic  11.2 us (3%)
    pallas_call x1, Pallas kernels, attention(): pl.pallas_call(attn_kernel, out_shape=[half] * 4 + grads, grid_spec=pltpu...  86.1 us
    ppermute x13, waiting for transfers between devices, mirror(): return lax.ppermute(array, 'z', [(i, i ^ flip) for i in range(4)])  53.1 us
    ppermute x6, starting transfers between devices, route(): lax.ppermute(to(step), second, [(i, (i + step) % 4) for i in range(4)])  26.7 us
    ppermute x12, starting transfers between devices, ring(): lax.ppermute(array, axis, [(i, (i + step) % 4) for i in range(4)])  25.3 us
    ppermute x6, waiting for transfers between devices, route(): lax.ppermute(to(step), second, [(i, (i + step) % 4) for i in range(4)])  20 us
    ppermute x6, waiting for transfers between devices, unroute(): lax.ppermute(parts[off], first, [(i, (i - off) % 4) for i in range(4)])  17.5 us
    ppermute x13, starting transfers between devices, mirror(): return lax.ppermute(array, 'z', [(i, i ^ flip) for i in range(4)])  15 us
    unnamed x32, local copies, waits for them, and re-layouts  13.3 us
  transfers between devices with their start and end apart: 40, of which 15 were waited for; matrix products, arithmetic and copies ran while one was open for 4% of the time, Pallas kernels for 0%

profile of v2, /device:TPU:1, one launch (start us, length us, event | category | flops | bytes accessed | tf_op | source)
XLA Modules:
  0.0 344.2 jit_solution(16365093326883709905)
XLA Ops:
  17.3 2.6 collective-permute-start.9
  30.0 2.8 collective-permute-start.3
  36.9 2.7 collective-permute-start.13
  39.6 17.0 %collective-permute-start.12 = (f32[2,2,256,128]{3,2,1,0:T(8,128)S(1)}, f32[2,2,256,128]{3,2,1,0:T(8,128)S(1)}, u32[]{:S(2)}, u32[]{:S(2)}) collective-permute-start(f32[2,2,256,128]{3,2,1,0:T(8,128)S(1)} %pad_maximum_fusion.3), channel_id=1, source_target_pairs={{0,96},{32,0},{64,32},{96,64},{1,97},{33,1},{65,33},{97,65},{2,98}... | collective-permute-start | bytes 1572872 | tf_op jit(solution)/shard_map/ppermute | solution.py:238
  63.0 6.0 %collective-permute-done.13 = f32[2,2,256,128]{3,2,1,0:T(8,128)S(1)} collective-permute-done((f32[2,2,256,128]{3,2,1,0:T(8,128)S(1)}, f32[2,2,256,128]{3,2,1,0:T(8,128)S(1)}, u32[]{:S(2)}, u32[]{:S(2)}) %collective-permute-start.13) | collective-permute-done | bytes 524320 | tf_op jit(solution)/shard_map/ppermute | solution.py:238
  69.3 11.1 %collective-permute-done.7 = f32[2,2,256,128]{3,2,1,0:T(8,128)S(1)} collective-permute-done((f32[2,2,256,128]{3,2,1,0:T(8,128)S(1)}, f32[2,2,256,128]{3,2,1,0:T(8,128)S(1)}, u32[]{:S(2)}, u32[]{:S(2)}) %collective-permute-start.7) | collective-permute-done | bytes 524320 | tf_op jit(solution)/shard_map/ppermute | solution.py:238
  80.4 2.5 collective-permute-done.6
  83.3 3.8 %collective-permute-start.16 = (f32[2,2,256,128]{3,2,1,0:T(8,128)S(1)}, f32[2,2,256,128]{3,2,1,0:T(8,128)S(1)}, u32[]{:S(2)}, u32[]{:S(2)}) collective-permute-start(f32[2,2,256,128]{3,2,1,0:T(8,128)S(1)} %pad_maximum_fusion.7), channel_id=1, source_target_pairs={{0,6},{2,4},{4,2},{6,0},{1,7},{3,5},{5,3},{7,1},{8,14},{10,12},{12... | collective-permute-start | bytes 1572872 | tf_op jit(solution)/shard_map/ppermute | solution.py:217
  91.7 6.1 %collective-permute-done.16.s3 = f32[2,2,256,128]{3,2,1,0:T(8,128)S(1)} collective-permute-done((f32[2,2,256,128]{3,2,1,0:T(8,128)S(1)}, f32[2,2,256,128]{3,2,1,0:T(8,128)S(1)}, u32[]{:S(2)}, u32[]{:S(2)}) %collective-permute-start.16) | collective-permute-done | bytes 524320 | tf_op jit(solution)/shard_map/ppermute | solution.py:217
  98.9 10.2 %collective-permute-done.qr_ref = f32[256,512]{1,0:T(8,128)S(1)} collective-permute-done((f32[256,512]{1,0:T(8,128)}, f32[256,512]{1,0:T(8,128)S(1)}, u32[]{:S(2)}, u32[]{:S(2)}) %collective-permute-start) | collective-permute-done | bytes 524320 | tf_op jit(solution)/shard_map/ppermute | solution.py:217
  109.8 10.4 %collective-permute-done.1.dr_ref = f32[256,512]{1,0:T(8,128)S(1)} collective-permute-done((f32[256,512]{1,0:T(8,128)}, f32[256,512]{1,0:T(8,128)S(1)}, u32[]{:S(2)}, u32[]{:S(2)}) %collective-permute-start.1) | collective-permute-done | bytes 524320 | tf_op jit(solution)/shard_map/ppermute | solution.py:217
  131.9 86.1 %shard_map.84 = (f32[256,512]{1,0:T(8,128)S(1)}, f32[256,512]{1,0:T(8,128)S(1)}, f32[256,512]{1,0:T(8,128)S(1)}, f32[256,512]{1,0:T(8,128)S(1)}, f32[2,2,256,128...) custom-call(s32[4]{0:T(128)S(1)} %pad_add_fusion.info, ...), custom_call_target="tpu_custom_call" | custom-call | flops 24159191040 | bytes 20971520 | tf_op jit(solution)/shard_map/pallas_call | solution.py:181
  221.0 8.3 %collective-permute-done.21 = f32[2,2,256,128]{3,2,1,0:T(8,128)S(1)} collective-permute-done((f32[2,2,256,128]{3,2,1,0:T(8,128)S(1)}, f32[2,2,256,128]{3,2,1,0:T(8,128)S(1)}, u32[]{:S(2)}, u32[]{:S(2)}) %collective-permute-start.21) | collective-permute-done | bytes 524320 | tf_op jit(solution)/shard_map/ppermute | solution.py:217
  251.0 2.1 collective-permute-start.19
  257.3 18.0 %collective-permute-done.31 = f32[2,256,128]{2,1,0:T(8,128)S(1)} collective-permute-done((f32[2,256,128]{2,1,0:T(8,128)S(1)}, f32[2,256,128]{2,1,0:T(8,128)S(1)}, u32[]{:S(2)}, u32[]{:S(2)}) %collective-permute-start.31) | collective-permute-done | bytes 262176 | tf_op jit(solution)/shard_map/ppermute | solution.py:217
  275.5 8.0 %collective-permute-start.25 = (f32[2,2,256,128]{3,2,1,0:T(8,128)S(1)}, f32[2,2,256,128]{3,2,1,0:T(8,128)S(1)}, u32[]{:S(2)}, u32[]{:S(2)}) collective-permute-start(f32[2,2,256,128]{3,2,1,0:T(8,128)S(1)} %pad_maximum_fusion.8), channel_id=1, source_target_pairs={{0,24},{8,0},{16,8},{24,16},{1,25},{9,1},{17,9},{25,17},{2,26},{10... | collective-permute-start | bytes 1572872 | tf_op jit(solution)/shard_map/ppermute | solution.py:212
  283.6 2.2 collective-permute-start.24
  285.7 7.2 %collective-permute-start.23 = (f32[2,2,256,128]{3,2,1,0:T(8,128)S(1)}, f32[2,2,256,128]{3,2,1,0:T(8,128)S(1)}, u32[]{:S(2)}, u32[]{:S(2)}) collective-permute-start(f32[2,2,256,128]{3,2,1,0:T(8,128)S(1)} %pad_maximum_fusion.8), channel_id=1, source_target_pairs={{0,8},{8,16},{16,24},{24,0},{1,9},{9,17},{17,25},{25,1},{2,10},{10... | collective-permute-start | bytes 1572872 | tf_op jit(solution)/shard_map/ppermute | solution.py:212
  295.5 12.4 %collective-permute-done.23 = f32[2,2,256,128]{3,2,1,0:T(8,128)S(1)} collective-permute-done((f32[2,2,256,128]{3,2,1,0:T(8,128)S(1)}, f32[2,2,256,128]{3,2,1,0:T(8,128)S(1)}, u32[]{:S(2)}, u32[]{:S(2)}) %collective-permute-start.23) | collective-permute-done | bytes 524320 | tf_op jit(solution)/shard_map/ppermute | solution.py:212
  308.4 6.7 %collective-permute-done.37 = f32[2,256,128]{2,1,0:T(8,128)S(1)} collective-permute-done((f32[2,256,128]{2,1,0:T(8,128)S(1)}, f32[2,256,128]{2,1,0:T(8,128)S(1)}, u32[]{:S(2)}, u32[]{:S(2)}) %collective-permute-start.37) | collective-permute-done | bytes 262176 | tf_op jit(solution)/shard_map/ppermute | solution.py:258
  317.2 3.0 collective-permute-start.27
  320.5 2.3 collective-permute-done.28
  322.8 6.4 %collective-permute-done.27 = f32[2,256,128]{2,1,0:T(8,128)S(1)} collective-permute-done((f32[2,256,128]{2,1,0:T(8,128)S(1)}, f32[2,256,128]{2,1,0:T(8,128)S(1)}, u32[]{:S(2)}, u32[]{:S(2)}) %collective-permute-start.27) | collective-permute-done | bytes 262176 | tf_op jit(solution)/shard_map/ppermute | solution.py:258
  329.5 4.0 %collective-permute-start.38 = (f32[128,512]{1,0:T(8,128)S(1)}, f32[128,512]{1,0:T(8,128)S(1)}, u32[]{:S(2)}, u32[]{:S(2)}) collective-permute-start(f32[128,512]{1,0:T(8,128)S(1)} %constant_dynamic-slice_fusion.1), channel_id=1, source_target_pairs={{0,1},{1,0},{2,3},{3,2},{4,5},{5,4},{6,7},{7,6},{8,9},{9,8},{10,11... | collective-permute-start | bytes 786440 | tf_op jit(solution)/shard_map/ppermute | solution.py:330
  (166 shorter events, 56.0 us)
Async XLA Ops:
  7.2 115.5 %all-gather.2.cloned.1.call-start = ((), (), s32[]{:S(2)}) async-start(), calls=%async_computation | async-start | bytes 2621440 | tf_op jit(solution)/shard_map/all_gather | solution.py:289
  32.8 23.9 %collective-permute-start.4 = (f32[2,256,128]{2,1,0:T(8,128)S(1)}, f32[2,256,128]{2,1,0:T(8,128)S(1)}, u32[]{:S(2)}, u32[]{:S(2)}) collective-permute-start(f32[2,256,128]{2,1,0:T(8,128)S(1)} %pad_maximum_fusion.12), channel_id=1, source_target_pairs={{0,64},{32,96},{64,0},{96,32},{1,65},{33,97},{65,1},{97,33},{2,66}... | collective-permute-start | bytes 786440 | tf_op jit(solution)/shard_map/ppermute | solution.py:212
  34.0 22.7 %collective-permute-start.5 = (f32[2,256,128]{2,1,0:T(8,128)S(1)}, f32[2,256,128]{2,1,0:T(8,128)S(1)}, u32[]{:S(2)}, u32[]{:S(2)}) collective-permute-start(f32[2,256,128]{2,1,0:T(8,128)S(1)} %pad_maximum_fusion.12), channel_id=1, source_target_pairs={{0,32},{32,64},{64,96},{96,0},{1,33},{33,65},{65,97},{97,1},{2,34}... | collective-permute-start | bytes 786440 | tf_op jit(solution)/shard_map/ppermute | solution.py:212
  35.4 25.6 %collective-permute-start.14 = (f32[2,2,256,128]{3,2,1,0:T(8,128)S(1)}, f32[2,2,256,128]{3,2,1,0:T(8,128)S(1)}, u32[]{:S(2)}, u32[]{:S(2)}) collective-permute-start(f32[2,2,256,128]{3,2,1,0:T(8,128)S(1)} %pad_maximum_fusion.5), channel_id=1, source_target_pairs={{0,32},{32,64},{64,96},{96,0},{1,33},{33,65},{65,97},{97,1},{2,34}... | collective-permute-start | bytes 1572872 | tf_op jit(solution)/shard_map/ppermute | solution.py:238
  36.9 32.2 %collective-permute-start.13 = (f32[2,2,256,128]{3,2,1,0:T(8,128)S(1)}, f32[2,2,256,128]{3,2,1,0:T(8,128)S(1)}, u32[]{:S(2)}, u32[]{:S(2)}) collective-permute-start(f32[2,2,256,128]{3,2,1,0:T(8,128)S(1)} %pad_maximum_fusion.4), channel_id=1, source_target_pairs={{0,64},{32,96},{64,0},{96,32},{1,65},{33,97},{65,1},{97,33},{2,66}... | collective-permute-start | bytes 1572872 | tf_op jit(solution)/shard_map/ppermute | solution.py:238
  39.6 29.4 %collective-permute-start.12 = (f32[2,2,256,128]{3,2,1,0:T(8,128)S(1)}, f32[2,2,256,128]{3,2,1,0:T(8,128)S(1)}, u32[]{:S(2)}, u32[]{:S(2)}) collective-permute-start(f32[2,2,256,128]{3,2,1,0:T(8,128)S(1)} %pad_maximum_fusion.3), channel_id=1, source_target_pairs={{0,96},{32,0},{64,32},{96,64},{1,97},{33,1},{65,33},{97,65},{2,98}... | collective-permute-start | bytes 1572872 | tf_op jit(solution)/shard_map/ppermute | solution.py:238
  58.5 21.9 %collective-permute-start.7 = (f32[2,2,256,128]{3,2,1,0:T(8,128)S(1)}, f32[2,2,256,128]{3,2,1,0:T(8,128)S(1)}, u32[]{:S(2)}, u32[]{:S(2)}) collective-permute-start(f32[2,2,256,128]{3,2,1,0:T(8,128)S(1)} %pad_maximum_fusion.1), channel_id=1, source_target_pairs={{0,16},{8,24},{16,0},{24,8},{1,17},{9,25},{17,1},{25,9},{2,18},{10... | collective-permute-start | bytes 1572872 | tf_op jit(solution)/shard_map/ppermute | solution.py:238
  61.0 21.9 %collective-permute-start.6 = (f32[2,2,256,128]{3,2,1,0:T(8,128)S(1)}, f32[2,2,256,128]{3,2,1,0:T(8,128)S(1)}, u32[]{:S(2)}, u32[]{:S(2)}) collective-permute-start(f32[2,2,256,128]{3,2,1,0:T(8,128)S(1)} %pad_maximum_fusion), channel_id=1, source_target_pairs={{0,24},{8,0},{16,8},{24,16},{1,25},{9,1},{17,9},{25,17},{2,26},{10... | collective-permute-start | bytes 1572872 | tf_op jit(solution)/shard_map/ppermute | solution.py:238
  88.0 21.1 %collective-permute-start = (f32[256,512]{1,0:T(8,128)}, f32[256,512]{1,0:T(8,128)S(1)}, u32[]{:S(2)}, u32[]{:S(2)}) collective-permute-start(f32[256,512]{1,0:T(8,128)} %constant_dynamic-slice_fusion.41), channel_id=1, source_target_pairs={{0,6},{2,4},{4,2},{6,0},{1,7},{3,5},{5,3},{7,1},{8,14},{10,12},{12... | collective-permute-start | bytes 1572872 | tf_op jit(solution)/shard_map/ppermute | solution.py:217
  89.7 30.6 %collective-permute-start.1 = (f32[256,512]{1,0:T(8,128)}, f32[256,512]{1,0:T(8,128)S(1)}, u32[]{:S(2)}, u32[]{:S(2)}) collective-permute-start(f32[256,512]{1,0:T(8,128)} %constant_dynamic-slice_fusion.40), channel_id=1, source_target_pairs={{0,6},{2,4},{4,2},{6,0},{1,7},{3,5},{5,3},{7,1},{8,14},{10,12},{12... | collective-permute-start | bytes 1572872 | tf_op jit(solution)/shard_map/ppermute | solution.py:217
  91.6 29.5 %collective-permute-start.15 = (f32[2,2,256,128]{3,2,1,0:T(8,128)S(1)}, f32[2,2,256,128]{3,2,1,0:T(8,128)S(1)}, u32[]{:S(2)}, u32[]{:S(2)}) collective-permute-start(f32[2,2,256,128]{3,2,1,0:T(8,128)S(1)} %pad_maximum_fusion.6.s0), channel_id=1, source_target_pairs={{0,2},{2,0},{4,6},{6,4},{1,3},{3,1},{5,7},{7,5},{8,10},{10,8},{12,... | collective-permute-start | bytes 1572872 | tf_op jit(solution)/shard_map/ppermute | solution.py:217
  97.8 24.1 %collective-permute-start.17 = (f32[2,2,256,128]{3,2,1,0:T(8,128)S(1)}, f32[2,2,256,128]{3,2,1,0:T(8,128)S(1)}, u32[]{:S(2)}, u32[]{:S(2)}) collective-permute-start(f32[2,2,256,128]{3,2,1,0:T(8,128)S(1)} %collective-permute-done.16.s3), channel_id=1, source_target_pairs={{0,2},{2,0},{4,6},{6,4},{1,3},{3,1},{5,7},{7,5},{8,10},{10,8},{12,... | collective-permute-start | bytes 1572872 | tf_op jit(solution)/shard_map/ppermute | solution.py:217
  218.0 37.7 %collective-permute-start.20 = (f32[2,2,256,128]{3,2,1,0:T(8,128)}, f32[2,2,256,128]{3,2,1,0:T(8,128)S(1)}, u32[]{:S(2)}, u32[]{:S(2)}) collective-permute-start(f32[2,2,256,128]{3,2,1,0:T(8,128)} %get-tuple-element.21), channel_id=1, source_target_pairs={{0,2},{2,0},{4,6},{6,4},{1,3},{3,1},{5,7},{7,5},{8,10},{10,8},{12,... | collective-permute-start | bytes 1572872 | tf_op jit(solution)/shard_map/ppermute | solution.py:217
  219.5 31.5 %collective-permute-start.30 = (f32[2,256,128]{2,1,0:T(8,128)}, f32[2,256,128]{2,1,0:T(8,128)}, u32[]{:S(2)}, u32[]{:S(2)}) collective-permute-start(f32[2,256,128]{2,1,0:T(8,128)} %get-tuple-element.27), channel_id=1, source_target_pairs={{0,2},{2,0},{4,6},{6,4},{1,3},{3,1},{5,7},{7,5},{8,10},{10,8},{12,... | collective-permute-start | bytes 786440 | tf_op jit(solution)/shard_map/ppermute | solution.py:217
  219.5 34.5 %collective-permute-start.29 = (f32[2,256,128]{2,1,0:T(8,128)S(1)}, f32[2,256,128]{2,1,0:T(8,128)}, u32[]{:S(2)}, u32[]{:S(2)}) collective-permute-start(f32[2,256,128]{2,1,0:T(8,128)S(1)} %get-tuple-element.25), channel_id=1, source_target_pairs={{0,2},{2,0},{4,6},{6,4},{1,3},{3,1},{5,7},{7,5},{8,10},{10,8},{12,... | collective-permute-start | bytes 786440 | tf_op jit(solution)/shard_map/ppermute | solution.py:217
  230.1 25.8 %collective-permute-start.22 = (f32[2,2,256,128]{3,2,1,0:T(8,128)}, f32[2,2,256,128]{3,2,1,0:T(8,128)}, u32[]{:S(2)}, u32[]{:S(2)}) collective-permute-start(f32[2,2,256,128]{3,2,1,0:T(8,128)} %add.735), channel_id=1, source_target_pairs={{0,6},{2,4},{4,2},{6,0},{1,7},{3,5},{5,3},{7,1},{8,14},{10,12},{12... | collective-permute-start | bytes 1572872 | tf_op jit(solution)/shard_map/ppermute | solution.py:217
  250.3 83.2 %collective-permute-start.18 = (f32[256,512]{1,0:T(8,128)}, f32[256,512]{1,0:T(8,128)S(1)}, u32[]{:S(2)}, u32[]{:S(2)}) collective-permute-start(f32[256,512]{1,0:T(8,128)} %copy-done.5), channel_id=1, source_target_pairs={{0,6},{2,4},{4,2},{6,0},{1,7},{3,5},{5,3},{7,1},{8,14},{10,12},{12... | collective-permute-start | bytes 1572872 | tf_op jit(solution)/shard_map/ppermute | solution.py:217
  251.0 83.7 %collective-permute-start.19 = (f32[256,512]{1,0:T(8,128)S(1)}, f32[256,512]{1,0:T(8,128)S(1)}, u32[]{:S(2)}, u32[]{:S(2)}) collective-permute-start(f32[256,512]{1,0:T(8,128)S(1)} %get-tuple-element.19), channel_id=1, source_target_pairs={{0,6},{2,4},{4,2},{6,0},{1,7},{3,5},{5,3},{7,1},{8,14},{10,12},{12... | collective-permute-start | bytes 1572872 | tf_op jit(solution)/shard_map/ppermute | solution.py:217
  254.0 21.3 %collective-permute-start.31 = (f32[2,256,128]{2,1,0:T(8,128)S(1)}, f32[2,256,128]{2,1,0:T(8,128)S(1)}, u32[]{:S(2)}, u32[]{:S(2)}) collective-permute-start(f32[2,256,128]{2,1,0:T(8,128)S(1)} %add.780), channel_id=1, source_target_pairs={{0,6},{2,4},{4,2},{6,0},{1,7},{3,5},{5,3},{7,1},{8,14},{10,12},{12... | collective-permute-start | bytes 786440 | tf_op jit(solution)/shard_map/ppermute | solution.py:217
  257.2 18.4 %collective-permute-start.34 = (f32[2,2,256,128]{3,2,1,0:T(8,128)S(1)}, f32[2,2,256,128]{3,2,1,0:T(8,128)S(1)}, u32[]{:S(2)}, u32[]{:S(2)}) collective-permute-start(f32[2,2,256,128]{3,2,1,0:T(8,128)S(1)} %pad_maximum_fusion.9), channel_id=1, source_target_pairs={{0,96},{32,0},{64,32},{96,64},{1,97},{33,1},{65,33},{97,65},{2,98}... | collective-permute-start | bytes 1572872 | tf_op jit(solution)/shard_map/ppermute | solution.py:212
  257.2 26.3 %collective-permute-start.33 = (f32[2,2,256,128]{3,2,1,0:T(8,128)S(1)}, f32[2,2,256,128]{3,2,1,0:T(8,128)S(1)}, u32[]{:S(2)}, u32[]{:S(2)}) collective-permute-start(f32[2,2,256,128]{3,2,1,0:T(8,128)S(1)} %pad_maximum_fusion.9), channel_id=1, source_target_pairs={{0,64},{32,96},{64,0},{96,32},{1,65},{33,97},{65,1},{97,33},{2,66}... | collective-permute-start | bytes 1572872 | tf_op jit(solution)/shard_map/ppermute | solution.py:212
  285.7 22.2 %collective-permute-start.23 = (f32[2,2,256,128]{3,2,1,0:T(8,128)S(1)}, f32[2,2,256,128]{3,2,1,0:T(8,128)S(1)}, u32[]{:S(2)}, u32[]{:S(2)}) collective-permute-start(f32[2,2,256,128]{3,2,1,0:T(8,128)S(1)} %pad_maximum_fusion.8), channel_id=1, source_target_pairs={{0,8},{8,16},{16,24},{24,0},{1,9},{9,17},{17,25},{25,1},{2,10},{10... | collective-permute-start | bytes 1572872 | tf_op jit(solution)/shard_map/ppermute | solution.py:212
  293.5 21.7 %collective-permute-start.37 = (f32[2,256,128]{2,1,0:T(8,128)S(1)}, f32[2,256,128]{2,1,0:T(8,128)S(1)}, u32[]{:S(2)}, u32[]{:S(2)}) collective-permute-start(f32[2,256,128]{2,1,0:T(8,128)S(1)} %bitcast_add_fusion), channel_id=1, source_target_pairs={{0,8},{8,16},{16,24},{24,0},{1,9},{9,17},{17,25},{25,1},{2,10},{10... | collective-permute-start | bytes 786440 | tf_op jit(solution)/shard_map/ppermute | solution.py:258
  294.3 22.9 %collective-permute-start.36 = (f32[2,256,128]{2,1,0:T(8,128)S(1)}, f32[2,256,128]{2,1,0:T(8,128)S(1)}, u32[]{:S(2)}, u32[]{:S(2)}) collective-permute-start(f32[2,256,128]{2,1,0:T(8,128)S(1)} %bitcast_add_fusion.6), channel_id=1, source_target_pairs={{0,16},{8,24},{16,0},{24,8},{1,17},{9,25},{17,1},{25,9},{2,18},{10... | collective-permute-start | bytes 786440 | tf_op jit(solution)/shard_map/ppermute | solution.py:258
  (32 other events, 224.5 us)
Sparse Core Ops, SparseCore 0:
  34.1 33.2 all-gather.1

commit v3 on v0

v3 whole, which is shorter than its diff:
```python
import math

import jax
import jax.numpy as jnp
from jax import lax
from jax.experimental import pallas as pl
from jax.experimental.pallas import tpu as pltpu
from jax.sharding import Mesh, PartitionSpec as P

W = 128
T = 256

SCALE = 1.0 / math.sqrt(W)
LOG2E = math.log2(math.e)
LN2 = math.log(2.0)
BF = jnp.bfloat16
F32 = jnp.float32
BLK = 4 * T
HP = 2
STEPS = 4 // HP
R = HP * T

def split(x):
    hi = x.astype(BF)
    return hi, (x - hi.astype(F32)).astype(BF)

def twice(x, axis):
    return jnp.concatenate([x, x], axis=axis)

def mm(a, b):
    return lax.dot_general(a, b, (((1,), (0,)), ((), ())), preferred_element_type=F32)

def turned(x):
    return jnp.concatenate([x[:, i * W:(i + 1) * W].T for i in range(HP)], axis=1)

def upright(x):
    return jnp.concatenate([x[:, i * T:(i + 1) * T].T for i in range(HP)], axis=1)

def stacked(x):
    return jnp.concatenate([x[:, i * W:(i + 1) * W] for i in range(HP)], axis=0)

def left(x):
    hi, lo = split(x)
    return jnp.concatenate([hi, hi, lo, lo], axis=0)

def right(x):
    hi, lo = split(x)
    return twice(jnp.concatenate([hi, lo], axis=1), 0)

def fill(ref, rows, cat, tr):
    x = ref[...]
    hi, lo = split(x)
    if cat is not None:
        cat[rows, 0:W] = hi
        cat[rows, W:2 * W] = lo
    if tr is not None:
        hit, lot = split(x.T)
        tr[0:W, rows] = hit
        tr[W:2 * W, rows] = lot

def values_sum(tr, hi, lo):
    a = mm(tr, hi)
    return a[0:W] + a[W:2 * W] + mm(tr[0:W], lo)

def halves(x):
    return x[:, 0:W] + x[:, W:2 * W]

def own_refs(own_ref, head, c):
    return [own_ref.at[c, i, head] for i in range(2)]

def near_far(u, near, far):
    return jnp.where(u == 0, near[...], far[...])

def own_forward(info, ql_ref, qr_ref, own_ref, p_ref, m_ref, l_ref, ot_ref, kc, vt):
    u = pl.program_id(0)

    @pl.when((u == 0) & (pl.program_id(1) == 0))
    def _():
        for c in range(4):
            k, v = own_refs(own_ref, info[1], c)
            fill(k, slice(c * T, (c + 1) * T), kc, None)
            fill(v, slice(c * T, (c + 1) * T), None, vt)

    quarter = jnp.where(u == 0, info[0], 3 - info[0])
    q = left(turned(near_far(u, ql_ref, qr_ref)) * (SCALE * LOG2E))
    s = mm(twice(kc[...], 1), q)
    token = lax.broadcasted_iota(jnp.int32, (BLK, R), 1) & (T - 1)
    ahead = lax.broadcasted_iota(jnp.int32, (BLK, R), 0) - token
    s = jnp.where(ahead <= quarter * T, s, -jnp.inf)
    m = jnp.max(s, axis=0, keepdims=True)
    p = jnp.exp2(s - m)
    p_ref[0] = p
    m_ref[0] = m
    l_ref[0] = jnp.sum(p, axis=0, keepdims=True)
    hi, lo = split(p)
    ot_ref[0] = values_sum(vt[...], hi, lo)

def picked(info, ql_ref, qr_ref, dl_ref, dr_ref, s00, s01, s02, s03, s10, s11, s12, s13,
           m0_ref, l0_ref, ot0_ref, ol_ref, or_ref, dq_ref, c_ref, rd_ref,
           g00, g01, g02, g03, g10, g11, g12, g13,
           kc, vc, kt, vt, s_sc, phi, plo, dk_acc, dv_acc):
    u, step = pl.program_id(0), pl.program_id(1)
    pieces = ((s00, s01, s02, s03), (s10, s11, s12, s13))

    @pl.when((u == 0) & (step == 0))
    def _():
        for j in range(2):
            for x in range(4):
                rows = slice((j * 4 + x) * T, (j * 4 + x + 1) * T)
                fill(pieces[j][x].at[0], rows, kc, kt)
                fill(pieces[j][x].at[1], rows, vc, vt)
        dk_acc[...] = jnp.zeros_like(dk_acc)
        dv_acc[...] = jnp.zeros_like(dv_acc)

    q = near_far(u, ql_ref, qr_ref) * (SCALE * LOG2E)
    do = near_far(u, dl_ref, dr_ref)
    qt = left(turned(q))
    m0 = m0_ref[0]
    m = m0
    for j in range(2):
        rows = slice(j * BLK, (j + 1) * BLK)
        s = mm(twice(kc[rows, :], 1), qt)
        s = jnp.where(info[2 + j] > 0, s, -jnp.inf)
        s_sc[rows, :] = s
        m = jnp.maximum(m, jnp.max(s, axis=0, keepdims=True))
    shrink = jnp.exp2(m0 - m)
    l = l0_ref[0] * shrink
    ot = ot0_ref[0] * shrink
    for j in range(2):
        rows = slice(j * BLK, (j + 1) * BLK)
        p = jnp.exp2(s_sc[rows, :] - m)
        s_sc[rows, :] = p
        hi, lo = split(p)
        phi[rows, :] = hi
        plo[rows, :] = lo
        l = l + jnp.sum(p, axis=0, keepdims=True)
        ot = ot + values_sum(vt[:, rows], hi, lo)
    inv = 1.0 / l
    ot = ot * inv
    dot = turned(do) * inv
    rd = jnp.sum(dot * ot, axis=0, keepdims=True)
    c_ref[0] = inv * shrink
    rd_ref[0] = rd * shrink
    o = upright(ot)

    @pl.when(u == 0)
    def _():
        ol_ref[...] = o

    @pl.when(u == 1)
    def _():
        or_ref[...] = o

    dt = left(dot)
    d2 = right(stacked(upright(dot)))
    q2 = right(stacked(q))
    dq = jnp.zeros((W, R), F32)
    for j in range(2):
        rows = slice(j * BLK, (j + 1) * BLK)
        dp = mm(twice(vc[rows, :], 1), dt)
        hi, lo = split(s_sc[rows, :] * (dp - rd))
        dq = dq + values_sum(kt[:, rows], hi, lo)
        dv_acc[rows, :] += halves(mm(jnp.concatenate([phi[rows, :], plo[rows, :]], axis=1), d2))
        dk_acc[rows, :] += halves(mm(jnp.concatenate([hi, lo], axis=1), q2))
    dq_ref[0] = dq

    @pl.when((u == 1) & (step == STEPS - 1))
    def _():
        for j, out in enumerate(((g00, g01, g02, g03), (g10, g11, g12, g13))):
            for x in range(4):
                rows = slice((j * 4 + x) * T, (j * 4 + x + 1) * T)
                out[x][0] = dk_acc[rows, :] * LN2
                out[x][1] = dv_acc[rows, :]

def own_backward(info, ql_ref, qr_ref, dl_ref, dr_ref, own_ref, p_ref, c_ref, rd_ref, dq_ref,
                 gl_ref, gr_ref, h0, h1, h2, h3, vc, kt, dk_acc, dv_acc):
    u, step = pl.program_id(0), pl.program_id(1)

    @pl.when((u == 0) & (step == 0))
    def _():
        for c in range(4):
            k, v = own_refs(own_ref, info[1], c)
            fill(k, slice(c * T, (c + 1) * T), None, kt)
            fill(v, slice(c * T, (c + 1) * T), vc, None)
        dk_acc[...] = jnp.zeros_like(dk_acc)
        dv_acc[...] = jnp.zeros_like(dv_acc)

    q = near_far(u, ql_ref, qr_ref) * (SCALE * LOG2E)
    dot = turned(near_far(u, dl_ref, dr_ref)) * c_ref[0]
    p = p_ref[0]
    hi, lo = split(p)
    dv_acc[...] += halves(mm(jnp.concatenate([hi, lo], axis=1), right(stacked(upright(dot)))))
    dp = mm(twice(vc[...], 1), left(dot))
    hi, lo = split(p * (dp - rd_ref[0]))
    dk_acc[...] += halves(mm(jnp.concatenate([hi, lo], axis=1), right(stacked(q))))
    dq = upright(dq_ref[0] + values_sum(kt[...], hi, lo)) * SCALE

    @pl.when(u == 0)
    def _():
        gl_ref[...] = dq

    @pl.when(u == 1)
    def _():
        gr_ref[...] = dq

    @pl.when((u == 1) & (step == STEPS - 1))
    def _():
        for x, out in enumerate((h0, h1, h2, h3)):
            rows = pl.ds(pl.multiple_of((info[0] ^ x) * T, T), T)
            out[0] = dk_acc[rows, :] * LN2
            out[1] = dv_acc[rows, :]

def tile(shape):
    return pl.BlockSpec((1,) + shape[1:], lambda u, h, i: (u * STEPS + h, 0, 0))

def whole(shape):
    return pl.BlockSpec(shape, lambda u, h, i: (0,) * len(shape))

NEAR = pl.BlockSpec((T, HP * W), lambda u, h, i: (0, i[1] * STEPS + h))
FAR = pl.BlockSpec((T, HP * W), lambda u, h, i: (0, h))
FIRST = pl.BlockSpec((T, HP * W), lambda u, h, i: (0, jnp.where(u == 0, h, STEPS - 1)))
SECOND = pl.BlockSpec((T, HP * W), lambda u, h, i: (0, jnp.where(u == 0, 0, h)))
PROBS, ROW, TURNED = (2 * STEPS, BLK, R), (2 * STEPS, 1, R), (2 * STEPS, W, R)
HALF, PIECE = (T, 4 * W), (2, T, W)

def kernel(body, ins, outs, out_shapes, scratch, flops, limit):
    return pl.pallas_call(
        body,
        out_shape=[jax.ShapeDtypeStruct(s, F32) for s in out_shapes],
        grid_spec=pltpu.PrefetchScalarGridSpec(
            num_scalar_prefetch=1,
            grid=(2, STEPS),
            in_specs=ins,
            out_specs=outs,
            scratch_shapes=[pltpu.VMEM(s, d) for s, d in scratch],
        ),
        compiler_params=pltpu.CompilerParams(
            dimension_semantics=("arbitrary", "arbitrary"), vmem_limit_bytes=limit << 20),
        cost_estimate=pl.CostEstimate(
            flops=flops, transcendentals=0, bytes_accessed=16 << 20),
        name=body.__name__,
    )

UNIT = 2 * 2048 * BLK * W * 4

def call_own_forward(info, q, q_far, own):
    return kernel(
        own_forward,
        [NEAR, FAR, whole(own.shape)],
        [tile(PROBS), tile(ROW), tile(ROW), tile(TURNED)],
        [PROBS, ROW, ROW, TURNED],
        [((BLK, 2 * W), BF), ((2 * W, BLK), BF)],
        2 * UNIT, 30,
    )(info, q, q_far, own)

def call_picked(info, q, q_far, do, do_far, pieces, m, l, ot):
    return kernel(
        picked,
        [NEAR, FAR, NEAR, FAR] + [whole(PIECE)] * 8 + [tile(ROW), tile(ROW), tile(TURNED)],
        [FIRST, SECOND, tile(TURNED), tile(ROW), tile(ROW)] + [whole(PIECE)] * 8,
        [HALF, HALF, TURNED, ROW, ROW] + [PIECE] * 8,
        [((2 * BLK, 2 * W), BF), ((2 * BLK, 2 * W), BF), ((2 * W, 2 * BLK), BF), ((2 * W, 2 * BLK), BF),
         ((2 * BLK, R), F32), ((2 * BLK, R), BF), ((2 * BLK, R), BF),
         ((2 * BLK, W), F32), ((2 * BLK, W), F32)],
        10 * UNIT, 52,
    )(info, q, q_far, do, do_far, *pieces, m, l, ot)

def call_own_backward(info, q, q_far, do, do_far, own, p, c, rd, dq):
    return kernel(
        own_backward,
        [NEAR, FAR, NEAR, FAR, whole(own.shape), tile(PROBS), tile(ROW), tile(ROW), tile(TURNED)],
        [FIRST, SECOND] + [whole(PIECE)] * 4,
        [HALF, HALF] + [PIECE] * 4,
        [((BLK, 2 * W), BF), ((2 * W, BLK), BF), ((BLK, W), F32), ((BLK, W), F32)],
        3 * UNIT, 40,
    )(info, q, q_far, do, do_far, own, p, c, rd, dq)

HEADS = (2, T, W)

def glue(body, args, outs, limit=24):
    return pl.pallas_call(
        body,
        out_shape=[jax.ShapeDtypeStruct(s, F32) for s in outs],
        in_specs=[pl.BlockSpec(memory_space=pltpu.SMEM)]
        + [pl.BlockSpec(memory_space=pltpu.VMEM)] * (len(args) - 1),
        out_specs=[pl.BlockSpec(memory_space=pltpu.VMEM)] * len(outs),
        compiler_params=pltpu.CompilerParams(vmem_limit_bytes=limit << 20),
        cost_estimate=pl.CostEstimate(
            flops=0, transcendentals=0, bytes_accessed=(len(args) + len(outs)) * HEADS[0] * T * W * 4),
        name=body.__name__.strip("_"),
    )(*args)

def shift(array, axis, step):
    if step == 0:
        return array
    return lax.ppermute(array, axis, [(i, (i + step) % 4) for i in range(4)])

def mirror(array, flip):
    return lax.ppermute(array, "z", [(i, i ^ flip) for i in range(4)])

def chosen(table, y, x, j):
    block = jnp.maximum(table[y * 4 + x, 1 + j], 0)
    return block // 4, block % 4

def assemble(spot, keys, values, other_keys, other_values, k_ref, v_ref, kv_ref):
    core = spot[0]
    for h in range(2):
        cols = pl.ds(pl.multiple_of((core * 2 + h) * W, W), W)
        for i, (mine, other, out) in enumerate(
                ((keys, other_keys, k_ref), (values, other_values, v_ref))):
            for ref, half in ((mine, core), (other, 1 - core)):
                rows = pl.ds(pl.multiple_of(half * (T // 2), T // 2), T // 2)
                a = ref[:, cols]
                out[h, rows, :] = a
                kv_ref[i, h, rows, :] = a

def pick(j, table, *refs):
    y, x = lax.axis_index("y"), lax.axis_index("x")
    k_in, v_in, k_out, v_out = (refs[i:i + 4] for i in range(0, 16, 4))
    for step in range(4):
        row, _ = chosen(table, y, (x + step) % 4, j)
        _, column = chosen(table, (y + step) % 4, x, j)
        for off, arrays, out in (((y - row) % 4, k_in, k_out), ((x - column) % 4, v_in, v_out)):
            for i in range(4):
                @pl.when(off == i)
                def _(source=arrays[i], out=out[step]):
                    out[...] = source[...]

def pick0(*refs):
    pick(0, *refs)

def pick1(*refs):
    pick(1, *refs)

def join(j, table, *refs):
    y, x = lax.axis_index("y"), lax.axis_index("x")
    head = lax.axis_index("z") // 2
    row, column = chosen(table, y, x, j)
    k_in, v_in, (same, cross) = refs[0:4], refs[4:8], refs[8:10]
    for i in range(4):
        for n, off, source in ((0, (x - column) % 4, k_in[i]), (1, (y - row) % 4, v_in[i])):
            @pl.when(off == i)
            def _(n=n, source=source):
                same[n] = source[head]
                cross[n] = source[1 - head]

def join0(*refs):
    join(0, *refs)

def join1(*refs):
    join(1, *refs)

def spread(spot, kept, added, passed, k_out, v_out):
    head = spot[1]
    for n, out in ((0, k_out), (1, v_out)):
        out[head] = kept[n] + added[n]
        out[1 - head] = passed[n]

def collect(j, table, *refs):
    y, x = lax.axis_index("y"), lax.axis_index("x")
    if j == 0:
        k_in, v_in, k_out, v_out = (refs[i:i + 4] for i in range(0, 16, 4))
        for ref in k_out + v_out:
            ref[...] = jnp.zeros_like(ref)
    else:
        k_in, v_in, k_old, v_old, k_out, v_out = (refs[i:i + 4] for i in range(0, 24, 4))
        for ref, old in zip(k_out + v_out, k_old + v_old):
            ref[...] = old[...]
    for step in range(4):
        row, column = chosen(table, y, (x - step) % 4, j)
        row2, column2 = chosen(table, (y - step) % 4, x, j)
        for hit, off, source, out in (
                (column == x, (y - row) % 4, k_in[step], k_out),
                (row2 == y, (x - column2) % 4, v_in[step], v_out)):
            for i in range(4):
                @pl.when(hit & (off == i))
                def _(source=source, ref=out[i]):
                    ref[...] += source[...]

def collect0(*refs):
    collect(0, *refs)

def collect1(*refs):
    collect(1, *refs)

def shards(queries, keys, values, cotangent, selected):
    core, z = lax.axis_index("head"), lax.axis_index("z")
    y, x = lax.axis_index("y"), lax.axis_index("x")
    head = z // 2
    mine = lax.dynamic_slice(selected, (y * 4 + x, 1), (1, 2))[0]
    info = jnp.concatenate([jnp.stack([z, head]), (mine >= 0).astype(jnp.int32)])
    spot = jnp.stack([core, head])
    swap = [(0, 1), (1, 0)]

    far = 1 - head
    q_far, do_far = (
        mirror(lax.dynamic_slice_in_dim(a, far * 4 * W, 4 * W, 1), 3)
        for a in (queries, cotangent)
    )
    other = [lax.ppermute(a, "head", swap) for a in (keys, values)]
    k, v, kv = glue(assemble, (spot, keys, values, *other), (HEADS, HEADS, (2,) + HEADS))
    own = lax.all_gather(kv, "z", axis=0)

    k_along = [shift(k, "y", s) for s in range(4)]
    v_along = [shift(v, "x", s) for s in range(4)]
    pieces = []
    for pick_j, join_j in ((pick0, join0), (pick1, join1)):
        sent = glue(pick_j, (selected, *k_along, *v_along), (HEADS,) * 8)
        k_got = [shift(sent[s], "x", s) for s in range(4)]
        v_got = [shift(sent[4 + s], "y", s) for s in range(4)]
        same, cross = glue(join_j, (selected, *k_got, *v_got), (HEADS, HEADS))
        p1 = mirror(same, 1)
        p3 = mirror(cross, 3)
        pieces += [same, p1, mirror(p3, 1), p3]

    p, m, l, ot = call_own_forward(info, queries, q_far, own)
    out = call_picked(info, queries, q_far, cotangent, do_far, pieces, m, l, ot)
    o_near, o_far, dq, c, rd = out[:5]
    last = call_own_backward(info, queries, q_far, cotangent, do_far, own, p, c, rd, dq)

    def reduced(g):
        passed = mirror(g[3] + mirror(g[2], 1), 3)
        return glue(spread, (spot, g[0], mirror(g[1], 1), passed), (HEADS, HEADS))

    sums = ()
    for j, collect_j in enumerate((collect0, collect1)):
        k_part, v_part = reduced(out[5 + 4 * j:9 + 4 * j])
        arrived = [shift(k_part, "x", s) for s in range(4)]
        arrived += [shift(v_part, "y", s) for s in range(4)]
        sums = glue(collect_j, (selected, *arrived, *sums), (HEADS,) * 8)
    own_k, own_v = reduced(last[2:6])
    grad_k = own_k + sum(shift(sums[s], "y", (4 - s) % 4) for s in range(4))
    grad_v = own_v + sum(shift(sums[4 + s], "x", (4 - s) % 4) for s in range(4))

    half = T // 2

    def home(a):
        keep = lax.dynamic_slice_in_dim(a, core * half, half, 1)
        back = lax.ppermute(lax.dynamic_slice_in_dim(a, (1 - core) * half, half, 1), "head", swap)
        low, high = jnp.where(core == 0, keep, back), jnp.where(core == 0, back, keep)
        return jnp.concatenate([low[0], low[1], high[0], high[1]], 1)

    def sides(a, b):
        return jnp.where(head == 0, jnp.concatenate([a, b], 1), jnp.concatenate([b, a], 1))

    return (
        sides(o_near, mirror(o_far, 3)),
        sides(last[0], mirror(last[1], 3)),
        home(grad_k),
        home(grad_v),
    )

def solution(mesh):
    grid = Mesh(mesh.devices.reshape(4, 4, 4, 2), ("y", "x", "z", "head"))
    tokens = ("y", "x", "z")
    wide, narrow = P(tokens, "head"), P(tokens + ("head",), None)
    return jax.shard_map(
        shards,
        mesh=grid,
        in_specs=(wide, narrow, narrow, wide, P()),
        out_specs=(wide, wide, narrow, narrow),
        check_vma=False,
    )
```

time: 1190 us -> 263 us (0.22)
  waiting for transfers between devices: 810 us -> 24.3 us
  matrix products: 167 us -> 0 us
  blocking collectives: 115 us -> 0 us
  starting transfers between devices: 0.16 us -> 112 us
  Pallas kernels: 0 us -> 73.5 us
  local copies, waits for them, and re-layouts: 52.6 us -> 26.5 us
  other arithmetic: 21.8 us -> 8.73 us
    reduce_scatter x2 -> x0, waiting for transfers between devices: 646 us -> none  [the longest x1 332 us: shards(): lax.psum_scatter(value_gradient_total.reshape(seq_rows, width), 'ctx', sc...]
    dot_general x6 -> x0, matrix products: 167 us -> none  [the longest x1 34.7 us: shards(): jnp.einsum('hgts,thgd->shd', probs, cotangent_block, precision=highest)]
    all_gather x2 -> x1, waiting for transfers between devices: 164 us -> 0.02 us  [shards(): own = lax.all_gather(kv, 'z', axis=0)]
    all_to_all x4 -> x0, blocking collectives: 115 us -> none  [the longest x1 54.7 us: shards(): lax.all_to_all(owned_k, 'head', split_axis=0, concat_axis=1, tiled=True)]
    ppermute x0 -> x59, starting transfers between devices: none -> 112 us  [the longest x36 60.4 us: shift(): return lax.ppermute(array, axis, [(i, (i + step) % 4) for i in range(4)])]
    pallas_call x0 -> x13, Pallas kernels: none -> 73.5 us  [the longest x1 37.7 us: call_picked(): kernel(picked, [NEAR, FAR, NEAR, FAR] + [whole(PIECE)] * 8 + [tile(ROW),...]
    ppermute x0 -> x59, waiting for transfers between devices: none -> 24.2 us  [the longest x36 16.2 us: shift(): return lax.ppermute(array, axis, [(i, (i + step) % 4) for i in range(4)])]
    another operation x2 -> x0, local copies, waits for them, and re-layouts: 15.3 us -> none
  transfers between devices with their start and end apart: 4 -> 60, of which waited for: 4 -> 13; matrix products, arithmetic and copies ran while one was open for 7% -> 4% of each run, Pallas kernels for 0% -> 13%
where the time goes in v3:
time: 263 us; the launch traced here: 259 us
  starting transfers between devices  112 us (43%)
  Pallas kernels  73.5 us (28%)
  local copies, waits for them, and re-layouts  26.5 us (10%)
  waiting for transfers between devices  24.3 us (9%)
  between operations  14.6 us (6%)
  other arithmetic  8.73 us (3%)
    ppermute x36, starting transfers between devices, shift(): return lax.ppermute(array, axis, [(i, (i + step) % 4) for i in range(4)])  60.4 us
    pallas_call x1, Pallas kernels, call_picked(): kernel(picked, [NEAR, FAR, NEAR, FAR] + [whole(PIECE)] * 8 + [tile(ROW),...  37.7 us
    ppermute x19, starting transfers between devices, mirror(): return lax.ppermute(array, 'z', [(i, i ^ flip) for i in range(4)])  31.9 us
    unnamed x75, local copies, waits for them, and re-layouts  24.2 us
    ppermute x2, starting transfers between devices, home(): lax.ppermute(lax.dynamic_slice_in_dim(a, (1 - core) * half, half, 1), 'he...  17.9 us
    ppermute x36, waiting for transfers between devices, shift(): return lax.ppermute(array, axis, [(i, (i + step) % 4) for i in range(4)])  16.2 us
    pallas_call x1, Pallas kernels, call_own_backward(): kernel(own_backward, [NEAR, FAR, NEAR, FAR, whole(own.shape), tile(PROBS)...  13.8 us
    pallas_call x10, Pallas kernels, glue(): pl.pallas_call(body, out_shape=[jax.ShapeDtypeStruct(s, F32) for s in out...  12.6 us
  transfers between devices with their start and end apart: 60, of which 13 were waited for; matrix products, arithmetic and copies ran while one was open for 4% of the time, Pallas kernels for 13%

profile of v3, /device:TPU:1, one launch (start us, length us, event | category | flops | bytes accessed | tf_op | source)
XLA Modules:
  0.0 259.3 jit_solution(13520353596224769485)
XLA Ops:
  15.3 2.6 %collective-permute-start.5 = (f32[2,256,128]{2,1,0:T(8,128)S(1)}, f32[2,256,128]{2,1,0:T(8,128)S(1)}, u32[]{:S(2)}, u32[]{:S(2)}) collective-permute-start(f32[2,256,128]{2,1,0:T(8,128)S(1)} %get-tuple-element.72.refs_1_), channel_id=1, source_target_pairs={{0,64},{32,96},{64,0},{96,32},{1,65},{33,97},{65,1},{97,33},{2,66}... | collective-permute-start | bytes 786440 | tf_op jit(solution)/shard_map/ppermute | solution.py:296
  26.1 3.5 %collective-permute-done.5.refs_3_ = f32[2,256,128]{2,1,0:T(8,128)S(1)} collective-permute-done((f32[2,256,128]{2,1,0:T(8,128)S(1)}, f32[2,256,128]{2,1,0:T(8,128)S(1)}, u32[]{:S(2)}, u32[]{:S(2)}) %collective-permute-start.5) | collective-permute-done | bytes 262176 | tf_op jit(solution)/shard_map/ppermute | solution.py:296
  29.6 3.8 %collective-permute-done.8.refs_7_ = f32[2,256,128]{2,1,0:T(8,128)S(1)} collective-permute-done((f32[2,256,128]{2,1,0:T(8,128)S(1)}, f32[2,256,128]{2,1,0:T(8,128)S(1)}, u32[]{:S(2)}, u32[]{:S(2)}) %collective-permute-start.8) | collective-permute-done | bytes 262176 | tf_op jit(solution)/shard_map/ppermute | solution.py:296
  36.0 3.5 %collective-permute-start.10 = (f32[2,256,128]{2,1,0:T(8,128)S(1)}, f32[2,256,128]{2,1,0:T(8,128)S(1)}, u32[]{:S(2)}, u32[]{:S(2)}) collective-permute-start(f32[2,256,128]{2,1,0:T(8,128)S(1)} %get-tuple-element.75), channel_id=1, source_target_pairs={{0,8},{8,16},{16,24},{24,0},{1,9},{9,17},{17,25},{25,1},{2,10},{10... | collective-permute-start | bytes 786440 | tf_op jit(solution)/shard_map/ppermute | solution.py:296
  52.5 3.0 %collective-permute-start.20 = (f32[2,256,128]{2,1,0:T(8,128)}, f32[2,256,128]{2,1,0:T(8,128)S(1)}, u32[]{:S(2)}, u32[]{:S(2)}) collective-permute-start(f32[2,256,128]{2,1,0:T(8,128)} %get-tuple-element.86), channel_id=1, source_target_pairs={{0,16},{8,24},{16,0},{24,8},{1,17},{9,25},{17,1},{25,9},{2,18},{10... | collective-permute-start | bytes 786440 | tf_op jit(solution)/shard_map/ppermute | solution.py:296
  56.7 3.8 %collective-permute-start = (f32[256,512]{1,0:T(8,128)S(1)}, f32[256,512]{1,0:T(8,128)}, u32[]{:S(2)}, u32[]{:S(2)}) collective-permute-start(f32[256,512]{1,0:T(8,128)S(1)} %constant_dynamic-slice_fusion.3), channel_id=1, source_target_pairs={{0,6},{2,4},{4,2},{6,0},{1,7},{3,5},{5,3},{7,1},{8,14},{10,12},{12... | collective-permute-start | bytes 1572872 | tf_op jit(solution)/shard_map/ppermute | solution.py:299
  72.1 3.4 %collective-permute-start.17 = (f32[2,256,128]{2,1,0:T(8,128)}, f32[2,256,128]{2,1,0:T(8,128)S(1)}, u32[]{:S(2)}, u32[]{:S(2)}) collective-permute-start(f32[2,256,128]{2,1,0:T(8,128)} %get-tuple-element.83), channel_id=1, source_target_pairs={{0,6},{2,4},{4,2},{6,0},{1,7},{3,5},{5,3},{7,1},{8,14},{10,12},{12... | collective-permute-start | bytes 786440 | tf_op jit(solution)/shard_map/ppermute | solution.py:299
  80.0 2.8 %collective-permute-start.1 = (f32[256,512]{1,0:T(8,128)S(1)}, f32[256,512]{1,0:T(8,128)S(1)}, u32[]{:S(2)}, u32[]{:S(2)}) collective-permute-start(f32[256,512]{1,0:T(8,128)S(1)} %constant_dynamic-slice_fusion.2), channel_id=1, source_target_pairs={{0,6},{2,4},{4,2},{6,0},{1,7},{3,5},{5,3},{7,1},{8,14},{10,12},{12... | collective-permute-start | bytes 1572872 | tf_op jit(solution)/shard_map/ppermute | solution.py:299
  84.6 2.5 collective-permute-done.26.s13
  89.0 9.4 %own_forward.1 = (f32[4,1024,512]{2,1,0:T(8,128)S(1)}, f32[4,1,512]{2,1,0:T(1,128)S(1)}, f32[4,1,512]{2,1,0:T(1,128)S(1)}, f32[4,128,512]{2,1,0:T(8,128)S(1)}) custom-call(s32[4]{0:T(128)S(1)} %pad_add_fusion.info, f32[256,1024]{1,0:T(8,128)S(1)} %copy-done, f32[256,512]{1,0:T(8,128)} %collective-permute-done.qr_ref, f32[4,2,2,256,128]{4,3,2,1,0:T(8,128)S(1)} %bitcast.20), custom_call_target="tpu_custom_call" | custom-call | flops 4294967296 | bytes 16777216 | tf_op jit(solution)/shard_map/own_forward/pallas_call | solution.py:247
  98.4 3.3 %copy-done.28 = f32[4,1024,512]{2,1,0:T(8,128)} copy-done((f32[4,1024,512]{2,1,0:T(8,128)}, f32[4,1024,512]{2,1,0:T(8,128)S(1)}, u32[]{:S(2)}) %copy-start.28) | copy-done | bytes 8388632
  103.7 37.7 %picked.1 = (f32[256,512]{1,0:T(8,128)}, f32[256,512]{1,0:T(8,128)}, f32[4,128,512]{2,1,0:T(8,128)}, f32[4,1,512]{2,1,0:T(1,128)S(1)}, f32[4,1,512]{2,1,0:T(1,12...) custom-call(s32[4]{0:T(128)S(1)} %pad_add_fusion.info, ...), custom_call_target="tpu_custom_call" | custom-call | flops 21474836480 | bytes 16777216 | tf_op jit(solution)/shard_map/picked/pallas_call | solution.py:257
  149.6 11.2 %collective-permute-start.44 = (f32[2,256,128]{2,1,0:T(8,128)S(1)}, f32[2,256,128]{2,1,0:T(8,128)S(1)}, u32[]{:S(2)}, u32[]{:S(2)}) collective-permute-start(f32[2,256,128]{2,1,0:T(8,128)S(1)} %add.57), channel_id=1, source_target_pairs={{0,6},{2,4},{4,2},{6,0},{1,7},{3,5},{5,3},{7,1},{8,14},{10,12},{12... | collective-permute-start | bytes 786440 | tf_op jit(solution)/shard_map/ppermute | solution.py:299
  162.1 13.8 %own_backward.1 = (f32[256,512]{1,0:T(8,128)S(1)}, f32[256,512]{1,0:T(8,128)S(1)}, f32[2,256,128]{2,1,0:T(8,128)S(1)}, f32[2,256,128]{2,1,0:T(8,128)}, f32[2,256...) custom-call(s32[4]{0:T(128)S(1)} %pad_add_fusion.info, f32[256,1024]{1,0:T(8,128)S(1)} %copy-done.1, ...), custom_call_target="tpu_custom_call" | custom-call | flops 6442450944 | bytes 16777216 | tf_op jit(solution)/shard_map/own_backward/pallas_call | solution.py:269
  177.0 2.9 %collective-permute-start.37 = (f32[2,256,128]{2,1,0:T(8,128)S(1)}, f32[2,256,128]{2,1,0:T(8,128)S(1)}, u32[]{:S(2)}, u32[]{:S(2)}) collective-permute-start(f32[2,256,128]{2,1,0:T(8,128)S(1)} %get-tuple-element.115.refs_1_), channel_id=1, source_target_pairs={{0,16},{8,24},{16,0},{24,8},{1,17},{9,25},{17,1},{25,9},{2,18},{10... | collective-permute-start | bytes 786440 | tf_op jit(solution)/shard_map/ppermute | solution.py:296
  181.0 2.8 %collective-permute-start.46 = (f32[2,256,128]{2,1,0:T(8,128)S(1)}, f32[2,256,128]{2,1,0:T(8,128)S(1)}, u32[]{:S(2)}, u32[]{:S(2)}) collective-permute-start(f32[2,256,128]{2,1,0:T(8,128)S(1)} %get-tuple-element.121.refs_1_), channel_id=1, source_target_pairs={{0,16},{8,24},{16,0},{24,8},{1,17},{9,25},{17,1},{25,9},{2,18},{10... | collective-permute-start | bytes 786440 | tf_op jit(solution)/shard_map/ppermute | solution.py:296
  183.8 9.2 %collective-permute-start.48 = (f32[2,256,128]{2,1,0:T(8,128)S(1)}, f32[2,256,128]{2,1,0:T(8,128)S(1)}, u32[]{:S(2)}, u32[]{:S(2)}) collective-permute-start(f32[2,256,128]{2,1,0:T(8,128)S(1)} %get-tuple-element.122.refs_5_), channel_id=1, source_target_pairs={{0,32},{32,64},{64,96},{96,0},{1,33},{33,65},{65,97},{97,1},{2,34}... | collective-permute-start | bytes 786440 | tf_op jit(solution)/shard_map/ppermute | solution.py:296
  196.7 6.5 %collective-permute-start.39 = (f32[2,256,128]{2,1,0:T(8,128)S(1)}, f32[2,256,128]{2,1,0:T(8,128)S(1)}, u32[]{:S(2)}, u32[]{:S(2)}) collective-permute-start(f32[2,256,128]{2,1,0:T(8,128)S(1)} %get-tuple-element.116.refs_5_), channel_id=1, source_target_pairs={{0,32},{32,64},{64,96},{96,0},{1,33},{33,65},{65,97},{97,1},{2,34}... | collective-permute-start | bytes 786440 | tf_op jit(solution)/shard_map/ppermute | solution.py:296
  211.6 5.5 %collective-permute-done.40.refs_7_ = f32[2,256,128]{2,1,0:T(8,128)S(1)} collective-permute-done((f32[2,256,128]{2,1,0:T(8,128)S(1)}, f32[2,256,128]{2,1,0:T(8,128)S(1)}, u32[]{:S(2)}, u32[]{:S(2)}) %collective-permute-start.40) | collective-permute-done | bytes 262176 | tf_op jit(solution)/shard_map/ppermute | solution.py:296
  219.3 2.6 collective-permute-start.55
  221.9 2.7 %maximum_select_fusion = f32[256,1024]{1,0:T(8,128)} fusion(f32[256,512]{1,0:T(8,128)} %copy-done.31, f32[256,512]{1,0:T(8,128)} %get-tuple-element.98, pred[]{:T(512)S(6)} %eq.4), kind=kLoop, calls=%fused_computation | loop fusion | flops 786432 | bytes 2097153 | tf_op jit(solution)/shard_map/jit(_where)/select_n | solution.py:444
  227.7 2.6 %collective-permute-start.52 = (f32[2,256,128]{2,1,0:T(8,128)S(1)}, f32[2,256,128]{2,1,0:T(8,128)S(1)}, u32[]{:S(2)}, u32[]{:S(2)}) collective-permute-start(f32[2,256,128]{2,1,0:T(8,128)S(1)} %get-tuple-element.133), channel_id=1, source_target_pairs={{0,64},{32,96},{64,0},{96,32},{1,65},{33,97},{65,1},{97,33},{2,66}... | collective-permute-start | bytes 786440 | tf_op jit(solution)/shard_map/ppermute | solution.py:296
  231.6 12.9 %collective-permute-start.58 = (f32[2,128,128]{2,1,0:T(8,128)S(1)}, f32[2,128,128]{2,1,0:T(8,128)S(1)}, u32[]{:S(2)}, u32[]{:S(2)}) collective-permute-start(f32[2,128,128]{2,1,0:T(8,128)S(1)} %constant_dynamic-slice_fusion), channel_id=1, source_target_pairs={{0,1},{1,0},{2,3},{3,2},{4,5},{5,4},{6,7},{7,6},{8,9},{9,8},{10,11... | collective-permute-start | bytes 393224 | tf_op jit(solution)/shard_map/ppermute | solution.py:439
  244.6 5.0 %collective-permute-start.54 = (f32[2,128,128]{2,1,0:T(8,128)S(1)}, f32[2,128,128]{2,1,0:T(8,128)S(1)}, u32[]{:S(2)}, u32[]{:S(2)}) collective-permute-start(f32[2,128,128]{2,1,0:T(8,128)S(1)} %constant_dynamic-slice_fusion.1), channel_id=1, source_target_pairs={{0,1},{1,0},{2,3},{3,2},{4,5},{5,4},{6,7},{7,6},{8,9},{9,8},{10,11... | collective-permute-start | bytes 393224 | tf_op jit(solution)/shard_map/ppermute | solution.py:439
  (206 shorter events, 87.8 us)
Async XLA Ops:
  7.2 80.2 %all-gather.3.cloned.1.call-start = ((), (), s32[]{:S(2)}) async-start(), calls=%async_computation | async-start | bytes 2621440 | tf_op jit(solution)/shard_map/all_gather | solution.py:402
  15.3 14.3 %collective-permute-start.5 = (f32[2,256,128]{2,1,0:T(8,128)S(1)}, f32[2,256,128]{2,1,0:T(8,128)S(1)}, u32[]{:S(2)}, u32[]{:S(2)}) collective-permute-start(f32[2,256,128]{2,1,0:T(8,128)S(1)} %get-tuple-element.72.refs_1_), channel_id=1, source_target_pairs={{0,64},{32,96},{64,0},{96,32},{1,65},{33,97},{65,1},{97,33},{2,66}... | collective-permute-start | bytes 786440 | tf_op jit(solution)/shard_map/ppermute | solution.py:296
  41.8 14.8 %collective-permute-start.13 = (f32[2,256,128]{2,1,0:T(8,128)}, f32[2,256,128]{2,1,0:T(8,128)}, u32[]{:S(2)}, u32[]{:S(2)}) collective-permute-start(f32[2,256,128]{2,1,0:T(8,128)} %get-tuple-element.79), channel_id=1, source_target_pairs={{0,32},{32,64},{64,96},{96,0},{1,33},{33,65},{65,97},{97,1},{2,34}... | collective-permute-start | bytes 786440 | tf_op jit(solution)/shard_map/ppermute | solution.py:296
  42.2 18.3 %collective-permute-start.14 = (f32[2,256,128]{2,1,0:T(8,128)}, f32[2,256,128]{2,1,0:T(8,128)}, u32[]{:S(2)}, u32[]{:S(2)}) collective-permute-start(f32[2,256,128]{2,1,0:T(8,128)} %get-tuple-element.80), channel_id=1, source_target_pairs={{0,64},{32,96},{64,0},{96,32},{1,65},{33,97},{65,1},{97,33},{2,66}... | collective-permute-start | bytes 786440 | tf_op jit(solution)/shard_map/ppermute | solution.py:296
  56.7 26.4 %collective-permute-start = (f32[256,512]{1,0:T(8,128)S(1)}, f32[256,512]{1,0:T(8,128)}, u32[]{:S(2)}, u32[]{:S(2)}) collective-permute-start(f32[256,512]{1,0:T(8,128)S(1)} %constant_dynamic-slice_fusion.3), channel_id=1, source_target_pairs={{0,6},{2,4},{4,2},{6,0},{1,7},{3,5},{5,3},{7,1},{8,14},{10,12},{12... | collective-permute-start | bytes 1572872 | tf_op jit(solution)/shard_map/ppermute | solution.py:299
  80.0 22.7 %collective-permute-start.1 = (f32[256,512]{1,0:T(8,128)S(1)}, f32[256,512]{1,0:T(8,128)S(1)}, u32[]{:S(2)}, u32[]{:S(2)}) collective-permute-start(f32[256,512]{1,0:T(8,128)S(1)} %constant_dynamic-slice_fusion.2), channel_id=1, source_target_pairs={{0,6},{2,4},{4,2},{6,0},{1,7},{3,5},{5,3},{7,1},{8,14},{10,12},{12... | collective-permute-start | bytes 1572872 | tf_op jit(solution)/shard_map/ppermute | solution.py:299
  83.0 19.7 %collective-permute-start.16 = (f32[2,256,128]{2,1,0:T(8,128)S(1)}, f32[2,256,128]{2,1,0:T(8,128)}, u32[]{:S(2)}, u32[]{:S(2)}) collective-permute-start(f32[2,256,128]{2,1,0:T(8,128)S(1)} %get-tuple-element.82.s00), channel_id=1, source_target_pairs={{0,2},{2,0},{4,6},{6,4},{1,3},{3,1},{5,7},{7,5},{8,10},{10,8},{12,... | collective-permute-start | bytes 786440 | tf_op jit(solution)/shard_map/ppermute | solution.py:299
  83.1 19.7 %collective-permute-start.25 = (f32[2,256,128]{2,1,0:T(8,128)}, f32[2,256,128]{2,1,0:T(8,128)S(1)}, u32[]{:S(2)}, u32[]{:S(2)}) collective-permute-start(f32[2,256,128]{2,1,0:T(8,128)} %copy-done.23), channel_id=1, source_target_pairs={{0,2},{2,0},{4,6},{6,4},{1,3},{3,1},{5,7},{7,5},{8,10},{10,8},{12,... | collective-permute-start | bytes 786440 | tf_op jit(solution)/shard_map/ppermute | solution.py:299
  84.5 18.3 %collective-permute-start.18 = (f32[2,256,128]{2,1,0:T(8,128)S(1)}, f32[2,256,128]{2,1,0:T(8,128)S(1)}, u32[]{:S(2)}, u32[]{:S(2)}) collective-permute-start(f32[2,256,128]{2,1,0:T(8,128)S(1)} %collective-permute-done.17.s03), channel_id=1, source_target_pairs={{0,2},{2,0},{4,6},{6,4},{1,3},{3,1},{5,7},{7,5},{8,10},{10,8},{12,... | collective-permute-start | bytes 786440 | tf_op jit(solution)/shard_map/ppermute | solution.py:299
  87.1 15.7 %collective-permute-start.27 = (f32[2,256,128]{2,1,0:T(8,128)}, f32[2,256,128]{2,1,0:T(8,128)}, u32[]{:S(2)}, u32[]{:S(2)}) collective-permute-start(f32[2,256,128]{2,1,0:T(8,128)} %collective-permute-done.26.s13), channel_id=1, source_target_pairs={{0,2},{2,0},{4,6},{6,4},{1,3},{3,1},{5,7},{7,5},{8,10},{10,8},{12,... | collective-permute-start | bytes 786440 | tf_op jit(solution)/shard_map/ppermute | solution.py:299
  143.0 33.3 %collective-permute-start.33 = (f32[2,256,128]{2,1,0:T(8,128)S(1)}, f32[2,256,128]{2,1,0:T(8,128)S(1)}, u32[]{:S(2)}, u32[]{:S(2)}) collective-permute-start(f32[2,256,128]{2,1,0:T(8,128)S(1)} %get-tuple-element.112), channel_id=1, source_target_pairs={{0,2},{2,0},{4,6},{6,4},{1,3},{3,1},{5,7},{7,5},{8,10},{10,8},{12,... | collective-permute-start | bytes 786440 | tf_op jit(solution)/shard_map/ppermute | solution.py:299
  144.4 35.5 %collective-permute-start.42 = (f32[2,256,128]{2,1,0:T(8,128)S(1)}, f32[2,256,128]{2,1,0:T(8,128)S(1)}, u32[]{:S(2)}, u32[]{:S(2)}) collective-permute-start(f32[2,256,128]{2,1,0:T(8,128)S(1)} %get-tuple-element.118), channel_id=1, source_target_pairs={{0,2},{2,0},{4,6},{6,4},{1,3},{3,1},{5,7},{7,5},{8,10},{10,8},{12,... | collective-permute-start | bytes 786440 | tf_op jit(solution)/shard_map/ppermute | solution.py:299
  147.7 28.6 %collective-permute-start.35 = (f32[2,256,128]{2,1,0:T(8,128)S(1)}, f32[2,256,128]{2,1,0:T(8,128)S(1)}, u32[]{:S(2)}, u32[]{:S(2)}) collective-permute-start(f32[2,256,128]{2,1,0:T(8,128)S(1)} %add.56), channel_id=1, source_target_pairs={{0,6},{2,4},{4,2},{6,0},{1,7},{3,5},{5,3},{7,1},{8,14},{10,12},{12... | collective-permute-start | bytes 786440 | tf_op jit(solution)/shard_map/ppermute | solution.py:299
  149.6 30.3 %collective-permute-start.44 = (f32[2,256,128]{2,1,0:T(8,128)S(1)}, f32[2,256,128]{2,1,0:T(8,128)S(1)}, u32[]{:S(2)}, u32[]{:S(2)}) collective-permute-start(f32[2,256,128]{2,1,0:T(8,128)S(1)} %add.57), channel_id=1, source_target_pairs={{0,6},{2,4},{4,2},{6,0},{1,7},{3,5},{5,3},{7,1},{8,14},{10,12},{12... | collective-permute-start | bytes 786440 | tf_op jit(solution)/shard_map/ppermute | solution.py:299
  177.0 15.9 %collective-permute-start.37 = (f32[2,256,128]{2,1,0:T(8,128)S(1)}, f32[2,256,128]{2,1,0:T(8,128)S(1)}, u32[]{:S(2)}, u32[]{:S(2)}) collective-permute-start(f32[2,256,128]{2,1,0:T(8,128)S(1)} %get-tuple-element.115.refs_1_), channel_id=1, source_target_pairs={{0,16},{8,24},{16,0},{24,8},{1,17},{9,25},{17,1},{25,9},{2,18},{10... | collective-permute-start | bytes 786440 | tf_op jit(solution)/shard_map/ppermute | solution.py:296
  181.0 14.4 %collective-permute-start.46 = (f32[2,256,128]{2,1,0:T(8,128)S(1)}, f32[2,256,128]{2,1,0:T(8,128)S(1)}, u32[]{:S(2)}, u32[]{:S(2)}) collective-permute-start(f32[2,256,128]{2,1,0:T(8,128)S(1)} %get-tuple-element.121.refs_1_), channel_id=1, source_target_pairs={{0,16},{8,24},{16,0},{24,8},{1,17},{9,25},{17,1},{25,9},{2,18},{10... | collective-permute-start | bytes 786440 | tf_op jit(solution)/shard_map/ppermute | solution.py:296
  195.4 23.1 %collective-permute-start.28 = (f32[256,512]{1,0:T(8,128)S(1)}, f32[256,512]{1,0:T(8,128)S(1)}, u32[]{:S(2)}, u32[]{:S(2)}) collective-permute-start(f32[256,512]{1,0:T(8,128)S(1)} %copy-done.33), channel_id=1, source_target_pairs={{0,6},{2,4},{4,2},{6,0},{1,7},{3,5},{5,3},{7,1},{8,14},{10,12},{12... | collective-permute-start | bytes 1572872 | tf_op jit(solution)/shard_map/ppermute | solution.py:299
  208.9 15.6 %collective-permute-start.30 = (f32[2,256,128]{2,1,0:T(8,128)}, f32[2,256,128]{2,1,0:T(8,128)S(1)}, u32[]{:S(2)}, u32[]{:S(2)}) collective-permute-start(f32[2,256,128]{2,1,0:T(8,128)} %get-tuple-element.107), channel_id=1, source_target_pairs={{0,2},{2,0},{4,6},{6,4},{1,3},{3,1},{5,7},{7,5},{8,10},{10,8},{12,... | collective-permute-start | bytes 786440 | tf_op jit(solution)/shard_map/ppermute | solution.py:299
  210.0 15.7 %collective-permute-start.32 = (f32[2,256,128]{2,1,0:T(8,128)}, f32[2,256,128]{2,1,0:T(8,128)S(1)}, u32[]{:S(2)}, u32[]{:S(2)}) collective-permute-start(f32[2,256,128]{2,1,0:T(8,128)} %add.55), channel_id=1, source_target_pairs={{0,6},{2,4},{4,2},{6,0},{1,7},{3,5},{5,3},{7,1},{8,14},{10,12},{12... | collective-permute-start | bytes 786440 | tf_op jit(solution)/shard_map/ppermute | solution.py:299
  224.5 25.0 %collective-permute-start.29 = (f32[256,512]{1,0:T(8,128)}, f32[256,512]{1,0:T(8,128)S(1)}, u32[]{:S(2)}, u32[]{:S(2)}) collective-permute-start(f32[256,512]{1,0:T(8,128)} %copy-done.19), channel_id=1, source_target_pairs={{0,6},{2,4},{4,2},{6,0},{1,7},{3,5},{5,3},{7,1},{8,14},{10,12},{12... | collective-permute-start | bytes 1572872 | tf_op jit(solution)/shard_map/ppermute | solution.py:299
  226.2 18.3 %collective-permute-start.53 = (f32[2,256,128]{2,1,0:T(8,128)S(1)}, f32[2,256,128]{2,1,0:T(8,128)S(1)}, u32[]{:S(2)}, u32[]{:S(2)}) collective-permute-start(f32[2,256,128]{2,1,0:T(8,128)S(1)} %get-tuple-element.134), channel_id=1, source_target_pairs={{0,32},{32,64},{64,96},{96,0},{1,33},{33,65},{65,97},{97,1},{2,34}... | collective-permute-start | bytes 786440 | tf_op jit(solution)/shard_map/ppermute | solution.py:296
  227.7 16.8 %collective-permute-start.52 = (f32[2,256,128]{2,1,0:T(8,128)S(1)}, f32[2,256,128]{2,1,0:T(8,128)S(1)}, u32[]{:S(2)}, u32[]{:S(2)}) collective-permute-start(f32[2,256,128]{2,1,0:T(8,128)S(1)} %get-tuple-element.133), channel_id=1, source_target_pairs={{0,64},{32,96},{64,0},{96,32},{1,65},{33,97},{65,1},{97,33},{2,66}... | collective-permute-start | bytes 786440 | tf_op jit(solution)/shard_map/ppermute | solution.py:296
  230.3 14.2 %collective-permute-start.51 = (f32[2,256,128]{2,1,0:T(8,128)S(1)}, f32[2,256,128]{2,1,0:T(8,128)S(1)}, u32[]{:S(2)}, u32[]{:S(2)}) collective-permute-start(f32[2,256,128]{2,1,0:T(8,128)S(1)} %get-tuple-element.132), channel_id=1, source_target_pairs={{0,96},{32,0},{64,32},{96,64},{1,97},{33,1},{65,33},{97,65},{2,98}... | collective-permute-start | bytes 786440 | tf_op jit(solution)/shard_map/ppermute | solution.py:296
  231.6 19.1 %collective-permute-start.58 = (f32[2,128,128]{2,1,0:T(8,128)S(1)}, f32[2,128,128]{2,1,0:T(8,128)S(1)}, u32[]{:S(2)}, u32[]{:S(2)}) collective-permute-start(f32[2,128,128]{2,1,0:T(8,128)S(1)} %constant_dynamic-slice_fusion), channel_id=1, source_target_pairs={{0,1},{1,0},{2,3},{3,2},{4,5},{5,4},{6,7},{7,6},{8,9},{9,8},{10,11... | collective-permute-start | bytes 393224 | tf_op jit(solution)/shard_map/ppermute | solution.py:439
  (73 other events, 911.9 us)
Sparse Core Ops, SparseCore 0:
  14.0 33.2 all-gather.2

commit v4 on v3

--- a/solution.py
+++ b/solution.py
@@ -95,20 +95,19 @@
     hi, lo = split(p)
     ot_ref[0] = values_sum(vt[...], hi, lo)
 
-def picked(info, ql_ref, qr_ref, dl_ref, dr_ref, s00, s01, s02, s03, s10, s11, s12, s13,
-           m0_ref, l0_ref, ot0_ref, ol_ref, or_ref, dq_ref, c_ref, rd_ref,
-           g00, g01, g02, g03, g10, g11, g12, g13,
+def picked(info, ql_ref, qr_ref, dl_ref, dr_ref, s0, s1, s2, s3,
+           m0_ref, l0_ref, ot0_ref, ol_ref, or_ref, dq_ref, c_ref, rd_ref, g0, g1, g2, g3,
            kc, vc, kt, vt, s_sc, phi, plo, dk_acc, dv_acc):
     u, step = pl.program_id(0), pl.program_id(1)
-    pieces = ((s00, s01, s02, s03), (s10, s11, s12, s13))
 
     @pl.when((u == 0) & (step == 0))
     def _():
         for j in range(2):
             for x in range(4):
                 rows = slice((j * 4 + x) * T, (j * 4 + x + 1) * T)
-                fill(pieces[j][x].at[0], rows, kc, kt)
-                fill(pieces[j][x].at[1], rows, vc, vt)
+                piece = (s0, s1, s2, s3)[x]
+                fill(piece.at[j, 0], rows, kc, kt)
+                fill(piece.at[j, 1], rows, vc, vt)
         dk_acc[...] = jnp.zeros_like(dk_acc)
         dv_acc[...] = jnp.zeros_like(dv_acc)
 
@@ -166,11 +165,11 @@
 
     @pl.when((u == 1) & (step == STEPS - 1))
     def _():
-        for j, out in enumerate(((g00, g01, g02, g03), (g10, g11, g12, g13))):
-            for x in range(4):
+        for j in range(2):
+            for x, out in enumerate((g0, g1, g2, g3)):
                 rows = slice((j * 4 + x) * T, (j * 4 + x + 1) * T)
-                out[x][0] = dk_acc[rows, :] * LN2
-                out[x][1] = dv_acc[rows, :]
+                out[j, 0] = dk_acc[rows, :] * LN2
+                out[j, 1] = dv_acc[rows, :]
 
 def own_backward(info, ql_ref, qr_ref, dl_ref, dr_ref, own_ref, p_ref, c_ref, rd_ref, dq_ref,
                  gl_ref, gr_ref, h0, h1, h2, h3, vc, kt, dk_acc, dv_acc):
@@ -221,12 +220,12 @@
 FIRST = pl.BlockSpec((T, HP * W), lambda u, h, i: (0, jnp.where(u == 0, h, STEPS - 1)))
 SECOND = pl.BlockSpec((T, HP * W), lambda u, h, i: (0, jnp.where(u == 0, 0, h)))
 PROBS, ROW, TURNED = (2 * STEPS, BLK, R), (2 * STEPS, 1, R), (2 * STEPS, W, R)
-HALF, PIECE = (T, 4 * W), (2, T, W)
+HALF, PIECE, PAIR = (T, 4 * W), (2, T, W), (2, 2, T, W)
 
 def kernel(body, ins, outs, out_shapes, scratch, flops, limit):
     return pl.pallas_call(
         body,
-        out_shape=[jax.ShapeDtypeStruct(s, F32) for s in out_shapes],
+        out_shape=[pltpu.HBM(s, F32) for s in out_shapes],
         grid_spec=pltpu.PrefetchScalarGridSpec(
             num_scalar_prefetch=1,
             grid=(2, STEPS),
@@ -256,9 +255,9 @@
 def call_picked(info, q, q_far, do, do_far, pieces, m, l, ot):
     return kernel(
         picked,
-        [NEAR, FAR, NEAR, FAR] + [whole(PIECE)] * 8 + [tile(ROW), tile(ROW), tile(TURNED)],
-        [FIRST, SECOND, tile(TURNED), tile(ROW), tile(ROW)] + [whole(PIECE)] * 8,
-        [HALF, HALF, TURNED, ROW, ROW] + [PIECE] * 8,
+        [NEAR, FAR, NEAR, FAR] + [whole(PAIR)] * 4 + [tile(ROW), tile(ROW), tile(TURNED)],
+        [FIRST, SECOND, tile(TURNED), tile(ROW), tile(ROW)] + [whole(PAIR)] * 4,
+        [HALF, HALF, TURNED, ROW, ROW] + [PAIR] * 4,
         [((2 * BLK, 2 * W), BF), ((2 * BLK, 2 * W), BF), ((2 * W, 2 * BLK), BF), ((2 * W, 2 * BLK), BF),
          ((2 * BLK, R), F32), ((2 * BLK, R), BF), ((2 * BLK, R), BF),
          ((2 * BLK, W), F32), ((2 * BLK, W), F32)],
@@ -277,18 +276,29 @@
 
 HEADS = (2, T, W)
 
-def glue(body, args, outs, limit=24):
+def glue(body, args, outs, copies):
+    spec = lambda shape: pl.BlockSpec(shape, lambda i: (0,) * len(shape))
+    if copies:
+        spec = lambda shape: pl.BlockSpec(memory_space=pl.ANY)
+    arrays = args[1:]
     return pl.pallas_call(
         body,
-        out_shape=[jax.ShapeDtypeStruct(s, F32) for s in outs],
-        in_specs=[pl.BlockSpec(memory_space=pltpu.SMEM)]
-        + [pl.BlockSpec(memory_space=pltpu.VMEM)] * (len(args) - 1),
-        out_specs=[pl.BlockSpec(memory_space=pltpu.VMEM)] * len(outs),
-        compiler_params=pltpu.CompilerParams(vmem_limit_bytes=limit << 20),
+        out_shape=[pltpu.HBM(s, F32) for s in outs],
+        grid=(1,),
+        in_specs=[pl.BlockSpec(memory_space=pltpu.SMEM)] + [spec(a.shape) for a in arrays],
+        out_specs=[spec(s) for s in outs],
+        scratch_shapes=[pltpu.SemaphoreType.DMA((copies,))] if copies else [],
+        compiler_params=pltpu.CompilerParams(
+            dimension_semantics=("arbitrary",), vmem_limit_bytes=(4 if copies else 20) << 20),
         cost_estimate=pl.CostEstimate(
-            flops=0, transcendentals=0, bytes_accessed=(len(args) + len(outs)) * HEADS[0] * T * W * 4),
-        name=body.__name__.strip("_"),
-    )(*args)
+            flops=0, transcendentals=0,
+            bytes_accessed=4 * sum(math.prod(s) for s in [a.shape for a in arrays] + list(outs))),
+        name=body.__name__,
+    )(args[0], *arrays)
+
+def finish(pairs, sems):
+    for n, (source, target) in enumerate(pairs):
+        pltpu.make_async_copy(source, target, sems.at[n]).wait()
 
 def shift(array, axis, step):
     if step == 0:
@@ -302,86 +312,85 @@
     block = jnp.maximum(table[y * 4 + x, 1 + j], 0)
     return block // 4, block % 4
 
-def assemble(spot, keys, values, other_keys, other_values, k_ref, v_ref, kv_ref):
+def assemble(spot, keys, values, other_keys, other_values, k_ref, v_ref, kv_ref, sems):
     core = spot[0]
+    pairs = []
     for h in range(2):
         cols = pl.ds(pl.multiple_of((core * 2 + h) * W, W), W)
         for i, (mine, other, out) in enumerate(
                 ((keys, other_keys, k_ref), (values, other_values, v_ref))):
             for ref, half in ((mine, core), (other, 1 - core)):
                 rows = pl.ds(pl.multiple_of(half * (T // 2), T // 2), T // 2)
-                a = ref[:, cols]
-                out[h, rows, :] = a
-                kv_ref[i, h, rows, :] = a
-
-def pick(j, table, *refs):
+                pairs += [(ref.at[:, cols], out.at[h, rows, :]),
+                          (ref.at[:, cols], kv_ref.at[i, h, rows, :])]
+    for n, (source, target) in enumerate(pairs):
+        pltpu.make_async_copy(source, target, sems.at[n]).start()
+    finish(pairs, sems)
+
+def pick(table, *refs):
+    y, x = lax.axis_index("y"), lax.axis_index("x")
+    k_in, v_in, k_out, v_out, sems = refs[0:4], refs[4:8], refs[8:11], refs[11:14], refs[14]
+    pairs = []
+    for step in (1, 2, 3):
+        for j in range(2):
+            row, _ = chosen(table, y, (x + step) % 4, j)
+            _, column = chosen(table, (y + step) % 4, x, j)
+            for off, arrays, out in (((y - row) % 4, k_in, k_out), ((x - column) % 4, v_in, v_out)):
+                target = out[step - 1].at[j]
+                for i in range(4):
+                    @pl.when(off == i)
+                    def _(source=arrays[i], target=target, n=len(pairs)):
+                        pltpu.make_async_copy(source, target, sems.at[n]).start()
+                pairs.append((arrays[0], target))
+    finish(pairs, sems)
+
+def join(table, *refs):
+    y, x = lax.axis_index("y"), lax.axis_index("x")
+    head = lax.axis_index("z") // 2
+    k_along, v_along, k_in, v_in = refs[0:4], refs[4:8], refs[8:11], refs[11:14]
+    same, cross, sems = refs[14:]
+    pairs = []
+    for j in range(2):
+        row, column = chosen(table, y, x, j)
+        for n, near, off, along, got in (
+                (0, (y - row) % 4, (x - column) % 4, k_along, k_in),
+                (1, (x - column) % 4, (y - row) % 4, v_along, v_in)):
+            for h, out in ((head, same), (1 - head, cross)):
+                target = out.at[j, n]
+                for i in range(4):
+                    @pl.when((off == 0) & (near == i))
+                    def _(source=along[i].at[h], target=target, at=len(pairs)):
+                        pltpu.make_async_copy(source, target, sems.at[at]).start()
+                for i in range(3):
+                    @pl.when(off == i + 1)
+                    def _(source=got[i].at[j, h], target=target, at=len(pairs)):
+                        pltpu.make_async_copy(source, target, sems.at[at]).start()
+                pairs.append((along[0].at[h], target))
+    finish(pairs, sems)
+
+def spread(spot, mine, added, passed, passed2, k_out, v_out):
+    head = spot[1]
+    for j in range(mine.shape[0]):
+        for n, out in ((0, k_out), (1, v_out)):
+            out[j, head] = mine[j, n] + added[j, n]
+            out[j, 1 - head] = passed[j, n] + passed2[j, n]
+
+def collect(table, *refs):
     y, x = lax.axis_index("y"), lax.axis_index("x")
     k_in, v_in, k_out, v_out = (refs[i:i + 4] for i in range(0, 16, 4))
+    for ref in k_out + v_out:
+        ref[...] = jnp.zeros_like(ref)
     for step in range(4):
-        row, _ = chosen(table, y, (x + step) % 4, j)
-        _, column = chosen(table, (y + step) % 4, x, j)
-        for off, arrays, out in (((y - row) % 4, k_in, k_out), ((x - column) % 4, v_in, v_out)):
-            for i in range(4):
-                @pl.when(off == i)
-                def _(source=arrays[i], out=out[step]):
-                    out[...] = source[...]
-
-def pick0(*refs):
-    pick(0, *refs)
-
-def pick1(*refs):
-    pick(1, *refs)
-
-def join(j, table, *refs):
-    y, x = lax.axis_index("y"), lax.axis_index("x")
-    head = lax.axis_index("z") // 2
-    row, column = chosen(table, y, x, j)
-    k_in, v_in, (same, cross) = refs[0:4], refs[4:8], refs[8:10]
-    for i in range(4):
-        for n, off, source in ((0, (x - column) % 4, k_in[i]), (1, (y - row) % 4, v_in[i])):
-            @pl.when(off == i)
-            def _(n=n, source=source):
-                same[n] = source[head]
-                cross[n] = source[1 - head]
-
-def join0(*refs):
-    join(0, *refs)
-
-def join1(*refs):
-    join(1, *refs)
-
-def spread(spot, kept, added, passed, k_out, v_out):
-    head = spot[1]
-    for n, out in ((0, k_out), (1, v_out)):
-        out[head] = kept[n] + added[n]
-        out[1 - head] = passed[n]
-
-def collect(j, table, *refs):
-    y, x = lax.axis_index("y"), lax.axis_index("x")
-    if j == 0:
-        k_in, v_in, k_out, v_out = (refs[i:i + 4] for i in range(0, 16, 4))
-        for ref in k_out + v_out:
-            ref[...] = jnp.zeros_like(ref)
-    else:
-        k_in, v_in, k_old, v_old, k_out, v_out = (refs[i:i + 4] for i in range(0, 24, 4))
-        for ref, old in zip(k_out + v_out, k_old + v_old):
-            ref[...] = old[...]
-    for step in range(4):
-        row, column = chosen(table, y, (x - step) % 4, j)
-        row2, column2 = chosen(table, (y - step) % 4, x, j)
-        for hit, off, source, out in (
-                (column == x, (y - row) % 4, k_in[step], k_out),
-                (row2 == y, (x - column2) % 4, v_in[step], v_out)):
-            for i in range(4):
-                @pl.when(hit & (off == i))
-                def _(source=source, ref=out[i]):
-                    ref[...] += source[...]
-
-def collect0(*refs):
-    collect(0, *refs)
-
-def collect1(*refs):
-    collect(1, *refs)
+        for j in range(2):
+            row, column = chosen(table, y, (x - step) % 4, j)
+            row2, column2 = chosen(table, (y - step) % 4, x, j)
+            for hit, off, source, out in (
+                    (column == x, (y - row) % 4, k_in[step], k_out),
+                    (row2 == y, (x - column2) % 4, v_in[step], v_out)):
+                for i in range(4):
+                    @pl.when(hit & (off == i))
+                    def _(source=source, ref=out[i], j=j):
+                        ref[...] += source[j]
 
 def shards(queries, keys, values, cotangent, selected):
     core, z = lax.axis_index("head"), lax.axis_index("z")
@@ -398,20 +407,16 @@
         for a in (queries, cotangent)
     )
     other = [lax.ppermute(a, "head", swap) for a in (keys, values)]
-    k, v, kv = glue(assemble, (spot, keys, values, *other), (HEADS, HEADS, (2,) + HEADS))
+    k, v, kv = glue(assemble, (spot, keys, values, *other), (HEADS, HEADS, (2,) + HEADS), 16)
     own = lax.all_gather(kv, "z", axis=0)
 
     k_along = [shift(k, "y", s) for s in range(4)]
     v_along = [shift(v, "x", s) for s in range(4)]
-    pieces = []
-    for pick_j, join_j in ((pick0, join0), (pick1, join1)):
-        sent = glue(pick_j, (selected, *k_along, *v_along), (HEADS,) * 8)
-        k_got = [shift(sent[s], "x", s) for s in range(4)]
-        v_got = [shift(sent[4 + s], "y", s) for s in range(4)]
-        same, cross = glue(join_j, (selected, *k_got, *v_got), (HEADS, HEADS))
-        p1 = mirror(same, 1)
-        p3 = mirror(cross, 3)
-        pieces += [same, p1, mirror(p3, 1), p3]
+    sent = glue(pick, (selected, *k_along, *v_along), (PAIR,) * 6, 12)
+    k_got = [shift(sent[s], "x", s + 1) for s in range(3)]
+    v_got = [shift(sent[s + 3], "y", s + 1) for s in range(3)]
+    same, cross = glue(join, (selected, *k_along, *v_along, *k_got, *v_got), (PAIR, PAIR), 8)
+    pieces = [same, mirror(same, 1), mirror(cross, 2), mirror(cross, 3)]
 
     p, m, l, ot = call_own_forward(info, queries, q_far, own)
     out = call_picked(info, queries, q_far, cotangent, do_far, pieces, m, l, ot)
@@ -419,18 +424,15 @@
     last = call_own_backward(info, queries, q_far, cotangent, do_far, own, p, c, rd, dq)
 
     def reduced(g):
-        passed = mirror(g[3] + mirror(g[2], 1), 3)
-        return glue(spread, (spot, g[0], mirror(g[1], 1), passed), (HEADS, HEADS))
-
-    sums = ()
-    for j, collect_j in enumerate((collect0, collect1)):
-        k_part, v_part = reduced(out[5 + 4 * j:9 + 4 * j])
-        arrived = [shift(k_part, "x", s) for s in range(4)]
-        arrived += [shift(v_part, "y", s) for s in range(4)]
-        sums = glue(collect_j, (selected, *arrived, *sums), (HEADS,) * 8)
-    own_k, own_v = reduced(last[2:6])
-    grad_k = own_k + sum(shift(sums[s], "y", (4 - s) % 4) for s in range(4))
-    grad_v = own_v + sum(shift(sums[4 + s], "x", (4 - s) % 4) for s in range(4))
+        arrived = [g[0]] + [mirror(g[flip], flip) for flip in (1, 2, 3)]
+        return glue(spread, (spot, *arrived), (g[0].shape,) * 2, 0)
+
+    k_part, v_part = reduced(out[5:9])
+    arrived = [shift(k_part, "x", s) for s in range(4)] + [shift(v_part, "y", s) for s in range(4)]
+    sums = glue(collect, (selected, *arrived), (HEADS,) * 8, 0)
+    own_k, own_v = reduced([a[None] for a in last[2:6]])
+    grad_k = own_k[0] + sum(shift(sums[s], "y", (4 - s) % 4) for s in range(4))
+    grad_v = own_v[0] + sum(shift(sums[4 + s], "x", (4 - s) % 4) for s in range(4))
 
     half = T // 2
 

time: 263 us -> 269 us (1.023)
  waiting for transfers between devices: 24.3 us -> 83 us
  starting transfers between devices: 112 us -> 70.2 us
  local copies, waits for them, and re-layouts: 26.5 us -> 19.9 us
    ppermute x19 -> x13, waiting for transfers between devices: 6.49 us -> 40.9 us  [mirror(): return lax.ppermute(array, 'z', [(i, i ^ flip) for i in range(4)])]
    ppermute x36 -> x24, waiting for transfers between devices: 16.2 us -> 40.6 us  [shift(): return lax.ppermute(array, axis, [(i, (i + step) % 4) for i in range(4)])]
    ppermute x36 -> x24, starting transfers between devices: 60.4 us -> 40.4 us  [shift(): return lax.ppermute(array, axis, [(i, (i + step) % 4) for i in range(4)])]
    ppermute x19 -> x13, starting transfers between devices: 31.9 us -> 17.9 us  [mirror(): return lax.ppermute(array, 'z', [(i, i ^ flip) for i in range(4)])]
    unnamed x75 -> x55, local copies, waits for them, and re-layouts: 24.2 us -> 16.1 us
    ppermute x2, starting transfers between devices: 17.9 us -> 10.3 us  [home(): lax.ppermute(lax.dynamic_slice_in_dim(a, (1 - core) * half, half, 1), 'he...]
    pallas_call x11 -> x7, Pallas kernels: 50.3 us -> 49.9 us  [the longest x1 38.1 us: call_picked(): kernel(picked, [NEAR, FAR, NEAR, FAR] + [whole(PAIR)] * 4 + [tile(ROW), t...]
  transfers between devices with their start and end apart: 60 -> 42, of which waited for: 13 -> 15; matrix products, arithmetic and copies ran while one was open for 4% -> 4% of each run, Pallas kernels for 13% -> 12%
where the time goes in v4:
time: 269 us; the launch traced here: 268 us
  waiting for transfers between devices  83 us (31%)
  Pallas kernels  73.7 us (27%)
  starting transfers between devices  70.2 us (26%)
  local copies, waits for them, and re-layouts  19.9 us (7%)
  between operations  14.3 us (5%)
  other arithmetic  6.33 us (2%)
    ppermute x13, waiting for transfers between devices, mirror(): return lax.ppermute(array, 'z', [(i, i ^ flip) for i in range(4)])  40.9 us
    ppermute x24, waiting for transfers between devices, shift(): return lax.ppermute(array, axis, [(i, (i + step) % 4) for i in range(4)])  40.6 us
    ppermute x24, starting transfers between devices, shift(): return lax.ppermute(array, axis, [(i, (i + step) % 4) for i in range(4)])  40.4 us
    pallas_call x1, Pallas kernels, call_picked(): kernel(picked, [NEAR, FAR, NEAR, FAR] + [whole(PAIR)] * 4 + [tile(ROW), t...  38.1 us
    ppermute x13, starting transfers between devices, mirror(): return lax.ppermute(array, 'z', [(i, i ^ flip) for i in range(4)])  17.9 us
    unnamed x55, local copies, waits for them, and re-layouts  16.1 us
    pallas_call x1, Pallas kernels, call_own_backward(): kernel(own_backward, [NEAR, FAR, NEAR, FAR, whole(own.shape), tile(PROBS)...  14.2 us
    pallas_call x6, Pallas kernels, glue(): pl.pallas_call(body, out_shape=[pltpu.HBM(s, F32) for s in outs], grid=(1...  11.9 us
  transfers between devices with their start and end apart: 42, of which 15 were waited for; matrix products, arithmetic and copies ran while one was open for 4% of the time, Pallas kernels for 12%

profile of v4, /device:TPU:1, one launch (start us, length us, event | category | flops | bytes accessed | tf_op | source)
XLA Modules:
  0.0 267.5 jit_solution(1290285029709654851)
XLA Ops:
  15.5 2.6 collective-permute-start.5
  26.5 3.5 %collective-permute-done.5.refs_2_ = f32[2,256,128]{2,1,0:T(8,128)S(1)} collective-permute-done((f32[2,256,128]{2,1,0:T(8,128)}, f32[2,256,128]{2,1,0:T(8,128)S(1)}, u32[]{:S(2)}, u32[]{:S(2)}) %collective-permute-start.5) | collective-permute-done | bytes 262176 | tf_op jit(solution)/shard_map/ppermute | solution.py:306
  30.0 3.8 %collective-permute-done.8.refs_6_ = f32[2,256,128]{2,1,0:T(8,128)S(1)} collective-permute-done((f32[2,256,128]{2,1,0:T(8,128)}, f32[2,256,128]{2,1,0:T(8,128)S(1)}, u32[]{:S(2)}, u32[]{:S(2)}) %collective-permute-start.8) | collective-permute-done | bytes 262176 | tf_op jit(solution)/shard_map/ppermute | solution.py:306
  38.1 3.5 %collective-permute-start.10 = (f32[2,2,256,128]{3,2,1,0:T(8,128)}, f32[2,2,256,128]{3,2,1,0:T(8,128)S(1)}, u32[]{:S(2)}, u32[]{:S(2)}) collective-permute-start(f32[2,2,256,128]{3,2,1,0:T(8,128)} %get-tuple-element.48), channel_id=1, source_target_pairs={{0,8},{8,16},{16,24},{24,0},{1,9},{9,17},{17,25},{25,1},{2,10},{10... | collective-permute-start | bytes 1572872 | tf_op jit(solution)/shard_map/ppermute | solution.py:306
  44.7 8.2 %collective-permute-done.10.refs_8_ = f32[2,2,256,128]{3,2,1,0:T(8,128)S(1)} collective-permute-done((f32[2,2,256,128]{3,2,1,0:T(8,128)}, f32[2,2,256,128]{3,2,1,0:T(8,128)S(1)}, u32[]{:S(2)}, u32[]{:S(2)}) %collective-permute-start.10) | collective-permute-done | bytes 524320 | tf_op jit(solution)/shard_map/ppermute | solution.py:306
  54.8 9.8 %collective-permute-done.11.refs_9_ = f32[2,2,256,128]{3,2,1,0:T(8,128)S(1)} collective-permute-done((f32[2,2,256,128]{3,2,1,0:T(8,128)}, f32[2,2,256,128]{3,2,1,0:T(8,128)S(1)}, u32[]{:S(2)}, u32[]{:S(2)}) %collective-permute-start.11) | collective-permute-done | bytes 524320 | tf_op jit(solution)/shard_map/ppermute | solution.py:306
  64.6 3.8 %collective-permute-start = (f32[256,512]{1,0:T(8,128)}, f32[256,512]{1,0:T(8,128)S(1)}, u32[]{:S(2)}, u32[]{:S(2)}) collective-permute-start(f32[256,512]{1,0:T(8,128)} %constant_dynamic-slice_fusion.3), channel_id=1, source_target_pairs={{0,6},{2,4},{4,2},{6,0},{1,7},{3,5},{5,3},{7,1},{8,14},{10,12},{12... | collective-permute-start | bytes 1572872 | tf_op jit(solution)/shard_map/ppermute | solution.py:309
  75.8 3.3 %collective-permute-start.17 = (f32[2,2,256,128]{3,2,1,0:T(8,128)}, f32[2,2,256,128]{3,2,1,0:T(8,128)S(1)}, u32[]{:S(2)}, u32[]{:S(2)}) collective-permute-start(f32[2,2,256,128]{3,2,1,0:T(8,128)} %get-tuple-element.55), channel_id=1, source_target_pairs={{0,4},{2,6},{4,0},{6,2},{1,5},{3,7},{5,1},{7,3},{8,12},{10,14},{12... | collective-permute-start | bytes 1572872 | tf_op jit(solution)/shard_map/ppermute | solution.py:309
  82.2 9.5 %own_forward.1 = (f32[4,1024,512]{2,1,0:T(8,128)}, f32[4,1,512]{2,1,0:T(1,128)}, f32[4,1,512]{2,1,0:T(1,128)}, f32[4,128,512]{2,1,0:T(8,128)}) custom-call(s32[4]{0:T(128)S(1)} %pad_add_fusion.info, f32[256,1024]{1,0:T(8,128)S(1)} %copy-done.7, f32[256,512]{1,0:T(8,128)S(1)} %collective-permute-done.qr_ref, f32[4,2,2,256,128]{4,3,2,1,0:T(8,128)S(1)} %bitcast.29), custom_call_target="tpu_custom_call" | custom-call | flops 4294967296 | bytes 16777216 | tf_op jit(solution)/shard_map/own_forward/pallas_call | solution.py:246
  91.7 8.4 %collective-permute-done.1.dr_ref = f32[256,512]{1,0:T(8,128)} collective-permute-done((f32[256,512]{1,0:T(8,128)}, f32[256,512]{1,0:T(8,128)}, u32[]{:S(2)}, u32[]{:S(2)}) %collective-permute-start.1) | collective-permute-done | bytes 524320 | tf_op jit(solution)/shard_map/ppermute | solution.py:309
  101.1 11.4 %collective-permute-done.18.s3 = f32[2,2,256,128]{3,2,1,0:T(8,128)S(1)} collective-permute-done((f32[2,2,256,128]{3,2,1,0:T(8,128)}, f32[2,2,256,128]{3,2,1,0:T(8,128)S(1)}, u32[]{:S(2)}, u32[]{:S(2)}) %collective-permute-start.18) | collective-permute-done | bytes 524320 | tf_op jit(solution)/shard_map/ppermute | solution.py:309
  114.6 38.1 %picked.1 = (f32[256,512]{1,0:T(8,128)}, f32[256,512]{1,0:T(8,128)}, f32[4,128,512]{2,1,0:T(8,128)}, f32[4,1,512]{2,1,0:T(1,128)}, f32[4,1,512]{2,1,0:T(1,128)},...) custom-call(s32[4]{0:T(128)S(1)} %pad_add_fusion.info, ...), custom_call_target="tpu_custom_call" | custom-call | flops 21474836480 | bytes 16777216 | tf_op jit(solution)/shard_map/picked/pallas_call | solution.py:256
  152.8 3.6 %collective-permute-start.25 = (f32[2,2,256,128]{3,2,1,0:T(8,128)}, f32[2,2,256,128]{3,2,1,0:T(8,128)S(1)}, u32[]{:S(2)}, u32[]{:S(2)}) collective-permute-start(f32[2,2,256,128]{3,2,1,0:T(8,128)} %get-tuple-element.75), channel_id=1, source_target_pairs={{0,4},{2,6},{4,0},{6,2},{1,5},{3,7},{5,1},{7,3},{8,12},{10,14},{12... | collective-permute-start | bytes 1572872 | tf_op jit(solution)/shard_map/ppermute | solution.py:309
  156.6 7.0 %collective-permute-done.24.added = f32[2,2,256,128]{3,2,1,0:T(8,128)S(1)} collective-permute-done((f32[2,2,256,128]{3,2,1,0:T(8,128)}, f32[2,2,256,128]{3,2,1,0:T(8,128)S(1)}, u32[]{:S(2)}, u32[]{:S(2)}) %collective-permute-start.24) | collective-permute-done | bytes 524320 | tf_op jit(solution)/shard_map/ppermute | solution.py:309
  163.7 13.1 %collective-permute-done.25.passed = f32[2,2,256,128]{3,2,1,0:T(8,128)S(1)} collective-permute-done((f32[2,2,256,128]{3,2,1,0:T(8,128)}, f32[2,2,256,128]{3,2,1,0:T(8,128)S(1)}, u32[]{:S(2)}, u32[]{:S(2)}) %collective-permute-start.25) | collective-permute-done | bytes 524320 | tf_op jit(solution)/shard_map/ppermute | solution.py:309
  179.5 4.9 %collective-permute-start.28 = (f32[2,2,256,128]{3,2,1,0:T(8,128)}, f32[2,2,256,128]{3,2,1,0:T(8,128)S(1)}, u32[]{:S(2)}, u32[]{:S(2)}) collective-permute-start(f32[2,2,256,128]{3,2,1,0:T(8,128)} %get-tuple-element.77.refs_0_), channel_id=1, source_target_pairs={{0,16},{8,24},{16,0},{24,8},{1,17},{9,25},{17,1},{25,9},{2,18},{10... | collective-permute-start | bytes 1572872 | tf_op jit(solution)/shard_map/ppermute | solution.py:306
  188.9 13.1 %collective-permute-done.28.refs_2_ = f32[2,2,256,128]{3,2,1,0:T(8,128)S(1)} collective-permute-done((f32[2,2,256,128]{3,2,1,0:T(8,128)}, f32[2,2,256,128]{3,2,1,0:T(8,128)S(1)}, u32[]{:S(2)}, u32[]{:S(2)}) %collective-permute-start.28) | collective-permute-done | bytes 524320 | tf_op jit(solution)/shard_map/ppermute | solution.py:306
  204.7 14.2 %own_backward.1 = (f32[256,512]{1,0:T(8,128)}, f32[256,512]{1,0:T(8,128)}, f32[2,256,128]{2,1,0:T(8,128)}, f32[2,256,128]{2,1,0:T(8,128)}, f32[2,256,128]{2,1,0:T(8,128)}, /*index=5*/f32[2,256,128]{2,1,0:T(8,128)}) custom-call(s32[4]{0:T(128)S(1)} %pad_add_fusion.info, f32[256,1024]{1,0:T(8,128)S(1)} %copy-done.8, ...), custom_call_target="tpu_custom_call" | custom-call | flops 6442450944 | bytes 16777216 | tf_op jit(solution)/shard_map/own_backward/pallas_call | solution.py:268
  222.9 3.0 %collect.1 = (f32[2,256,128]{2,1,0:T(8,128)}, f32[2,256,128]{2,1,0:T(8,128)}, f32[2,256,128]{2,1,0:T(8,128)}, f32[2,256,128]{2,1,0:T(8,128)}, f32[2,256,128]{2,1...) custom-call(s32[16,3]{1,0:T(8,128)S(1)} %copy.13.table, ...), custom_call_target="tpu_custom_call" | custom-call | bytes 6291456 | tf_op jit(solution)/shard_map/collect/pallas_call | solution.py:284
  225.9 4.5 %collective-permute-start.39 = (f32[2,256,128]{2,1,0:T(8,128)}, f32[2,256,128]{2,1,0:T(8,128)S(1)}, u32[]{:S(2)}, u32[]{:S(2)}) collective-permute-start(f32[2,256,128]{2,1,0:T(8,128)} %get-tuple-element.87), channel_id=1, source_target_pairs={{0,8},{8,16},{16,24},{24,0},{1,9},{9,17},{17,25},{25,1},{2,10},{10... | collective-permute-start | bytes 786440 | tf_op jit(solution)/shard_map/ppermute | solution.py:306
  230.4 2.6 collective-permute-start.38
  239.5 3.7 %collective-permute-start.34 = (f32[2,256,128]{2,1,0:T(8,128)}, f32[2,256,128]{2,1,0:T(8,128)S(1)}, u32[]{:S(2)}, u32[]{:S(2)}) collective-permute-start(f32[2,256,128]{2,1,0:T(8,128)} %get-tuple-element.81), channel_id=1, source_target_pairs={{0,64},{32,96},{64,0},{96,32},{1,65},{33,97},{65,1},{97,33},{2,66}... | collective-permute-start | bytes 786440 | tf_op jit(solution)/shard_map/ppermute | solution.py:306
  246.4 6.5 %collective-permute-start.40 = (f32[2,128,128]{2,1,0:T(8,128)S(1)}, f32[2,128,128]{2,1,0:T(8,128)S(1)}, u32[]{:S(2)}, u32[]{:S(2)}) collective-permute-start(f32[2,128,128]{2,1,0:T(8,128)S(1)} %constant_dynamic-slice_fusion), channel_id=1, source_target_pairs={{0,1},{1,0},{2,3},{3,2},{4,5},{5,4},{6,7},{7,6},{8,9},{9,8},{10,11... | collective-permute-start | bytes 393224 | tf_op jit(solution)/shard_map/ppermute | solution.py:441
  254.1 3.8 %collective-permute-start.36 = (f32[2,128,128]{2,1,0:T(8,128)S(1)}, f32[2,128,128]{2,1,0:T(8,128)S(1)}, u32[]{:S(2)}, u32[]{:S(2)}) collective-permute-start(f32[2,128,128]{2,1,0:T(8,128)S(1)} %constant_dynamic-slice_fusion.1), channel_id=1, source_target_pairs={{0,1},{1,0},{2,3},{3,2},{4,5},{5,4},{6,7},{7,6},{8,9},{9,8},{10,11... | collective-permute-start | bytes 393224 | tf_op jit(solution)/shard_map/ppermute | solution.py:441
  (143 shorter events, 67.3 us)
Async XLA Ops:
  7.2 72.2 %all-gather.3.cloned.1.call-start = ((), (), s32[]{:S(2)}) async-start(), calls=%async_computation | async-start | bytes 2621440 | tf_op jit(solution)/shard_map/all_gather | solution.py:411
  15.5 14.5 %collective-permute-start.5 = (f32[2,256,128]{2,1,0:T(8,128)}, f32[2,256,128]{2,1,0:T(8,128)S(1)}, u32[]{:S(2)}, u32[]{:S(2)}) collective-permute-start(f32[2,256,128]{2,1,0:T(8,128)} %get-tuple-element.46.refs_0_), channel_id=1, source_target_pairs={{0,64},{32,96},{64,0},{96,32},{1,65},{33,97},{65,1},{97,33},{2,66}... | collective-permute-start | bytes 786440 | tf_op jit(solution)/shard_map/ppermute | solution.py:306
  38.1 14.8 %collective-permute-start.10 = (f32[2,2,256,128]{3,2,1,0:T(8,128)}, f32[2,2,256,128]{3,2,1,0:T(8,128)S(1)}, u32[]{:S(2)}, u32[]{:S(2)}) collective-permute-start(f32[2,2,256,128]{3,2,1,0:T(8,128)} %get-tuple-element.48), channel_id=1, source_target_pairs={{0,8},{8,16},{16,24},{24,0},{1,9},{9,17},{17,25},{25,1},{2,10},{10... | collective-permute-start | bytes 1572872 | tf_op jit(solution)/shard_map/ppermute | solution.py:306
  41.7 22.9 %collective-permute-start.11 = (f32[2,2,256,128]{3,2,1,0:T(8,128)}, f32[2,2,256,128]{3,2,1,0:T(8,128)S(1)}, u32[]{:S(2)}, u32[]{:S(2)}) collective-permute-start(f32[2,2,256,128]{3,2,1,0:T(8,128)} %get-tuple-element.49), channel_id=1, source_target_pairs={{0,16},{8,24},{16,0},{24,8},{1,17},{9,25},{17,1},{25,9},{2,18},{10... | collective-permute-start | bytes 1572872 | tf_op jit(solution)/shard_map/ppermute | solution.py:306
  42.4 27.9 %collective-permute-start.12 = (f32[2,2,256,128]{3,2,1,0:T(8,128)}, f32[2,2,256,128]{3,2,1,0:T(8,128)S(1)}, u32[]{:S(2)}, u32[]{:S(2)}) collective-permute-start(f32[2,2,256,128]{3,2,1,0:T(8,128)} %get-tuple-element.50), channel_id=1, source_target_pairs={{0,24},{8,0},{16,8},{24,16},{1,25},{9,1},{17,9},{25,17},{2,26},{10... | collective-permute-start | bytes 1572872 | tf_op jit(solution)/shard_map/ppermute | solution.py:306
  44.2 26.1 %collective-permute-start.13 = (f32[2,2,256,128]{3,2,1,0:T(8,128)}, f32[2,2,256,128]{3,2,1,0:T(8,128)S(1)}, u32[]{:S(2)}, u32[]{:S(2)}) collective-permute-start(f32[2,2,256,128]{3,2,1,0:T(8,128)} %get-tuple-element.51), channel_id=1, source_target_pairs={{0,32},{32,64},{64,96},{96,0},{1,33},{33,65},{65,97},{97,1},{2,34}... | collective-permute-start | bytes 1572872 | tf_op jit(solution)/shard_map/ppermute | solution.py:306
  44.6 25.7 %collective-permute-start.14 = (f32[2,2,256,128]{3,2,1,0:T(8,128)}, f32[2,2,256,128]{3,2,1,0:T(8,128)S(1)}, u32[]{:S(2)}, u32[]{:S(2)}) collective-permute-start(f32[2,2,256,128]{3,2,1,0:T(8,128)} %get-tuple-element.52), channel_id=1, source_target_pairs={{0,64},{32,96},{64,0},{96,32},{1,65},{33,97},{65,1},{97,33},{2,66}... | collective-permute-start | bytes 1572872 | tf_op jit(solution)/shard_map/ppermute | solution.py:306
  52.9 17.4 %collective-permute-start.15 = (f32[2,2,256,128]{3,2,1,0:T(8,128)}, f32[2,2,256,128]{3,2,1,0:T(8,128)S(1)}, u32[]{:S(2)}, u32[]{:S(2)}) collective-permute-start(f32[2,2,256,128]{3,2,1,0:T(8,128)} %get-tuple-element.53), channel_id=1, source_target_pairs={{0,96},{32,0},{64,32},{96,64},{1,97},{33,1},{65,33},{97,65},{2,98}... | collective-permute-start | bytes 1572872 | tf_op jit(solution)/shard_map/ppermute | solution.py:306
  64.6 14.8 %collective-permute-start = (f32[256,512]{1,0:T(8,128)}, f32[256,512]{1,0:T(8,128)S(1)}, u32[]{:S(2)}, u32[]{:S(2)}) collective-permute-start(f32[256,512]{1,0:T(8,128)} %constant_dynamic-slice_fusion.3), channel_id=1, source_target_pairs={{0,6},{2,4},{4,2},{6,0},{1,7},{3,5},{5,3},{7,1},{8,14},{10,12},{12... | collective-permute-start | bytes 1572872 | tf_op jit(solution)/shard_map/ppermute | solution.py:309
  70.2 29.9 %collective-permute-start.1 = (f32[256,512]{1,0:T(8,128)}, f32[256,512]{1,0:T(8,128)}, u32[]{:S(2)}, u32[]{:S(2)}) collective-permute-start(f32[256,512]{1,0:T(8,128)} %constant_dynamic-slice_fusion.2), channel_id=1, source_target_pairs={{0,6},{2,4},{4,2},{6,0},{1,7},{3,5},{5,3},{7,1},{8,14},{10,12},{12... | collective-permute-start | bytes 1572872 | tf_op jit(solution)/shard_map/ppermute | solution.py:309
  74.1 26.1 %collective-permute-start.16 = (f32[2,2,256,128]{3,2,1,0:T(8,128)}, f32[2,2,256,128]{3,2,1,0:T(8,128)S(1)}, u32[]{:S(2)}, u32[]{:S(2)}) collective-permute-start(f32[2,2,256,128]{3,2,1,0:T(8,128)} %get-tuple-element.54.s0), channel_id=1, source_target_pairs={{0,2},{2,0},{4,6},{6,4},{1,3},{3,1},{5,7},{7,5},{8,10},{10,8},{12,... | collective-permute-start | bytes 1572872 | tf_op jit(solution)/shard_map/ppermute | solution.py:309
  75.8 25.3 %collective-permute-start.17 = (f32[2,2,256,128]{3,2,1,0:T(8,128)}, f32[2,2,256,128]{3,2,1,0:T(8,128)S(1)}, u32[]{:S(2)}, u32[]{:S(2)}) collective-permute-start(f32[2,2,256,128]{3,2,1,0:T(8,128)} %get-tuple-element.55), channel_id=1, source_target_pairs={{0,4},{2,6},{4,0},{6,2},{1,5},{3,7},{5,1},{7,3},{8,12},{10,14},{12... | collective-permute-start | bytes 1572872 | tf_op jit(solution)/shard_map/ppermute | solution.py:309
  79.1 33.3 %collective-permute-start.18 = (f32[2,2,256,128]{3,2,1,0:T(8,128)}, f32[2,2,256,128]{3,2,1,0:T(8,128)S(1)}, u32[]{:S(2)}, u32[]{:S(2)}) collective-permute-start(f32[2,2,256,128]{3,2,1,0:T(8,128)} %get-tuple-element.55), channel_id=1, source_target_pairs={{0,6},{2,4},{4,2},{6,0},{1,7},{3,5},{5,3},{7,1},{8,14},{10,12},{12... | collective-permute-start | bytes 1572872 | tf_op jit(solution)/shard_map/ppermute | solution.py:309
  152.8 24.0 %collective-permute-start.25 = (f32[2,2,256,128]{3,2,1,0:T(8,128)}, f32[2,2,256,128]{3,2,1,0:T(8,128)S(1)}, u32[]{:S(2)}, u32[]{:S(2)}) collective-permute-start(f32[2,2,256,128]{3,2,1,0:T(8,128)} %get-tuple-element.75), channel_id=1, source_target_pairs={{0,4},{2,6},{4,0},{6,2},{1,5},{3,7},{5,1},{7,3},{8,12},{10,14},{12... | collective-permute-start | bytes 1572872 | tf_op jit(solution)/shard_map/ppermute | solution.py:309
  156.4 20.4 %collective-permute-start.26 = (f32[2,2,256,128]{3,2,1,0:T(8,128)}, f32[2,2,256,128]{3,2,1,0:T(8,128)S(1)}, u32[]{:S(2)}, u32[]{:S(2)}) collective-permute-start(f32[2,2,256,128]{3,2,1,0:T(8,128)} %get-tuple-element.76), channel_id=1, source_target_pairs={{0,6},{2,4},{4,2},{6,0},{1,7},{3,5},{5,3},{7,1},{8,14},{10,12},{12... | collective-permute-start | bytes 1572872 | tf_op jit(solution)/shard_map/ppermute | solution.py:309
  179.5 22.6 %collective-permute-start.28 = (f32[2,2,256,128]{3,2,1,0:T(8,128)}, f32[2,2,256,128]{3,2,1,0:T(8,128)S(1)}, u32[]{:S(2)}, u32[]{:S(2)}) collective-permute-start(f32[2,2,256,128]{3,2,1,0:T(8,128)} %get-tuple-element.77.refs_0_), channel_id=1, source_target_pairs={{0,16},{8,24},{16,0},{24,8},{1,17},{9,25},{17,1},{25,9},{2,18},{10... | collective-permute-start | bytes 1572872 | tf_op jit(solution)/shard_map/ppermute | solution.py:306
  184.4 53.5 %collective-permute-start.19 = (f32[256,512]{1,0:T(8,128)}, f32[256,512]{1,0:T(8,128)S(1)}, u32[]{:S(2)}, u32[]{:S(2)}) collective-permute-start(f32[256,512]{1,0:T(8,128)} %get-tuple-element.61), channel_id=1, source_target_pairs={{0,6},{2,4},{4,2},{6,0},{1,7},{3,5},{5,3},{7,1},{8,14},{10,12},{12... | collective-permute-start | bytes 1572872 | tf_op jit(solution)/shard_map/ppermute | solution.py:309
  184.9 34.0 %collective-permute-start.29 = (f32[2,2,256,128]{3,2,1,0:T(8,128)}, f32[2,2,256,128]{3,2,1,0:T(8,128)S(1)}, u32[]{:S(2)}, u32[]{:S(2)}) collective-permute-start(f32[2,2,256,128]{3,2,1,0:T(8,128)} %get-tuple-element.77.refs_0_), channel_id=1, source_target_pairs={{0,24},{8,0},{16,8},{24,16},{1,25},{9,1},{17,9},{25,17},{2,26},{10... | collective-permute-start | bytes 1572872 | tf_op jit(solution)/shard_map/ppermute | solution.py:306
  187.0 33.4 %collective-permute-start.30 = (f32[2,2,256,128]{3,2,1,0:T(8,128)}, f32[2,2,256,128]{3,2,1,0:T(8,128)S(1)}, u32[]{:S(2)}, u32[]{:S(2)}) collective-permute-start(f32[2,2,256,128]{3,2,1,0:T(8,128)} %get-tuple-element.78.refs_4_), channel_id=1, source_target_pairs={{0,32},{32,64},{64,96},{96,0},{1,33},{33,65},{65,97},{97,1},{2,34}... | collective-permute-start | bytes 1572872 | tf_op jit(solution)/shard_map/ppermute | solution.py:306
  188.9 32.2 %collective-permute-start.31 = (f32[2,2,256,128]{3,2,1,0:T(8,128)}, f32[2,2,256,128]{3,2,1,0:T(8,128)S(1)}, u32[]{:S(2)}, u32[]{:S(2)}) collective-permute-start(f32[2,2,256,128]{3,2,1,0:T(8,128)} %get-tuple-element.78.refs_4_), channel_id=1, source_target_pairs={{0,64},{32,96},{64,0},{96,32},{1,65},{33,97},{65,1},{97,33},{2,66}... | collective-permute-start | bytes 1572872 | tf_op jit(solution)/shard_map/ppermute | solution.py:306
  202.1 20.9 %collective-permute-start.32 = (f32[2,2,256,128]{3,2,1,0:T(8,128)}, f32[2,2,256,128]{3,2,1,0:T(8,128)S(1)}, u32[]{:S(2)}, u32[]{:S(2)}) collective-permute-start(f32[2,2,256,128]{3,2,1,0:T(8,128)} %get-tuple-element.78.refs_4_), channel_id=1, source_target_pairs={{0,96},{32,0},{64,32},{96,64},{1,97},{33,1},{65,33},{97,65},{2,98}... | collective-permute-start | bytes 1572872 | tf_op jit(solution)/shard_map/ppermute | solution.py:306
  221.1 13.8 %collective-permute-start.23 = (f32[1,2,256,128]{3,2,1,0:T(8,128)}, f32[1,2,256,128]{3,2,1,0:T(8,128)S(1)}, u32[]{:S(2)}, u32[]{:S(2)}) collective-permute-start(f32[1,2,256,128]{3,2,1,0:T(8,128)} %bitcast.31), channel_id=1, source_target_pairs={{0,6},{2,4},{4,2},{6,0},{1,7},{3,5},{5,3},{7,1},{8,14},{10,12},{12... | collective-permute-start | bytes 786440 | tf_op jit(solution)/shard_map/ppermute | solution.py:309
  234.9 23.0 %collective-permute-start.20 = (f32[256,512]{1,0:T(8,128)}, f32[256,512]{1,0:T(8,128)S(1)}, u32[]{:S(2)}, u32[]{:S(2)}) collective-permute-start(f32[256,512]{1,0:T(8,128)} %get-tuple-element.67), channel_id=1, source_target_pairs={{0,6},{2,4},{4,2},{6,0},{1,7},{3,5},{5,3},{7,1},{8,14},{10,12},{12... | collective-permute-start | bytes 1572872 | tf_op jit(solution)/shard_map/ppermute | solution.py:309
  239.1 13.9 %collective-permute-start.35 = (f32[2,256,128]{2,1,0:T(8,128)}, f32[2,256,128]{2,1,0:T(8,128)S(1)}, u32[]{:S(2)}, u32[]{:S(2)}) collective-permute-start(f32[2,256,128]{2,1,0:T(8,128)} %get-tuple-element.82), channel_id=1, source_target_pairs={{0,32},{32,64},{64,96},{96,0},{1,33},{33,65},{65,97},{97,1},{2,34}... | collective-permute-start | bytes 786440 | tf_op jit(solution)/shard_map/ppermute | solution.py:306
  (45 other events, 697.4 us)
Sparse Core Ops, SparseCore 0:
  14.2 33.2 all-gather.2

commit v5 on v4

--- a/solution.py
+++ b/solution.py
@@ -276,14 +276,14 @@
 
 HEADS = (2, T, W)
 
-def glue(body, args, outs, copies):
+def glue(body, args, outs, copies, hbm=False):
     spec = lambda shape: pl.BlockSpec(shape, lambda i: (0,) * len(shape))
     if copies:
         spec = lambda shape: pl.BlockSpec(memory_space=pl.ANY)
     arrays = args[1:]
     return pl.pallas_call(
         body,
-        out_shape=[pltpu.HBM(s, F32) for s in outs],
+        out_shape=[(pltpu.HBM if hbm else jax.ShapeDtypeStruct)(s, F32) for s in outs],
         grid=(1,),
         in_specs=[pl.BlockSpec(memory_space=pltpu.SMEM)] + [spec(a.shape) for a in arrays],
         out_specs=[spec(s) for s in outs],
@@ -304,6 +304,14 @@
     if step == 0:
         return array
     return lax.ppermute(array, axis, [(i, (i + step) % 4) for i in range(4)])
+
+def after(array, *others):
+    return lax.optimization_barrier((array, *others))[0]
+
+def ring(array, axis, late):
+    one = shift(array, axis, 1)
+    two = shift(after(array, one) if late else array, axis, 2)
+    return [array, one, two, shift(array, axis, 3)]
 
 def mirror(array, flip):
     return lax.ppermute(array, "z", [(i, i ^ flip) for i in range(4)])
@@ -410,12 +418,13 @@
     k, v, kv = glue(assemble, (spot, keys, values, *other), (HEADS, HEADS, (2,) + HEADS), 16)
     own = lax.all_gather(kv, "z", axis=0)
 
-    k_along = [shift(k, "y", s) for s in range(4)]
-    v_along = [shift(v, "x", s) for s in range(4)]
-    sent = glue(pick, (selected, *k_along, *v_along), (PAIR,) * 6, 12)
+    k_along = ring(k, "y", False)
+    v_along = ring(v, "x", True)
+    sent = glue(pick, (selected, *k_along, *v_along), (PAIR,) * 6, 12, hbm=True)
     k_got = [shift(sent[s], "x", s + 1) for s in range(3)]
-    v_got = [shift(sent[s + 3], "y", s + 1) for s in range(3)]
-    same, cross = glue(join, (selected, *k_along, *v_along, *k_got, *v_got), (PAIR, PAIR), 8)
+    v_one = shift(sent[3], "y", 1)
+    v_got = [v_one, shift(after(sent[4], v_one), "y", 2), shift(sent[5], "y", 3)]
+    same, cross = glue(join, (after(selected, q_far, do_far), *k_along, *v_along, *k_got, *v_got), (PAIR, PAIR), 8)
     pieces = [same, mirror(same, 1), mirror(cross, 2), mirror(cross, 3)]
 
     p, m, l, ot = call_own_forward(info, queries, q_far, own)
@@ -423,16 +432,18 @@
     o_near, o_far, dq, c, rd = out[:5]
     last = call_own_backward(info, queries, q_far, cotangent, do_far, own, p, c, rd, dq)
 
-    def reduced(g):
+    def reduced(g, *others):
         arrived = [g[0]] + [mirror(g[flip], flip) for flip in (1, 2, 3)]
+        arrived[3] = after(arrived[3], *others)
         return glue(spread, (spot, *arrived), (g[0].shape,) * 2, 0)
 
-    k_part, v_part = reduced(out[5:9])
-    arrived = [shift(k_part, "x", s) for s in range(4)] + [shift(v_part, "y", s) for s in range(4)]
+    k_part, v_part = reduced(out[5:9], last[0])
+    arrived = ring(k_part, "x", False) + ring(v_part, "y", True)
     sums = glue(collect, (selected, *arrived), (HEADS,) * 8, 0)
     own_k, own_v = reduced([a[None] for a in last[2:6]])
     grad_k = own_k[0] + sum(shift(sums[s], "y", (4 - s) % 4) for s in range(4))
-    grad_v = own_v[0] + sum(shift(sums[4 + s], "x", (4 - s) % 4) for s in range(4))
+    v_back = shift(sums[5], "x", 3)
+    grad_v = own_v[0] + sums[4] + v_back + shift(after(sums[6], v_back), "x", 2) + shift(sums[7], "x", 1)
 
     half = T // 2
 

time: 269 us -> 277 us (1.030)
  the two profiles are of different devices: /device:TPU:1 before, /device:TPU:9 now
where the time goes in v5:
time: 277 us
  starting transfers between devices  104 us (38%)
  Pallas kernels  78.4 us (28%)
  waiting for transfers between devices  53.3 us (19%)
  local copies, waits for them, and re-layouts  19.2 us (7%)
  between operations  14.3 us (5%)
  other arithmetic  7.89 us (3%)
    ppermute x24, starting transfers between devices, shift(): return lax.ppermute(array, axis, [(i, (i + step) % 4) for i in range(4)])  68.4 us
    pallas_call x1, Pallas kernels, call_picked(): kernel(picked, [NEAR, FAR, NEAR, FAR] + [whole(PAIR)] * 4 + [tile(ROW), t...  38.1 us
    ppermute x13, waiting for transfers between devices, mirror(): return lax.ppermute(array, 'z', [(i, i ^ flip) for i in range(4)])  26.2 us
    ppermute x24, waiting for transfers between devices, shift(): return lax.ppermute(array, axis, [(i, (i + step) % 4) for i in range(4)])  25.5 us
    ppermute x13, starting transfers between devices, mirror(): return lax.ppermute(array, 'z', [(i, i ^ flip) for i in range(4)])  23 us
    pallas_call x6, Pallas kernels, glue(): pl.pallas_call(body, out_shape=[(pltpu.HBM if hbm else jax.ShapeDtypeStru...  16.5 us
    unnamed x49, local copies, waits for them, and re-layouts  16.1 us
    pallas_call x1, Pallas kernels, call_own_backward(): kernel(own_backward, [NEAR, FAR, NEAR, FAR, whole(own.shape), tile(PROBS)...  14.2 us
  transfers between devices with their start and end apart: 42, of which 14 were waited for; matrix products, arithmetic and copies ran while one was open for 4% of the time, Pallas kernels for 14%

profile of v5, /device:TPU:9, one launch (start us, length us, event | category | flops | bytes accessed | tf_op | source)
XLA Modules:
  0.0 277.2 jit_solution(10128266324038688970)
XLA Ops:
  25.3 3.8 %collective-permute-start = (f32[256,512]{1,0:T(8,128)S(1)}, f32[256,512]{1,0:T(8,128)S(1)}, u32[]{:S(2)}, u32[]{:S(2)}) collective-permute-start(f32[256,512]{1,0:T(8,128)S(1)} %constant_dynamic-slice_fusion.3), channel_id=1, source_target_pairs={{0,6},{2,4},{4,2},{6,0},{1,7},{3,5},{5,3},{7,1},{8,14},{10,12},{12... | collective-permute-start | bytes 1572872 | tf_op jit(solution)/shard_map/ppermute | solution.py:317
  35.0 3.8 %collective-permute-start.1 = (f32[256,512]{1,0:T(8,128)S(1)}, f32[256,512]{1,0:T(8,128)S(1)}, u32[]{:S(2)}, u32[]{:S(2)}) collective-permute-start(f32[256,512]{1,0:T(8,128)S(1)} %constant_dynamic-slice_fusion.2), channel_id=1, source_target_pairs={{0,6},{2,4},{4,2},{6,0},{1,7},{3,5},{5,3},{7,1},{8,14},{10,12},{12... | collective-permute-start | bytes 1572872 | tf_op jit(solution)/shard_map/ppermute | solution.py:317
  44.2 2.8 %collective-permute-start.12 = (f32[2,2,256,128]{3,2,1,0:T(8,128)}, f32[2,2,256,128]{3,2,1,0:T(8,128)}, u32[]{:S(2)}, u32[]{:S(2)}) collective-permute-start(f32[2,2,256,128]{3,2,1,0:T(8,128)} %get-tuple-element.58), channel_id=1, source_target_pairs={{0,24},{8,0},{16,8},{24,16},{1,25},{9,1},{17,9},{25,17},{2,26},{10... | collective-permute-start | bytes 1572872 | tf_op jit(solution)/shard_map/ppermute | solution.py:306
  47.0 5.0 %collective-permute-done.qr_ref = f32[256,512]{1,0:T(8,128)S(1)} collective-permute-done((f32[256,512]{1,0:T(8,128)S(1)}, f32[256,512]{1,0:T(8,128)S(1)}, u32[]{:S(2)}, u32[]{:S(2)}) %collective-permute-start) | collective-permute-done | bytes 524320 | tf_op jit(solution)/shard_map/ppermute | solution.py:317
  53.0 15.1 %collective-permute-done.1.dr_ref = f32[256,512]{1,0:T(8,128)S(1)} collective-permute-done((f32[256,512]{1,0:T(8,128)S(1)}, f32[256,512]{1,0:T(8,128)S(1)}, u32[]{:S(2)}, u32[]{:S(2)}) %collective-permute-start.1) | collective-permute-done | bytes 524320 | tf_op jit(solution)/shard_map/ppermute | solution.py:317
  71.6 11.4 %collective-permute-done.14.refs_12_ = f32[2,2,256,128]{3,2,1,0:T(8,128)} collective-permute-done((f32[2,2,256,128]{3,2,1,0:T(8,128)}, f32[2,2,256,128]{3,2,1,0:T(8,128)}, u32[]{:S(2)}, u32[]{:S(2)}) %collective-permute-start.14) | collective-permute-done | bytes 524320 | tf_op jit(solution)/shard_map/ppermute | solution.py:306
  83.1 9.9 %join.1 = (f32[2,2,256,128]{3,2,1,0:T(8,128)}, f32[2,2,256,128]{3,2,1,0:T(8,128)}) custom-call(s32[16,3]{1,0:T(8,128)S(1)} %copy.13.table, f32[2,256,128]{2,1,0:T(8,128)S(1)} %get-tuple-element.53.refs_0_, f32[2,256,128]{2,1,0:T(8,128)S(1)} %collective-permute-done.4.refs_1_, f32[2,256,128]{2,1,0:T(8,128)S(1)} %collective-permute-done.5.refs_2_, ...), custom_call_target="tpu_custom_call" | custom-call | bytes 6291456 | tf_op jit(solution)/shard_map/join/pallas_call | solution.py:284
  101.0 9.5 %own_forward.1 = (f32[4,1024,512]{2,1,0:T(8,128)}, f32[4,1,512]{2,1,0:T(1,128)}, f32[4,1,512]{2,1,0:T(1,128)}, f32[4,128,512]{2,1,0:T(8,128)}) custom-call(s32[4]{0:T(128)S(1)} %pad_add_fusion.info, f32[256,1024]{1,0:T(8,128)S(1)} %copy-done.1, f32[256,512]{1,0:T(8,128)S(1)} %copy-done.10, f32[4,2,2,256,128]{4,3,2,1,0:T(8,128)S(1)} %bitcast.35), custom_call_target="tpu_custom_call" | custom-call | flops 4294967296 | bytes 16777216 | tf_op jit(solution)/shard_map/own_forward/pallas_call | solution.py:246
  110.6 5.4 %collective-permute-done.17.s2 = f32[2,2,256,128]{3,2,1,0:T(8,128)S(1)} collective-permute-done((f32[2,2,256,128]{3,2,1,0:T(8,128)}, f32[2,2,256,128]{3,2,1,0:T(8,128)S(1)}, u32[]{:S(2)}, u32[]{:S(2)}) %collective-permute-start.17) | collective-permute-done | bytes 524320 | tf_op jit(solution)/shard_map/ppermute | solution.py:317
  120.5 38.1 %picked.1 = (f32[256,512]{1,0:T(8,128)}, f32[256,512]{1,0:T(8,128)}, f32[4,128,512]{2,1,0:T(8,128)}, f32[4,1,512]{2,1,0:T(1,128)}, f32[4,1,512]{2,1,0:T(1,128)},...) custom-call(s32[4]{0:T(128)S(1)} %pad_add_fusion.info, ...), custom_call_target="tpu_custom_call" | custom-call | flops 21474836480 | bytes 16777216 | tf_op jit(solution)/shard_map/picked/pallas_call | solution.py:256
  158.6 2.5 collective-permute-start.26
  165.2 14.2 %own_backward.1 = (f32[256,512]{1,0:T(8,128)}, f32[256,512]{1,0:T(8,128)}, f32[2,256,128]{2,1,0:T(8,128)}, f32[2,256,128]{2,1,0:T(8,128)}, f32[2,256,128]{2,1,0:T(8,128)}, /*index=5*/f32[2,256,128]{2,1,0:T(8,128)}) custom-call(s32[4]{0:T(128)S(1)} %pad_add_fusion.info, f32[256,1024]{1,0:T(8,128)S(1)} %copy-done.2, f32[256,512]{1,0:T(8,128)S(1)} %copy-done.11, ...), custom_call_target="tpu_custom_call" | custom-call | flops 6442450944 | bytes 16777216 | tf_op jit(solution)/shard_map/own_backward/pallas_call | solution.py:268
  182.0 10.1 %collective-permute-start.28 = (f32[2,2,256,128]{3,2,1,0:T(8,128)S(1)}, f32[2,2,256,128]{3,2,1,0:T(8,128)S(1)}, u32[]{:S(2)}, u32[]{:S(2)}) collective-permute-start(f32[2,2,256,128]{3,2,1,0:T(8,128)S(1)} %get-tuple-element.87.refs_0_), channel_id=1, source_target_pairs={{0,16},{8,24},{16,0},{24,8},{1,17},{9,25},{17,1},{25,9},{2,18},{10... | collective-permute-start | bytes 1572872 | tf_op jit(solution)/shard_map/ppermute | solution.py:306
  193.6 13.3 %collective-permute-start.31 = (f32[2,2,256,128]{3,2,1,0:T(8,128)S(1)}, f32[2,2,256,128]{3,2,1,0:T(8,128)S(1)}, u32[]{:S(2)}, u32[]{:S(2)}) collective-permute-start(f32[2,2,256,128]{3,2,1,0:T(8,128)S(1)} %get-tuple-element.89.refs_4_), channel_id=1, source_target_pairs={{0,64},{32,96},{64,0},{96,32},{1,65},{33,97},{65,1},{97,33},{2,66}... | collective-permute-start | bytes 1572872 | tf_op jit(solution)/shard_map/ppermute | solution.py:306
  206.8 2.5 collective-permute-start.20
  209.4 2.6 collective-permute-done.29.refs_3_
  214.4 3.9 %collective-permute-done.31.refs_6_ = f32[2,2,256,128]{3,2,1,0:T(8,128)S(1)} collective-permute-done((f32[2,2,256,128]{3,2,1,0:T(8,128)S(1)}, f32[2,2,256,128]{3,2,1,0:T(8,128)S(1)}, u32[]{:S(2)}, u32[]{:S(2)}) %collective-permute-start.31) | collective-permute-done | bytes 524320 | tf_op jit(solution)/shard_map/ppermute | solution.py:306
  220.7 4.5 %collective-permute-start.33 = (f32[2,256,128]{2,1,0:T(8,128)S(1)}, f32[2,256,128]{2,1,0:T(8,128)}, u32[]{:S(2)}, u32[]{:S(2)}) collective-permute-start(f32[2,256,128]{2,1,0:T(8,128)S(1)} %get-tuple-element.91), channel_id=1, source_target_pairs={{0,96},{32,0},{64,32},{96,64},{1,97},{33,1},{65,33},{97,65},{2,98}... | collective-permute-start | bytes 786440 | tf_op jit(solution)/shard_map/ppermute | solution.py:306
  225.3 7.4 %collective-permute-start.34 = (f32[2,256,128]{2,1,0:T(8,128)S(1)}, f32[2,256,128]{2,1,0:T(8,128)}, u32[]{:S(2)}, u32[]{:S(2)}) collective-permute-start(f32[2,256,128]{2,1,0:T(8,128)S(1)} %get-tuple-element.92), channel_id=1, source_target_pairs={{0,64},{32,96},{64,0},{96,32},{1,65},{33,97},{65,1},{97,33},{2,66}... | collective-permute-start | bytes 786440 | tf_op jit(solution)/shard_map/ppermute | solution.py:306
  232.7 11.4 %collective-permute-start.35 = (f32[2,256,128]{2,1,0:T(8,128)S(1)}, f32[2,256,128]{2,1,0:T(8,128)}, u32[]{:S(2)}, u32[]{:S(2)}) collective-permute-start(f32[2,256,128]{2,1,0:T(8,128)S(1)} %get-tuple-element.93), channel_id=1, source_target_pairs={{0,32},{32,64},{64,96},{96,0},{1,33},{33,65},{65,97},{97,1},{2,34}... | collective-permute-start | bytes 786440 | tf_op jit(solution)/shard_map/ppermute | solution.py:306
  245.7 2.6 collective-permute-start.19
  248.3 2.7 maximum_select_fusion.1
  252.3 6.0 %collective-permute-start.36 = (f32[2,128,128]{2,1,0:T(8,128)S(1)}, f32[2,128,128]{2,1,0:T(8,128)S(1)}, u32[]{:S(2)}, u32[]{:S(2)}) collective-permute-start(f32[2,128,128]{2,1,0:T(8,128)S(1)} %constant_dynamic-slice_fusion.1), channel_id=1, source_target_pairs={{0,1},{1,0},{2,3},{3,2},{4,5},{5,4},{6,7},{7,6},{8,9},{9,8},{10,11... | collective-permute-start | bytes 393224 | tf_op jit(solution)/shard_map/ppermute | solution.py:452
  261.6 6.0 %collective-permute-start.40 = (f32[2,128,128]{2,1,0:T(8,128)S(1)}, f32[2,128,128]{2,1,0:T(8,128)S(1)}, u32[]{:S(2)}, u32[]{:S(2)}) collective-permute-start(f32[2,128,128]{2,1,0:T(8,128)S(1)} %constant_dynamic-slice_fusion), channel_id=1, source_target_pairs={{0,1},{1,0},{2,3},{3,2},{4,5},{5,4},{6,7},{7,6},{8,9},{9,8},{10,11... | collective-permute-start | bytes 393224 | tf_op jit(solution)/shard_map/ppermute | solution.py:452
  (138 shorter events, 68.2 us)
Async XLA Ops:
  7.2 90.0 %all-gather.3.cloned.1.call-start = ((), (), s32[]{:S(2)}) async-start(), calls=%async_computation | async-start | bytes 2621440 | tf_op jit(solution)/shard_map/all_gather | solution.py:419
  25.3 26.7 %collective-permute-start = (f32[256,512]{1,0:T(8,128)S(1)}, f32[256,512]{1,0:T(8,128)S(1)}, u32[]{:S(2)}, u32[]{:S(2)}) collective-permute-start(f32[256,512]{1,0:T(8,128)S(1)} %constant_dynamic-slice_fusion.3), channel_id=1, source_target_pairs={{0,6},{2,4},{4,2},{6,0},{1,7},{3,5},{5,3},{7,1},{8,14},{10,12},{12... | collective-permute-start | bytes 1572872 | tf_op jit(solution)/shard_map/ppermute | solution.py:317
  35.0 33.1 %collective-permute-start.1 = (f32[256,512]{1,0:T(8,128)S(1)}, f32[256,512]{1,0:T(8,128)S(1)}, u32[]{:S(2)}, u32[]{:S(2)}) collective-permute-start(f32[256,512]{1,0:T(8,128)S(1)} %constant_dynamic-slice_fusion.2), channel_id=1, source_target_pairs={{0,6},{2,4},{4,2},{6,0},{1,7},{3,5},{5,3},{7,1},{8,14},{10,12},{12... | collective-permute-start | bytes 1572872 | tf_op jit(solution)/shard_map/ppermute | solution.py:317
  38.8 32.8 %collective-permute-start.10 = (f32[2,2,256,128]{3,2,1,0:T(8,128)}, f32[2,2,256,128]{3,2,1,0:T(8,128)S(1)}, u32[]{:S(2)}, u32[]{:S(2)}) collective-permute-start(f32[2,2,256,128]{3,2,1,0:T(8,128)} %get-tuple-element.56), channel_id=1, source_target_pairs={{0,8},{8,16},{16,24},{24,0},{1,9},{9,17},{17,25},{25,1},{2,10},{10... | collective-permute-start | bytes 1572872 | tf_op jit(solution)/shard_map/ppermute | solution.py:306
  40.1 31.5 %collective-permute-start.11 = (f32[2,2,256,128]{3,2,1,0:T(8,128)}, f32[2,2,256,128]{3,2,1,0:T(8,128)}, u32[]{:S(2)}, u32[]{:S(2)}) collective-permute-start(f32[2,2,256,128]{3,2,1,0:T(8,128)} %get-tuple-element.57), channel_id=1, source_target_pairs={{0,16},{8,24},{16,0},{24,8},{1,17},{9,25},{17,1},{25,9},{2,18},{10... | collective-permute-start | bytes 1572872 | tf_op jit(solution)/shard_map/ppermute | solution.py:306
  44.2 27.4 %collective-permute-start.12 = (f32[2,2,256,128]{3,2,1,0:T(8,128)}, f32[2,2,256,128]{3,2,1,0:T(8,128)}, u32[]{:S(2)}, u32[]{:S(2)}) collective-permute-start(f32[2,2,256,128]{3,2,1,0:T(8,128)} %get-tuple-element.58), channel_id=1, source_target_pairs={{0,24},{8,0},{16,8},{24,16},{1,25},{9,1},{17,9},{25,17},{2,26},{10... | collective-permute-start | bytes 1572872 | tf_op jit(solution)/shard_map/ppermute | solution.py:306
  52.8 18.8 %collective-permute-start.15 = (f32[2,2,256,128]{3,2,1,0:T(8,128)}, f32[2,2,256,128]{3,2,1,0:T(8,128)}, u32[]{:S(2)}, u32[]{:S(2)}) collective-permute-start(f32[2,2,256,128]{3,2,1,0:T(8,128)} %get-tuple-element.62), channel_id=1, source_target_pairs={{0,96},{32,0},{64,32},{96,64},{1,97},{33,1},{65,33},{97,65},{2,98}... | collective-permute-start | bytes 1572872 | tf_op jit(solution)/shard_map/ppermute | solution.py:306
  93.2 22.8 %collective-permute-start.17 = (f32[2,2,256,128]{3,2,1,0:T(8,128)}, f32[2,2,256,128]{3,2,1,0:T(8,128)S(1)}, u32[]{:S(2)}, u32[]{:S(2)}) collective-permute-start(f32[2,2,256,128]{3,2,1,0:T(8,128)} %get-tuple-element.64), channel_id=1, source_target_pairs={{0,4},{2,6},{4,0},{6,2},{1,5},{3,7},{5,1},{7,3},{8,12},{10,14},{12... | collective-permute-start | bytes 1572872 | tf_op jit(solution)/shard_map/ppermute | solution.py:317
  94.5 21.5 %collective-permute-start.18 = (f32[2,2,256,128]{3,2,1,0:T(8,128)}, f32[2,2,256,128]{3,2,1,0:T(8,128)S(1)}, u32[]{:S(2)}, u32[]{:S(2)}) collective-permute-start(f32[2,2,256,128]{3,2,1,0:T(8,128)} %get-tuple-element.64), channel_id=1, source_target_pairs={{0,6},{2,4},{4,2},{6,0},{1,7},{3,5},{5,3},{7,1},{8,14},{10,12},{12... | collective-permute-start | bytes 1572872 | tf_op jit(solution)/shard_map/ppermute | solution.py:317
  158.6 20.8 %collective-permute-start.26 = (f32[2,2,256,128]{3,2,1,0:T(8,128)}, f32[2,2,256,128]{3,2,1,0:T(8,128)S(1)}, u32[]{:S(2)}, u32[]{:S(2)}) collective-permute-start(f32[2,2,256,128]{3,2,1,0:T(8,128)} %get-tuple-element.85), channel_id=1, source_target_pairs={{0,6},{2,4},{4,2},{6,0},{1,7},{3,5},{5,3},{7,1},{8,14},{10,12},{12... | collective-permute-start | bytes 1572872 | tf_op jit(solution)/shard_map/ppermute | solution.py:317
  161.1 18.3 %collective-permute-start.24 = (f32[2,2,256,128]{3,2,1,0:T(8,128)}, f32[2,2,256,128]{3,2,1,0:T(8,128)S(1)}, u32[]{:S(2)}, u32[]{:S(2)}) collective-permute-start(f32[2,2,256,128]{3,2,1,0:T(8,128)} %get-tuple-element.83), channel_id=1, source_target_pairs={{0,2},{2,0},{4,6},{6,4},{1,3},{3,1},{5,7},{7,5},{8,10},{10,8},{12,... | collective-permute-start | bytes 1572872 | tf_op jit(solution)/shard_map/ppermute | solution.py:317
  161.1 18.9 %collective-permute-start.25 = (f32[2,2,256,128]{3,2,1,0:T(8,128)}, f32[2,2,256,128]{3,2,1,0:T(8,128)S(1)}, u32[]{:S(2)}, u32[]{:S(2)}) collective-permute-start(f32[2,2,256,128]{3,2,1,0:T(8,128)} %get-tuple-element.84), channel_id=1, source_target_pairs={{0,4},{2,6},{4,0},{6,2},{1,5},{3,7},{5,1},{7,3},{8,12},{10,14},{12... | collective-permute-start | bytes 1572872 | tf_op jit(solution)/shard_map/ppermute | solution.py:317
  180.7 26.1 %collective-permute-start.27 = (f32[2,2,256,128]{3,2,1,0:T(8,128)S(1)}, f32[2,2,256,128]{3,2,1,0:T(8,128)S(1)}, u32[]{:S(2)}, u32[]{:S(2)}) collective-permute-start(f32[2,2,256,128]{3,2,1,0:T(8,128)S(1)} %get-tuple-element.87.refs_0_), channel_id=1, source_target_pairs={{0,8},{8,16},{16,24},{24,0},{1,9},{9,17},{17,25},{25,1},{2,10},{10... | collective-permute-start | bytes 1572872 | tf_op jit(solution)/shard_map/ppermute | solution.py:306
  182.0 27.3 %collective-permute-start.28 = (f32[2,2,256,128]{3,2,1,0:T(8,128)S(1)}, f32[2,2,256,128]{3,2,1,0:T(8,128)S(1)}, u32[]{:S(2)}, u32[]{:S(2)}) collective-permute-start(f32[2,2,256,128]{3,2,1,0:T(8,128)S(1)} %get-tuple-element.87.refs_0_), channel_id=1, source_target_pairs={{0,16},{8,24},{16,0},{24,8},{1,17},{9,25},{17,1},{25,9},{2,18},{10... | collective-permute-start | bytes 1572872 | tf_op jit(solution)/shard_map/ppermute | solution.py:306
  192.2 19.8 %collective-permute-start.29 = (f32[2,2,256,128]{3,2,1,0:T(8,128)S(1)}, f32[2,2,256,128]{3,2,1,0:T(8,128)S(1)}, u32[]{:S(2)}, u32[]{:S(2)}) collective-permute-start(f32[2,2,256,128]{3,2,1,0:T(8,128)S(1)} %get-tuple-element.87.refs_0_), channel_id=1, source_target_pairs={{0,24},{8,0},{16,8},{24,16},{1,25},{9,1},{17,9},{25,17},{2,26},{10... | collective-permute-start | bytes 1572872 | tf_op jit(solution)/shard_map/ppermute | solution.py:306
  192.2 21.1 %collective-permute-start.32 = (f32[2,2,256,128]{3,2,1,0:T(8,128)S(1)}, f32[2,2,256,128]{3,2,1,0:T(8,128)S(1)}, u32[]{:S(2)}, u32[]{:S(2)}) collective-permute-start(f32[2,2,256,128]{3,2,1,0:T(8,128)S(1)} %get-tuple-element.89.refs_4_), channel_id=1, source_target_pairs={{0,96},{32,0},{64,32},{96,64},{1,97},{33,1},{65,33},{97,65},{2,98}... | collective-permute-start | bytes 1572872 | tf_op jit(solution)/shard_map/ppermute | solution.py:306
  193.6 24.7 %collective-permute-start.31 = (f32[2,2,256,128]{3,2,1,0:T(8,128)S(1)}, f32[2,2,256,128]{3,2,1,0:T(8,128)S(1)}, u32[]{:S(2)}, u32[]{:S(2)}) collective-permute-start(f32[2,2,256,128]{3,2,1,0:T(8,128)S(1)} %get-tuple-element.89.refs_4_), channel_id=1, source_target_pairs={{0,64},{32,96},{64,0},{96,32},{1,65},{33,97},{65,1},{97,33},{2,66}... | collective-permute-start | bytes 1572872 | tf_op jit(solution)/shard_map/ppermute | solution.py:306
  206.8 38.9 %collective-permute-start.20 = (f32[256,512]{1,0:T(8,128)}, f32[256,512]{1,0:T(8,128)}, u32[]{:S(2)}, u32[]{:S(2)}) collective-permute-start(f32[256,512]{1,0:T(8,128)} %get-tuple-element.76), channel_id=1, source_target_pairs={{0,6},{2,4},{4,2},{6,0},{1,7},{3,5},{5,3},{7,1},{8,14},{10,12},{12... | collective-permute-start | bytes 1572872 | tf_op jit(solution)/shard_map/ppermute | solution.py:317
  213.3 19.4 %collective-permute-start.23 = (f32[1,2,256,128]{3,2,1,0:T(8,128)}, f32[1,2,256,128]{3,2,1,0:T(8,128)S(1)}, u32[]{:S(2)}, u32[]{:S(2)}) collective-permute-start(f32[1,2,256,128]{3,2,1,0:T(8,128)} %bitcast.37), channel_id=1, source_target_pairs={{0,6},{2,4},{4,2},{6,0},{1,7},{3,5},{5,3},{7,1},{8,14},{10,12},{12... | collective-permute-start | bytes 786440 | tf_op jit(solution)/shard_map/ppermute | solution.py:317
  219.7 31.2 %collective-permute-start.37 = (f32[2,256,128]{2,1,0:T(8,128)S(1)}, f32[2,256,128]{2,1,0:T(8,128)}, u32[]{:S(2)}, u32[]{:S(2)}) collective-permute-start(f32[2,256,128]{2,1,0:T(8,128)S(1)} %get-tuple-element.96), channel_id=1, source_target_pairs={{0,24},{8,0},{16,8},{24,16},{1,25},{9,1},{17,9},{25,17},{2,26},{10... | collective-permute-start | bytes 786440 | tf_op jit(solution)/shard_map/ppermute | solution.py:306
  220.7 30.2 %collective-permute-start.33 = (f32[2,256,128]{2,1,0:T(8,128)S(1)}, f32[2,256,128]{2,1,0:T(8,128)}, u32[]{:S(2)}, u32[]{:S(2)}) collective-permute-start(f32[2,256,128]{2,1,0:T(8,128)S(1)} %get-tuple-element.91), channel_id=1, source_target_pairs={{0,96},{32,0},{64,32},{96,64},{1,97},{33,1},{65,33},{97,65},{2,98}... | collective-permute-start | bytes 786440 | tf_op jit(solution)/shard_map/ppermute | solution.py:306
  225.3 25.8 %collective-permute-start.34 = (f32[2,256,128]{2,1,0:T(8,128)S(1)}, f32[2,256,128]{2,1,0:T(8,128)}, u32[]{:S(2)}, u32[]{:S(2)}) collective-permute-start(f32[2,256,128]{2,1,0:T(8,128)S(1)} %get-tuple-element.92), channel_id=1, source_target_pairs={{0,64},{32,96},{64,0},{96,32},{1,65},{33,97},{65,1},{97,33},{2,66}... | collective-permute-start | bytes 786440 | tf_op jit(solution)/shard_map/ppermute | solution.py:306
  232.7 18.4 %collective-permute-start.35 = (f32[2,256,128]{2,1,0:T(8,128)S(1)}, f32[2,256,128]{2,1,0:T(8,128)}, u32[]{:S(2)}, u32[]{:S(2)}) collective-permute-start(f32[2,256,128]{2,1,0:T(8,128)S(1)} %get-tuple-element.93), channel_id=1, source_target_pairs={{0,32},{32,64},{64,96},{96,0},{1,33},{33,65},{65,97},{97,1},{2,34}... | collective-permute-start | bytes 786440 | tf_op jit(solution)/shard_map/ppermute | solution.py:306
  245.7 21.9 %collective-permute-start.19 = (f32[256,512]{1,0:T(8,128)}, f32[256,512]{1,0:T(8,128)S(1)}, u32[]{:S(2)}, u32[]{:S(2)}) collective-permute-start(f32[256,512]{1,0:T(8,128)} %get-tuple-element.70), channel_id=1, source_target_pairs={{0,6},{2,4},{4,2},{6,0},{1,7},{3,5},{5,3},{7,1},{8,14},{10,12},{12... | collective-permute-start | bytes 1572872 | tf_op jit(solution)/shard_map/ppermute | solution.py:317
  (42 other events, 534.0 us)
Sparse Core Ops, SparseCore 0:
  13.3 48.2 all-gather.2

commit v6 on v4

v6 whole, which is shorter than its diff:
```python
import math

import jax
import jax.numpy as jnp
from jax import lax
from jax.experimental import pallas as pl
from jax.experimental.pallas import tpu as pltpu
from jax.sharding import Mesh, PartitionSpec as P

W = 128
T = 256

SCALE = 1.0 / math.sqrt(W)
LOG2E = math.log2(math.e)
LN2 = math.log(2.0)
BF = jnp.bfloat16
F32 = jnp.float32
BLK = 4 * T
HP = 2
STEPS = 4 // HP
R = HP * T

def split(x):
    hi = x.astype(BF)
    return hi, (x - hi.astype(F32)).astype(BF)

def twice(x, axis):
    return jnp.concatenate([x, x], axis=axis)

def mm(a, b):
    return lax.dot_general(a, b, (((1,), (0,)), ((), ())), preferred_element_type=F32)

def turned(x):
    return jnp.concatenate([x[:, i * W:(i + 1) * W].T for i in range(HP)], axis=1)

def upright(x):
    return jnp.concatenate([x[:, i * T:(i + 1) * T].T for i in range(HP)], axis=1)

def stacked(x):
    return jnp.concatenate([x[:, i * W:(i + 1) * W] for i in range(HP)], axis=0)

def left(x):
    hi, lo = split(x)
    return jnp.concatenate([hi, hi, lo, lo], axis=0)

def right(x):
    hi, lo = split(x)
    return twice(jnp.concatenate([hi, lo], axis=1), 0)

def fill(x, rows, cat, tr):
    hi, lo = split(x)
    if cat is not None:
        cat[rows, 0:W] = hi
        cat[rows, W:2 * W] = lo
    if tr is not None:
        hit, lot = split(x.T)
        tr[0:W, rows] = hit
        tr[W:2 * W, rows] = lot

def values_sum(tr, hi, lo):
    a = mm(tr, hi)
    return a[0:W] + a[W:2 * W] + mm(tr[0:W], lo)

def halves(x):
    return x[:, 0:W] + x[:, W:2 * W]

def own_quarter(info, mine_ref, other_ref, c):
    core = info[4]
    cols = pl.ds(pl.multiple_of((2 * core + info[1]) * W, W), W)
    a, b = mine_ref[c, :, cols], other_ref[c]
    return jnp.where(core == 0, a, b), jnp.where(core == 0, b, a)

def near_far(u, near, far):
    return jnp.where(u == 0, near[...], far[...])

def own_forward(info, ql_ref, qr_ref, mine_ref, other_ref, p_ref, m_ref, l_ref, ot_ref, kc, vt):
    u = pl.program_id(0)

    @pl.when((u == 0) & (pl.program_id(1) == 0))
    def _():
        for c in range(4):
            k, v = own_quarter(info, mine_ref, other_ref, c)
            fill(k, slice(c * T, (c + 1) * T), kc, None)
            fill(v, slice(c * T, (c + 1) * T), None, vt)

    quarter = jnp.where(u == 0, info[0], 3 - info[0])
    q = left(turned(near_far(u, ql_ref, qr_ref)) * (SCALE * LOG2E))
    s = mm(twice(kc[...], 1), q)
    token = lax.broadcasted_iota(jnp.int32, (BLK, R), 1) & (T - 1)
    ahead = lax.broadcasted_iota(jnp.int32, (BLK, R), 0) - token
    s = jnp.where(ahead <= quarter * T, s, -jnp.inf)
    m = jnp.max(s, axis=0, keepdims=True)
    p = jnp.exp2(s - m)
    p_ref[0] = p
    m_ref[0] = m
    l_ref[0] = jnp.sum(p, axis=0, keepdims=True)
    hi, lo = split(p)
    ot_ref[0] = values_sum(vt[...], hi, lo)

def picked(info, ql_ref, qr_ref, dl_ref, dr_ref, s0, s1, s2, s3,
           m0_ref, l0_ref, ot0_ref, ol_ref, or_ref, dq_ref, c_ref, rd_ref, g0, g1, g2, g3,
           kc, vc, kt, vt, s_sc, phi, plo, dk_acc, dv_acc):
    u, step = pl.program_id(0), pl.program_id(1)

    @pl.when((u == 0) & (step == 0))
    def _():
        for j in range(2):
            for x in range(4):
                rows = slice((j * 4 + x) * T, (j * 4 + x + 1) * T)
                piece = (s0, s1, s2, s3)[x]
                fill(piece[j, info[4]], rows, kc, kt)
                fill(piece[j, 1 - info[4]], rows, vc, vt)
        dk_acc[...] = jnp.zeros_like(dk_acc)
        dv_acc[...] = jnp.zeros_like(dv_acc)

    q = near_far(u, ql_ref, qr_ref) * (SCALE * LOG2E)
    do = near_far(u, dl_ref, dr_ref)
    qt = left(turned(q))
    m0 = m0_ref[0]
    m = m0
    for j in range(2):
        rows = slice(j * BLK, (j + 1) * BLK)
        s = mm(twice(kc[rows, :], 1), qt)
        s = jnp.where(info[2 + j] > 0, s, -jnp.inf)
        s_sc[rows, :] = s
        m = jnp.maximum(m, jnp.max(s, axis=0, keepdims=True))
    shrink = jnp.exp2(m0 - m)
    l = l0_ref[0] * shrink
    ot = ot0_ref[0] * shrink
    for j in range(2):
        rows = slice(j * BLK, (j + 1) * BLK)
        p = jnp.exp2(s_sc[rows, :] - m)
        s_sc[rows, :] = p
        hi, lo = split(p)
        phi[rows, :] = hi
        plo[rows, :] = lo
        l = l + jnp.sum(p, axis=0, keepdims=True)
        ot = ot + values_sum(vt[:, rows], hi, lo)
    inv = 1.0 / l
    ot = ot * inv
    dot = turned(do) * inv
    rd = jnp.sum(dot * ot, axis=0, keepdims=True)
    c_ref[0] = inv * shrink
    rd_ref[0] = rd * shrink
    o = upright(ot)

    @pl.when(u == 0)
    def _():
        ol_ref[...] = o

    @pl.when(u == 1)
    def _():
        or_ref[...] = o

    dt = left(dot)
    d2 = right(stacked(upright(dot)))
    q2 = right(stacked(q))
    dq = jnp.zeros((W, R), F32)
    for j in range(2):
        rows = slice(j * BLK, (j + 1) * BLK)
        dp = mm(twice(vc[rows, :], 1), dt)
        hi, lo = split(s_sc[rows, :] * (dp - rd))
        dq = dq + values_sum(kt[:, rows], hi, lo)
        dv_acc[rows, :] += halves(mm(jnp.concatenate([phi[rows, :], plo[rows, :]], axis=1), d2))
        dk_acc[rows, :] += halves(mm(jnp.concatenate([hi, lo], axis=1), q2))
    dq_ref[0] = dq

    @pl.when((u == 1) & (step == STEPS - 1))
    def _():
        for j in range(2):
            for x, out in enumerate((g0, g1, g2, g3)):
                rows = slice((j * 4 + x) * T, (j * 4 + x + 1) * T)
                out[j, info[4]] = dk_acc[rows, :] * LN2
                out[j, 1 - info[4]] = dv_acc[rows, :]

def own_backward(info, ql_ref, qr_ref, dl_ref, dr_ref, mine_ref, other_ref, p_ref, c_ref, rd_ref, dq_ref,
                 gl_ref, gr_ref, h0, h1, h2, h3, vc, kt, dk_acc, dv_acc):
    u, step = pl.program_id(0), pl.program_id(1)

    @pl.when((u == 0) & (step == 0))
    def _():
        for c in range(4):
            k, v = own_quarter(info, mine_ref, other_ref, c)
            fill(k, slice(c * T, (c + 1) * T), None, kt)
            fill(v, slice(c * T, (c + 1) * T), vc, None)
        dk_acc[...] = jnp.zeros_like(dk_acc)
        dv_acc[...] = jnp.zeros_like(dv_acc)

    q = near_far(u, ql_ref, qr_ref) * (SCALE * LOG2E)
    dot = turned(near_far(u, dl_ref, dr_ref)) * c_ref[0]
    p = p_ref[0]
    hi, lo = split(p)
    dv_acc[...] += halves(mm(jnp.concatenate([hi, lo], axis=1), right(stacked(upright(dot)))))
    dp = mm(twice(vc[...], 1), left(dot))
    hi, lo = split(p * (dp - rd_ref[0]))
    dk_acc[...] += halves(mm(jnp.concatenate([hi, lo], axis=1), right(stacked(q))))
    dq = upright(dq_ref[0] + values_sum(kt[...], hi, lo)) * SCALE

    @pl.when(u == 0)
    def _():
        gl_ref[...] = dq

    @pl.when(u == 1)
    def _():
        gr_ref[...] = dq

    @pl.when((u == 1) & (step == STEPS - 1))
    def _():
        for x, out in enumerate((h0, h1, h2, h3)):
            rows = pl.ds(pl.multiple_of((info[0] ^ x) * T, T), T)
            out[info[4]] = dk_acc[rows, :] * LN2
            out[1 - info[4]] = dv_acc[rows, :]

def tile(shape):
    return pl.BlockSpec((1,) + shape[1:], lambda u, h, i: (u * STEPS + h, 0, 0))

def whole(shape):
    return pl.BlockSpec(shape, lambda u, h, i: (0,) * len(shape))

NEAR = pl.BlockSpec((T, HP * W), lambda u, h, i: (0, i[1] * STEPS + h))
FAR = pl.BlockSpec((T, HP * W), lambda u, h, i: (0, h))
FIRST = pl.BlockSpec((T, HP * W), lambda u, h, i: (0, jnp.where(u == 0, h, STEPS - 1)))
SECOND = pl.BlockSpec((T, HP * W), lambda u, h, i: (0, jnp.where(u == 0, 0, h)))
PROBS, ROW, TURNED = (2 * STEPS, BLK, R), (2 * STEPS, 1, R), (2 * STEPS, W, R)
HALF, PIECE, PAIR = (T, 4 * W), (2, T, W), (2, 2, T, W)

def kernel(body, ins, outs, out_shapes, scratch, flops, limit):
    return pl.pallas_call(
        body,
        out_shape=[pltpu.HBM(s, F32) for s in out_shapes],
        grid_spec=pltpu.PrefetchScalarGridSpec(
            num_scalar_prefetch=1,
            grid=(2, STEPS),
            in_specs=ins,
            out_specs=outs,
            scratch_shapes=[pltpu.VMEM(s, d) for s, d in scratch],
        ),
        compiler_params=pltpu.CompilerParams(
            dimension_semantics=("arbitrary", "arbitrary"), vmem_limit_bytes=limit << 20),
        cost_estimate=pl.CostEstimate(
            flops=flops, transcendentals=0, bytes_accessed=16 << 20),
        name=body.__name__,
    )

UNIT = 2 * 2048 * BLK * W * 4

def call_own_forward(info, q, q_far, mine, other):
    return kernel(
        own_forward,
        [NEAR, FAR, whole(mine.shape), whole(other.shape)],
        [tile(PROBS), tile(ROW), tile(ROW), tile(TURNED)],
        [PROBS, ROW, ROW, TURNED],
        [((BLK, 2 * W), BF), ((2 * W, BLK), BF)],
        2 * UNIT, 30,
    )(info, q, q_far, mine, other)

def call_picked(info, q, q_far, do, do_far, pieces, m, l, ot):
    return kernel(
        picked,
        [NEAR, FAR, NEAR, FAR] + [whole(PAIR)] * 4 + [tile(ROW), tile(ROW), tile(TURNED)],
        [FIRST, SECOND, tile(TURNED), tile(ROW), tile(ROW)] + [whole(PAIR)] * 4,
        [HALF, HALF, TURNED, ROW, ROW] + [PAIR] * 4,
        [((2 * BLK, 2 * W), BF), ((2 * BLK, 2 * W), BF), ((2 * W, 2 * BLK), BF), ((2 * W, 2 * BLK), BF),
         ((2 * BLK, R), F32), ((2 * BLK, R), BF), ((2 * BLK, R), BF),
         ((2 * BLK, W), F32), ((2 * BLK, W), F32)],
        10 * UNIT, 52,
    )(info, q, q_far, do, do_far, *pieces, m, l, ot)

def call_own_backward(info, q, q_far, do, do_far, mine, other, p, c, rd, dq):
    return kernel(
        own_backward,
        [NEAR, FAR, NEAR, FAR, whole(mine.shape), whole(other.shape), tile(PROBS), tile(ROW), tile(ROW), tile(TURNED)],
        [FIRST, SECOND] + [whole(PIECE)] * 4,
        [HALF, HALF] + [PIECE] * 4,
        [((BLK, 2 * W), BF), ((2 * W, BLK), BF), ((BLK, W), F32), ((BLK, W), F32)],
        3 * UNIT, 40,
    )(info, q, q_far, do, do_far, mine, other, p, c, rd, dq)

FULL, HEADS = (T, 4 * W), (4, T, W)
SWAP = [(0, 1), (1, 0)]
PLACE = ("y", "x", "head")

def glue(body, args, outs, copies, hbm=False):
    spec = lambda shape: pl.BlockSpec(shape, lambda i: (0,) * len(shape))
    if copies:
        spec = lambda shape: pl.BlockSpec(memory_space=pl.ANY)
    arrays = args[1:]
    return pl.pallas_call(
        body,
        out_shape=[(pltpu.HBM if hbm else jax.ShapeDtypeStruct)(s, F32) for s in outs],
        grid=(1,),
        in_specs=[pl.BlockSpec(memory_space=pltpu.SMEM)] + [spec(a.shape) for a in arrays],
        out_specs=[spec(s) for s in outs],
        scratch_shapes=[pltpu.SemaphoreType.DMA((copies,))] if copies else [],
        compiler_params=pltpu.CompilerParams(
            dimension_semantics=("arbitrary",), vmem_limit_bytes=(4 if copies else 20) << 20),
        cost_estimate=pl.CostEstimate(
            flops=0, transcendentals=0,
            bytes_accessed=4 * sum(math.prod(s) for s in [a.shape for a in arrays] + list(outs))),
        name=body.__name__,
    )(args[0], *arrays)

def copy_all(pairs, sems):
    copies = [pltpu.make_async_copy(a, b, sems.at[n]) for n, (a, b) in enumerate(pairs)]
    for c in copies:
        c.start()
    for c in copies:
        c.wait()

def travel(array, step, stage):
    pairs = []
    for y in range(4):
        for x in range(4):
            for core in range(2):
                ty, tx = (y + step) % 4, x
                if core != stage:
                    ty, tx = y, (x + step) % 4
                pairs.append(((y * 4 + x) * 2 + core, (ty * 4 + tx) * 2 + core))
    return lax.ppermute(array, PLACE, pairs)

def mirror(array, flip):
    return lax.ppermute(array, "z", [(i, i ^ flip) for i in range(4)])

def swap(array):
    return lax.ppermute(array, "head", SWAP)

def after(array, *others):
    return lax.optimization_barrier((array, *others))[0]

def place():
    core, y, x = (lax.axis_index(a) for a in ("head", "y", "x"))
    return core, jnp.where(core == 0, y, x), jnp.where(core == 0, x, y)

def chosen(table, first, second, core, j):
    block = jnp.where(core == 0, first * 4 + second, second * 4 + first)
    other = jnp.maximum(table[block, 1 + j], 0)
    y, x = other // 4, other % 4
    return jnp.where(core == 0, y, x), jnp.where(core == 0, x, y)

def assemble(spot, keys, values, other, full, sems):
    core = spot[0]
    half = T // 2
    for i, ref in enumerate((keys, values)):
        @pl.when(core == i)
        def _(ref=ref):
            pltpu.make_async_copy(ref, full.at[pl.ds(pl.multiple_of(core * half, half), half)], sems.at[0]).start()
    pltpu.make_async_copy(other, full.at[pl.ds(pl.multiple_of((1 - core) * half, half), half)], sems.at[1]).start()
    for n in range(2):
        pltpu.make_async_copy(other, full.at[pl.ds(n * half, half)], sems.at[n]).wait()

def pick(table, *refs):
    core, here, there = place()
    along, out, sems = refs[0:4], refs[4:7], refs[7]
    waits = []
    for step in (1, 2, 3):
        for j in range(2):
            first, _ = chosen(table, here, (there + step) % 4, core, j)
            for i in range(4):
                @pl.when((here - first) % 4 == i)
                def _(source=along[i], target=out[step - 1].at[j], n=len(waits)):
                    pltpu.make_async_copy(source, target, sems.at[n]).start()
            waits.append((along[0], out[step - 1].at[j]))
    for n, (source, target) in enumerate(waits):
        pltpu.make_async_copy(source, target, sems.at[n]).wait()

def join(table, *refs):
    core, here, there = place()
    along, got, (mine, send), sems = refs[0:4], refs[4:7], refs[7:9], refs[9]
    waits = []
    for j in range(2):
        first, second = chosen(table, here, there, core, j)
        near, off = (here - first) % 4, (there - second) % 4
        for c, out in ((core, mine), (1 - core, send)):
            for i in range(2):
                cols = pl.ds(pl.multiple_of((2 * c + i) * W, W), W)
                target, n = out.at[j, i], len(waits)
                for k in range(4):
                    @pl.when((off == 0) & (near == k))
                    def _(source=along[k].at[:, cols], target=target, n=n):
                        pltpu.make_async_copy(source, target, sems.at[n]).start()
                for k in range(3):
                    @pl.when(off == k + 1)
                    def _(source=got[k].at[j, :, cols], target=target, n=n):
                        pltpu.make_async_copy(source, target, sems.at[n]).start()
                waits.append((along[0].at[:, cols], target))
    for n, (source, target) in enumerate(waits):
        pltpu.make_async_copy(source, target, sems.at[n]).wait()

def arrange(spot, mine, other, same, cross, sems):
    head = spot[1]
    copy_all([(ref.at[j, h], out.at[j, n]) for j in range(2)
              for n, ref in enumerate((mine, other))
              for h, out in ((head, same), (1 - head, cross))], sems)

def spread(spot, mine, added, passed, passed2, keep, send):
    head = spot[1]
    for j in range(mine.shape[0]):
        for n, out in ((0, keep), (1, send)):
            out[j, head] = mine[j, n] + added[j, n]
            out[j, 1 - head] = passed[j, n] + passed2[j, n]

def gather_heads(spot, keep, other, full, sems):
    core = spot[0]
    copy_all([(ref.at[j], full.at[j, pl.ds(2 * c, 2)]) for j in range(2)
              for c, ref in ((core, keep), (1 - core, other))], sems)

def collect(table, *refs):
    core, here, there = place()
    got, out = refs[0:4], refs[4:8]
    for ref in out:
        ref[...] = jnp.zeros_like(ref)
    for step in range(4):
        for j in range(2):
            first, second = chosen(table, here, (there - step) % 4, core, j)
            for i in range(4):
                @pl.when((second == there) & ((here - first) % 4 == i))
                def _(source=got[step], ref=out[i], j=j):
                    ref[...] += source[j]

def shards(queries, keys, values, cotangent, selected):
    core, z = lax.axis_index("head"), lax.axis_index("z")
    head = z // 2
    mine = lax.dynamic_slice(selected, (lax.axis_index("y") * 4 + lax.axis_index("x"), 1), (1, 2))[0]
    info = jnp.concatenate([jnp.stack([z, head]), (mine >= 0).astype(jnp.int32), core[None]])
    spot = jnp.stack([core, head])
    far = 1 - head
    q_far, do_far = (
        mirror(lax.dynamic_slice_in_dim(a, far * 4 * W, 4 * W, 1), 3)
        for a in (queries, cotangent)
    )
    got = swap(jnp.where(core == 0, values, keys))
    (full,) = glue(assemble, (spot, keys, values, got), (FULL,), 2)
    own = lax.all_gather(full, "z", axis=0)
    own_other = swap(lax.dynamic_slice_in_dim(own, (2 * (1 - core) + head) * W, W, 2))

    along = [full] + [travel(full, s, 0) for s in (1, 2, 3)]
    sent = glue(pick, (selected, *along), ((2,) + FULL,) * 3, 6, hbm=True)
    got = [travel(sent[s - 1], s, 1) for s in (1, 2, 3)]
    kept, send = glue(join, (after(selected, q_far, do_far), *along, *got), (PAIR, PAIR), 8)
    same, cross = glue(arrange, (spot, kept, swap(send)), (PAIR, PAIR), 8)
    pieces = [same] + [mirror(a, flip) for a, flip in ((same, 1), (cross, 2), (cross, 3))]

    p, m, l, ot = call_own_forward(info, queries, q_far, own, own_other)
    out = call_picked(info, queries, q_far, cotangent, do_far, pieces, m, l, ot)
    o_near, o_far, dq, c, rd = out[:5]
    last = call_own_backward(info, queries, q_far, cotangent, do_far, own, own_other, p, c, rd, dq)

    def reduced(g, *others):
        arrived = [g[0]] + [mirror(g[flip], flip) for flip in (1, 2, 3)]
        arrived[3] = after(arrived[3], *others)
        keep, send = glue(spread, (spot, *arrived), (g[0].shape,) * 2, 0)
        return keep, swap(send)

    (terms,) = glue(gather_heads, (spot, *reduced(out[5:9], last[0])), ((2,) + HEADS,), 4)
    arrived = [terms] + [travel(terms, s, 1) for s in (1, 2, 3)]
    sums = glue(collect, (selected, *arrived), (HEADS,) * 4, 0)
    low, high = reduced([a[None] for a in last[2:6]])
    total = sums[0] + sum(travel(sums[s], 4 - s, 0) for s in (1, 2, 3))
    total = total + jnp.where(
        core == 0, jnp.concatenate([low[0], high[0]], 0), jnp.concatenate([high[0], low[0]], 0)
    )

    half = T // 2

    def tokens(which):
        a = lax.dynamic_slice_in_dim(total, which * half, half, 1)
        return jnp.concatenate([a[h] for h in range(4)], 1)

    keep, back = tokens(core), swap(tokens(1 - core))

    def sides(a, b):
        return jnp.where(head == 0, jnp.concatenate([a, b], 1), jnp.concatenate([b, a], 1))

    return (
        sides(o_near, mirror(o_far, 3)),
        sides(last[0], mirror(last[1], 3)),
        jnp.where(core == 0, keep, back),
        jnp.where(core == 0, back, keep),
    )

def solution(mesh):
    grid = Mesh(mesh.devices.reshape(4, 4, 4, 2), ("y", "x", "z", "head"))
    tokens = ("y", "x", "z")
    wide, narrow = P(tokens, "head"), P(tokens + ("head",), None)
    return jax.shard_map(
        shards,
        mesh=grid,
        in_specs=(wide, narrow, narrow, wide, P()),
        out_specs=(wide, wide, narrow, narrow),
        check_vma=False,
    )
```

time: 269 us -> 353 us (1.31)
  Pallas kernels: 73.7 us -> 136 us
  starting transfers between devices: 70.2 us -> 89.9 us
  waiting for transfers between devices: 83 us -> 91.7 us
  local copies, waits for them, and re-layouts: 19.9 us -> 15.4 us
    pallas_call x8 -> x10, Pallas kernels: 35.6 us -> 97.6 us  [the longest x8 73.9 us: glue(): pl.pallas_call(body, out_shape=[(pltpu.HBM if hbm else jax.ShapeDtypeStru...]
    ppermute x28 -> x18, starting transfers between devices: 52.3 us -> 74.9 us  [the longest x12 44.5 us: travel(): return lax.ppermute(array, PLACE, pairs)]
    unnamed x55 -> x49, local copies, waits for them, and re-layouts: 16.1 us -> 9.65 us
    ppermute x13, waiting for transfers between devices: 40.9 us -> 45.4 us  [mirror(): return lax.ppermute(array, 'z', [(i, i ^ flip) for i in range(4)])]
    ppermute x28 -> x18, waiting for transfers between devices: 42.2 us -> 46.3 us  [the longest x12 42.8 us: travel(): return lax.ppermute(array, PLACE, pairs)]
  transfers between devices with their start and end apart: 42 -> 32, of which waited for: 15 -> 18; matrix products, arithmetic and copies ran while one was open for 4% -> 3% of each run, Pallas kernels for 12% -> 27%
where the time goes in v6:
time: 353 us
  Pallas kernels  136 us (39%)
  waiting for transfers between devices  91.7 us (26%)
  starting transfers between devices  89.9 us (25%)
  local copies, waits for them, and re-layouts  15.4 us (4%)
  between operations  14.3 us (4%)
  other arithmetic  5.9 us (2%)
    pallas_call x8, Pallas kernels, glue(): pl.pallas_call(body, out_shape=[(pltpu.HBM if hbm else jax.ShapeDtypeStru...  73.9 us
    ppermute x13, waiting for transfers between devices, mirror(): return lax.ppermute(array, 'z', [(i, i ^ flip) for i in range(4)])  45.4 us
    ppermute x12, starting transfers between devices, travel(): return lax.ppermute(array, PLACE, pairs)  44.5 us
    ppermute x12, waiting for transfers between devices, travel(): return lax.ppermute(array, PLACE, pairs)  42.8 us
    pallas_call x1, Pallas kernels, call_picked(): kernel(picked, [NEAR, FAR, NEAR, FAR] + [whole(PAIR)] * 4 + [tile(ROW), t...  38.1 us
    ppermute x6, starting transfers between devices, swap(): return lax.ppermute(array, 'head', SWAP)  30.4 us
    ppermute x13, starting transfers between devices, mirror(): return lax.ppermute(array, 'z', [(i, i ^ flip) for i in range(4)])  14.9 us
    pallas_call x1, Pallas kernels, call_own_backward(): kernel(own_backward, [NEAR, FAR, NEAR, FAR, whole(mine.shape), whole(othe...  14.2 us
  transfers between devices with their start and end apart: 32, of which 18 were waited for; matrix products, arithmetic and copies ran while one was open for 3% of the time, Pallas kernels for 27%

profile of v6, /device:TPU:1, one launch (start us, length us, event | category | flops | bytes accessed | tf_op | source)
XLA Modules:
  0.0 352.9 jit_solution(8217027570656636084)
XLA Ops:
  19.2 4.8 %collective-permute-done.3.refs_1_ = f32[256,512]{1,0:T(8,128)S(1)} collective-permute-done((f32[256,512]{1,0:T(8,128)}, f32[256,512]{1,0:T(8,128)S(1)}, u32[]{:S(2)}, u32[]{:S(2)}) %collective-permute-start.3) | collective-permute-done | bytes 524320 | tf_op jit(solution)/shard_map/ppermute | solution.py:319
  24.0 6.7 %collective-permute-done.4.refs_2_ = f32[256,512]{1,0:T(8,128)S(1)} collective-permute-done((f32[256,512]{1,0:T(8,128)}, f32[256,512]{1,0:T(8,128)S(1)}, u32[]{:S(2)}, u32[]{:S(2)}) %collective-permute-start.4) | collective-permute-done | bytes 524320 | tf_op jit(solution)/shard_map/ppermute | solution.py:319
  30.7 49.5 %pick.1 = (f32[2,256,512]{2,1,0:T(8,128)}, f32[2,256,512]{2,1,0:T(8,128)}, f32[2,256,512]{2,1,0:T(8,128)}) custom-call(s32[16,3]{1,0:T(8,128)S(1)} %copy.9.table, f32[256,512]{1,0:T(8,128)} %assemble.1.refs_0_, f32[256,512]{1,0:T(8,128)S(1)} %collective-permute-done.3.refs_1_, f32[256,512]{1,0:T(8,128)S(1)} %collective-permute-done.4.refs_2_, ...), custom_call_target="tpu_custom_call" | custom-call | bytes 5242880 | tf_op jit(solution)/shard_map/pick/pallas_call | solution.py:288
  80.2 32.8 %collective-permute-start.6 = (f32[2,256,512]{2,1,0:T(8,128)}, f32[2,256,512]{2,1,0:T(8,128)S(1)}, u32[]{:S(2)}, u32[]{:S(2)}) collective-permute-start(f32[2,256,512]{2,1,0:T(8,128)} %get-tuple-element.41), channel_id=1, source_target_pairs={{0,8},{1,33},{8,16},{9,41},{16,24},{17,49},{24,0},{25,57},{32,40},... | collective-permute-start | bytes 3145736 | tf_op jit(solution)/shard_map/ppermute | solution.py:319
  117.5 3.8 %collective-permute-start = (f32[256,512]{1,0:T(8,128)}, f32[256,512]{1,0:T(8,128)S(1)}, u32[]{:S(2)}, u32[]{:S(2)}) collective-permute-start(f32[256,512]{1,0:T(8,128)} %constant_dynamic-slice_fusion.2), channel_id=1, source_target_pairs={{0,6},{2,4},{4,2},{6,0},{1,7},{3,5},{5,3},{7,1},{8,14},{10,12},{12... | collective-permute-start | bytes 1572872 | tf_op jit(solution)/shard_map/ppermute | solution.py:322
  123.1 4.9 %collective-permute-done.qr_ref = f32[256,512]{1,0:T(8,128)S(1)} collective-permute-done((f32[256,512]{1,0:T(8,128)}, f32[256,512]{1,0:T(8,128)S(1)}, u32[]{:S(2)}, u32[]{:S(2)}) %collective-permute-start) | collective-permute-done | bytes 524320 | tf_op jit(solution)/shard_map/ppermute | solution.py:322
  128.8 4.9 %collective-permute-done.1.dr_ref = f32[256,512]{1,0:T(8,128)} collective-permute-done((f32[256,512]{1,0:T(8,128)}, f32[256,512]{1,0:T(8,128)}, u32[]{:S(2)}, u32[]{:S(2)}) %collective-permute-start.1) | collective-permute-done | bytes 524320 | tf_op jit(solution)/shard_map/ppermute | solution.py:322
  133.8 2.6 collective-permute-done.7.refs_5_
  137.1 17.8 %join.1 = (f32[2,2,256,128]{3,2,1,0:T(8,128)S(1)}, f32[2,2,256,128]{3,2,1,0:T(8,128)}) custom-call(s32[16,3]{1,0:T(8,128)S(1)} %copy.10.table, f32[256,512]{1,0:T(8,128)} %assemble.1.refs_0_, f32[256,512]{1,0:T(8,128)S(1)} %collective-permute-done.3.refs_1_, f32[256,512]{1,0:T(8,128)S(1)} %collective-permute-done.4.refs_2_, ...), custom_call_target="tpu_custom_call" | custom-call | bytes 6291456 | tf_op jit(solution)/shard_map/join/pallas_call | solution.py:288
  155.0 20.9 %collective-permute-start.9 = (f32[2,2,256,128]{3,2,1,0:T(8,128)}, f32[2,2,256,128]{3,2,1,0:T(8,128)S(1)}, u32[]{:S(2)}, u32[]{:S(2)}) collective-permute-start(f32[2,2,256,128]{3,2,1,0:T(8,128)} %get-tuple-element.45), channel_id=1, source_target_pairs={{0,1},{1,0},{2,3},{3,2},{4,5},{5,4},{6,7},{7,6},{8,9},{9,8},{10,11... | collective-permute-start | bytes 1572872 | tf_op jit(solution)/shard_map/ppermute | solution.py:325
  181.5 3.3 collective-permute-start.11
  187.9 9.5 %own_forward.1 = (f32[4,1024,512]{2,1,0:T(8,128)}, f32[4,1,512]{2,1,0:T(1,128)}, f32[4,1,512]{2,1,0:T(1,128)}, f32[4,128,512]{2,1,0:T(8,128)}) custom-call(s32[5]{0:T(128)S(1)} %pad_add_fusion.info, f32[256,1024]{1,0:T(8,128)S(1)} %copy-done.3, f32[256,512]{1,0:T(8,128)S(1)} %copy-done.10, f32[4,256,512]{2,1,0:T(8,128)S(1)} %bitcast.29, ...), custom_call_target="tpu_custom_call" | custom-call | flops 4294967296 | bytes 16777216 | tf_op jit(solution)/shard_map/own_forward/pallas_call | solution.py:248
  197.4 10.3 %collective-permute-done.11.s2 = f32[2,2,256,128]{3,2,1,0:T(8,128)S(1)} collective-permute-done((f32[2,2,256,128]{3,2,1,0:T(8,128)S(1)}, f32[2,2,256,128]{3,2,1,0:T(8,128)S(1)}, u32[]{:S(2)}, u32[]{:S(2)}) %collective-permute-start.11) | collective-permute-done | bytes 524320 | tf_op jit(solution)/shard_map/ppermute | solution.py:322
  211.2 38.1 %picked.1 = (f32[256,512]{1,0:T(8,128)}, f32[256,512]{1,0:T(8,128)}, f32[4,128,512]{2,1,0:T(8,128)}, f32[4,1,512]{2,1,0:T(1,128)}, f32[4,1,512]{2,1,0:T(1,128)},...) custom-call(s32[5]{0:T(128)S(1)} %pad_add_fusion.info, ...), custom_call_target="tpu_custom_call" | custom-call | flops 21474836480 | bytes 16777216 | tf_op jit(solution)/shard_map/picked/pallas_call | solution.py:258
  249.7 3.5 %collective-permute-start.17 = (f32[2,2,256,128]{3,2,1,0:T(8,128)}, f32[2,2,256,128]{3,2,1,0:T(8,128)S(1)}, u32[]{:S(2)}, u32[]{:S(2)}) collective-permute-start(f32[2,2,256,128]{3,2,1,0:T(8,128)} %get-tuple-element.61), channel_id=1, source_target_pairs={{0,4},{2,6},{4,0},{6,2},{1,5},{3,7},{5,1},{7,3},{8,12},{10,14},{12... | collective-permute-start | bytes 1572872 | tf_op jit(solution)/shard_map/ppermute | solution.py:322
  255.8 14.2 %own_backward.1 = (f32[256,512]{1,0:T(8,128)}, f32[256,512]{1,0:T(8,128)}, f32[2,256,128]{2,1,0:T(8,128)}, f32[2,256,128]{2,1,0:T(8,128)}, f32[2,256,128]{2,1,0:T(8,128)}, /*index=5*/f32[2,256,128]{2,1,0:T(8,128)}) custom-call(s32[5]{0:T(128)S(1)} %pad_add_fusion.info, f32[256,1024]{1,0:T(8,128)S(1)} %copy-done.4, f32[256,512]{1,0:T(8,128)S(1)} %copy-done.10, ...), custom_call_target="tpu_custom_call" | custom-call | flops 6442450944 | bytes 16777216 | tf_op jit(solution)/shard_map/own_backward/pallas_call | solution.py:270
  270.1 4.4 %collective-permute-done.17.passed = f32[2,2,256,128]{3,2,1,0:T(8,128)S(1)} collective-permute-done((f32[2,2,256,128]{3,2,1,0:T(8,128)}, f32[2,2,256,128]{3,2,1,0:T(8,128)S(1)}, u32[]{:S(2)}, u32[]{:S(2)}) %collective-permute-start.17) | collective-permute-done | bytes 524320 | tf_op jit(solution)/shard_map/ppermute | solution.py:322
  275.1 3.2 collective-permute-start.19
  280.7 2.6 collective-permute-start.22
  283.5 23.4 %collective-permute-done.20.refs_1_ = f32[2,4,256,128]{3,2,1,0:T(8,128)S(1)} collective-permute-done((f32[2,4,256,128]{3,2,1,0:T(8,128)S(1)}, f32[2,4,256,128]{3,2,1,0:T(8,128)S(1)}, u32[]{:S(2)}, u32[]{:S(2)}) %collective-permute-start.20) | collective-permute-done | bytes 1048608 | tf_op jit(solution)/shard_map/ppermute | solution.py:319
  310.4 4.6 %collective-permute-done.27.passed = f32[1,2,256,128]{3,2,1,0:T(8,128)S(1)} collective-permute-done((f32[1,2,256,128]{3,2,1,0:T(8,128)S(1)}, f32[1,2,256,128]{3,2,1,0:T(8,128)S(1)}, u32[]{:S(2)}, u32[]{:S(2)}) %collective-permute-start.27) | collective-permute-done | bytes 262176 | tf_op jit(solution)/shard_map/ppermute | solution.py:322
  320.6 4.0 %collective-permute-done.25 = f32[4,256,128]{2,1,0:T(8,128)} collective-permute-done((f32[4,256,128]{2,1,0:T(8,128)S(1)}, f32[4,256,128]{2,1,0:T(8,128)}, u32[]{:S(2)}, u32[]{:S(2)}) %collective-permute-start.25) | collective-permute-done | bytes 524320 | tf_op jit(solution)/shard_map/ppermute | solution.py:319
  328.6 4.2 %collective-permute-done.15 = f32[256,512]{1,0:T(8,128)S(1)} collective-permute-done((f32[256,512]{1,0:T(8,128)}, f32[256,512]{1,0:T(8,128)S(1)}, u32[]{:S(2)}, u32[]{:S(2)}) %collective-permute-start.15) | collective-permute-done | bytes 524320 | tf_op jit(solution)/shard_map/ppermute | solution.py:322
  333.9 10.1 %collective-permute-done.14 = f32[256,512]{1,0:T(8,128)S(1)} collective-permute-done((f32[256,512]{1,0:T(8,128)}, f32[256,512]{1,0:T(8,128)S(1)}, u32[]{:S(2)}, u32[]{:S(2)}) %collective-permute-start.14) | collective-permute-done | bytes 524320 | tf_op jit(solution)/shard_map/ppermute | solution.py:322
  (115 shorter events, 54.6 us)
Async XLA Ops:
  7.2 168.7 %all-gather.3.cloned.1.call-start = ((), (), s32[]{:S(2)}) async-start(), calls=%async_computation | async-start | bytes 2621440 | tf_op jit(solution)/shard_map/all_gather | solution.py:433
  15.5 15.1 %collective-permute-start.4 = (f32[256,512]{1,0:T(8,128)}, f32[256,512]{1,0:T(8,128)S(1)}, u32[]{:S(2)}, u32[]{:S(2)}) collective-permute-start(f32[256,512]{1,0:T(8,128)} %assemble.1.refs_0_), channel_id=1, source_target_pairs={{0,64},{1,17},{8,72},{9,25},{16,80},{17,1},{24,88},{25,9},{32,96},... | collective-permute-start | bytes 1572872 | tf_op jit(solution)/shard_map/ppermute | solution.py:319
  18.0 12.7 %collective-permute-start.5 = (f32[256,512]{1,0:T(8,128)}, f32[256,512]{1,0:T(8,128)S(1)}, u32[]{:S(2)}, u32[]{:S(2)}) collective-permute-start(f32[256,512]{1,0:T(8,128)} %assemble.1.refs_0_), channel_id=1, source_target_pairs={{0,96},{1,25},{8,104},{9,1},{16,112},{17,9},{24,120},{25,17},{32,0... | collective-permute-start | bytes 1572872 | tf_op jit(solution)/shard_map/ppermute | solution.py:319
  80.2 53.6 %collective-permute-start.6 = (f32[2,256,512]{2,1,0:T(8,128)}, f32[2,256,512]{2,1,0:T(8,128)S(1)}, u32[]{:S(2)}, u32[]{:S(2)}) collective-permute-start(f32[2,256,512]{2,1,0:T(8,128)} %get-tuple-element.41), channel_id=1, source_target_pairs={{0,8},{1,33},{8,16},{9,41},{16,24},{17,49},{24,0},{25,57},{32,40},... | collective-permute-start | bytes 3145736 | tf_op jit(solution)/shard_map/ppermute | solution.py:319
  113.1 23.3 %collective-permute-start.7 = (f32[2,256,512]{2,1,0:T(8,128)}, f32[2,256,512]{2,1,0:T(8,128)}, u32[]{:S(2)}, u32[]{:S(2)}) collective-permute-start(f32[2,256,512]{2,1,0:T(8,128)} %get-tuple-element.42), channel_id=1, source_target_pairs={{0,16},{1,65},{8,24},{9,73},{16,0},{17,81},{24,8},{25,89},{32,48},... | collective-permute-start | bytes 3145736 | tf_op jit(solution)/shard_map/ppermute | solution.py:319
  113.1 24.1 %collective-permute-start.8 = (f32[2,256,512]{2,1,0:T(8,128)}, f32[2,256,512]{2,1,0:T(8,128)}, u32[]{:S(2)}, u32[]{:S(2)}) collective-permute-start(f32[2,256,512]{2,1,0:T(8,128)} %get-tuple-element.43), channel_id=1, source_target_pairs={{0,24},{1,97},{8,0},{9,105},{16,8},{17,113},{24,16},{25,121},{32,5... | collective-permute-start | bytes 3145736 | tf_op jit(solution)/shard_map/ppermute | solution.py:319
  155.0 22.8 %collective-permute-start.9 = (f32[2,2,256,128]{3,2,1,0:T(8,128)}, f32[2,2,256,128]{3,2,1,0:T(8,128)S(1)}, u32[]{:S(2)}, u32[]{:S(2)}) collective-permute-start(f32[2,2,256,128]{3,2,1,0:T(8,128)} %get-tuple-element.45), channel_id=1, source_target_pairs={{0,1},{1,0},{2,3},{3,2},{4,5},{5,4},{6,7},{7,6},{8,9},{9,8},{10,11... | collective-permute-start | bytes 1572872 | tf_op jit(solution)/shard_map/ppermute | solution.py:325
  179.8 17.6 %collective-permute-start.10 = (f32[2,2,256,128]{3,2,1,0:T(8,128)S(1)}, f32[2,2,256,128]{3,2,1,0:T(8,128)S(1)}, u32[]{:S(2)}, u32[]{:S(2)}) collective-permute-start(f32[2,2,256,128]{3,2,1,0:T(8,128)S(1)} %get-tuple-element.46.s0), channel_id=1, source_target_pairs={{0,2},{2,0},{4,6},{6,4},{1,3},{3,1},{5,7},{7,5},{8,10},{10,8},{12,... | collective-permute-start | bytes 1572872 | tf_op jit(solution)/shard_map/ppermute | solution.py:322
  181.5 26.2 %collective-permute-start.11 = (f32[2,2,256,128]{3,2,1,0:T(8,128)S(1)}, f32[2,2,256,128]{3,2,1,0:T(8,128)S(1)}, u32[]{:S(2)}, u32[]{:S(2)}) collective-permute-start(f32[2,2,256,128]{3,2,1,0:T(8,128)S(1)} %get-tuple-element.47), channel_id=1, source_target_pairs={{0,4},{2,6},{4,0},{6,2},{1,5},{3,7},{5,1},{7,3},{8,12},{10,14},{12... | collective-permute-start | bytes 1572872 | tf_op jit(solution)/shard_map/ppermute | solution.py:322
  184.8 25.0 %collective-permute-start.12 = (f32[2,2,256,128]{3,2,1,0:T(8,128)S(1)}, f32[2,2,256,128]{3,2,1,0:T(8,128)}, u32[]{:S(2)}, u32[]{:S(2)}) collective-permute-start(f32[2,2,256,128]{3,2,1,0:T(8,128)S(1)} %get-tuple-element.47), channel_id=1, source_target_pairs={{0,6},{2,4},{4,2},{6,0},{1,7},{3,5},{5,3},{7,1},{8,14},{10,12},{12... | collective-permute-start | bytes 1572872 | tf_op jit(solution)/shard_map/ppermute | solution.py:322
  249.3 20.8 %collective-permute-start.18 = (f32[2,2,256,128]{3,2,1,0:T(8,128)}, f32[2,2,256,128]{3,2,1,0:T(8,128)S(1)}, u32[]{:S(2)}, u32[]{:S(2)}) collective-permute-start(f32[2,2,256,128]{3,2,1,0:T(8,128)} %get-tuple-element.62), channel_id=1, source_target_pairs={{0,6},{2,4},{4,2},{6,0},{1,7},{3,5},{5,3},{7,1},{8,14},{10,12},{12... | collective-permute-start | bytes 1572872 | tf_op jit(solution)/shard_map/ppermute | solution.py:322
  249.7 20.4 %collective-permute-start.16 = (f32[2,2,256,128]{3,2,1,0:T(8,128)}, f32[2,2,256,128]{3,2,1,0:T(8,128)S(1)}, u32[]{:S(2)}, u32[]{:S(2)}) collective-permute-start(f32[2,2,256,128]{3,2,1,0:T(8,128)} %get-tuple-element.60), channel_id=1, source_target_pairs={{0,2},{2,0},{4,6},{6,4},{1,3},{3,1},{5,7},{7,5},{8,10},{10,8},{12,... | collective-permute-start | bytes 1572872 | tf_op jit(solution)/shard_map/ppermute | solution.py:322
  249.7 24.8 %collective-permute-start.17 = (f32[2,2,256,128]{3,2,1,0:T(8,128)}, f32[2,2,256,128]{3,2,1,0:T(8,128)S(1)}, u32[]{:S(2)}, u32[]{:S(2)}) collective-permute-start(f32[2,2,256,128]{3,2,1,0:T(8,128)} %get-tuple-element.61), channel_id=1, source_target_pairs={{0,4},{2,6},{4,0},{6,2},{1,5},{3,7},{5,1},{7,3},{8,12},{10,14},{12... | collective-permute-start | bytes 1572872 | tf_op jit(solution)/shard_map/ppermute | solution.py:322
  280.5 26.5 %collective-permute-start.20 = (f32[2,4,256,128]{3,2,1,0:T(8,128)S(1)}, f32[2,4,256,128]{3,2,1,0:T(8,128)S(1)}, u32[]{:S(2)}, u32[]{:S(2)}) collective-permute-start(f32[2,4,256,128]{3,2,1,0:T(8,128)S(1)} %gather_heads.1.refs_0_), channel_id=1, source_target_pairs={{0,8},{1,33},{8,16},{9,41},{16,24},{17,49},{24,0},{25,57},{32,40},... | collective-permute-start | bytes 3145736 | tf_op jit(solution)/shard_map/ppermute | solution.py:319
  280.6 26.4 %collective-permute-start.21 = (f32[2,4,256,128]{3,2,1,0:T(8,128)S(1)}, f32[2,4,256,128]{3,2,1,0:T(8,128)S(1)}, u32[]{:S(2)}, u32[]{:S(2)}) collective-permute-start(f32[2,4,256,128]{3,2,1,0:T(8,128)S(1)} %gather_heads.1.refs_0_), channel_id=1, source_target_pairs={{0,16},{1,65},{8,24},{9,73},{16,0},{17,81},{24,8},{25,89},{32,48},... | collective-permute-start | bytes 3145736 | tf_op jit(solution)/shard_map/ppermute | solution.py:319
  280.7 26.9 %collective-permute-start.22 = (f32[2,4,256,128]{3,2,1,0:T(8,128)S(1)}, f32[2,4,256,128]{3,2,1,0:T(8,128)S(1)}, u32[]{:S(2)}, u32[]{:S(2)}) collective-permute-start(f32[2,4,256,128]{3,2,1,0:T(8,128)S(1)} %gather_heads.1.refs_0_), channel_id=1, source_target_pairs={{0,24},{1,97},{8,0},{9,105},{16,8},{17,113},{24,16},{25,121},{32,5... | collective-permute-start | bytes 3145736 | tf_op jit(solution)/shard_map/ppermute | solution.py:319
  283.2 25.8 %collective-permute-start.28 = (f32[1,2,256,128]{3,2,1,0:T(8,128)S(1)}, f32[1,2,256,128]{3,2,1,0:T(8,128)S(1)}, u32[]{:S(2)}, u32[]{:S(2)}) collective-permute-start(f32[1,2,256,128]{3,2,1,0:T(8,128)S(1)} %bitcast.34), channel_id=1, source_target_pairs={{0,6},{2,4},{4,2},{6,0},{1,7},{3,5},{5,3},{7,1},{8,14},{10,12},{12... | collective-permute-start | bytes 786440 | tf_op jit(solution)/shard_map/ppermute | solution.py:322
  283.5 26.9 %collective-permute-start.26 = (f32[1,2,256,128]{3,2,1,0:T(8,128)S(1)}, f32[1,2,256,128]{3,2,1,0:T(8,128)S(1)}, u32[]{:S(2)}, u32[]{:S(2)}) collective-permute-start(f32[1,2,256,128]{3,2,1,0:T(8,128)S(1)} %bitcast.33), channel_id=1, source_target_pairs={{0,2},{2,0},{4,6},{6,4},{1,3},{3,1},{5,7},{7,5},{8,10},{10,8},{12,... | collective-permute-start | bytes 786440 | tf_op jit(solution)/shard_map/ppermute | solution.py:322
  308.9 11.7 %collective-permute-start.23 = (f32[4,256,128]{2,1,0:T(8,128)S(1)}, f32[4,256,128]{2,1,0:T(8,128)S(1)}, u32[]{:S(2)}, u32[]{:S(2)}) collective-permute-start(f32[4,256,128]{2,1,0:T(8,128)S(1)} %get-tuple-element.67), channel_id=1, source_target_pairs={{0,96},{1,25},{8,104},{9,1},{16,112},{17,9},{24,120},{25,17},{32,0... | collective-permute-start | bytes 1572872 | tf_op jit(solution)/shard_map/ppermute | solution.py:319
  309.0 11.6 %collective-permute-start.24 = (f32[4,256,128]{2,1,0:T(8,128)S(1)}, f32[4,256,128]{2,1,0:T(8,128)}, u32[]{:S(2)}, u32[]{:S(2)}) collective-permute-start(f32[4,256,128]{2,1,0:T(8,128)S(1)} %get-tuple-element.68), channel_id=1, source_target_pairs={{0,64},{1,17},{8,72},{9,25},{16,80},{17,1},{24,88},{25,9},{32,96},... | collective-permute-start | bytes 1572872 | tf_op jit(solution)/shard_map/ppermute | solution.py:319
  309.1 15.5 %collective-permute-start.25 = (f32[4,256,128]{2,1,0:T(8,128)S(1)}, f32[4,256,128]{2,1,0:T(8,128)}, u32[]{:S(2)}, u32[]{:S(2)}) collective-permute-start(f32[4,256,128]{2,1,0:T(8,128)S(1)} %get-tuple-element.69), channel_id=1, source_target_pairs={{0,32},{1,9},{8,40},{9,17},{16,48},{17,25},{24,56},{25,1},{32,64},... | collective-permute-start | bytes 1572872 | tf_op jit(solution)/shard_map/ppermute | solution.py:319
  317.9 14.9 %collective-permute-start.15 = (f32[256,512]{1,0:T(8,128)}, f32[256,512]{1,0:T(8,128)S(1)}, u32[]{:S(2)}, u32[]{:S(2)}) collective-permute-start(f32[256,512]{1,0:T(8,128)} %get-tuple-element.58), channel_id=1, source_target_pairs={{0,6},{2,4},{4,2},{6,0},{1,7},{3,5},{5,3},{7,1},{8,14},{10,12},{12... | collective-permute-start | bytes 1572872 | tf_op jit(solution)/shard_map/ppermute | solution.py:322
  319.0 25.0 %collective-permute-start.14 = (f32[256,512]{1,0:T(8,128)}, f32[256,512]{1,0:T(8,128)S(1)}, u32[]{:S(2)}, u32[]{:S(2)}) collective-permute-start(f32[256,512]{1,0:T(8,128)} %get-tuple-element.52), channel_id=1, source_target_pairs={{0,6},{2,4},{4,2},{6,0},{1,7},{3,5},{5,3},{7,1},{8,14},{10,12},{12... | collective-permute-start | bytes 1572872 | tf_op jit(solution)/shard_map/ppermute | solution.py:322
  326.1 19.1 %collective-permute-start.30 = (f32[128,512]{1,0:T(8,128)S(1)}, f32[128,512]{1,0:T(8,128)S(1)}, u32[]{:S(2)}, u32[]{:S(2)}) collective-permute-start(f32[128,512]{1,0:T(8,128)S(1)} %pad_maximum_fusion.1), channel_id=1, source_target_pairs={{0,1},{1,0},{2,3},{3,2},{4,5},{5,4},{6,7},{7,6},{8,9},{9,8},{10,11... | collective-permute-start | bytes 786440 | tf_op jit(solution)/shard_map/ppermute | solution.py:325
  (32 other events, 352.7 us)
Sparse Core Ops, SparseCore 0:
  14.3 33.2 all-gather.2

commit v7 on v6

--- a/solution.py
+++ b/solution.py
@@ -66,8 +66,7 @@
 
 def own_quarter(info, mine_ref, other_ref, c):
     core = info[4]
-    cols = pl.ds(pl.multiple_of((2 * core + info[1]) * W, W), W)
-    a, b = mine_ref[c, :, cols], other_ref[c]
+    a, b = mine_ref[c, 2 * core + info[1]], other_ref[c]
     return jnp.where(core == 0, a, b), jnp.where(core == 0, b, a)
 
 def near_far(u, near, far):
@@ -224,6 +223,9 @@
 PROBS, ROW, TURNED = (2 * STEPS, BLK, R), (2 * STEPS, 1, R), (2 * STEPS, W, R)
 HALF, PIECE, PAIR = (T, 4 * W), (2, T, W), (2, 2, T, W)
 
+def in_hbm(*arrays):
+    return [pltpu.with_memory_space_constraint(a, pltpu.HBM) for a in arrays]
+
 def kernel(body, ins, outs, out_shapes, scratch, flops, limit):
     return pl.pallas_call(
         body,
@@ -252,7 +254,7 @@
         [PROBS, ROW, ROW, TURNED],
         [((BLK, 2 * W), BF), ((2 * W, BLK), BF)],
         2 * UNIT, 30,
-    )(info, q, q_far, mine, other)
+    )(info, *in_hbm(q), q_far, *in_hbm(mine), other)
 
 def call_picked(info, q, q_far, do, do_far, pieces, m, l, ot):
     return kernel(
@@ -264,7 +266,7 @@
          ((2 * BLK, R), F32), ((2 * BLK, R), BF), ((2 * BLK, R), BF),
          ((2 * BLK, W), F32), ((2 * BLK, W), F32)],
         10 * UNIT, 52,
-    )(info, q, q_far, do, do_far, *pieces, m, l, ot)
+    )(info, *in_hbm(q), q_far, *in_hbm(do), do_far, *pieces, *in_hbm(m, l, ot))
 
 def call_own_backward(info, q, q_far, do, do_far, mine, other, p, c, rd, dq):
     return kernel(
@@ -274,9 +276,9 @@
         [HALF, HALF] + [PIECE] * 4,
         [((BLK, 2 * W), BF), ((2 * W, BLK), BF), ((BLK, W), F32), ((BLK, W), F32)],
         3 * UNIT, 40,
-    )(info, q, q_far, do, do_far, mine, other, p, c, rd, dq)
-
-FULL, HEADS = (T, 4 * W), (4, T, W)
+    )(info, *in_hbm(q), q_far, *in_hbm(do), do_far, *in_hbm(mine), other, *in_hbm(p, c, rd, dq))
+
+HEADS = (4, T, W)
 SWAP = [(0, 1), (1, 0)]
 PLACE = ("y", "x", "head")
 
@@ -340,13 +342,18 @@
 def assemble(spot, keys, values, other, full, sems):
     core = spot[0]
     half = T // 2
-    for i, ref in enumerate((keys, values)):
-        @pl.when(core == i)
-        def _(ref=ref):
-            pltpu.make_async_copy(ref, full.at[pl.ds(pl.multiple_of(core * half, half), half)], sems.at[0]).start()
-    pltpu.make_async_copy(other, full.at[pl.ds(pl.multiple_of((1 - core) * half, half), half)], sems.at[1]).start()
-    for n in range(2):
-        pltpu.make_async_copy(other, full.at[pl.ds(n * half, half)], sems.at[n]).wait()
+    here, there = (pl.ds(pl.multiple_of(c * half, half), half) for c in (core, 1 - core))
+    for h in range(4):
+        cols = slice(h * W, (h + 1) * W)
+        for i, ref in enumerate((keys, values)):
+            @pl.when(core == i)
+            def _(ref=ref, cols=cols, h=h):
+                pltpu.make_async_copy(ref.at[:, cols], full.at[h, here], sems.at[h]).start()
+        pltpu.make_async_copy(other.at[:, cols], full.at[h, there], sems.at[4 + h]).start()
+    for h in range(4):
+        cols = slice(h * W, (h + 1) * W)
+        pltpu.make_async_copy(keys.at[:, cols], full.at[h, here], sems.at[h]).wait()
+        pltpu.make_async_copy(other.at[:, cols], full.at[h, there], sems.at[4 + h]).wait()
 
 def pick(table, *refs):
     core, here, there = place()
@@ -371,18 +378,16 @@
         first, second = chosen(table, here, there, core, j)
         near, off = (here - first) % 4, (there - second) % 4
         for c, out in ((core, mine), (1 - core, send)):
-            for i in range(2):
-                cols = pl.ds(pl.multiple_of((2 * c + i) * W, W), W)
-                target, n = out.at[j, i], len(waits)
-                for k in range(4):
-                    @pl.when((off == 0) & (near == k))
-                    def _(source=along[k].at[:, cols], target=target, n=n):
-                        pltpu.make_async_copy(source, target, sems.at[n]).start()
-                for k in range(3):
-                    @pl.when(off == k + 1)
-                    def _(source=got[k].at[j, :, cols], target=target, n=n):
-                        pltpu.make_async_copy(source, target, sems.at[n]).start()
-                waits.append((along[0].at[:, cols], target))
+            heads, target, n = pl.ds(2 * c, 2), out.at[j], len(waits)
+            for k in range(4):
+                @pl.when((off == 0) & (near == k))
+                def _(source=along[k].at[heads], target=target, n=n):
+                    pltpu.make_async_copy(source, target, sems.at[n]).start()
+            for k in range(3):
+                @pl.when(off == k + 1)
+                def _(source=got[k].at[j, heads], target=target, n=n):
+                    pltpu.make_async_copy(source, target, sems.at[n]).start()
+            waits.append((along[0].at[heads], target))
     for n, (source, target) in enumerate(waits):
         pltpu.make_async_copy(source, target, sems.at[n]).wait()
 
@@ -429,14 +434,14 @@
         for a in (queries, cotangent)
     )
     got = swap(jnp.where(core == 0, values, keys))
-    (full,) = glue(assemble, (spot, keys, values, got), (FULL,), 2)
+    (full,) = glue(assemble, (spot, *in_hbm(keys, values), got), (HEADS,), 8)
     own = lax.all_gather(full, "z", axis=0)
-    own_other = swap(lax.dynamic_slice_in_dim(own, (2 * (1 - core) + head) * W, W, 2))
+    own_other = swap(lax.dynamic_index_in_dim(own, 2 * (1 - core) + head, 1, keepdims=False))
 
     along = [full] + [travel(full, s, 0) for s in (1, 2, 3)]
-    sent = glue(pick, (selected, *along), ((2,) + FULL,) * 3, 6, hbm=True)
+    sent = glue(pick, (selected, *along), ((2,) + HEADS,) * 3, 6, hbm=True)
     got = [travel(sent[s - 1], s, 1) for s in (1, 2, 3)]
-    kept, send = glue(join, (after(selected, q_far, do_far), *along, *got), (PAIR, PAIR), 8)
+    kept, send = glue(join, (after(selected, q_far, do_far), *along, *got), (PAIR, PAIR), 4)
     same, cross = glue(arrange, (spot, kept, swap(send)), (PAIR, PAIR), 8)
     pieces = [same] + [mirror(a, flip) for a, flip in ((same, 1), (cross, 2), (cross, 3))]
 
@@ -453,7 +458,8 @@
 
     (terms,) = glue(gather_heads, (spot, *reduced(out[5:9], last[0])), ((2,) + HEADS,), 4)
     arrived = [terms] + [travel(terms, s, 1) for s in (1, 2, 3)]
-    sums = glue(collect, (selected, *arrived), (HEADS,) * 4, 0)
+    o_far, dq_far = mirror(o_far, 3), mirror(last[1], 3)
+    sums = glue(collect, (after(selected, o_far, dq_far), *arrived), (HEADS,) * 4, 0)
     low, high = reduced([a[None] for a in last[2:6]])
     total = sums[0] + sum(travel(sums[s], 4 - s, 0) for s in (1, 2, 3))
     total = total + jnp.where(
@@ -472,8 +478,8 @@
         return jnp.where(head == 0, jnp.concatenate([a, b], 1), jnp.concatenate([b, a], 1))
 
     return (
-        sides(o_near, mirror(o_far, 3)),
-        sides(last[0], mirror(last[1], 3)),
+        sides(o_near, o_far),
+        sides(last[0], dq_far),
         jnp.where(core == 0, keep, back),
         jnp.where(core == 0, back, keep),
     )

time: 353 us -> 351 us (level)
  starting transfers between devices: 89.9 us -> 128 us
  Pallas kernels: 136 us -> 116 us
  waiting for transfers between devices: 91.7 us -> 77.7 us
  local copies, waits for them, and re-layouts: 15.4 us -> 8.35 us
    ppermute x6, starting transfers between devices: 30.4 us -> 65.5 us  [swap(): return lax.ppermute(array, 'head', SWAP)]
    ppermute x12, waiting for transfers between devices: 42.8 us -> 19.2 us  [travel(): return lax.ppermute(array, PLACE, pairs)]
    pallas_call x8, Pallas kernels: 73.9 us -> 52.6 us  [glue(): pl.pallas_call(body, out_shape=[(pltpu.HBM if hbm else jax.ShapeDtypeStru...]
    ppermute x13, waiting for transfers between devices: 45.4 us -> 54.7 us  [mirror(): return lax.ppermute(array, 'z', [(i, i ^ flip) for i in range(4)])]
    unnamed x49 -> x33, local copies, waits for them, and re-layouts: 9.65 us -> 2.53 us
  transfers between devices with their start and end apart: 32 -> 32, of which waited for: 18 -> 15; matrix products, arithmetic and copies ran while one was open for 3% -> 2% of each run, Pallas kernels for 27% -> 19%
where the time goes in v7:
time: 351 us
  starting transfers between devices  128 us (36%)
  Pallas kernels  116 us (33%)
  waiting for transfers between devices  77.7 us (22%)
  between operations  14.2 us (4%)
  local copies, waits for them, and re-layouts  8.35 us (2%)
  other arithmetic  5.78 us (2%)
    ppermute x6, starting transfers between devices, swap(): return lax.ppermute(array, 'head', SWAP)  65.5 us
    ppermute x13, waiting for transfers between devices, mirror(): return lax.ppermute(array, 'z', [(i, i ^ flip) for i in range(4)])  54.7 us
    pallas_call x8, Pallas kernels, glue(): pl.pallas_call(body, out_shape=[(pltpu.HBM if hbm else jax.ShapeDtypeStru...  52.6 us
    ppermute x12, starting transfers between devices, travel(): return lax.ppermute(array, PLACE, pairs)  45.7 us
    pallas_call x1, Pallas kernels, call_picked(): kernel(picked, [NEAR, FAR, NEAR, FAR] + [whole(PAIR)] * 4 + [tile(ROW), t...  37.8 us
    ppermute x12, waiting for transfers between devices, travel(): return lax.ppermute(array, PLACE, pairs)  19.2 us
    ppermute x13, starting transfers between devices, mirror(): return lax.ppermute(array, 'z', [(i, i ^ flip) for i in range(4)])  17.3 us
    pallas_call x1, Pallas kernels, call_own_backward(): kernel(own_backward, [NEAR, FAR, NEAR, FAR, whole(mine.shape), whole(othe...  15 us
  transfers between devices with their start and end apart: 32, of which 15 were waited for; matrix products, arithmetic and copies ran while one was open for 2% of the time, Pallas kernels for 19%

profile of v7, /device:TPU:1, one launch (start us, length us, event | category | flops | bytes accessed | tf_op | source)
XLA Modules:
  0.0 351.0 jit_solution(9573109984727613782)
XLA Ops:
  10.9 9.7 %assemble.1.refs_0_ = f32[4,256,128]{2,1,0:T(8,128)} custom-call(s32[2]{0:T(128)S(1)} %pad_add_fusion.1.spot, f32[128,512]{1,0:T(8,128)} %keys.1, f32[128,512]{1,0:T(8,128)} %values.1, f32[128,512]{1,0:T(8,128)S(1)} %collective-permute-done.2.other), custom_call_target="tpu_custom_call" | custom-call | bytes 1310720 | tf_op jit(solution)/shard_map/assemble/pallas_call | solution.py:290
  25.6 4.8 %collective-permute-done.3.refs_1_ = f32[4,256,128]{2,1,0:T(8,128)S(1)} collective-permute-done((f32[4,256,128]{2,1,0:T(8,128)}, f32[4,256,128]{2,1,0:T(8,128)S(1)}, u32[]{:S(2)}, u32[]{:S(2)}) %collective-permute-start.3) | collective-permute-done | bytes 524320 | tf_op jit(solution)/shard_map/ppermute | solution.py:321
  30.4 6.7 %collective-permute-done.4.refs_2_ = f32[4,256,128]{2,1,0:T(8,128)S(1)} collective-permute-done((f32[4,256,128]{2,1,0:T(8,128)}, f32[4,256,128]{2,1,0:T(8,128)S(1)}, u32[]{:S(2)}, u32[]{:S(2)}) %collective-permute-start.4) | collective-permute-done | bytes 524320 | tf_op jit(solution)/shard_map/ppermute | solution.py:321
  37.1 17.8 %pick.1 = (f32[2,4,256,128]{3,2,1,0:T(8,128)}, f32[2,4,256,128]{3,2,1,0:T(8,128)}, f32[2,4,256,128]{3,2,1,0:T(8,128)}) custom-call(s32[16,3]{1,0:T(8,128)S(1)} %copy.12.table, f32[4,256,128]{2,1,0:T(8,128)} %assemble.1.refs_0_, f32[4,256,128]{2,1,0:T(8,128)S(1)} %collective-permute-done.3.refs_1_, f32[4,256,128]{2,1,0:T(8,128)S(1)} %collective-permute-done.4.refs_2_, ...), custom_call_target="tpu_custom_call" | custom-call | bytes 5242880 | tf_op jit(solution)/shard_map/pick/pallas_call | solution.py:290
  54.9 32.8 %collective-permute-start.6 = (f32[2,4,256,128]{3,2,1,0:T(8,128)}, f32[2,4,256,128]{3,2,1,0:T(8,128)S(1)}, u32[]{:S(2)}, u32[]{:S(2)}) collective-permute-start(f32[2,4,256,128]{3,2,1,0:T(8,128)} %get-tuple-element.42), channel_id=1, source_target_pairs={{0,8},{1,33},{8,16},{9,41},{16,24},{17,49},{24,0},{25,57},{32,40},... | collective-permute-start | bytes 3145736 | tf_op jit(solution)/shard_map/ppermute | solution.py:321
  93.3 3.8 %collective-permute-start = (f32[256,512]{1,0:T(8,128)}, f32[256,512]{1,0:T(8,128)S(1)}, u32[]{:S(2)}, u32[]{:S(2)}) collective-permute-start(f32[256,512]{1,0:T(8,128)} %constant_dynamic-slice_fusion.1), channel_id=1, source_target_pairs={{0,6},{2,4},{4,2},{6,0},{1,7},{3,5},{5,3},{7,1},{8,14},{10,12},{12... | collective-permute-start | bytes 1572872 | tf_op jit(solution)/shard_map/ppermute | solution.py:324
  98.9 4.9 %collective-permute-done.qr_ref = f32[256,512]{1,0:T(8,128)S(1)} collective-permute-done((f32[256,512]{1,0:T(8,128)}, f32[256,512]{1,0:T(8,128)S(1)}, u32[]{:S(2)}, u32[]{:S(2)}) %collective-permute-start) | collective-permute-done | bytes 524320 | tf_op jit(solution)/shard_map/ppermute | solution.py:324
  104.6 4.9 %collective-permute-done.1.dr_ref = f32[256,512]{1,0:T(8,128)} collective-permute-done((f32[256,512]{1,0:T(8,128)}, f32[256,512]{1,0:T(8,128)}, u32[]{:S(2)}, u32[]{:S(2)}) %collective-permute-start.1) | collective-permute-done | bytes 524320 | tf_op jit(solution)/shard_map/ppermute | solution.py:324
  109.6 3.4 collective-permute-done.7.refs_5_
  113.1 17.7 %join.1 = (f32[2,2,256,128]{3,2,1,0:T(8,128)S(1)}, f32[2,2,256,128]{3,2,1,0:T(8,128)}) custom-call(s32[16,3]{1,0:T(8,128)S(1)} %copy.13.table, f32[4,256,128]{2,1,0:T(8,128)} %assemble.1.refs_0_, f32[4,256,128]{2,1,0:T(8,128)S(1)} %collective-permute-done.3.refs_1_, f32[4,256,128]{2,1,0:T(8,128)S(1)} %collective-permute-done.4.refs_2_, ...), custom_call_target="tpu_custom_call" | custom-call | bytes 6291456 | tf_op jit(solution)/shard_map/join/pallas_call | solution.py:290
  130.8 51.4 %collective-permute-start.9 = (f32[2,2,256,128]{3,2,1,0:T(8,128)}, f32[2,2,256,128]{3,2,1,0:T(8,128)S(1)}, u32[]{:S(2)}, u32[]{:S(2)}) collective-permute-start(f32[2,2,256,128]{3,2,1,0:T(8,128)} %get-tuple-element.46), channel_id=1, source_target_pairs={{0,1},{1,0},{2,3},{3,2},{4,5},{5,4},{6,7},{7,6},{8,9},{9,8},{10,11... | collective-permute-start | bytes 1572872 | tf_op jit(solution)/shard_map/ppermute | solution.py:327
  187.8 3.3 collective-permute-start.11
  191.4 11.1 %own_forward.1 = (f32[4,1024,512]{2,1,0:T(8,128)}, f32[4,1,512]{2,1,0:T(1,128)}, f32[4,1,512]{2,1,0:T(1,128)}, f32[4,128,512]{2,1,0:T(8,128)}) custom-call(s32[5]{0:T(128)S(1)} %pad_add_fusion.info, f32[256,1024]{1,0:T(8,128)} %ql_ref.5, f32[256,512]{1,0:T(8,128)S(1)} %copy-done.4, f32[4,4,256,128]{3,2,1,0:T(8,128)} %bitcast.32, ...), custom_call_target="tpu_custom_call" | custom-call | flops 4294967296 | bytes 16777216 | tf_op jit(solution)/shard_map/own_forward/pallas_call | solution.py:250
  202.5 11.5 %collective-permute-done.11.s2 = f32[2,2,256,128]{3,2,1,0:T(8,128)S(1)} collective-permute-done((f32[2,2,256,128]{3,2,1,0:T(8,128)S(1)}, f32[2,2,256,128]{3,2,1,0:T(8,128)S(1)}, u32[]{:S(2)}, u32[]{:S(2)}) %collective-permute-start.11) | collective-permute-done | bytes 524320 | tf_op jit(solution)/shard_map/ppermute | solution.py:324
  216.1 37.8 %picked.1 = (f32[256,512]{1,0:T(8,128)}, f32[256,512]{1,0:T(8,128)}, f32[4,128,512]{2,1,0:T(8,128)}, f32[4,1,512]{2,1,0:T(1,128)}, f32[4,1,512]{2,1,0:T(1,128)},...) custom-call(s32[5]{0:T(128)S(1)} %pad_add_fusion.info, ...), custom_call_target="tpu_custom_call" | custom-call | flops 21474836480 | bytes 16777216 | tf_op jit(solution)/shard_map/picked/pallas_call | solution.py:260
  254.3 3.5 %collective-permute-start.17 = (f32[2,2,256,128]{3,2,1,0:T(8,128)}, f32[2,2,256,128]{3,2,1,0:T(8,128)S(1)}, u32[]{:S(2)}, u32[]{:S(2)}) collective-permute-start(f32[2,2,256,128]{3,2,1,0:T(8,128)} %get-tuple-element.63), channel_id=1, source_target_pairs={{0,4},{2,6},{4,0},{6,2},{1,5},{3,7},{5,1},{7,3},{8,12},{10,14},{12... | collective-permute-start | bytes 1572872 | tf_op jit(solution)/shard_map/ppermute | solution.py:324
  257.9 15.0 %own_backward.1 = (f32[256,512]{1,0:T(8,128)}, f32[256,512]{1,0:T(8,128)}, f32[2,256,128]{2,1,0:T(8,128)}, f32[2,256,128]{2,1,0:T(8,128)}, f32[2,256,128]{2,1,0:T(8,128)}, /*index=5*/f32[2,256,128]{2,1,0:T(8,128)}) custom-call(s32[5]{0:T(128)S(1)} %pad_add_fusion.info, f32[256,1024]{1,0:T(8,128)} %ql_ref.5, f32[256,512]{1,0:T(8,128)S(1)} %copy-done.4, ...), custom_call_target="tpu_custom_call" | custom-call | flops 6442450944 | bytes 16777216 | tf_op jit(solution)/shard_map/own_backward/pallas_call | solution.py:272
  272.9 6.1 %collective-permute-done.17.passed = f32[2,2,256,128]{3,2,1,0:T(8,128)S(1)} collective-permute-done((f32[2,2,256,128]{3,2,1,0:T(8,128)}, f32[2,2,256,128]{3,2,1,0:T(8,128)S(1)}, u32[]{:S(2)}, u32[]{:S(2)}) %collective-permute-start.17) | collective-permute-done | bytes 524320 | tf_op jit(solution)/shard_map/ppermute | solution.py:324
  279.7 3.2 collective-permute-start.19
  290.6 11.0 %collective-permute-done.15 = f32[256,512]{1,0:T(8,128)S(1)} collective-permute-done((f32[256,512]{1,0:T(8,128)S(1)}, f32[256,512]{1,0:T(8,128)S(1)}, u32[]{:S(2)}, u32[]{:S(2)}) %collective-permute-start.15) | collective-permute-done | bytes 524320 | tf_op jit(solution)/shard_map/ppermute | solution.py:324
  301.9 10.9 %collective-permute-done.14 = f32[256,512]{1,0:T(8,128)S(1)} collective-permute-done((f32[256,512]{1,0:T(8,128)S(1)}, f32[256,512]{1,0:T(8,128)S(1)}, u32[]{:S(2)}, u32[]{:S(2)}) %collective-permute-start.14) | collective-permute-done | bytes 524320 | tf_op jit(solution)/shard_map/ppermute | solution.py:324
  324.8 4.6 %collective-permute-start.29 = (f32[1,2,256,128]{3,2,1,0:T(8,128)S(1)}, f32[1,2,256,128]{3,2,1,0:T(8,128)S(1)}, u32[]{:S(2)}, u32[]{:S(2)}) collective-permute-start(f32[1,2,256,128]{3,2,1,0:T(8,128)S(1)} %get-tuple-element.77), channel_id=1, source_target_pairs={{0,1},{1,0},{2,3},{3,2},{4,5},{5,4},{6,7},{7,6},{8,9},{9,8},{10,11... | collective-permute-start | bytes 786440 | tf_op jit(solution)/shard_map/ppermute | solution.py:327
  330.5 4.3 %collective-permute-done.25 = f32[4,256,128]{2,1,0:T(8,128)S(1)} collective-permute-done((f32[4,256,128]{2,1,0:T(8,128)}, f32[4,256,128]{2,1,0:T(8,128)S(1)}, u32[]{:S(2)}, u32[]{:S(2)}) %collective-permute-start.25) | collective-permute-done | bytes 524320 | tf_op jit(solution)/shard_map/ppermute | solution.py:321
  336.2 4.8 %collective-permute-start.30 = (f32[128,512]{1,0:T(8,128)S(1)}, f32[128,512]{1,0:T(8,128)S(1)}, u32[]{:S(2)}, u32[]{:S(2)}) collective-permute-start(f32[128,512]{1,0:T(8,128)S(1)} %pad_maximum_fusion.1), channel_id=1, source_target_pairs={{0,1},{1,0},{2,3},{3,2},{4,5},{5,4},{6,7},{7,6},{8,9},{9,8},{10,11... | collective-permute-start | bytes 786440 | tf_op jit(solution)/shard_map/ppermute | solution.py:327
  (100 shorter events, 51.7 us)
Async XLA Ops:
  7.2 175.0 %all-gather.3.cloned.1.call-start = ((), (), s32[]{:S(2)}) async-start(), calls=%async_computation | async-start | bytes 2621440 | tf_op jit(solution)/shard_map/all_gather | solution.py:438
  21.9 15.1 %collective-permute-start.4 = (f32[4,256,128]{2,1,0:T(8,128)}, f32[4,256,128]{2,1,0:T(8,128)S(1)}, u32[]{:S(2)}, u32[]{:S(2)}) collective-permute-start(f32[4,256,128]{2,1,0:T(8,128)} %assemble.1.refs_0_), channel_id=1, source_target_pairs={{0,64},{1,17},{8,72},{9,25},{16,80},{17,1},{24,88},{25,9},{32,96},... | collective-permute-start | bytes 1572872 | tf_op jit(solution)/shard_map/ppermute | solution.py:321
  24.4 12.7 %collective-permute-start.5 = (f32[4,256,128]{2,1,0:T(8,128)}, f32[4,256,128]{2,1,0:T(8,128)S(1)}, u32[]{:S(2)}, u32[]{:S(2)}) collective-permute-start(f32[4,256,128]{2,1,0:T(8,128)} %assemble.1.refs_0_), channel_id=1, source_target_pairs={{0,96},{1,25},{8,104},{9,1},{16,112},{17,9},{24,120},{25,17},{32,0... | collective-permute-start | bytes 1572872 | tf_op jit(solution)/shard_map/ppermute | solution.py:321
  54.9 54.7 %collective-permute-start.6 = (f32[2,4,256,128]{3,2,1,0:T(8,128)}, f32[2,4,256,128]{3,2,1,0:T(8,128)S(1)}, u32[]{:S(2)}, u32[]{:S(2)}) collective-permute-start(f32[2,4,256,128]{3,2,1,0:T(8,128)} %get-tuple-element.42), channel_id=1, source_target_pairs={{0,8},{1,33},{8,16},{9,41},{16,24},{17,49},{24,0},{25,57},{32,40},... | collective-permute-start | bytes 3145736 | tf_op jit(solution)/shard_map/ppermute | solution.py:321
  87.7 25.3 %collective-permute-start.7 = (f32[2,4,256,128]{3,2,1,0:T(8,128)}, f32[2,4,256,128]{3,2,1,0:T(8,128)}, u32[]{:S(2)}, u32[]{:S(2)}) collective-permute-start(f32[2,4,256,128]{3,2,1,0:T(8,128)} %get-tuple-element.43), channel_id=1, source_target_pairs={{0,16},{1,65},{8,24},{9,73},{16,0},{17,81},{24,8},{25,89},{32,48},... | collective-permute-start | bytes 3145736 | tf_op jit(solution)/shard_map/ppermute | solution.py:321
  89.4 23.6 %collective-permute-start.8 = (f32[2,4,256,128]{3,2,1,0:T(8,128)}, f32[2,4,256,128]{3,2,1,0:T(8,128)}, u32[]{:S(2)}, u32[]{:S(2)}) collective-permute-start(f32[2,4,256,128]{3,2,1,0:T(8,128)} %get-tuple-element.44), channel_id=1, source_target_pairs={{0,24},{1,97},{8,0},{9,105},{16,8},{17,113},{24,16},{25,121},{32,5... | collective-permute-start | bytes 3145736 | tf_op jit(solution)/shard_map/ppermute | solution.py:321
  93.3 10.5 %collective-permute-start = (f32[256,512]{1,0:T(8,128)}, f32[256,512]{1,0:T(8,128)S(1)}, u32[]{:S(2)}, u32[]{:S(2)}) collective-permute-start(f32[256,512]{1,0:T(8,128)} %constant_dynamic-slice_fusion.1), channel_id=1, source_target_pairs={{0,6},{2,4},{4,2},{6,0},{1,7},{3,5},{5,3},{7,1},{8,14},{10,12},{12... | collective-permute-start | bytes 1572872 | tf_op jit(solution)/shard_map/ppermute | solution.py:324
  98.9 10.6 %collective-permute-start.1 = (f32[256,512]{1,0:T(8,128)}, f32[256,512]{1,0:T(8,128)}, u32[]{:S(2)}, u32[]{:S(2)}) collective-permute-start(f32[256,512]{1,0:T(8,128)} %constant_dynamic-slice_fusion), channel_id=1, source_target_pairs={{0,6},{2,4},{4,2},{6,0},{1,7},{3,5},{5,3},{7,1},{8,14},{10,12},{12... | collective-permute-start | bytes 1572872 | tf_op jit(solution)/shard_map/ppermute | solution.py:324
  130.8 53.3 %collective-permute-start.9 = (f32[2,2,256,128]{3,2,1,0:T(8,128)}, f32[2,2,256,128]{3,2,1,0:T(8,128)S(1)}, u32[]{:S(2)}, u32[]{:S(2)}) collective-permute-start(f32[2,2,256,128]{3,2,1,0:T(8,128)} %get-tuple-element.46), channel_id=1, source_target_pairs={{0,1},{1,0},{2,3},{3,2},{4,5},{5,4},{6,7},{7,6},{8,9},{9,8},{10,11... | collective-permute-start | bytes 1572872 | tf_op jit(solution)/shard_map/ppermute | solution.py:327
  186.1 16.3 %collective-permute-start.10 = (f32[2,2,256,128]{3,2,1,0:T(8,128)S(1)}, f32[2,2,256,128]{3,2,1,0:T(8,128)S(1)}, u32[]{:S(2)}, u32[]{:S(2)}) collective-permute-start(f32[2,2,256,128]{3,2,1,0:T(8,128)S(1)} %get-tuple-element.47.s0), channel_id=1, source_target_pairs={{0,2},{2,0},{4,6},{6,4},{1,3},{3,1},{5,7},{7,5},{8,10},{10,8},{12,... | collective-permute-start | bytes 1572872 | tf_op jit(solution)/shard_map/ppermute | solution.py:324
  187.8 26.2 %collective-permute-start.11 = (f32[2,2,256,128]{3,2,1,0:T(8,128)S(1)}, f32[2,2,256,128]{3,2,1,0:T(8,128)S(1)}, u32[]{:S(2)}, u32[]{:S(2)}) collective-permute-start(f32[2,2,256,128]{3,2,1,0:T(8,128)S(1)} %get-tuple-element.48), channel_id=1, source_target_pairs={{0,4},{2,6},{4,0},{6,2},{1,5},{3,7},{5,1},{7,3},{8,12},{10,14},{12... | collective-permute-start | bytes 1572872 | tf_op jit(solution)/shard_map/ppermute | solution.py:324
  191.1 25.0 %collective-permute-start.12 = (f32[2,2,256,128]{3,2,1,0:T(8,128)S(1)}, f32[2,2,256,128]{3,2,1,0:T(8,128)}, u32[]{:S(2)}, u32[]{:S(2)}) collective-permute-start(f32[2,2,256,128]{3,2,1,0:T(8,128)S(1)} %get-tuple-element.48), channel_id=1, source_target_pairs={{0,6},{2,4},{4,2},{6,0},{1,7},{3,5},{5,3},{7,1},{8,14},{10,12},{12... | collective-permute-start | bytes 1572872 | tf_op jit(solution)/shard_map/ppermute | solution.py:324
  253.9 19.0 %collective-permute-start.18 = (f32[2,2,256,128]{3,2,1,0:T(8,128)}, f32[2,2,256,128]{3,2,1,0:T(8,128)S(1)}, u32[]{:S(2)}, u32[]{:S(2)}) collective-permute-start(f32[2,2,256,128]{3,2,1,0:T(8,128)} %get-tuple-element.64), channel_id=1, source_target_pairs={{0,6},{2,4},{4,2},{6,0},{1,7},{3,5},{5,3},{7,1},{8,14},{10,12},{12... | collective-permute-start | bytes 1572872 | tf_op jit(solution)/shard_map/ppermute | solution.py:324
  254.3 18.6 %collective-permute-start.16 = (f32[2,2,256,128]{3,2,1,0:T(8,128)}, f32[2,2,256,128]{3,2,1,0:T(8,128)S(1)}, u32[]{:S(2)}, u32[]{:S(2)}) collective-permute-start(f32[2,2,256,128]{3,2,1,0:T(8,128)} %get-tuple-element.62), channel_id=1, source_target_pairs={{0,2},{2,0},{4,6},{6,4},{1,3},{3,1},{5,7},{7,5},{8,10},{10,8},{12,... | collective-permute-start | bytes 1572872 | tf_op jit(solution)/shard_map/ppermute | solution.py:324
  254.3 24.7 %collective-permute-start.17 = (f32[2,2,256,128]{3,2,1,0:T(8,128)}, f32[2,2,256,128]{3,2,1,0:T(8,128)S(1)}, u32[]{:S(2)}, u32[]{:S(2)}) collective-permute-start(f32[2,2,256,128]{3,2,1,0:T(8,128)} %get-tuple-element.63), channel_id=1, source_target_pairs={{0,4},{2,6},{4,0},{6,2},{1,5},{3,7},{5,1},{7,3},{8,12},{10,14},{12... | collective-permute-start | bytes 1572872 | tf_op jit(solution)/shard_map/ppermute | solution.py:324
  285.1 28.6 %collective-permute-start.20 = (f32[2,4,256,128]{3,2,1,0:T(8,128)S(1)}, f32[2,4,256,128]{3,2,1,0:T(8,128)S(1)}, u32[]{:S(2)}, u32[]{:S(2)}) collective-permute-start(f32[2,4,256,128]{3,2,1,0:T(8,128)S(1)} %gather_heads.1.refs_0_), channel_id=1, source_target_pairs={{0,8},{1,33},{8,16},{9,41},{16,24},{17,49},{24,0},{25,57},{32,40},... | collective-permute-start | bytes 3145736 | tf_op jit(solution)/shard_map/ppermute | solution.py:321
  285.2 30.0 %collective-permute-start.21 = (f32[2,4,256,128]{3,2,1,0:T(8,128)S(1)}, f32[2,4,256,128]{3,2,1,0:T(8,128)S(1)}, u32[]{:S(2)}, u32[]{:S(2)}) collective-permute-start(f32[2,4,256,128]{3,2,1,0:T(8,128)S(1)} %gather_heads.1.refs_0_), channel_id=1, source_target_pairs={{0,16},{1,65},{8,24},{9,73},{16,0},{17,81},{24,8},{25,89},{32,48},... | collective-permute-start | bytes 3145736 | tf_op jit(solution)/shard_map/ppermute | solution.py:321
  285.3 29.9 %collective-permute-start.22 = (f32[2,4,256,128]{3,2,1,0:T(8,128)S(1)}, f32[2,4,256,128]{3,2,1,0:T(8,128)}, u32[]{:S(2)}, u32[]{:S(2)}) collective-permute-start(f32[2,4,256,128]{3,2,1,0:T(8,128)S(1)} %gather_heads.1.refs_0_), channel_id=1, source_target_pairs={{0,24},{1,97},{8,0},{9,105},{16,8},{17,113},{24,16},{25,121},{32,5... | collective-permute-start | bytes 3145736 | tf_op jit(solution)/shard_map/ppermute | solution.py:321
  287.9 13.7 %collective-permute-start.15 = (f32[256,512]{1,0:T(8,128)S(1)}, f32[256,512]{1,0:T(8,128)S(1)}, u32[]{:S(2)}, u32[]{:S(2)}) collective-permute-start(f32[256,512]{1,0:T(8,128)S(1)} %copy-done.15), channel_id=1, source_target_pairs={{0,6},{2,4},{4,2},{6,0},{1,7},{3,5},{5,3},{7,1},{8,14},{10,12},{12... | collective-permute-start | bytes 1572872 | tf_op jit(solution)/shard_map/ppermute | solution.py:324
  288.2 24.6 %collective-permute-start.14 = (f32[256,512]{1,0:T(8,128)S(1)}, f32[256,512]{1,0:T(8,128)S(1)}, u32[]{:S(2)}, u32[]{:S(2)}) collective-permute-start(f32[256,512]{1,0:T(8,128)S(1)} %copy-done.12), channel_id=1, source_target_pairs={{0,6},{2,4},{4,2},{6,0},{1,7},{3,5},{5,3},{7,1},{8,14},{10,12},{12... | collective-permute-start | bytes 1572872 | tf_op jit(solution)/shard_map/ppermute | solution.py:324
  301.6 17.6 %collective-permute-start.28 = (f32[1,2,256,128]{3,2,1,0:T(8,128)}, f32[1,2,256,128]{3,2,1,0:T(8,128)S(1)}, u32[]{:S(2)}, u32[]{:S(2)}) collective-permute-start(f32[1,2,256,128]{3,2,1,0:T(8,128)} %bitcast.8), channel_id=1, source_target_pairs={{0,6},{2,4},{4,2},{6,0},{1,7},{3,5},{5,3},{7,1},{8,14},{10,12},{12... | collective-permute-start | bytes 786440 | tf_op jit(solution)/shard_map/ppermute | solution.py:324
  319.1 11.4 %collective-permute-start.23 = (f32[4,256,128]{2,1,0:T(8,128)}, f32[4,256,128]{2,1,0:T(8,128)S(1)}, u32[]{:S(2)}, u32[]{:S(2)}) collective-permute-start(f32[4,256,128]{2,1,0:T(8,128)} %get-tuple-element.69), channel_id=1, source_target_pairs={{0,96},{1,25},{8,104},{9,1},{16,112},{17,9},{24,120},{25,17},{32,0... | collective-permute-start | bytes 1572872 | tf_op jit(solution)/shard_map/ppermute | solution.py:321
  319.1 11.4 %collective-permute-start.24 = (f32[4,256,128]{2,1,0:T(8,128)}, f32[4,256,128]{2,1,0:T(8,128)S(1)}, u32[]{:S(2)}, u32[]{:S(2)}) collective-permute-start(f32[4,256,128]{2,1,0:T(8,128)} %get-tuple-element.70), channel_id=1, source_target_pairs={{0,64},{1,17},{8,72},{9,25},{16,80},{17,1},{24,88},{25,9},{32,96},... | collective-permute-start | bytes 1572872 | tf_op jit(solution)/shard_map/ppermute | solution.py:321
  319.1 15.7 %collective-permute-start.25 = (f32[4,256,128]{2,1,0:T(8,128)}, f32[4,256,128]{2,1,0:T(8,128)S(1)}, u32[]{:S(2)}, u32[]{:S(2)}) collective-permute-start(f32[4,256,128]{2,1,0:T(8,128)} %get-tuple-element.71), channel_id=1, source_target_pairs={{0,32},{1,9},{8,40},{9,17},{16,48},{17,25},{24,56},{25,1},{32,64},... | collective-permute-start | bytes 1572872 | tf_op jit(solution)/shard_map/ppermute | solution.py:321
  (24 other events, 236.4 us)
Sparse Core Ops, SparseCore 0:
  20.7 33.2 all-gather.2

commit v8 on v7

--- a/solution.py
+++ b/solution.py
@@ -282,32 +282,22 @@
 SWAP = [(0, 1), (1, 0)]
 PLACE = ("y", "x", "head")
 
-def glue(body, args, outs, copies, hbm=False):
+def glue(body, args, outs):
     spec = lambda shape: pl.BlockSpec(shape, lambda i: (0,) * len(shape))
-    if copies:
-        spec = lambda shape: pl.BlockSpec(memory_space=pl.ANY)
     arrays = args[1:]
     return pl.pallas_call(
         body,
-        out_shape=[(pltpu.HBM if hbm else jax.ShapeDtypeStruct)(s, F32) for s in outs],
+        out_shape=[jax.ShapeDtypeStruct(s, F32) for s in outs],
         grid=(1,),
         in_specs=[pl.BlockSpec(memory_space=pltpu.SMEM)] + [spec(a.shape) for a in arrays],
         out_specs=[spec(s) for s in outs],
-        scratch_shapes=[pltpu.SemaphoreType.DMA((copies,))] if copies else [],
         compiler_params=pltpu.CompilerParams(
-            dimension_semantics=("arbitrary",), vmem_limit_bytes=(4 if copies else 20) << 20),
+            dimension_semantics=("arbitrary",), vmem_limit_bytes=20 << 20),
         cost_estimate=pl.CostEstimate(
             flops=0, transcendentals=0,
             bytes_accessed=4 * sum(math.prod(s) for s in [a.shape for a in arrays] + list(outs))),
         name=body.__name__,
     )(args[0], *arrays)
-
-def copy_all(pairs, sems):
-    copies = [pltpu.make_async_copy(a, b, sems.at[n]) for n, (a, b) in enumerate(pairs)]
-    for c in copies:
-        c.start()
-    for c in copies:
-        c.wait()
 
 def travel(array, step, stage):
     pairs = []
@@ -339,63 +329,49 @@
     y, x = other // 4, other % 4
     return jnp.where(core == 0, y, x), jnp.where(core == 0, x, y)
 
-def assemble(spot, keys, values, other, full, sems):
+def assemble(spot, keys, values, other, full):
     core = spot[0]
     half = T // 2
     here, there = (pl.ds(pl.multiple_of(c * half, half), half) for c in (core, 1 - core))
     for h in range(4):
         cols = slice(h * W, (h + 1) * W)
-        for i, ref in enumerate((keys, values)):
-            @pl.when(core == i)
-            def _(ref=ref, cols=cols, h=h):
-                pltpu.make_async_copy(ref.at[:, cols], full.at[h, here], sems.at[h]).start()
-        pltpu.make_async_copy(other.at[:, cols], full.at[h, there], sems.at[4 + h]).start()
-    for h in range(4):
-        cols = slice(h * W, (h + 1) * W)
-        pltpu.make_async_copy(keys.at[:, cols], full.at[h, here], sems.at[h]).wait()
-        pltpu.make_async_copy(other.at[:, cols], full.at[h, there], sems.at[4 + h]).wait()
+        full[h, here] = jnp.where(core == 0, keys[:, cols], values[:, cols])
+        full[h, there] = other[:, cols]
 
 def pick(table, *refs):
     core, here, there = place()
-    along, out, sems = refs[0:4], refs[4:7], refs[7]
-    waits = []
+    along, out = refs[0:4], refs[4:7]
     for step in (1, 2, 3):
         for j in range(2):
             first, _ = chosen(table, here, (there + step) % 4, core, j)
             for i in range(4):
                 @pl.when((here - first) % 4 == i)
-                def _(source=along[i], target=out[step - 1].at[j], n=len(waits)):
-                    pltpu.make_async_copy(source, target, sems.at[n]).start()
-            waits.append((along[0], out[step - 1].at[j]))
-    for n, (source, target) in enumerate(waits):
-        pltpu.make_async_copy(source, target, sems.at[n]).wait()
+                def _(source=along[i], ref=out[step - 1], j=j):
+                    ref[j] = source[...]
 
 def join(table, *refs):
     core, here, there = place()
-    along, got, (mine, send), sems = refs[0:4], refs[4:7], refs[7:9], refs[9]
-    waits = []
+    along, got, (mine, send) = refs[0:4], refs[4:7], refs[7:9]
     for j in range(2):
         first, second = chosen(table, here, there, core, j)
         near, off = (here - first) % 4, (there - second) % 4
         for c, out in ((core, mine), (1 - core, send)):
-            heads, target, n = pl.ds(2 * c, 2), out.at[j], len(waits)
+            heads = pl.ds(2 * c, 2)
             for k in range(4):
                 @pl.when((off == 0) & (near == k))
-                def _(source=along[k].at[heads], target=target, n=n):
-                    pltpu.make_async_copy(source, target, sems.at[n]).start()
+                def _(source=along[k], out=out, heads=heads, j=j):
+                    out[j] = source[heads]
             for k in range(3):
                 @pl.when(off == k + 1)
-                def _(source=got[k].at[j, heads], target=target, n=n):
-                    pltpu.make_async_copy(source, target, sems.at[n]).start()
-            waits.append((along[0].at[heads], target))
-    for n, (source, target) in enumerate(waits):
-        pltpu.make_async_copy(source, target, sems.at[n]).wait()
-
-def arrange(spot, mine, other, same, cross, sems):
+                def _(source=got[k], out=out, heads=heads, j=j):
+                    out[j] = source[j, heads]
+
+def arrange(spot, mine, other, same, cross):
     head = spot[1]
-    copy_all([(ref.at[j, h], out.at[j, n]) for j in range(2)
-              for n, ref in enumerate((mine, other))
-              for h, out in ((head, same), (1 - head, cross))], sems)
+    for j in range(2):
+        for n, ref in enumerate((mine, other)):
+            same[j, n] = ref[j, head]
+            cross[j, n] = ref[j, 1 - head]
 
 def spread(spot, mine, added, passed, passed2, keep, send):
     head = spot[1]
@@ -404,10 +380,11 @@
             out[j, head] = mine[j, n] + added[j, n]
             out[j, 1 - head] = passed[j, n] + passed2[j, n]
 
-def gather_heads(spot, keep, other, full, sems):
+def gather_heads(spot, keep, other, full):
     core = spot[0]
-    copy_all([(ref.at[j], full.at[j, pl.ds(2 * c, 2)]) for j in range(2)
-              for c, ref in ((core, keep), (1 - core, other))], sems)
+    for j in range(2):
+        full[j, pl.ds(2 * core, 2)] = keep[j]
+        full[j, pl.ds(2 * (1 - core), 2)] = other[j]
 
 def collect(table, *refs):
     core, here, there = place()
@@ -434,15 +411,15 @@
         for a in (queries, cotangent)
     )
     got = swap(jnp.where(core == 0, values, keys))
-    (full,) = glue(assemble, (spot, *in_hbm(keys, values), got), (HEADS,), 8)
+    (full,) = glue(assemble, (spot, *in_hbm(keys, values), got), (HEADS,))
     own = lax.all_gather(full, "z", axis=0)
     own_other = swap(lax.dynamic_index_in_dim(own, 2 * (1 - core) + head, 1, keepdims=False))
 
     along = [full] + [travel(full, s, 0) for s in (1, 2, 3)]
-    sent = glue(pick, (selected, *along), ((2,) + HEADS,) * 3, 6, hbm=True)
+    sent = glue(pick, (selected, *along), ((2,) + HEADS,) * 3)
     got = [travel(sent[s - 1], s, 1) for s in (1, 2, 3)]
-    kept, send = glue(join, (after(selected, q_far, do_far), *along, *got), (PAIR, PAIR), 4)
-    same, cross = glue(arrange, (spot, kept, swap(send)), (PAIR, PAIR), 8)
+    kept, send = glue(join, (after(selected, q_far, do_far), *along, *got), (PAIR, PAIR))
+    same, cross = glue(arrange, (spot, kept, swap(send)), (PAIR, PAIR))
     pieces = [same] + [mirror(a, flip) for a, flip in ((same, 1), (cross, 2), (cross, 3))]
 
     p, m, l, ot = call_own_forward(info, queries, q_far, own, own_other)
@@ -453,14 +430,14 @@
     def reduced(g, *others):
         arrived = [g[0]] + [mirror(g[flip], flip) for flip in (1, 2, 3)]
         arrived[3] = after(arrived[3], *others)
-        keep, send = glue(spread, (spot, *arrived), (g[0].shape,) * 2, 0)
+        keep, send = glue(spread, (spot, *arrived), (g[0].shape,) * 2)
         return keep, swap(send)
 
-    (terms,) = glue(gather_heads, (spot, *reduced(out[5:9], last[0])), ((2,) + HEADS,), 4)
+    (terms,) = glue(gather_heads, (spot, *reduced(out[5:9], last[0])), ((2,) + HEADS,))
     arrived = [terms] + [travel(terms, s, 1) for s in (1, 2, 3)]
     o_far, dq_far = mirror(o_far, 3), mirror(last[1], 3)
-    sums = glue(collect, (after(selected, o_far, dq_far), *arrived), (HEADS,) * 4, 0)
-    low, high = reduced([a[None] for a in last[2:6]])
+    sums = glue(collect, (after(selected, o_far), *arrived), (HEADS,) * 4)
+    low, high = reduced([a[None] for a in last[2:6]], dq_far)
     total = sums[0] + sum(travel(sums[s], 4 - s, 0) for s in (1, 2, 3))
     total = total + jnp.where(
         core == 0, jnp.concatenate([low[0], high[0]], 0), jnp.concatenate([high[0], low[0]], 0)

time: 351 us -> 242 us (0.69)
  starting transfers between devices: 128 us -> 47.6 us
  Pallas kernels: 116 us -> 77.1 us
  waiting for transfers between devices: 77.7 us -> 87.8 us
    ppermute x6, starting transfers between devices: 65.5 us -> 8.15 us  [swap(): return lax.ppermute(array, 'head', SWAP)]
    pallas_call x8, Pallas kernels: 52.6 us -> 13.2 us  [glue(): pl.pallas_call(body, out_shape=[jax.ShapeDtypeStruct(s, F32) for s in out...]
    ppermute x12, starting transfers between devices: 45.7 us -> 20.7 us  [travel(): return lax.ppermute(array, PLACE, pairs)]
    ppermute x12, waiting for transfers between devices: 19.2 us -> 27.8 us  [travel(): return lax.ppermute(array, PLACE, pairs)]
  transfers between devices with their start and end apart: 32 -> 32, of which waited for: 15 -> 15; matrix products, arithmetic and copies ran while one was open for 2% -> 4% of each run, Pallas kernels for 19% -> 15%
where the time goes in v8:
time: 242 us
  waiting for transfers between devices  87.8 us (36%)
  Pallas kernels  77.1 us (32%)
  starting transfers between devices  47.6 us (20%)
  between operations  14.2 us (6%)
  local copies, waits for them, and re-layouts  8.33 us (3%)
  other arithmetic  6.93 us (3%)
    ppermute x13, waiting for transfers between devices, mirror(): return lax.ppermute(array, 'z', [(i, i ^ flip) for i in range(4)])  55.9 us
    pallas_call x1, Pallas kernels, call_picked(): kernel(picked, [NEAR, FAR, NEAR, FAR] + [whole(PAIR)] * 4 + [tile(ROW), t...  37.8 us
    ppermute x12, waiting for transfers between devices, travel(): return lax.ppermute(array, PLACE, pairs)  27.8 us
    ppermute x12, starting transfers between devices, travel(): return lax.ppermute(array, PLACE, pairs)  20.7 us
    ppermute x13, starting transfers between devices, mirror(): return lax.ppermute(array, 'z', [(i, i ^ flip) for i in range(4)])  18.7 us
    pallas_call x1, Pallas kernels, call_own_backward(): kernel(own_backward, [NEAR, FAR, NEAR, FAR, whole(mine.shape), whole(othe...  15 us
    pallas_call x8, Pallas kernels, glue(): pl.pallas_call(body, out_shape=[jax.ShapeDtypeStruct(s, F32) for s in out...  13.2 us
    pallas_call x1, Pallas kernels, call_own_forward(): kernel(own_forward, [NEAR, FAR, whole(mine.shape), whole(other.shape)], [...  11 us
  transfers between devices with their start and end apart: 32, of which 15 were waited for; matrix products, arithmetic and copies ran while one was open for 4% of the time, Pallas kernels for 15%

profile of v8, /device:TPU:1, one launch (start us, length us, event | category | flops | bytes accessed | tf_op | source)
XLA Modules:
  0.0 242.0 jit_solution(16272766591479734263)
XLA Ops:
  14.2 2.5 %collective-permute-start.4 = (f32[4,256,128]{2,1,0:T(8,128)}, f32[4,256,128]{2,1,0:T(8,128)S(1)}, u32[]{:S(2)}, u32[]{:S(2)}) collective-permute-start(f32[4,256,128]{2,1,0:T(8,128)} %assemble.1.refs_0_), channel_id=1, source_target_pairs={{0,64},{1,17},{8,72},{9,25},{16,80},{17,1},{24,88},{25,9},{32,96},... | collective-permute-start | bytes 1572872 | tf_op jit(solution)/shard_map/ppermute | solution.py:311
  17.9 4.8 %collective-permute-done.3.refs_1_ = f32[4,256,128]{2,1,0:T(8,128)S(1)} collective-permute-done((f32[4,256,128]{2,1,0:T(8,128)}, f32[4,256,128]{2,1,0:T(8,128)S(1)}, u32[]{:S(2)}, u32[]{:S(2)}) %collective-permute-start.3) | collective-permute-done | bytes 524320 | tf_op jit(solution)/shard_map/ppermute | solution.py:311
  22.6 6.7 %collective-permute-done.4.refs_2_ = f32[4,256,128]{2,1,0:T(8,128)S(1)} collective-permute-done((f32[4,256,128]{2,1,0:T(8,128)}, f32[4,256,128]{2,1,0:T(8,128)S(1)}, u32[]{:S(2)}, u32[]{:S(2)}) %collective-permute-start.4) | collective-permute-done | bytes 524320 | tf_op jit(solution)/shard_map/ppermute | solution.py:311
  29.3 3.2 %pick.1 = (f32[2,4,256,128]{3,2,1,0:T(8,128)}, f32[2,4,256,128]{3,2,1,0:T(8,128)}, f32[2,4,256,128]{3,2,1,0:T(8,128)}) custom-call(s32[16,3]{1,0:T(8,128)S(1)} %copy.12.table, f32[4,256,128]{2,1,0:T(8,128)} %assemble.1.refs_0_, f32[4,256,128]{2,1,0:T(8,128)S(1)} %collective-permute-done.3.refs_1_, f32[4,256,128]{2,1,0:T(8,128)S(1)} %collective-permute-done.4.refs_2_, ...), custom_call_target="tpu_custom_call" | custom-call | bytes 5242880 | tf_op jit(solution)/shard_map/pick/pallas_call | solution.py:288
  33.5 2.6 %collective-permute-start.7 = (f32[2,4,256,128]{3,2,1,0:T(8,128)}, f32[2,4,256,128]{3,2,1,0:T(8,128)}, u32[]{:S(2)}, u32[]{:S(2)}) collective-permute-start(f32[2,4,256,128]{3,2,1,0:T(8,128)} %get-tuple-element.44), channel_id=1, source_target_pairs={{0,16},{1,65},{8,24},{9,73},{16,0},{17,81},{24,8},{25,89},{32,48},... | collective-permute-start | bytes 3145736 | tf_op jit(solution)/shard_map/ppermute | solution.py:311
  39.1 3.8 %collective-permute-start = (f32[256,512]{1,0:T(8,128)}, f32[256,512]{1,0:T(8,128)S(1)}, u32[]{:S(2)}, u32[]{:S(2)}) collective-permute-start(f32[256,512]{1,0:T(8,128)} %constant_dynamic-slice_fusion.1), channel_id=1, source_target_pairs={{0,6},{2,4},{4,2},{6,0},{1,7},{3,5},{5,3},{7,1},{8,14},{10,12},{12... | collective-permute-start | bytes 1572872 | tf_op jit(solution)/shard_map/ppermute | solution.py:314
  44.7 11.8 %collective-permute-done.qr_ref = f32[256,512]{1,0:T(8,128)S(1)} collective-permute-done((f32[256,512]{1,0:T(8,128)}, f32[256,512]{1,0:T(8,128)S(1)}, u32[]{:S(2)}, u32[]{:S(2)}) %collective-permute-start) | collective-permute-done | bytes 524320 | tf_op jit(solution)/shard_map/ppermute | solution.py:314
  57.3 10.4 %collective-permute-done.1.dr_ref = f32[256,512]{1,0:T(8,128)} collective-permute-done((f32[256,512]{1,0:T(8,128)}, f32[256,512]{1,0:T(8,128)}, u32[]{:S(2)}, u32[]{:S(2)}) %collective-permute-start.1) | collective-permute-done | bytes 524320 | tf_op jit(solution)/shard_map/ppermute | solution.py:314
  67.8 2.7 %join.1 = (f32[2,2,256,128]{3,2,1,0:T(8,128)S(1)}, f32[2,2,256,128]{3,2,1,0:T(8,128)}) custom-call(s32[16,3]{1,0:T(8,128)S(1)} %copy.13.table, f32[4,256,128]{2,1,0:T(8,128)} %assemble.1.refs_0_, f32[4,256,128]{2,1,0:T(8,128)S(1)} %collective-permute-done.3.refs_1_, f32[4,256,128]{2,1,0:T(8,128)S(1)} %collective-permute-done.4.refs_2_, ...), custom_call_target="tpu_custom_call" | custom-call | bytes 6291456 | tf_op jit(solution)/shard_map/join/pallas_call | solution.py:288
  78.7 11.0 %own_forward.1 = (f32[4,1024,512]{2,1,0:T(8,128)}, f32[4,1,512]{2,1,0:T(1,128)}, f32[4,1,512]{2,1,0:T(1,128)}, f32[4,128,512]{2,1,0:T(8,128)}) custom-call(s32[5]{0:T(128)S(1)} %pad_add_fusion.info, f32[256,1024]{1,0:T(8,128)} %ql_ref.5, f32[256,512]{1,0:T(8,128)S(1)} %copy-done.4, f32[4,4,256,128]{3,2,1,0:T(8,128)} %bitcast.32, ...), custom_call_target="tpu_custom_call" | custom-call | flops 4294967296 | bytes 16777216 | tf_op jit(solution)/shard_map/own_forward/pallas_call | solution.py:250
  89.7 9.8 %collective-permute-done.11.s2 = f32[2,2,256,128]{3,2,1,0:T(8,128)S(1)} collective-permute-done((f32[2,2,256,128]{3,2,1,0:T(8,128)S(1)}, f32[2,2,256,128]{3,2,1,0:T(8,128)S(1)}, u32[]{:S(2)}, u32[]{:S(2)}) %collective-permute-start.11) | collective-permute-done | bytes 524320 | tf_op jit(solution)/shard_map/ppermute | solution.py:314
  101.6 37.8 %picked.1 = (f32[256,512]{1,0:T(8,128)}, f32[256,512]{1,0:T(8,128)}, f32[4,128,512]{2,1,0:T(8,128)}, f32[4,1,512]{2,1,0:T(1,128)}, f32[4,1,512]{2,1,0:T(1,128)},...) custom-call(s32[5]{0:T(128)S(1)} %pad_add_fusion.info, ...), custom_call_target="tpu_custom_call" | custom-call | flops 21474836480 | bytes 16777216 | tf_op jit(solution)/shard_map/picked/pallas_call | solution.py:260
  143.3 15.0 %own_backward.1 = (f32[256,512]{1,0:T(8,128)}, f32[256,512]{1,0:T(8,128)}, f32[2,256,128]{2,1,0:T(8,128)}, f32[2,256,128]{2,1,0:T(8,128)}, f32[2,256,128]{2,1,0:T(8,128)}, /*index=5*/f32[2,256,128]{2,1,0:T(8,128)}) custom-call(s32[5]{0:T(128)S(1)} %pad_add_fusion.info, f32[256,1024]{1,0:T(8,128)} %ql_ref.5, f32[256,512]{1,0:T(8,128)S(1)} %copy-done.4, ...), custom_call_target="tpu_custom_call" | custom-call | flops 6442450944 | bytes 16777216 | tf_op jit(solution)/shard_map/own_backward/pallas_call | solution.py:272
  158.4 6.2 %collective-permute-done.17.passed = f32[2,2,256,128]{3,2,1,0:T(8,128)S(1)} collective-permute-done((f32[2,2,256,128]{3,2,1,0:T(8,128)}, f32[2,2,256,128]{3,2,1,0:T(8,128)S(1)}, u32[]{:S(2)}, u32[]{:S(2)}) %collective-permute-start.17) | collective-permute-done | bytes 524320 | tf_op jit(solution)/shard_map/ppermute | solution.py:314
  165.2 3.2 %collective-permute-start.19 = (f32[2,2,256,128]{3,2,1,0:T(8,128)S(1)}, f32[2,2,256,128]{3,2,1,0:T(8,128)S(1)}, u32[]{:S(2)}, u32[]{:S(2)}) collective-permute-start(f32[2,2,256,128]{3,2,1,0:T(8,128)S(1)} %get-tuple-element.68), channel_id=1, source_target_pairs={{0,1},{1,0},{2,3},{3,2},{4,5},{5,4},{6,7},{7,6},{8,9},{9,8},{10,11... | collective-permute-start | bytes 1572872 | tf_op jit(solution)/shard_map/ppermute | solution.py:317
  171.2 2.4 %collective-permute-start.21 = (f32[2,4,256,128]{3,2,1,0:T(8,128)S(1)}, f32[2,4,256,128]{3,2,1,0:T(8,128)S(1)}, u32[]{:S(2)}, u32[]{:S(2)}) collective-permute-start(f32[2,4,256,128]{3,2,1,0:T(8,128)S(1)} %gather_heads.1.refs_0_), channel_id=1, source_target_pairs={{0,16},{1,65},{8,24},{9,73},{16,0},{17,81},{24,8},{25,89},{32,48},... | collective-permute-start | bytes 3145736 | tf_op jit(solution)/shard_map/ppermute | solution.py:311
  177.5 10.1 %collective-permute-done.14 = f32[256,512]{1,0:T(8,128)S(1)} collective-permute-done((f32[256,512]{1,0:T(8,128)S(1)}, f32[256,512]{1,0:T(8,128)S(1)}, u32[]{:S(2)}, u32[]{:S(2)}) %collective-permute-start.14) | collective-permute-done | bytes 524320 | tf_op jit(solution)/shard_map/ppermute | solution.py:314
  188.5 2.8 %collective-permute-start.28 = (f32[1,2,256,128]{3,2,1,0:T(8,128)}, f32[1,2,256,128]{3,2,1,0:T(8,128)S(1)}, u32[]{:S(2)}, u32[]{:S(2)}) collective-permute-start(f32[1,2,256,128]{3,2,1,0:T(8,128)} %bitcast.8), channel_id=1, source_target_pairs={{0,6},{2,4},{4,2},{6,0},{1,7},{3,5},{5,3},{7,1},{8,14},{10,12},{12... | collective-permute-start | bytes 786440 | tf_op jit(solution)/shard_map/ppermute | solution.py:314
  191.4 6.0 %collective-permute-done.21.refs_2_ = f32[2,4,256,128]{3,2,1,0:T(8,128)S(1)} collective-permute-done((f32[2,4,256,128]{3,2,1,0:T(8,128)S(1)}, f32[2,4,256,128]{3,2,1,0:T(8,128)S(1)}, u32[]{:S(2)}, u32[]{:S(2)}) %collective-permute-start.21) | collective-permute-done | bytes 1048608 | tf_op jit(solution)/shard_map/ppermute | solution.py:311
  198.9 3.0 %collect.1 = (f32[4,256,128]{2,1,0:T(8,128)S(1)}, f32[4,256,128]{2,1,0:T(8,128)}, f32[4,256,128]{2,1,0:T(8,128)}, f32[4,256,128]{2,1,0:T(8,128)}) custom-call(s32[16,3]{1,0:T(8,128)S(1)} %copy.14.table, f32[2,4,256,128]{3,2,1,0:T(8,128)S(1)} %gather_heads.1.refs_0_, f32[2,4,256,128]{3,2,1,0:T(8,128)S(1)} %collective-permute-done.20.refs_1_, ...), custom_call_target="tpu_custom_call" | custom-call | bytes 6291456 | tf_op jit(solution)/shard_map/collect/pallas_call | solution.py:288
  204.7 5.5 %collective-permute-done.28.passed2 = f32[1,2,256,128]{3,2,1,0:T(8,128)S(1)} collective-permute-done((f32[1,2,256,128]{3,2,1,0:T(8,128)}, f32[1,2,256,128]{3,2,1,0:T(8,128)S(1)}, u32[]{:S(2)}, u32[]{:S(2)}) %collective-permute-start.28) | collective-permute-done | bytes 262176 | tf_op jit(solution)/shard_map/ppermute | solution.py:314
  210.1 4.6 %collective-permute-start.24 = (f32[4,256,128]{2,1,0:T(8,128)}, f32[4,256,128]{2,1,0:T(8,128)S(1)}, u32[]{:S(2)}, u32[]{:S(2)}) collective-permute-start(f32[4,256,128]{2,1,0:T(8,128)} %get-tuple-element.71), channel_id=1, source_target_pairs={{0,64},{1,17},{8,72},{9,25},{16,80},{17,1},{24,88},{25,9},{32,96},... | collective-permute-start | bytes 1572872 | tf_op jit(solution)/shard_map/ppermute | solution.py:311
  217.1 4.7 %collective-permute-done.24 = f32[4,256,128]{2,1,0:T(8,128)S(1)} collective-permute-done((f32[4,256,128]{2,1,0:T(8,128)}, f32[4,256,128]{2,1,0:T(8,128)S(1)}, u32[]{:S(2)}, u32[]{:S(2)}) %collective-permute-start.24) | collective-permute-done | bytes 524320 | tf_op jit(solution)/shard_map/ppermute | solution.py:311
  221.9 5.6 %collective-permute-done.25 = f32[4,256,128]{2,1,0:T(8,128)S(1)} collective-permute-done((f32[4,256,128]{2,1,0:T(8,128)}, f32[4,256,128]{2,1,0:T(8,128)S(1)}, u32[]{:S(2)}, u32[]{:S(2)}) %collective-permute-start.25) | collective-permute-done | bytes 524320 | tf_op jit(solution)/shard_map/ppermute | solution.py:311
  (94 shorter events, 51.6 us)
Async XLA Ops:
  7.2 64.7 %all-gather.3.cloned.1.call-start = ((), (), s32[]{:S(2)}) async-start(), calls=%async_computation | async-start | bytes 2621440 | tf_op jit(solution)/shard_map/all_gather | solution.py:415
  14.2 15.1 %collective-permute-start.4 = (f32[4,256,128]{2,1,0:T(8,128)}, f32[4,256,128]{2,1,0:T(8,128)S(1)}, u32[]{:S(2)}, u32[]{:S(2)}) collective-permute-start(f32[4,256,128]{2,1,0:T(8,128)} %assemble.1.refs_0_), channel_id=1, source_target_pairs={{0,64},{1,17},{8,72},{9,25},{16,80},{17,1},{24,88},{25,9},{32,96},... | collective-permute-start | bytes 1572872 | tf_op jit(solution)/shard_map/ppermute | solution.py:311
  16.6 12.7 %collective-permute-start.5 = (f32[4,256,128]{2,1,0:T(8,128)}, f32[4,256,128]{2,1,0:T(8,128)S(1)}, u32[]{:S(2)}, u32[]{:S(2)}) collective-permute-start(f32[4,256,128]{2,1,0:T(8,128)} %assemble.1.refs_0_), channel_id=1, source_target_pairs={{0,96},{1,25},{8,104},{9,1},{16,112},{17,9},{24,120},{25,17},{32,0... | collective-permute-start | bytes 1572872 | tf_op jit(solution)/shard_map/ppermute | solution.py:311
  32.5 35.4 %collective-permute-start.6 = (f32[2,4,256,128]{3,2,1,0:T(8,128)}, f32[2,4,256,128]{3,2,1,0:T(8,128)S(1)}, u32[]{:S(2)}, u32[]{:S(2)}) collective-permute-start(f32[2,4,256,128]{3,2,1,0:T(8,128)} %get-tuple-element.43), channel_id=1, source_target_pairs={{0,8},{1,33},{8,16},{9,41},{16,24},{17,49},{24,0},{25,57},{32,40},... | collective-permute-start | bytes 3145736 | tf_op jit(solution)/shard_map/ppermute | solution.py:311
  33.5 34.3 %collective-permute-start.7 = (f32[2,4,256,128]{3,2,1,0:T(8,128)}, f32[2,4,256,128]{3,2,1,0:T(8,128)}, u32[]{:S(2)}, u32[]{:S(2)}) collective-permute-start(f32[2,4,256,128]{3,2,1,0:T(8,128)} %get-tuple-element.44), channel_id=1, source_target_pairs={{0,16},{1,65},{8,24},{9,73},{16,0},{17,81},{24,8},{25,89},{32,48},... | collective-permute-start | bytes 3145736 | tf_op jit(solution)/shard_map/ppermute | solution.py:311
  36.1 31.7 %collective-permute-start.8 = (f32[2,4,256,128]{3,2,1,0:T(8,128)}, f32[2,4,256,128]{3,2,1,0:T(8,128)}, u32[]{:S(2)}, u32[]{:S(2)}) collective-permute-start(f32[2,4,256,128]{3,2,1,0:T(8,128)} %get-tuple-element.45), channel_id=1, source_target_pairs={{0,24},{1,97},{8,0},{9,105},{16,8},{17,113},{24,16},{25,121},{32,5... | collective-permute-start | bytes 3145736 | tf_op jit(solution)/shard_map/ppermute | solution.py:311
  39.1 17.5 %collective-permute-start = (f32[256,512]{1,0:T(8,128)}, f32[256,512]{1,0:T(8,128)S(1)}, u32[]{:S(2)}, u32[]{:S(2)}) collective-permute-start(f32[256,512]{1,0:T(8,128)} %constant_dynamic-slice_fusion.1), channel_id=1, source_target_pairs={{0,6},{2,4},{4,2},{6,0},{1,7},{3,5},{5,3},{7,1},{8,14},{10,12},{12... | collective-permute-start | bytes 1572872 | tf_op jit(solution)/shard_map/ppermute | solution.py:314
  44.7 23.0 %collective-permute-start.1 = (f32[256,512]{1,0:T(8,128)}, f32[256,512]{1,0:T(8,128)}, u32[]{:S(2)}, u32[]{:S(2)}) collective-permute-start(f32[256,512]{1,0:T(8,128)} %constant_dynamic-slice_fusion), channel_id=1, source_target_pairs={{0,6},{2,4},{4,2},{6,0},{1,7},{3,5},{5,3},{7,1},{8,14},{10,12},{12... | collective-permute-start | bytes 1572872 | tf_op jit(solution)/shard_map/ppermute | solution.py:314
  74.5 15.3 %collective-permute-start.10 = (f32[2,2,256,128]{3,2,1,0:T(8,128)S(1)}, f32[2,2,256,128]{3,2,1,0:T(8,128)S(1)}, u32[]{:S(2)}, u32[]{:S(2)}) collective-permute-start(f32[2,2,256,128]{3,2,1,0:T(8,128)S(1)} %get-tuple-element.48.s0), channel_id=1, source_target_pairs={{0,2},{2,0},{4,6},{6,4},{1,3},{3,1},{5,7},{7,5},{8,10},{10,8},{12,... | collective-permute-start | bytes 1572872 | tf_op jit(solution)/shard_map/ppermute | solution.py:314
  74.7 24.8 %collective-permute-start.11 = (f32[2,2,256,128]{3,2,1,0:T(8,128)S(1)}, f32[2,2,256,128]{3,2,1,0:T(8,128)S(1)}, u32[]{:S(2)}, u32[]{:S(2)}) collective-permute-start(f32[2,2,256,128]{3,2,1,0:T(8,128)S(1)} %get-tuple-element.49), channel_id=1, source_target_pairs={{0,4},{2,6},{4,0},{6,2},{1,5},{3,7},{5,1},{7,3},{8,12},{10,14},{12... | collective-permute-start | bytes 1572872 | tf_op jit(solution)/shard_map/ppermute | solution.py:314
  76.6 25.0 %collective-permute-start.12 = (f32[2,2,256,128]{3,2,1,0:T(8,128)S(1)}, f32[2,2,256,128]{3,2,1,0:T(8,128)}, u32[]{:S(2)}, u32[]{:S(2)}) collective-permute-start(f32[2,2,256,128]{3,2,1,0:T(8,128)S(1)} %get-tuple-element.49), channel_id=1, source_target_pairs={{0,6},{2,4},{4,2},{6,0},{1,7},{3,5},{5,3},{7,1},{8,14},{10,12},{12... | collective-permute-start | bytes 1572872 | tf_op jit(solution)/shard_map/ppermute | solution.py:314
  139.4 19.0 %collective-permute-start.18 = (f32[2,2,256,128]{3,2,1,0:T(8,128)}, f32[2,2,256,128]{3,2,1,0:T(8,128)S(1)}, u32[]{:S(2)}, u32[]{:S(2)}) collective-permute-start(f32[2,2,256,128]{3,2,1,0:T(8,128)} %get-tuple-element.65), channel_id=1, source_target_pairs={{0,6},{2,4},{4,2},{6,0},{1,7},{3,5},{5,3},{7,1},{8,14},{10,12},{12... | collective-permute-start | bytes 1572872 | tf_op jit(solution)/shard_map/ppermute | solution.py:314
  141.2 17.1 %collective-permute-start.16 = (f32[2,2,256,128]{3,2,1,0:T(8,128)}, f32[2,2,256,128]{3,2,1,0:T(8,128)S(1)}, u32[]{:S(2)}, u32[]{:S(2)}) collective-permute-start(f32[2,2,256,128]{3,2,1,0:T(8,128)} %get-tuple-element.63), channel_id=1, source_target_pairs={{0,2},{2,0},{4,6},{6,4},{1,3},{3,1},{5,7},{7,5},{8,10},{10,8},{12,... | collective-permute-start | bytes 1572872 | tf_op jit(solution)/shard_map/ppermute | solution.py:314
  141.2 23.3 %collective-permute-start.17 = (f32[2,2,256,128]{3,2,1,0:T(8,128)}, f32[2,2,256,128]{3,2,1,0:T(8,128)S(1)}, u32[]{:S(2)}, u32[]{:S(2)}) collective-permute-start(f32[2,2,256,128]{3,2,1,0:T(8,128)} %get-tuple-element.64), channel_id=1, source_target_pairs={{0,4},{2,6},{4,0},{6,2},{1,5},{3,7},{5,1},{7,3},{8,12},{10,14},{12... | collective-permute-start | bytes 1572872 | tf_op jit(solution)/shard_map/ppermute | solution.py:314
  170.5 20.8 %collective-permute-start.20 = (f32[2,4,256,128]{3,2,1,0:T(8,128)S(1)}, f32[2,4,256,128]{3,2,1,0:T(8,128)S(1)}, u32[]{:S(2)}, u32[]{:S(2)}) collective-permute-start(f32[2,4,256,128]{3,2,1,0:T(8,128)S(1)} %gather_heads.1.refs_0_), channel_id=1, source_target_pairs={{0,8},{1,33},{8,16},{9,41},{16,24},{17,49},{24,0},{25,57},{32,40},... | collective-permute-start | bytes 3145736 | tf_op jit(solution)/shard_map/ppermute | solution.py:311
  171.2 26.1 %collective-permute-start.21 = (f32[2,4,256,128]{3,2,1,0:T(8,128)S(1)}, f32[2,4,256,128]{3,2,1,0:T(8,128)S(1)}, u32[]{:S(2)}, u32[]{:S(2)}) collective-permute-start(f32[2,4,256,128]{3,2,1,0:T(8,128)S(1)} %gather_heads.1.refs_0_), channel_id=1, source_target_pairs={{0,16},{1,65},{8,24},{9,73},{16,0},{17,81},{24,8},{25,89},{32,48},... | collective-permute-start | bytes 3145736 | tf_op jit(solution)/shard_map/ppermute | solution.py:311
  173.7 25.2 %collective-permute-start.22 = (f32[2,4,256,128]{3,2,1,0:T(8,128)S(1)}, f32[2,4,256,128]{3,2,1,0:T(8,128)}, u32[]{:S(2)}, u32[]{:S(2)}) collective-permute-start(f32[2,4,256,128]{3,2,1,0:T(8,128)S(1)} %gather_heads.1.refs_0_), channel_id=1, source_target_pairs={{0,24},{1,97},{8,0},{9,105},{16,8},{17,113},{24,16},{25,121},{32,5... | collective-permute-start | bytes 3145736 | tf_op jit(solution)/shard_map/ppermute | solution.py:311
  174.8 12.8 %collective-permute-start.14 = (f32[256,512]{1,0:T(8,128)S(1)}, f32[256,512]{1,0:T(8,128)S(1)}, u32[]{:S(2)}, u32[]{:S(2)}) collective-permute-start(f32[256,512]{1,0:T(8,128)S(1)} %copy-done.10), channel_id=1, source_target_pairs={{0,6},{2,4},{4,2},{6,0},{1,7},{3,5},{5,3},{7,1},{8,14},{10,12},{12... | collective-permute-start | bytes 1572872 | tf_op jit(solution)/shard_map/ppermute | solution.py:314
  177.2 37.6 %collective-permute-start.15 = (f32[256,512]{1,0:T(8,128)}, f32[256,512]{1,0:T(8,128)}, u32[]{:S(2)}, u32[]{:S(2)}) collective-permute-start(f32[256,512]{1,0:T(8,128)} %get-tuple-element.60), channel_id=1, source_target_pairs={{0,6},{2,4},{4,2},{6,0},{1,7},{3,5},{5,3},{7,1},{8,14},{10,12},{12... | collective-permute-start | bytes 1572872 | tf_op jit(solution)/shard_map/ppermute | solution.py:314
  188.5 21.7 %collective-permute-start.28 = (f32[1,2,256,128]{3,2,1,0:T(8,128)}, f32[1,2,256,128]{3,2,1,0:T(8,128)S(1)}, u32[]{:S(2)}, u32[]{:S(2)}) collective-permute-start(f32[1,2,256,128]{3,2,1,0:T(8,128)} %bitcast.8), channel_id=1, source_target_pairs={{0,6},{2,4},{4,2},{6,0},{1,7},{3,5},{5,3},{7,1},{8,14},{10,12},{12... | collective-permute-start | bytes 786440 | tf_op jit(solution)/shard_map/ppermute | solution.py:314
  191.4 23.5 %collective-permute-start.26 = (f32[1,2,256,128]{3,2,1,0:T(8,128)}, f32[1,2,256,128]{3,2,1,0:T(8,128)S(1)}, u32[]{:S(2)}, u32[]{:S(2)}) collective-permute-start(f32[1,2,256,128]{3,2,1,0:T(8,128)} %bitcast.35), channel_id=1, source_target_pairs={{0,2},{2,0},{4,6},{6,4},{1,3},{3,1},{5,7},{7,5},{8,10},{10,8},{12,... | collective-permute-start | bytes 786440 | tf_op jit(solution)/shard_map/ppermute | solution.py:314
  197.4 17.5 %collective-permute-start.27 = (f32[1,2,256,128]{3,2,1,0:T(8,128)}, f32[1,2,256,128]{3,2,1,0:T(8,128)S(1)}, u32[]{:S(2)}, u32[]{:S(2)}) collective-permute-start(f32[1,2,256,128]{3,2,1,0:T(8,128)} %bitcast.34), channel_id=1, source_target_pairs={{0,4},{2,6},{4,0},{6,2},{1,5},{3,7},{5,1},{7,3},{8,12},{10,14},{12... | collective-permute-start | bytes 786440 | tf_op jit(solution)/shard_map/ppermute | solution.py:314
  202.7 14.5 %collective-permute-start.23 = (f32[4,256,128]{2,1,0:T(8,128)}, f32[4,256,128]{2,1,0:T(8,128)S(1)}, u32[]{:S(2)}, u32[]{:S(2)}) collective-permute-start(f32[4,256,128]{2,1,0:T(8,128)} %get-tuple-element.70), channel_id=1, source_target_pairs={{0,96},{1,25},{8,104},{9,1},{16,112},{17,9},{24,120},{25,17},{32,0... | collective-permute-start | bytes 1572872 | tf_op jit(solution)/shard_map/ppermute | solution.py:311
  214.7 12.7 %collective-permute-start.25 = (f32[4,256,128]{2,1,0:T(8,128)}, f32[4,256,128]{2,1,0:T(8,128)S(1)}, u32[]{:S(2)}, u32[]{:S(2)}) collective-permute-start(f32[4,256,128]{2,1,0:T(8,128)} %get-tuple-element.72), channel_id=1, source_target_pairs={{0,32},{1,9},{8,40},{9,17},{16,48},{17,25},{24,56},{25,1},{32,64},... | collective-permute-start | bytes 1572872 | tf_op jit(solution)/shard_map/ppermute | solution.py:311
  (21 other events, 140.6 us)
Sparse Core Ops, SparseCore 0:
  12.9 33.9 all-gather.2

commit v9 on v8

--- a/solution.py
+++ b/solution.py
@@ -98,7 +98,7 @@
 
 def picked(info, ql_ref, qr_ref, dl_ref, dr_ref, s0, s1, s2, s3,
            m0_ref, l0_ref, ot0_ref, ol_ref, or_ref, dq_ref, c_ref, rd_ref, g0, g1, g2, g3,
-           kc, vc, kt, vt, s_sc, phi, plo, dk_acc, dv_acc):
+           kc, vc, kt, vt, s_sc, dk_acc, dv_acc):
     u, step = pl.program_id(0), pl.program_id(1)
 
     @pl.when((u == 0) & (step == 0))
@@ -131,8 +131,6 @@
         p = jnp.exp2(s_sc[rows, :] - m)
         s_sc[rows, :] = p
         hi, lo = split(p)
-        phi[rows, :] = hi
-        plo[rows, :] = lo
         l = l + jnp.sum(p, axis=0, keepdims=True)
         ot = ot + values_sum(vt[:, rows], hi, lo)
     inv = 1.0 / l
@@ -157,10 +155,12 @@
     dq = jnp.zeros((W, R), F32)
     for j in range(2):
         rows = slice(j * BLK, (j + 1) * BLK)
+        p = s_sc[rows, :]
+        p2 = jnp.concatenate(split(p), axis=1)
         dp = mm(twice(vc[rows, :], 1), dt)
-        hi, lo = split(s_sc[rows, :] * (dp - rd))
+        hi, lo = split(p * (dp - rd))
         dq = dq + values_sum(kt[:, rows], hi, lo)
-        dv_acc[rows, :] += halves(mm(jnp.concatenate([phi[rows, :], plo[rows, :]], axis=1), d2))
+        dv_acc[rows, :] += halves(mm(p2, d2))
         dk_acc[rows, :] += halves(mm(jnp.concatenate([hi, lo], axis=1), q2))
     dq_ref[0] = dq
 
@@ -263,7 +263,7 @@
         [FIRST, SECOND, tile(TURNED), tile(ROW), tile(ROW)] + [whole(PAIR)] * 4,
         [HALF, HALF, TURNED, ROW, ROW] + [PAIR] * 4,
         [((2 * BLK, 2 * W), BF), ((2 * BLK, 2 * W), BF), ((2 * W, 2 * BLK), BF), ((2 * W, 2 * BLK), BF),
-         ((2 * BLK, R), F32), ((2 * BLK, R), BF), ((2 * BLK, R), BF),
+         ((2 * BLK, R), F32),
          ((2 * BLK, W), F32), ((2 * BLK, W), F32)],
         10 * UNIT, 52,
     )(info, *in_hbm(q), q_far, *in_hbm(do), do_far, *pieces, *in_hbm(m, l, ot))
@@ -406,16 +406,18 @@
     info = jnp.concatenate([jnp.stack([z, head]), (mine >= 0).astype(jnp.int32), core[None]])
     spot = jnp.stack([core, head])
     far = 1 - head
-    q_far, do_far = (
-        mirror(lax.dynamic_slice_in_dim(a, far * 4 * W, 4 * W, 1), 3)
-        for a in (queries, cotangent)
-    )
     got = swap(jnp.where(core == 0, values, keys))
     (full,) = glue(assemble, (spot, *in_hbm(keys, values), got), (HEADS,))
     own = lax.all_gather(full, "z", axis=0)
     own_other = swap(lax.dynamic_index_in_dim(own, 2 * (1 - core) + head, 1, keepdims=False))
 
     along = [full] + [travel(full, s, 0) for s in (1, 2, 3)]
+
+    def turned_over(array, *others):
+        return mirror(lax.dynamic_slice_in_dim(after(array, *others), far * 4 * W, 4 * W, 1), 3)
+
+    q_far = turned_over(queries, along[1])
+    do_far = turned_over(cotangent, q_far)
     sent = glue(pick, (selected, *along), ((2,) + HEADS,) * 3)
     got = [travel(sent[s - 1], s, 1) for s in (1, 2, 3)]
     kept, send = glue(join, (after(selected, q_far, do_far), *along, *got), (PAIR, PAIR))
@@ -436,9 +438,9 @@
     (terms,) = glue(gather_heads, (spot, *reduced(out[5:9], last[0])), ((2,) + HEADS,))
     arrived = [terms] + [travel(terms, s, 1) for s in (1, 2, 3)]
     o_far, dq_far = mirror(o_far, 3), mirror(last[1], 3)
-    sums = glue(collect, (after(selected, o_far), *arrived), (HEADS,) * 4)
-    low, high = reduced([a[None] for a in last[2:6]], dq_far)
-    total = sums[0] + sum(travel(sums[s], 4 - s, 0) for s in (1, 2, 3))
+    low, high = reduced([a[None] for a in last[2:6]])
+    sums = glue(collect, (after(selected, o_far, low), *arrived), (HEADS,) * 4)
+    total = after(sums[0], dq_far) + sum(travel(sums[s], 4 - s, 0) for s in (1, 2, 3))
     total = total + jnp.where(
         core == 0, jnp.concatenate([low[0], high[0]], 0), jnp.concatenate([high[0], low[0]], 0)
     )

time: 242 us -> 239 us (0.988)
  local copies, waits for them, and re-layouts: 8.33 us -> 5.59 us
    ppermute x12, waiting for transfers between devices: 27.8 us -> 17.7 us  [travel(): return lax.ppermute(array, PLACE, pairs)]
    ppermute x13, waiting for transfers between devices: 55.9 us -> 64.1 us  [mirror(): return lax.ppermute(array, 'z', [(i, i ^ flip) for i in range(4)])]
  transfers between devices with their start and end apart: 32 -> 32, of which waited for: 15 -> 16; matrix products, arithmetic and copies ran while one was open for 4% -> 3% of each run, Pallas kernels for 15% -> 16%
where the time goes in v9:
time: 239 us
  waiting for transfers between devices  85.8 us (36%)
  Pallas kernels  76.5 us (32%)
  starting transfers between devices  49.5 us (21%)
  between operations  14.2 us (6%)
  other arithmetic  7 us (3%)
  local copies, waits for them, and re-layouts  5.59 us (2%)
    ppermute x13, waiting for transfers between devices, mirror(): return lax.ppermute(array, 'z', [(i, i ^ flip) for i in range(4)])  64.1 us
    pallas_call x1, Pallas kernels, call_picked(): kernel(picked, [NEAR, FAR, NEAR, FAR] + [whole(PAIR)] * 4 + [tile(ROW), t...  36.3 us
    ppermute x13, starting transfers between devices, mirror(): return lax.ppermute(array, 'z', [(i, i ^ flip) for i in range(4)])  20.3 us
    ppermute x12, starting transfers between devices, travel(): return lax.ppermute(array, PLACE, pairs)  20.2 us
    ppermute x12, waiting for transfers between devices, travel(): return lax.ppermute(array, PLACE, pairs)  17.7 us
    pallas_call x1, Pallas kernels, call_own_backward(): kernel(own_backward, [NEAR, FAR, NEAR, FAR, whole(mine.shape), whole(othe...  15 us
    pallas_call x8, Pallas kernels, glue(): pl.pallas_call(body, out_shape=[jax.ShapeDtypeStruct(s, F32) for s in out...  14.1 us
    pallas_call x1, Pallas kernels, call_own_forward(): kernel(own_forward, [NEAR, FAR, whole(mine.shape), whole(other.shape)], [...  11.1 us
  transfers between devices with their start and end apart: 32, of which 16 were waited for; matrix products, arithmetic and copies ran while one was open for 3% of the time, Pallas kernels for 16%

profile of v9, /device:TPU:1, one launch (start us, length us, event | category | flops | bytes accessed | tf_op | source)
XLA Modules:
  0.0 238.5 jit_solution(3996985734743792003)
XLA Ops:
  17.8 4.8 %collective-permute-done.1.refs_1_ = f32[4,256,128]{2,1,0:T(8,128)S(1)} collective-permute-done((f32[4,256,128]{2,1,0:T(8,128)}, f32[4,256,128]{2,1,0:T(8,128)S(1)}, u32[]{:S(2)}, u32[]{:S(2)}) %collective-permute-start.1) | collective-permute-done | bytes 524320 | tf_op jit(solution)/shard_map/ppermute | solution.py:311
  23.5 3.8 %collective-permute-start.2 = (f32[256,512]{1,0:T(8,128)}, f32[256,512]{1,0:T(8,128)S(1)}, u32[]{:S(2)}, u32[]{:S(2)}) collective-permute-start(f32[256,512]{1,0:T(8,128)} %constant_dynamic-slice_fusion.1), channel_id=1, source_target_pairs={{0,6},{2,4},{4,2},{6,0},{1,7},{3,5},{5,3},{7,1},{8,14},{10,12},{12... | collective-permute-start | bytes 1572872 | tf_op jit(solution)/shard_map/ppermute | solution.py:314
  29.4 3.2 %pick.1 = (f32[2,4,256,128]{3,2,1,0:T(8,128)}, f32[2,4,256,128]{3,2,1,0:T(8,128)}, f32[2,4,256,128]{3,2,1,0:T(8,128)}) custom-call(s32[16,3]{1,0:T(8,128)S(1)} %copy.12.table, f32[4,256,128]{2,1,0:T(8,128)} %assemble.1.refs_0_, f32[4,256,128]{2,1,0:T(8,128)S(1)} %collective-permute-done.1.refs_1_, f32[4,256,128]{2,1,0:T(8,128)S(1)} %collective-permute-done.4.refs_2_, ...), custom_call_target="tpu_custom_call" | custom-call | bytes 5242880 | tf_op jit(solution)/shard_map/pick/pallas_call | solution.py:288
  33.6 2.6 %collective-permute-start.7 = (f32[2,4,256,128]{3,2,1,0:T(8,128)}, f32[2,4,256,128]{3,2,1,0:T(8,128)}, u32[]{:S(2)}, u32[]{:S(2)}) collective-permute-start(f32[2,4,256,128]{3,2,1,0:T(8,128)} %get-tuple-element.48), channel_id=1, source_target_pairs={{0,16},{1,65},{8,24},{9,73},{16,0},{17,81},{24,8},{25,89},{32,48},... | collective-permute-start | bytes 3145736 | tf_op jit(solution)/shard_map/ppermute | solution.py:311
  37.3 12.8 %collective-permute-done.2.qr_ref = f32[256,512]{1,0:T(8,128)S(1)} collective-permute-done((f32[256,512]{1,0:T(8,128)}, f32[256,512]{1,0:T(8,128)S(1)}, u32[]{:S(2)}, u32[]{:S(2)}) %collective-permute-start.2) | collective-permute-done | bytes 524320 | tf_op jit(solution)/shard_map/ppermute | solution.py:314
  51.0 3.4 %collective-permute-start.3 = (f32[256,512]{1,0:T(8,128)}, f32[256,512]{1,0:T(8,128)}, u32[]{:S(2)}, u32[]{:S(2)}) collective-permute-start(f32[256,512]{1,0:T(8,128)} %constant_dynamic-slice_fusion), channel_id=1, source_target_pairs={{0,6},{2,4},{4,2},{6,0},{1,7},{3,5},{5,3},{7,1},{8,14},{10,12},{12... | collective-permute-start | bytes 1572872 | tf_op jit(solution)/shard_map/ppermute | solution.py:314
  54.4 12.7 %collective-permute-done.3.dr_ref = f32[256,512]{1,0:T(8,128)} collective-permute-done((f32[256,512]{1,0:T(8,128)}, f32[256,512]{1,0:T(8,128)}, u32[]{:S(2)}, u32[]{:S(2)}) %collective-permute-start.3) | collective-permute-done | bytes 524320 | tf_op jit(solution)/shard_map/ppermute | solution.py:314
  67.2 2.7 %join.1 = (f32[2,2,256,128]{3,2,1,0:T(8,128)S(1)}, f32[2,2,256,128]{3,2,1,0:T(8,128)}) custom-call(s32[16,3]{1,0:T(8,128)S(1)} %copy.13.table, f32[4,256,128]{2,1,0:T(8,128)} %assemble.1.refs_0_, f32[4,256,128]{2,1,0:T(8,128)S(1)} %collective-permute-done.1.refs_1_, f32[4,256,128]{2,1,0:T(8,128)S(1)} %collective-permute-done.4.refs_2_, ...), custom_call_target="tpu_custom_call" | custom-call | bytes 6291456 | tf_op jit(solution)/shard_map/join/pallas_call | solution.py:288
  74.2 2.8 %collective-permute-start.11 = (f32[2,2,256,128]{3,2,1,0:T(8,128)S(1)}, f32[2,2,256,128]{3,2,1,0:T(8,128)S(1)}, u32[]{:S(2)}, u32[]{:S(2)}) collective-permute-start(f32[2,2,256,128]{3,2,1,0:T(8,128)S(1)} %get-tuple-element.53), channel_id=1, source_target_pairs={{0,4},{2,6},{4,0},{6,2},{1,5},{3,7},{5,1},{7,3},{8,12},{10,14},{12... | collective-permute-start | bytes 1572872 | tf_op jit(solution)/shard_map/ppermute | solution.py:314
  78.3 11.1 %own_forward.1 = (f32[4,1024,512]{2,1,0:T(8,128)}, f32[4,1,512]{2,1,0:T(1,128)}, f32[4,1,512]{2,1,0:T(1,128)}, f32[4,128,512]{2,1,0:T(8,128)}) custom-call(s32[5]{0:T(128)S(1)} %pad_add_fusion.info, f32[256,1024]{1,0:T(8,128)} %ql_ref.5, f32[256,512]{1,0:T(8,128)S(1)} %copy-done.4, f32[4,4,256,128]{3,2,1,0:T(8,128)} %bitcast.32, ...), custom_call_target="tpu_custom_call" | custom-call | flops 4294967296 | bytes 16777216 | tf_op jit(solution)/shard_map/own_forward/pallas_call | solution.py:250
  89.3 10.5 %collective-permute-done.11.s2 = f32[2,2,256,128]{3,2,1,0:T(8,128)S(1)} collective-permute-done((f32[2,2,256,128]{3,2,1,0:T(8,128)S(1)}, f32[2,2,256,128]{3,2,1,0:T(8,128)S(1)}, u32[]{:S(2)}, u32[]{:S(2)}) %collective-permute-start.11) | collective-permute-done | bytes 524320 | tf_op jit(solution)/shard_map/ppermute | solution.py:314
  102.0 36.3 %picked.1 = (f32[256,512]{1,0:T(8,128)}, f32[256,512]{1,0:T(8,128)}, f32[4,128,512]{2,1,0:T(8,128)}, f32[4,1,512]{2,1,0:T(1,128)}, f32[4,1,512]{2,1,0:T(1,128)},...) custom-call(s32[5]{0:T(128)S(1)} %pad_add_fusion.info, ...), custom_call_target="tpu_custom_call" | custom-call | flops 21474836480 | bytes 16777216 | tf_op jit(solution)/shard_map/picked/pallas_call | solution.py:260
  139.4 2.8 %collective-permute-start.20 = (f32[2,2,256,128]{3,2,1,0:T(8,128)}, f32[2,2,256,128]{3,2,1,0:T(8,128)S(1)}, u32[]{:S(2)}, u32[]{:S(2)}) collective-permute-start(f32[2,2,256,128]{3,2,1,0:T(8,128)} %get-tuple-element.73), channel_id=1, source_target_pairs={{0,4},{2,6},{4,0},{6,2},{1,5},{3,7},{5,1},{7,3},{8,12},{10,14},{12... | collective-permute-start | bytes 1572872 | tf_op jit(solution)/shard_map/ppermute | solution.py:314
  142.2 15.0 %own_backward.1 = (f32[256,512]{1,0:T(8,128)}, f32[256,512]{1,0:T(8,128)}, f32[2,256,128]{2,1,0:T(8,128)}, f32[2,256,128]{2,1,0:T(8,128)}, f32[2,256,128]{2,1,0:T(8,128)}, /*index=5*/f32[2,256,128]{2,1,0:T(8,128)}) custom-call(s32[5]{0:T(128)S(1)} %pad_add_fusion.info, f32[256,1024]{1,0:T(8,128)} %ql_ref.5, f32[256,512]{1,0:T(8,128)S(1)} %copy-done.4, ...), custom_call_target="tpu_custom_call" | custom-call | flops 6442450944 | bytes 16777216 | tf_op jit(solution)/shard_map/own_backward/pallas_call | solution.py:272
  157.2 6.2 %collective-permute-done.20.passed = f32[2,2,256,128]{3,2,1,0:T(8,128)S(1)} collective-permute-done((f32[2,2,256,128]{3,2,1,0:T(8,128)}, f32[2,2,256,128]{3,2,1,0:T(8,128)S(1)}, u32[]{:S(2)}, u32[]{:S(2)}) %collective-permute-start.20) | collective-permute-done | bytes 524320 | tf_op jit(solution)/shard_map/ppermute | solution.py:314
  164.1 3.2 %collective-permute-start.22 = (f32[2,2,256,128]{3,2,1,0:T(8,128)S(1)}, f32[2,2,256,128]{3,2,1,0:T(8,128)S(1)}, u32[]{:S(2)}, u32[]{:S(2)}) collective-permute-start(f32[2,2,256,128]{3,2,1,0:T(8,128)S(1)} %get-tuple-element.77), channel_id=1, source_target_pairs={{0,1},{1,0},{2,3},{3,2},{4,5},{5,4},{6,7},{7,6},{8,9},{9,8},{10,11... | collective-permute-start | bytes 1572872 | tf_op jit(solution)/shard_map/ppermute | solution.py:317
  170.9 2.9 %collective-permute-start.24 = (f32[2,4,256,128]{3,2,1,0:T(8,128)S(1)}, f32[2,4,256,128]{3,2,1,0:T(8,128)S(1)}, u32[]{:S(2)}, u32[]{:S(2)}) collective-permute-start(f32[2,4,256,128]{3,2,1,0:T(8,128)S(1)} %gather_heads.1.refs_0_), channel_id=1, source_target_pairs={{0,16},{1,65},{8,24},{9,73},{16,0},{17,81},{24,8},{25,89},{32,48},... | collective-permute-start | bytes 3145736 | tf_op jit(solution)/shard_map/ppermute | solution.py:311
  175.5 6.0 %collective-permute-done.16.added = f32[1,2,256,128]{3,2,1,0:T(8,128)S(1)} collective-permute-done((f32[1,2,256,128]{3,2,1,0:T(8,128)S(1)}, f32[1,2,256,128]{3,2,1,0:T(8,128)S(1)}, u32[]{:S(2)}, u32[]{:S(2)}) %collective-permute-start.16) | collective-permute-done | bytes 262176 | tf_op jit(solution)/shard_map/ppermute | solution.py:314
  184.2 7.5 %collective-permute-done.17.passed = f32[1,2,256,128]{3,2,1,0:T(8,128)S(1)} collective-permute-done((f32[1,2,256,128]{3,2,1,0:T(8,128)S(1)}, f32[1,2,256,128]{3,2,1,0:T(8,128)S(1)}, u32[]{:S(2)}, u32[]{:S(2)}) %collective-permute-start.17) | collective-permute-done | bytes 262176 | tf_op jit(solution)/shard_map/ppermute | solution.py:314
  194.1 6.3 %collective-permute-done.14 = f32[256,512]{1,0:T(8,128)S(1)} collective-permute-done((f32[256,512]{1,0:T(8,128)S(1)}, f32[256,512]{1,0:T(8,128)S(1)}, u32[]{:S(2)}, u32[]{:S(2)}) %collective-permute-start.14) | collective-permute-done | bytes 524320 | tf_op jit(solution)/shard_map/ppermute | solution.py:314
  201.3 3.2 %collect.1 = (f32[4,256,128]{2,1,0:T(8,128)S(1)}, f32[4,256,128]{2,1,0:T(8,128)}, f32[4,256,128]{2,1,0:T(8,128)}, f32[4,256,128]{2,1,0:T(8,128)}) custom-call(s32[16,3]{1,0:T(8,128)S(1)} %copy.14.table, f32[2,4,256,128]{3,2,1,0:T(8,128)S(1)} %gather_heads.1.refs_0_, f32[2,4,256,128]{3,2,1,0:T(8,128)S(1)} %collective-permute-done.23.refs_1_, ...), custom_call_target="tpu_custom_call" | custom-call | bytes 6291456 | tf_op jit(solution)/shard_map/collect/pallas_call | solution.py:288
  205.3 3.7 %collective-permute-start.26 = (f32[4,256,128]{2,1,0:T(8,128)}, f32[4,256,128]{2,1,0:T(8,128)S(1)}, u32[]{:S(2)}, u32[]{:S(2)}) collective-permute-start(f32[4,256,128]{2,1,0:T(8,128)} %get-tuple-element.80), channel_id=1, source_target_pairs={{0,96},{1,25},{8,104},{9,1},{16,112},{17,9},{24,120},{25,17},{32,0... | collective-permute-start | bytes 1572872 | tf_op jit(solution)/shard_map/ppermute | solution.py:311
  216.1 3.0 %collective-permute-done.27 = f32[4,256,128]{2,1,0:T(8,128)S(1)} collective-permute-done((f32[4,256,128]{2,1,0:T(8,128)}, f32[4,256,128]{2,1,0:T(8,128)S(1)}, u32[]{:S(2)}, u32[]{:S(2)}) %collective-permute-start.27) | collective-permute-done | bytes 524320 | tf_op jit(solution)/shard_map/ppermute | solution.py:311
  219.1 5.6 %collective-permute-done.28 = f32[4,256,128]{2,1,0:T(8,128)S(1)} collective-permute-done((f32[4,256,128]{2,1,0:T(8,128)}, f32[4,256,128]{2,1,0:T(8,128)S(1)}, u32[]{:S(2)}, u32[]{:S(2)}) %collective-permute-start.28) | collective-permute-done | bytes 524320 | tf_op jit(solution)/shard_map/ppermute | solution.py:311
  (104 shorter events, 52.2 us)
Async XLA Ops:
  7.2 64.3 %all-gather.3.cloned.1.call-start = ((), (), s32[]{:S(2)}) async-start(), calls=%async_computation | async-start | bytes 2621440 | tf_op jit(solution)/shard_map/all_gather | solution.py:411
  12.9 9.8 %collective-permute-start.1 = (f32[4,256,128]{2,1,0:T(8,128)}, f32[4,256,128]{2,1,0:T(8,128)S(1)}, u32[]{:S(2)}, u32[]{:S(2)}) collective-permute-start(f32[4,256,128]{2,1,0:T(8,128)} %assemble.1.refs_0_), channel_id=1, source_target_pairs={{0,32},{1,9},{8,40},{9,17},{16,48},{17,25},{24,56},{25,1},{32,64},... | collective-permute-start | bytes 1572872 | tf_op jit(solution)/shard_map/ppermute | solution.py:311
  14.2 15.1 %collective-permute-start.4 = (f32[4,256,128]{2,1,0:T(8,128)}, f32[4,256,128]{2,1,0:T(8,128)S(1)}, u32[]{:S(2)}, u32[]{:S(2)}) collective-permute-start(f32[4,256,128]{2,1,0:T(8,128)} %assemble.1.refs_0_), channel_id=1, source_target_pairs={{0,64},{1,17},{8,72},{9,25},{16,80},{17,1},{24,88},{25,9},{32,96},... | collective-permute-start | bytes 1572872 | tf_op jit(solution)/shard_map/ppermute | solution.py:311
  16.7 12.7 %collective-permute-start.5 = (f32[4,256,128]{2,1,0:T(8,128)}, f32[4,256,128]{2,1,0:T(8,128)S(1)}, u32[]{:S(2)}, u32[]{:S(2)}) collective-permute-start(f32[4,256,128]{2,1,0:T(8,128)} %assemble.1.refs_0_), channel_id=1, source_target_pairs={{0,96},{1,25},{8,104},{9,1},{16,112},{17,9},{24,120},{25,17},{32,0... | collective-permute-start | bytes 1572872 | tf_op jit(solution)/shard_map/ppermute | solution.py:311
  23.5 26.5 %collective-permute-start.2 = (f32[256,512]{1,0:T(8,128)}, f32[256,512]{1,0:T(8,128)S(1)}, u32[]{:S(2)}, u32[]{:S(2)}) collective-permute-start(f32[256,512]{1,0:T(8,128)} %constant_dynamic-slice_fusion.1), channel_id=1, source_target_pairs={{0,6},{2,4},{4,2},{6,0},{1,7},{3,5},{5,3},{7,1},{8,14},{10,12},{12... | collective-permute-start | bytes 1572872 | tf_op jit(solution)/shard_map/ppermute | solution.py:314
  32.5 34.6 %collective-permute-start.6 = (f32[2,4,256,128]{3,2,1,0:T(8,128)}, f32[2,4,256,128]{3,2,1,0:T(8,128)S(1)}, u32[]{:S(2)}, u32[]{:S(2)}) collective-permute-start(f32[2,4,256,128]{3,2,1,0:T(8,128)} %get-tuple-element.47), channel_id=1, source_target_pairs={{0,8},{1,33},{8,16},{9,41},{16,24},{17,49},{24,0},{25,57},{32,40},... | collective-permute-start | bytes 3145736 | tf_op jit(solution)/shard_map/ppermute | solution.py:311
  33.6 33.6 %collective-permute-start.7 = (f32[2,4,256,128]{3,2,1,0:T(8,128)}, f32[2,4,256,128]{3,2,1,0:T(8,128)}, u32[]{:S(2)}, u32[]{:S(2)}) collective-permute-start(f32[2,4,256,128]{3,2,1,0:T(8,128)} %get-tuple-element.48), channel_id=1, source_target_pairs={{0,16},{1,65},{8,24},{9,73},{16,0},{17,81},{24,8},{25,89},{32,48},... | collective-permute-start | bytes 3145736 | tf_op jit(solution)/shard_map/ppermute | solution.py:311
  36.2 31.0 %collective-permute-start.8 = (f32[2,4,256,128]{3,2,1,0:T(8,128)}, f32[2,4,256,128]{3,2,1,0:T(8,128)}, u32[]{:S(2)}, u32[]{:S(2)}) collective-permute-start(f32[2,4,256,128]{3,2,1,0:T(8,128)} %get-tuple-element.49), channel_id=1, source_target_pairs={{0,24},{1,97},{8,0},{9,105},{16,8},{17,113},{24,16},{25,121},{32,5... | collective-permute-start | bytes 3145736 | tf_op jit(solution)/shard_map/ppermute | solution.py:311
  51.0 16.1 %collective-permute-start.3 = (f32[256,512]{1,0:T(8,128)}, f32[256,512]{1,0:T(8,128)}, u32[]{:S(2)}, u32[]{:S(2)}) collective-permute-start(f32[256,512]{1,0:T(8,128)} %constant_dynamic-slice_fusion), channel_id=1, source_target_pairs={{0,6},{2,4},{4,2},{6,0},{1,7},{3,5},{5,3},{7,1},{8,14},{10,12},{12... | collective-permute-start | bytes 1572872 | tf_op jit(solution)/shard_map/ppermute | solution.py:314
  74.1 15.3 %collective-permute-start.10 = (f32[2,2,256,128]{3,2,1,0:T(8,128)S(1)}, f32[2,2,256,128]{3,2,1,0:T(8,128)S(1)}, u32[]{:S(2)}, u32[]{:S(2)}) collective-permute-start(f32[2,2,256,128]{3,2,1,0:T(8,128)S(1)} %get-tuple-element.52.s0), channel_id=1, source_target_pairs={{0,2},{2,0},{4,6},{6,4},{1,3},{3,1},{5,7},{7,5},{8,10},{10,8},{12,... | collective-permute-start | bytes 1572872 | tf_op jit(solution)/shard_map/ppermute | solution.py:314
  74.2 25.7 %collective-permute-start.11 = (f32[2,2,256,128]{3,2,1,0:T(8,128)S(1)}, f32[2,2,256,128]{3,2,1,0:T(8,128)S(1)}, u32[]{:S(2)}, u32[]{:S(2)}) collective-permute-start(f32[2,2,256,128]{3,2,1,0:T(8,128)S(1)} %get-tuple-element.53), channel_id=1, source_target_pairs={{0,4},{2,6},{4,0},{6,2},{1,5},{3,7},{5,1},{7,3},{8,12},{10,14},{12... | collective-permute-start | bytes 1572872 | tf_op jit(solution)/shard_map/ppermute | solution.py:314
  77.0 25.0 %collective-permute-start.12 = (f32[2,2,256,128]{3,2,1,0:T(8,128)S(1)}, f32[2,2,256,128]{3,2,1,0:T(8,128)}, u32[]{:S(2)}, u32[]{:S(2)}) collective-permute-start(f32[2,2,256,128]{3,2,1,0:T(8,128)S(1)} %get-tuple-element.53), channel_id=1, source_target_pairs={{0,6},{2,4},{4,2},{6,0},{1,7},{3,5},{5,3},{7,1},{8,14},{10,12},{12... | collective-permute-start | bytes 1572872 | tf_op jit(solution)/shard_map/ppermute | solution.py:314
  138.2 19.0 %collective-permute-start.21 = (f32[2,2,256,128]{3,2,1,0:T(8,128)}, f32[2,2,256,128]{3,2,1,0:T(8,128)S(1)}, u32[]{:S(2)}, u32[]{:S(2)}) collective-permute-start(f32[2,2,256,128]{3,2,1,0:T(8,128)} %get-tuple-element.74), channel_id=1, source_target_pairs={{0,6},{2,4},{4,2},{6,0},{1,7},{3,5},{5,3},{7,1},{8,14},{10,12},{12... | collective-permute-start | bytes 1572872 | tf_op jit(solution)/shard_map/ppermute | solution.py:314
  139.4 17.8 %collective-permute-start.19 = (f32[2,2,256,128]{3,2,1,0:T(8,128)}, f32[2,2,256,128]{3,2,1,0:T(8,128)S(1)}, u32[]{:S(2)}, u32[]{:S(2)}) collective-permute-start(f32[2,2,256,128]{3,2,1,0:T(8,128)} %get-tuple-element.72), channel_id=1, source_target_pairs={{0,2},{2,0},{4,6},{6,4},{1,3},{3,1},{5,7},{7,5},{8,10},{10,8},{12,... | collective-permute-start | bytes 1572872 | tf_op jit(solution)/shard_map/ppermute | solution.py:314
  139.4 24.0 %collective-permute-start.20 = (f32[2,2,256,128]{3,2,1,0:T(8,128)}, f32[2,2,256,128]{3,2,1,0:T(8,128)S(1)}, u32[]{:S(2)}, u32[]{:S(2)}) collective-permute-start(f32[2,2,256,128]{3,2,1,0:T(8,128)} %get-tuple-element.73), channel_id=1, source_target_pairs={{0,4},{2,6},{4,0},{6,2},{1,5},{3,7},{5,1},{7,3},{8,12},{10,14},{12... | collective-permute-start | bytes 1572872 | tf_op jit(solution)/shard_map/ppermute | solution.py:314
  169.4 31.9 %collective-permute-start.23 = (f32[2,4,256,128]{3,2,1,0:T(8,128)S(1)}, f32[2,4,256,128]{3,2,1,0:T(8,128)S(1)}, u32[]{:S(2)}, u32[]{:S(2)}) collective-permute-start(f32[2,4,256,128]{3,2,1,0:T(8,128)S(1)} %gather_heads.1.refs_0_), channel_id=1, source_target_pairs={{0,8},{1,33},{8,16},{9,41},{16,24},{17,49},{24,0},{25,57},{32,40},... | collective-permute-start | bytes 3145736 | tf_op jit(solution)/shard_map/ppermute | solution.py:311
  170.9 30.4 %collective-permute-start.24 = (f32[2,4,256,128]{3,2,1,0:T(8,128)S(1)}, f32[2,4,256,128]{3,2,1,0:T(8,128)S(1)}, u32[]{:S(2)}, u32[]{:S(2)}) collective-permute-start(f32[2,4,256,128]{3,2,1,0:T(8,128)S(1)} %gather_heads.1.refs_0_), channel_id=1, source_target_pairs={{0,16},{1,65},{8,24},{9,73},{16,0},{17,81},{24,8},{25,89},{32,48},... | collective-permute-start | bytes 3145736 | tf_op jit(solution)/shard_map/ppermute | solution.py:311
  173.8 27.5 %collective-permute-start.25 = (f32[2,4,256,128]{3,2,1,0:T(8,128)S(1)}, f32[2,4,256,128]{3,2,1,0:T(8,128)}, u32[]{:S(2)}, u32[]{:S(2)}) collective-permute-start(f32[2,4,256,128]{3,2,1,0:T(8,128)S(1)} %gather_heads.1.refs_0_), channel_id=1, source_target_pairs={{0,24},{1,97},{8,0},{9,105},{16,8},{17,113},{24,16},{25,121},{32,5... | collective-permute-start | bytes 3145736 | tf_op jit(solution)/shard_map/ppermute | solution.py:311
  174.1 9.2 %collective-permute-start.18 = (f32[1,2,256,128]{3,2,1,0:T(8,128)S(1)}, f32[1,2,256,128]{3,2,1,0:T(8,128)S(1)}, u32[]{:S(2)}, u32[]{:S(2)}) collective-permute-start(f32[1,2,256,128]{3,2,1,0:T(8,128)S(1)} %bitcast.35), channel_id=1, source_target_pairs={{0,6},{2,4},{4,2},{6,0},{1,7},{3,5},{5,3},{7,1},{8,14},{10,12},{12... | collective-permute-start | bytes 786440 | tf_op jit(solution)/shard_map/ppermute | solution.py:314
  181.5 18.9 %collective-permute-start.14 = (f32[256,512]{1,0:T(8,128)S(1)}, f32[256,512]{1,0:T(8,128)S(1)}, u32[]{:S(2)}, u32[]{:S(2)}) collective-permute-start(f32[256,512]{1,0:T(8,128)S(1)} %copy-done.12), channel_id=1, source_target_pairs={{0,6},{2,4},{4,2},{6,0},{1,7},{3,5},{5,3},{7,1},{8,14},{10,12},{12... | collective-permute-start | bytes 1572872 | tf_op jit(solution)/shard_map/ppermute | solution.py:314
  191.7 20.7 %collective-permute-start.15 = (f32[256,512]{1,0:T(8,128)}, f32[256,512]{1,0:T(8,128)}, u32[]{:S(2)}, u32[]{:S(2)}) collective-permute-start(f32[256,512]{1,0:T(8,128)} %get-tuple-element.64), channel_id=1, source_target_pairs={{0,6},{2,4},{4,2},{6,0},{1,7},{3,5},{5,3},{7,1},{8,14},{10,12},{12... | collective-permute-start | bytes 1572872 | tf_op jit(solution)/shard_map/ppermute | solution.py:314
  205.3 10.8 %collective-permute-start.26 = (f32[4,256,128]{2,1,0:T(8,128)}, f32[4,256,128]{2,1,0:T(8,128)S(1)}, u32[]{:S(2)}, u32[]{:S(2)}) collective-permute-start(f32[4,256,128]{2,1,0:T(8,128)} %get-tuple-element.80), channel_id=1, source_target_pairs={{0,96},{1,25},{8,104},{9,1},{16,112},{17,9},{24,120},{25,17},{32,0... | collective-permute-start | bytes 1572872 | tf_op jit(solution)/shard_map/ppermute | solution.py:311
  209.0 10.1 %collective-permute-start.27 = (f32[4,256,128]{2,1,0:T(8,128)}, f32[4,256,128]{2,1,0:T(8,128)S(1)}, u32[]{:S(2)}, u32[]{:S(2)}) collective-permute-start(f32[4,256,128]{2,1,0:T(8,128)} %get-tuple-element.81), channel_id=1, source_target_pairs={{0,64},{1,17},{8,72},{9,25},{16,80},{17,1},{24,88},{25,9},{32,96},... | collective-permute-start | bytes 1572872 | tf_op jit(solution)/shard_map/ppermute | solution.py:311
  210.8 13.9 %collective-permute-start.28 = (f32[4,256,128]{2,1,0:T(8,128)}, f32[4,256,128]{2,1,0:T(8,128)S(1)}, u32[]{:S(2)}, u32[]{:S(2)}) collective-permute-start(f32[4,256,128]{2,1,0:T(8,128)} %get-tuple-element.82), channel_id=1, source_target_pairs={{0,32},{1,9},{8,40},{9,17},{16,48},{17,25},{24,56},{25,1},{32,64},... | collective-permute-start | bytes 1572872 | tf_op jit(solution)/shard_map/ppermute | solution.py:311
  (26 other events, 259.5 us)
Sparse Core Ops, SparseCore 0:
  13.0 44.6 all-gather.2

commit v10 on v9

--- a/solution.py
+++ b/solution.py
@@ -173,7 +173,7 @@
                 out[j, 1 - info[4]] = dv_acc[rows, :]
 
 def own_backward(info, ql_ref, qr_ref, dl_ref, dr_ref, mine_ref, other_ref, p_ref, c_ref, rd_ref, dq_ref,
-                 gl_ref, gr_ref, h0, h1, h2, h3, vc, kt, dk_acc, dv_acc):
+                 of_ref, gl_ref, far_ref, h0, h1, h2, h3, vc, kt, dk_acc, dv_acc):
     u, step = pl.program_id(0), pl.program_id(1)
 
     @pl.when((u == 0) & (step == 0))
@@ -201,7 +201,8 @@
 
     @pl.when(u == 1)
     def _():
-        gr_ref[...] = dq
+        far_ref[0] = of_ref[...]
+        far_ref[1] = dq
 
     @pl.when((u == 1) & (step == STEPS - 1))
     def _():
@@ -217,9 +218,10 @@
     return pl.BlockSpec(shape, lambda u, h, i: (0,) * len(shape))
 
 NEAR = pl.BlockSpec((T, HP * W), lambda u, h, i: (0, i[1] * STEPS + h))
-FAR = pl.BlockSpec((T, HP * W), lambda u, h, i: (0, h))
+FAR, FAR2 = (pl.BlockSpec((None, T, HP * W), lambda u, h, i, n=n: (n, 0, h)) for n in range(2))
 FIRST = pl.BlockSpec((T, HP * W), lambda u, h, i: (0, jnp.where(u == 0, h, STEPS - 1)))
 SECOND = pl.BlockSpec((T, HP * W), lambda u, h, i: (0, jnp.where(u == 0, 0, h)))
+BOTH = pl.BlockSpec((2, T, HP * W), lambda u, h, i: (0, 0, jnp.where(u == 0, 0, h)))
 PROBS, ROW, TURNED = (2 * STEPS, BLK, R), (2 * STEPS, 1, R), (2 * STEPS, W, R)
 HALF, PIECE, PAIR = (T, 4 * W), (2, T, W), (2, 2, T, W)
 
@@ -246,7 +248,7 @@
 
 UNIT = 2 * 2048 * BLK * W * 4
 
-def call_own_forward(info, q, q_far, mine, other):
+def call_own_forward(info, q, qd_far, mine, other):
     return kernel(
         own_forward,
         [NEAR, FAR, whole(mine.shape), whole(other.shape)],
@@ -254,29 +256,30 @@
         [PROBS, ROW, ROW, TURNED],
         [((BLK, 2 * W), BF), ((2 * W, BLK), BF)],
         2 * UNIT, 30,
-    )(info, *in_hbm(q), q_far, *in_hbm(mine), other)
-
-def call_picked(info, q, q_far, do, do_far, pieces, m, l, ot):
+    )(info, *in_hbm(q), qd_far, *in_hbm(mine), other)
+
+def call_picked(info, q, do, qd_far, pieces, m, l, ot):
     return kernel(
         picked,
-        [NEAR, FAR, NEAR, FAR] + [whole(PAIR)] * 4 + [tile(ROW), tile(ROW), tile(TURNED)],
+        [NEAR, FAR, NEAR, FAR2] + [whole(PAIR)] * 4 + [tile(ROW), tile(ROW), tile(TURNED)],
         [FIRST, SECOND, tile(TURNED), tile(ROW), tile(ROW)] + [whole(PAIR)] * 4,
         [HALF, HALF, TURNED, ROW, ROW] + [PAIR] * 4,
         [((2 * BLK, 2 * W), BF), ((2 * BLK, 2 * W), BF), ((2 * W, 2 * BLK), BF), ((2 * W, 2 * BLK), BF),
          ((2 * BLK, R), F32),
          ((2 * BLK, W), F32), ((2 * BLK, W), F32)],
         10 * UNIT, 52,
-    )(info, *in_hbm(q), q_far, *in_hbm(do), do_far, *pieces, *in_hbm(m, l, ot))
-
-def call_own_backward(info, q, q_far, do, do_far, mine, other, p, c, rd, dq):
+    )(info, *in_hbm(q), qd_far, *in_hbm(do), qd_far, *pieces, *in_hbm(m, l, ot))
+
+def call_own_backward(info, q, do, qd_far, mine, other, p, c, rd, dq, o_far):
     return kernel(
         own_backward,
-        [NEAR, FAR, NEAR, FAR, whole(mine.shape), whole(other.shape), tile(PROBS), tile(ROW), tile(ROW), tile(TURNED)],
-        [FIRST, SECOND] + [whole(PIECE)] * 4,
-        [HALF, HALF] + [PIECE] * 4,
+        [NEAR, FAR, NEAR, FAR2, whole(mine.shape), whole(other.shape), tile(PROBS), tile(ROW), tile(ROW),
+         tile(TURNED), SECOND],
+        [FIRST, BOTH] + [whole(PIECE)] * 4,
+        [HALF, (2,) + HALF] + [PIECE] * 4,
         [((BLK, 2 * W), BF), ((2 * W, BLK), BF), ((BLK, W), F32), ((BLK, W), F32)],
         3 * UNIT, 40,
-    )(info, *in_hbm(q), q_far, *in_hbm(do), do_far, *in_hbm(mine), other, *in_hbm(p, c, rd, dq))
+    )(info, *in_hbm(q), qd_far, *in_hbm(do), qd_far, *in_hbm(mine), other, *in_hbm(p, c, rd, dq, o_far))
 
 HEADS = (4, T, W)
 SWAP = [(0, 1), (1, 0)]
@@ -413,21 +416,21 @@
 
     along = [full] + [travel(full, s, 0) for s in (1, 2, 3)]
 
-    def turned_over(array, *others):
-        return mirror(lax.dynamic_slice_in_dim(after(array, *others), far * 4 * W, 4 * W, 1), 3)
-
-    q_far = turned_over(queries, along[1])
-    do_far = turned_over(cotangent, q_far)
+    queries_late, cotangent_late = lax.optimization_barrier((queries, cotangent, along[1]))[:2]
+    qd_far = mirror(
+        jnp.stack([lax.dynamic_slice_in_dim(a, far * 4 * W, 4 * W, 1)
+                   for a in (queries_late, cotangent_late)]), 3)
     sent = glue(pick, (selected, *along), ((2,) + HEADS,) * 3)
     got = [travel(sent[s - 1], s, 1) for s in (1, 2, 3)]
-    kept, send = glue(join, (after(selected, q_far, do_far), *along, *got), (PAIR, PAIR))
+    kept, send = glue(join, (after(selected, qd_far), *along, *got), (PAIR, PAIR))
     same, cross = glue(arrange, (spot, kept, swap(send)), (PAIR, PAIR))
     pieces = [same] + [mirror(a, flip) for a, flip in ((same, 1), (cross, 2), (cross, 3))]
 
-    p, m, l, ot = call_own_forward(info, queries, q_far, own, own_other)
-    out = call_picked(info, queries, q_far, cotangent, do_far, pieces, m, l, ot)
+    p, m, l, ot = call_own_forward(info, queries, qd_far, own, own_other)
+    out = call_picked(info, queries, cotangent, qd_far, pieces, m, l, ot)
     o_near, o_far, dq, c, rd = out[:5]
-    last = call_own_backward(info, queries, q_far, cotangent, do_far, own, own_other, p, c, rd, dq)
+    last = call_own_backward(
+        info, queries, cotangent, qd_far, own, own_other, p, c, rd, dq, o_far)
 
     def reduced(g, *others):
         arrived = [g[0]] + [mirror(g[flip], flip) for flip in (1, 2, 3)]
@@ -437,10 +440,10 @@
 
     (terms,) = glue(gather_heads, (spot, *reduced(out[5:9], last[0])), ((2,) + HEADS,))
     arrived = [terms] + [travel(terms, s, 1) for s in (1, 2, 3)]
-    o_far, dq_far = mirror(o_far, 3), mirror(last[1], 3)
+    back_far = mirror(last[1], 3)
     low, high = reduced([a[None] for a in last[2:6]])
-    sums = glue(collect, (after(selected, o_far, low), *arrived), (HEADS,) * 4)
-    total = after(sums[0], dq_far) + sum(travel(sums[s], 4 - s, 0) for s in (1, 2, 3))
+    sums = glue(collect, (after(selected, low), *arrived), (HEADS,) * 4)
+    total = after(sums[0], back_far) + sum(travel(sums[s], 4 - s, 0) for s in (1, 2, 3))
     total = total + jnp.where(
         core == 0, jnp.concatenate([low[0], high[0]], 0), jnp.concatenate([high[0], low[0]], 0)
     )
@@ -457,8 +460,8 @@
         return jnp.where(head == 0, jnp.concatenate([a, b], 1), jnp.concatenate([b, a], 1))
 
     return (
-        sides(o_near, o_far),
-        sides(last[0], dq_far),
+        sides(o_near, back_far[0]),
+        sides(last[0], back_far[1]),
         jnp.where(core == 0, keep, back),
         jnp.where(core == 0, back, keep),
     )

time: 239 us -> 249 us (1.042)
  waiting for transfers between devices: 85.8 us -> 106 us
  starting transfers between devices: 49.5 us -> 38.5 us
    ppermute x13 -> x11, waiting for transfers between devices: 64.1 us -> 85.9 us  [mirror(): return lax.ppermute(array, 'z', [(i, i ^ flip) for i in range(4)])]
    ppermute x13 -> x11, starting transfers between devices: 20.3 us -> 13.4 us  [mirror(): return lax.ppermute(array, 'z', [(i, i ^ flip) for i in range(4)])]
    ppermute x6, starting transfers between devices: 8.96 us -> 4.28 us  [swap(): return lax.ppermute(array, 'head', SWAP)]
  transfers between devices with their start and end apart: 32 -> 30, of which waited for: 16 -> 14; matrix products, arithmetic and copies ran while one was open for 3% -> 3% of each run, Pallas kernels for 16% -> 15%
where the time goes in v10:
time: 249 us
  waiting for transfers between devices  106 us (43%)
  Pallas kernels  76.1 us (31%)
  starting transfers between devices  38.5 us (15%)
  between operations  14.2 us (6%)
  local copies, waits for them, and re-layouts  7.73 us (3%)
  other arithmetic  5.78 us (2%)
    ppermute x11, waiting for transfers between devices, mirror(): return lax.ppermute(array, 'z', [(i, i ^ flip) for i in range(4)])  85.9 us
    pallas_call x1, Pallas kernels, call_picked(): kernel(picked, [NEAR, FAR, NEAR, FAR2] + [whole(PAIR)] * 4 + [tile(ROW),...  36.1 us
    ppermute x12, starting transfers between devices, travel(): return lax.ppermute(array, PLACE, pairs)  20.8 us
    ppermute x12, waiting for transfers between devices, travel(): return lax.ppermute(array, PLACE, pairs)  17.3 us
    pallas_call x1, Pallas kernels, call_own_backward(): kernel(own_backward, [NEAR, FAR, NEAR, FAR2, whole(mine.shape), whole(oth...  15.5 us
    ppermute x11, starting transfers between devices, mirror(): return lax.ppermute(array, 'z', [(i, i ^ flip) for i in range(4)])  13.4 us
    pallas_call x8, Pallas kernels, glue(): pl.pallas_call(body, out_shape=[jax.ShapeDtypeStruct(s, F32) for s in out...  13.4 us
    pallas_call x1, Pallas kernels, call_own_forward(): kernel(own_forward, [NEAR, FAR, whole(mine.shape), whole(other.shape)], [...  11.1 us
  transfers between devices with their start and end apart: 30, of which 14 were waited for; matrix products, arithmetic and copies ran while one was open for 3% of the time, Pallas kernels for 15%

profile of v10, /device:TPU:1, one launch (start us, length us, event | category | flops | bytes accessed | tf_op | source)
XLA Modules:
  0.0 248.6 jit_solution(3148443590333966017)
XLA Ops:
  11.0 1.9 assemble.1.refs_0_
  14.3 2.5 collective-permute-start.3
  18.0 4.8 %collective-permute-done.1.refs_1_ = f32[4,256,128]{2,1,0:T(8,128)S(1)} collective-permute-done((f32[4,256,128]{2,1,0:T(8,128)}, f32[4,256,128]{2,1,0:T(8,128)S(1)}, u32[]{:S(2)}, u32[]{:S(2)}) %collective-permute-start.1) | collective-permute-done | bytes 524320 | tf_op jit(solution)/shard_map/ppermute | solution.py:314
  25.0 3.9 %collective-permute-start.2 = (f32[2,256,512]{2,1,0:T(8,128)}, f32[2,256,512]{2,1,0:T(8,128)}, u32[]{:S(2)}, u32[]{:S(2)}) collective-permute-start(f32[2,256,512]{2,1,0:T(8,128)} %pad_maximum_fusion), channel_id=1, source_target_pairs={{0,6},{2,4},{4,2},{6,0},{1,7},{3,5},{5,3},{7,1},{8,14},{10,12},{12... | collective-permute-start | bytes 3145736 | tf_op jit(solution)/shard_map/ppermute | solution.py:317
  29.4 3.1 %pick.1 = (f32[2,4,256,128]{3,2,1,0:T(8,128)}, f32[2,4,256,128]{3,2,1,0:T(8,128)}, f32[2,4,256,128]{3,2,1,0:T(8,128)}) custom-call(s32[16,3]{1,0:T(8,128)S(1)} %copy.12.table, f32[4,256,128]{2,1,0:T(8,128)} %assemble.1.refs_0_, f32[4,256,128]{2,1,0:T(8,128)S(1)} %collective-permute-done.1.refs_1_, f32[4,256,128]{2,1,0:T(8,128)S(1)} %collective-permute-done.3.refs_2_, ...), custom_call_target="tpu_custom_call" | custom-call | bytes 5242880 | tf_op jit(solution)/shard_map/pick/pallas_call | solution.py:291
  33.6 2.6 %collective-permute-start.6 = (f32[2,4,256,128]{3,2,1,0:T(8,128)}, f32[2,4,256,128]{3,2,1,0:T(8,128)}, u32[]{:S(2)}, u32[]{:S(2)}) collective-permute-start(f32[2,4,256,128]{3,2,1,0:T(8,128)} %get-tuple-element.48), channel_id=1, source_target_pairs={{0,16},{1,65},{8,24},{9,73},{16,0},{17,81},{24,8},{25,89},{32,48},... | collective-permute-start | bytes 3145736 | tf_op jit(solution)/shard_map/ppermute | solution.py:314
  37.3 30.9 %collective-permute-done.2.qr_ref.dr_ref = f32[2,256,512]{2,1,0:T(8,128)} collective-permute-done((f32[2,256,512]{2,1,0:T(8,128)}, f32[2,256,512]{2,1,0:T(8,128)}, u32[]{:S(2)}, u32[]{:S(2)}) %collective-permute-start.2) | collective-permute-done | bytes 1048608 | tf_op jit(solution)/shard_map/ppermute | solution.py:317
  68.3 2.7 %join.1 = (f32[2,2,256,128]{3,2,1,0:T(8,128)S(1)}, f32[2,2,256,128]{3,2,1,0:T(8,128)}) custom-call(s32[16,3]{1,0:T(8,128)S(1)} %copy.13.table, f32[4,256,128]{2,1,0:T(8,128)} %assemble.1.refs_0_, f32[4,256,128]{2,1,0:T(8,128)S(1)} %collective-permute-done.1.refs_1_, f32[4,256,128]{2,1,0:T(8,128)S(1)} %collective-permute-done.3.refs_2_, ...), custom_call_target="tpu_custom_call" | custom-call | bytes 6291456 | tf_op jit(solution)/shard_map/join/pallas_call | solution.py:291
  74.9 2.2 collective-permute-start.11
  77.5 11.1 %own_forward.1 = (f32[4,1024,512]{2,1,0:T(8,128)}, f32[4,1,512]{2,1,0:T(1,128)}, f32[4,1,512]{2,1,0:T(1,128)}, f32[4,128,512]{2,1,0:T(8,128)}) custom-call(s32[5]{0:T(128)S(1)} %pad_add_fusion.info, f32[256,1024]{1,0:T(8,128)} %ql_ref.5, f32[2,256,512]{2,1,0:T(8,128)} %collective-permute-done.2.qr_ref.dr_ref, f32[4,4,256,128]{3,2,1,0:T(8,128)} %bitcast.40, ...), custom_call_target="tpu_custom_call" | custom-call | flops 4294967296 | bytes 16777216 | tf_op jit(solution)/shard_map/own_forward/pallas_call | solution.py:252
  89.1 12.1 %collective-permute-done.11.s3 = f32[2,2,256,128]{3,2,1,0:T(8,128)S(1)} collective-permute-done((f32[2,2,256,128]{3,2,1,0:T(8,128)S(1)}, f32[2,2,256,128]{3,2,1,0:T(8,128)S(1)}, u32[]{:S(2)}, u32[]{:S(2)}) %collective-permute-start.11) | collective-permute-done | bytes 524320 | tf_op jit(solution)/shard_map/ppermute | solution.py:317
  102.0 36.1 %picked.1 = (f32[256,512]{1,0:T(8,128)}, f32[256,512]{1,0:T(8,128)}, f32[4,128,512]{2,1,0:T(8,128)}, f32[4,1,512]{2,1,0:T(1,128)}, f32[4,1,512]{2,1,0:T(1,128)},...) custom-call(s32[5]{0:T(128)S(1)} %pad_add_fusion.info, ...), custom_call_target="tpu_custom_call" | custom-call | flops 21474836480 | bytes 16777216 | tf_op jit(solution)/shard_map/picked/pallas_call | solution.py:262
  138.3 3.8 %collective-permute-start.18 = (f32[2,2,256,128]{3,2,1,0:T(8,128)}, f32[2,2,256,128]{3,2,1,0:T(8,128)S(1)}, u32[]{:S(2)}, u32[]{:S(2)}) collective-permute-start(f32[2,2,256,128]{3,2,1,0:T(8,128)} %get-tuple-element.73), channel_id=1, source_target_pairs={{0,4},{2,6},{4,0},{6,2},{1,5},{3,7},{5,1},{7,3},{8,12},{10,14},{12... | collective-permute-start | bytes 1572872 | tf_op jit(solution)/shard_map/ppermute | solution.py:317
  142.1 15.5 %own_backward.1 = (f32[256,512]{1,0:T(8,128)}, f32[2,256,512]{2,1,0:T(8,128)}, f32[2,256,128]{2,1,0:T(8,128)}, f32[2,256,128]{2,1,0:T(8,128)}, f32[2,256,128]{2,1,0:T(8,128)}, /*index=5*/f32[2,256,128]{2,1,0:T(8,128)}) custom-call(s32[5]{0:T(128)S(1)} %pad_add_fusion.info, f32[256,1024]{1,0:T(8,128)} %ql_ref.5, ...), custom_call_target="tpu_custom_call" | custom-call | flops 6442450944 | bytes 16777216 | tf_op jit(solution)/shard_map/own_backward/pallas_call | solution.py:274
  157.6 7.1 %collective-permute-done.18.passed = f32[2,2,256,128]{3,2,1,0:T(8,128)S(1)} collective-permute-done((f32[2,2,256,128]{3,2,1,0:T(8,128)}, f32[2,2,256,128]{3,2,1,0:T(8,128)S(1)}, u32[]{:S(2)}, u32[]{:S(2)}) %collective-permute-start.18) | collective-permute-done | bytes 524320 | tf_op jit(solution)/shard_map/ppermute | solution.py:317
  170.6 2.5 %collective-permute-start.22 = (f32[2,4,256,128]{3,2,1,0:T(8,128)S(1)}, f32[2,4,256,128]{3,2,1,0:T(8,128)S(1)}, u32[]{:S(2)}, u32[]{:S(2)}) collective-permute-start(f32[2,4,256,128]{3,2,1,0:T(8,128)S(1)} %gather_heads.1.refs_0_), channel_id=1, source_target_pairs={{0,16},{1,65},{8,24},{9,73},{16,0},{17,81},{24,8},{25,89},{32,48},... | collective-permute-start | bytes 3145736 | tf_op jit(solution)/shard_map/ppermute | solution.py:314
  174.5 6.4 %collective-permute-done.14.added = f32[1,2,256,128]{3,2,1,0:T(8,128)S(1)} collective-permute-done((f32[1,2,256,128]{3,2,1,0:T(8,128)S(1)}, f32[1,2,256,128]{3,2,1,0:T(8,128)S(1)}, u32[]{:S(2)}, u32[]{:S(2)}) %collective-permute-start.14) | collective-permute-done | bytes 262176 | tf_op jit(solution)/shard_map/ppermute | solution.py:317
  180.9 2.6 %collective-permute-start.16 = (f32[1,2,256,128]{3,2,1,0:T(8,128)S(1)}, f32[1,2,256,128]{3,2,1,0:T(8,128)S(1)}, u32[]{:S(2)}, u32[]{:S(2)}) collective-permute-start(f32[1,2,256,128]{3,2,1,0:T(8,128)S(1)} %bitcast.43), channel_id=1, source_target_pairs={{0,6},{2,4},{4,2},{6,0},{1,7},{3,5},{5,3},{7,1},{8,14},{10,12},{12... | collective-permute-start | bytes 786440 | tf_op jit(solution)/shard_map/ppermute | solution.py:317
  183.5 21.4 %collective-permute-done.16.passed2 = f32[1,2,256,128]{3,2,1,0:T(8,128)S(1)} collective-permute-done((f32[1,2,256,128]{3,2,1,0:T(8,128)S(1)}, f32[1,2,256,128]{3,2,1,0:T(8,128)S(1)}, u32[]{:S(2)}, u32[]{:S(2)}) %collective-permute-start.16) | collective-permute-done | bytes 262176 | tf_op jit(solution)/shard_map/ppermute | solution.py:317
  204.9 7.4 %collective-permute-done.15.passed = f32[1,2,256,128]{3,2,1,0:T(8,128)S(1)} collective-permute-done((f32[1,2,256,128]{3,2,1,0:T(8,128)S(1)}, f32[1,2,256,128]{3,2,1,0:T(8,128)S(1)}, u32[]{:S(2)}, u32[]{:S(2)}) %collective-permute-start.15) | collective-permute-done | bytes 262176 | tf_op jit(solution)/shard_map/ppermute | solution.py:317
  213.7 3.1 %collect.1 = (f32[4,256,128]{2,1,0:T(8,128)S(1)}, f32[4,256,128]{2,1,0:T(8,128)}, f32[4,256,128]{2,1,0:T(8,128)}, f32[4,256,128]{2,1,0:T(8,128)}) custom-call(s32[16,3]{1,0:T(8,128)S(1)} %copy.14.table, f32[2,4,256,128]{3,2,1,0:T(8,128)S(1)} %gather_heads.1.refs_0_, f32[2,4,256,128]{3,2,1,0:T(8,128)S(1)} %collective-permute-done.21.refs_1_, ...), custom_call_target="tpu_custom_call" | custom-call | bytes 6291456 | tf_op jit(solution)/shard_map/collect/pallas_call | solution.py:291
  217.7 4.6 %collective-permute-start.24 = (f32[4,256,128]{2,1,0:T(8,128)}, f32[4,256,128]{2,1,0:T(8,128)S(1)}, u32[]{:S(2)}, u32[]{:S(2)}) collective-permute-start(f32[4,256,128]{2,1,0:T(8,128)} %get-tuple-element.80), channel_id=1, source_target_pairs={{0,96},{1,25},{8,104},{9,1},{16,112},{17,9},{24,120},{25,17},{32,0... | collective-permute-start | bytes 1572872 | tf_op jit(solution)/shard_map/ppermute | solution.py:314
  225.7 8.6 %collective-permute-done.24 = f32[4,256,128]{2,1,0:T(8,128)S(1)} collective-permute-done((f32[4,256,128]{2,1,0:T(8,128)}, f32[4,256,128]{2,1,0:T(8,128)S(1)}, u32[]{:S(2)}, u32[]{:S(2)}) %collective-permute-start.24) | collective-permute-done | bytes 524320 | tf_op jit(solution)/shard_map/ppermute | solution.py:314
  234.3 3.3 %collective-permute-done.26 = f32[4,256,128]{2,1,0:T(8,128)S(1)} collective-permute-done((f32[4,256,128]{2,1,0:T(8,128)}, f32[4,256,128]{2,1,0:T(8,128)S(1)}, u32[]{:S(2)}, u32[]{:S(2)}) %collective-permute-start.26) | collective-permute-done | bytes 524320 | tf_op jit(solution)/shard_map/ppermute | solution.py:314
  (91 shorter events, 34.2 us)
Async XLA Ops:
  7.2 64.8 %all-gather.3.cloned.1.call-start = ((), (), s32[]{:S(2)}) async-start(), calls=%async_computation | async-start | bytes 2621440 | tf_op jit(solution)/shard_map/all_gather | solution.py:414
  12.9 9.8 %collective-permute-start.1 = (f32[4,256,128]{2,1,0:T(8,128)}, f32[4,256,128]{2,1,0:T(8,128)S(1)}, u32[]{:S(2)}, u32[]{:S(2)}) collective-permute-start(f32[4,256,128]{2,1,0:T(8,128)} %assemble.1.refs_0_), channel_id=1, source_target_pairs={{0,32},{1,9},{8,40},{9,17},{16,48},{17,25},{24,56},{25,1},{32,64},... | collective-permute-start | bytes 1572872 | tf_op jit(solution)/shard_map/ppermute | solution.py:314
  14.3 15.1 %collective-permute-start.3 = (f32[4,256,128]{2,1,0:T(8,128)}, f32[4,256,128]{2,1,0:T(8,128)S(1)}, u32[]{:S(2)}, u32[]{:S(2)}) collective-permute-start(f32[4,256,128]{2,1,0:T(8,128)} %assemble.1.refs_0_), channel_id=1, source_target_pairs={{0,64},{1,17},{8,72},{9,25},{16,80},{17,1},{24,88},{25,9},{32,96},... | collective-permute-start | bytes 1572872 | tf_op jit(solution)/shard_map/ppermute | solution.py:314
  16.7 12.7 %collective-permute-start.4 = (f32[4,256,128]{2,1,0:T(8,128)}, f32[4,256,128]{2,1,0:T(8,128)S(1)}, u32[]{:S(2)}, u32[]{:S(2)}) collective-permute-start(f32[4,256,128]{2,1,0:T(8,128)} %assemble.1.refs_0_), channel_id=1, source_target_pairs={{0,96},{1,25},{8,104},{9,1},{16,112},{17,9},{24,120},{25,17},{32,0... | collective-permute-start | bytes 1572872 | tf_op jit(solution)/shard_map/ppermute | solution.py:314
  25.0 43.2 %collective-permute-start.2 = (f32[2,256,512]{2,1,0:T(8,128)}, f32[2,256,512]{2,1,0:T(8,128)}, u32[]{:S(2)}, u32[]{:S(2)}) collective-permute-start(f32[2,256,512]{2,1,0:T(8,128)} %pad_maximum_fusion), channel_id=1, source_target_pairs={{0,6},{2,4},{4,2},{6,0},{1,7},{3,5},{5,3},{7,1},{8,14},{10,12},{12... | collective-permute-start | bytes 3145736 | tf_op jit(solution)/shard_map/ppermute | solution.py:317
  32.5 35.7 %collective-permute-start.5 = (f32[2,4,256,128]{3,2,1,0:T(8,128)}, f32[2,4,256,128]{3,2,1,0:T(8,128)S(1)}, u32[]{:S(2)}, u32[]{:S(2)}) collective-permute-start(f32[2,4,256,128]{3,2,1,0:T(8,128)} %get-tuple-element.47), channel_id=1, source_target_pairs={{0,8},{1,33},{8,16},{9,41},{16,24},{17,49},{24,0},{25,57},{32,40},... | collective-permute-start | bytes 3145736 | tf_op jit(solution)/shard_map/ppermute | solution.py:314
  33.6 34.7 %collective-permute-start.6 = (f32[2,4,256,128]{3,2,1,0:T(8,128)}, f32[2,4,256,128]{3,2,1,0:T(8,128)}, u32[]{:S(2)}, u32[]{:S(2)}) collective-permute-start(f32[2,4,256,128]{3,2,1,0:T(8,128)} %get-tuple-element.48), channel_id=1, source_target_pairs={{0,16},{1,65},{8,24},{9,73},{16,0},{17,81},{24,8},{25,89},{32,48},... | collective-permute-start | bytes 3145736 | tf_op jit(solution)/shard_map/ppermute | solution.py:314
  36.2 32.1 %collective-permute-start.7 = (f32[2,4,256,128]{3,2,1,0:T(8,128)}, f32[2,4,256,128]{3,2,1,0:T(8,128)}, u32[]{:S(2)}, u32[]{:S(2)}) collective-permute-start(f32[2,4,256,128]{3,2,1,0:T(8,128)} %get-tuple-element.49), channel_id=1, source_target_pairs={{0,24},{1,97},{8,0},{9,105},{16,8},{17,113},{24,16},{25,121},{32,5... | collective-permute-start | bytes 3145736 | tf_op jit(solution)/shard_map/ppermute | solution.py:314
  74.5 14.6 %collective-permute-start.10 = (f32[2,2,256,128]{3,2,1,0:T(8,128)S(1)}, f32[2,2,256,128]{3,2,1,0:T(8,128)S(1)}, u32[]{:S(2)}, u32[]{:S(2)}) collective-permute-start(f32[2,2,256,128]{3,2,1,0:T(8,128)S(1)} %get-tuple-element.53), channel_id=1, source_target_pairs={{0,4},{2,6},{4,0},{6,2},{1,5},{3,7},{5,1},{7,3},{8,12},{10,14},{12... | collective-permute-start | bytes 1572872 | tf_op jit(solution)/shard_map/ppermute | solution.py:317
  74.9 26.2 %collective-permute-start.11 = (f32[2,2,256,128]{3,2,1,0:T(8,128)S(1)}, f32[2,2,256,128]{3,2,1,0:T(8,128)S(1)}, u32[]{:S(2)}, u32[]{:S(2)}) collective-permute-start(f32[2,2,256,128]{3,2,1,0:T(8,128)S(1)} %get-tuple-element.53), channel_id=1, source_target_pairs={{0,6},{2,4},{4,2},{6,0},{1,7},{3,5},{5,3},{7,1},{8,14},{10,12},{12... | collective-permute-start | bytes 1572872 | tf_op jit(solution)/shard_map/ppermute | solution.py:317
  77.1 24.0 %collective-permute-start.9 = (f32[2,2,256,128]{3,2,1,0:T(8,128)S(1)}, f32[2,2,256,128]{3,2,1,0:T(8,128)S(1)}, u32[]{:S(2)}, u32[]{:S(2)}) collective-permute-start(f32[2,2,256,128]{3,2,1,0:T(8,128)S(1)} %get-tuple-element.52.s0), channel_id=1, source_target_pairs={{0,2},{2,0},{4,6},{6,4},{1,3},{3,1},{5,7},{7,5},{8,10},{10,8},{12,... | collective-permute-start | bytes 1572872 | tf_op jit(solution)/shard_map/ppermute | solution.py:317
  138.1 19.5 %collective-permute-start.19 = (f32[2,2,256,128]{3,2,1,0:T(8,128)}, f32[2,2,256,128]{3,2,1,0:T(8,128)S(1)}, u32[]{:S(2)}, u32[]{:S(2)}) collective-permute-start(f32[2,2,256,128]{3,2,1,0:T(8,128)} %get-tuple-element.74), channel_id=1, source_target_pairs={{0,6},{2,4},{4,2},{6,0},{1,7},{3,5},{5,3},{7,1},{8,14},{10,12},{12... | collective-permute-start | bytes 1572872 | tf_op jit(solution)/shard_map/ppermute | solution.py:317
  138.3 19.3 %collective-permute-start.17 = (f32[2,2,256,128]{3,2,1,0:T(8,128)}, f32[2,2,256,128]{3,2,1,0:T(8,128)S(1)}, u32[]{:S(2)}, u32[]{:S(2)}) collective-permute-start(f32[2,2,256,128]{3,2,1,0:T(8,128)} %get-tuple-element.72), channel_id=1, source_target_pairs={{0,2},{2,0},{4,6},{6,4},{1,3},{3,1},{5,7},{7,5},{8,10},{10,8},{12,... | collective-permute-start | bytes 1572872 | tf_op jit(solution)/shard_map/ppermute | solution.py:317
  138.3 26.4 %collective-permute-start.18 = (f32[2,2,256,128]{3,2,1,0:T(8,128)}, f32[2,2,256,128]{3,2,1,0:T(8,128)S(1)}, u32[]{:S(2)}, u32[]{:S(2)}) collective-permute-start(f32[2,2,256,128]{3,2,1,0:T(8,128)} %get-tuple-element.73), channel_id=1, source_target_pairs={{0,4},{2,6},{4,0},{6,2},{1,5},{3,7},{5,1},{7,3},{8,12},{10,14},{12... | collective-permute-start | bytes 1572872 | tf_op jit(solution)/shard_map/ppermute | solution.py:317
  169.3 44.4 %collective-permute-start.21 = (f32[2,4,256,128]{3,2,1,0:T(8,128)S(1)}, f32[2,4,256,128]{3,2,1,0:T(8,128)S(1)}, u32[]{:S(2)}, u32[]{:S(2)}) collective-permute-start(f32[2,4,256,128]{3,2,1,0:T(8,128)S(1)} %gather_heads.1.refs_0_), channel_id=1, source_target_pairs={{0,8},{1,33},{8,16},{9,41},{16,24},{17,49},{24,0},{25,57},{32,40},... | collective-permute-start | bytes 3145736 | tf_op jit(solution)/shard_map/ppermute | solution.py:314
  170.6 43.1 %collective-permute-start.22 = (f32[2,4,256,128]{3,2,1,0:T(8,128)S(1)}, f32[2,4,256,128]{3,2,1,0:T(8,128)S(1)}, u32[]{:S(2)}, u32[]{:S(2)}) collective-permute-start(f32[2,4,256,128]{3,2,1,0:T(8,128)S(1)} %gather_heads.1.refs_0_), channel_id=1, source_target_pairs={{0,16},{1,65},{8,24},{9,73},{16,0},{17,81},{24,8},{25,89},{32,48},... | collective-permute-start | bytes 3145736 | tf_op jit(solution)/shard_map/ppermute | solution.py:314
  173.1 40.6 %collective-permute-start.23 = (f32[2,4,256,128]{3,2,1,0:T(8,128)S(1)}, f32[2,4,256,128]{3,2,1,0:T(8,128)}, u32[]{:S(2)}, u32[]{:S(2)}) collective-permute-start(f32[2,4,256,128]{3,2,1,0:T(8,128)S(1)} %gather_heads.1.refs_0_), channel_id=1, source_target_pairs={{0,24},{1,97},{8,0},{9,105},{16,8},{17,113},{24,16},{25,121},{32,5... | collective-permute-start | bytes 3145736 | tf_op jit(solution)/shard_map/ppermute | solution.py:314
  174.2 49.7 %collective-permute-start.13 = (f32[2,256,512]{2,1,0:T(8,128)}, f32[2,256,512]{2,1,0:T(8,128)}, u32[]{:S(2)}, u32[]{:S(2)}) collective-permute-start(f32[2,256,512]{2,1,0:T(8,128)} %get-tuple-element.63), channel_id=1, source_target_pairs={{0,6},{2,4},{4,2},{6,0},{1,7},{3,5},{5,3},{7,1},{8,14},{10,12},{12... | collective-permute-start | bytes 3145736 | tf_op jit(solution)/shard_map/ppermute | solution.py:317
  174.5 6.4 %collective-permute-start.14 = (f32[1,2,256,128]{3,2,1,0:T(8,128)S(1)}, f32[1,2,256,128]{3,2,1,0:T(8,128)S(1)}, u32[]{:S(2)}, u32[]{:S(2)}) collective-permute-start(f32[1,2,256,128]{3,2,1,0:T(8,128)S(1)} %bitcast.44), channel_id=1, source_target_pairs={{0,2},{2,0},{4,6},{6,4},{1,3},{3,1},{5,7},{7,5},{8,10},{10,8},{12,... | collective-permute-start | bytes 786440 | tf_op jit(solution)/shard_map/ppermute | solution.py:317
  180.9 24.0 %collective-permute-start.16 = (f32[1,2,256,128]{3,2,1,0:T(8,128)S(1)}, f32[1,2,256,128]{3,2,1,0:T(8,128)S(1)}, u32[]{:S(2)}, u32[]{:S(2)}) collective-permute-start(f32[1,2,256,128]{3,2,1,0:T(8,128)S(1)} %bitcast.43), channel_id=1, source_target_pairs={{0,6},{2,4},{4,2},{6,0},{1,7},{3,5},{5,3},{7,1},{8,14},{10,12},{12... | collective-permute-start | bytes 786440 | tf_op jit(solution)/shard_map/ppermute | solution.py:317
  204.9 7.4 %collective-permute-start.15 = (f32[1,2,256,128]{3,2,1,0:T(8,128)S(1)}, f32[1,2,256,128]{3,2,1,0:T(8,128)S(1)}, u32[]{:S(2)}, u32[]{:S(2)}) collective-permute-start(f32[1,2,256,128]{3,2,1,0:T(8,128)S(1)} %bitcast.42), channel_id=1, source_target_pairs={{0,4},{2,6},{4,0},{6,2},{1,5},{3,7},{5,1},{7,3},{8,12},{10,14},{12... | collective-permute-start | bytes 786440 | tf_op jit(solution)/shard_map/ppermute | solution.py:317
  217.7 16.6 %collective-permute-start.24 = (f32[4,256,128]{2,1,0:T(8,128)}, f32[4,256,128]{2,1,0:T(8,128)S(1)}, u32[]{:S(2)}, u32[]{:S(2)}) collective-permute-start(f32[4,256,128]{2,1,0:T(8,128)} %get-tuple-element.80), channel_id=1, source_target_pairs={{0,96},{1,25},{8,104},{9,1},{16,112},{17,9},{24,120},{25,17},{32,0... | collective-permute-start | bytes 1572872 | tf_op jit(solution)/shard_map/ppermute | solution.py:314
  222.2 12.1 %collective-permute-start.25 = (f32[4,256,128]{2,1,0:T(8,128)}, f32[4,256,128]{2,1,0:T(8,128)S(1)}, u32[]{:S(2)}, u32[]{:S(2)}) collective-permute-start(f32[4,256,128]{2,1,0:T(8,128)} %get-tuple-element.81), channel_id=1, source_target_pairs={{0,64},{1,17},{8,72},{9,25},{16,80},{17,1},{24,88},{25,9},{32,96},... | collective-permute-start | bytes 1572872 | tf_op jit(solution)/shard_map/ppermute | solution.py:314
  223.1 14.5 %collective-permute-start.26 = (f32[4,256,128]{2,1,0:T(8,128)}, f32[4,256,128]{2,1,0:T(8,128)S(1)}, u32[]{:S(2)}, u32[]{:S(2)}) collective-permute-start(f32[4,256,128]{2,1,0:T(8,128)} %get-tuple-element.82), channel_id=1, source_target_pairs={{0,32},{1,9},{8,40},{9,17},{16,48},{17,25},{24,56},{25,1},{32,64},... | collective-permute-start | bytes 1572872 | tf_op jit(solution)/shard_map/ppermute | solution.py:314
  (19 other events, 205.2 us)
Sparse Core Ops, SparseCore 0:
  13.0 48.6 all-gather.2

commit v11 on v9

--- a/solution.py
+++ b/solution.py
@@ -173,7 +173,7 @@
                 out[j, 1 - info[4]] = dv_acc[rows, :]
 
 def own_backward(info, ql_ref, qr_ref, dl_ref, dr_ref, mine_ref, other_ref, p_ref, c_ref, rd_ref, dq_ref,
-                 gl_ref, gr_ref, h0, h1, h2, h3, vc, kt, dk_acc, dv_acc):
+                 of_ref, gl_ref, far_ref, h0, h1, h2, h3, vc, kt, dk_acc, dv_acc):
     u, step = pl.program_id(0), pl.program_id(1)
 
     @pl.when((u == 0) & (step == 0))
@@ -201,7 +201,8 @@
 
     @pl.when(u == 1)
     def _():
-        gr_ref[...] = dq
+        far_ref[0] = of_ref[...]
+        far_ref[1] = dq
 
     @pl.when((u == 1) & (step == STEPS - 1))
     def _():
@@ -220,6 +221,7 @@
 FAR = pl.BlockSpec((T, HP * W), lambda u, h, i: (0, h))
 FIRST = pl.BlockSpec((T, HP * W), lambda u, h, i: (0, jnp.where(u == 0, h, STEPS - 1)))
 SECOND = pl.BlockSpec((T, HP * W), lambda u, h, i: (0, jnp.where(u == 0, 0, h)))
+BOTH = pl.BlockSpec((2, T, HP * W), lambda u, h, i: (0, 0, jnp.where(u == 0, 0, h)))
 PROBS, ROW, TURNED = (2 * STEPS, BLK, R), (2 * STEPS, 1, R), (2 * STEPS, W, R)
 HALF, PIECE, PAIR = (T, 4 * W), (2, T, W), (2, 2, T, W)
 
@@ -268,15 +270,16 @@
         10 * UNIT, 52,
     )(info, *in_hbm(q), q_far, *in_hbm(do), do_far, *pieces, *in_hbm(m, l, ot))
 
-def call_own_backward(info, q, q_far, do, do_far, mine, other, p, c, rd, dq):
+def call_own_backward(info, q, q_far, do, do_far, mine, other, p, c, rd, dq, o_far):
     return kernel(
         own_backward,
-        [NEAR, FAR, NEAR, FAR, whole(mine.shape), whole(other.shape), tile(PROBS), tile(ROW), tile(ROW), tile(TURNED)],
-        [FIRST, SECOND] + [whole(PIECE)] * 4,
-        [HALF, HALF] + [PIECE] * 4,
+        [NEAR, FAR, NEAR, FAR, whole(mine.shape), whole(other.shape), tile(PROBS), tile(ROW), tile(ROW),
+         tile(TURNED), SECOND],
+        [FIRST, BOTH] + [whole(PIECE)] * 4,
+        [HALF, (2,) + HALF] + [PIECE] * 4,
         [((BLK, 2 * W), BF), ((2 * W, BLK), BF), ((BLK, W), F32), ((BLK, W), F32)],
         3 * UNIT, 40,
-    )(info, *in_hbm(q), q_far, *in_hbm(do), do_far, *in_hbm(mine), other, *in_hbm(p, c, rd, dq))
+    )(info, *in_hbm(q), q_far, *in_hbm(do), do_far, *in_hbm(mine), other, *in_hbm(p, c, rd, dq, o_far))
 
 HEADS = (4, T, W)
 SWAP = [(0, 1), (1, 0)]
@@ -409,7 +412,6 @@
     got = swap(jnp.where(core == 0, values, keys))
     (full,) = glue(assemble, (spot, *in_hbm(keys, values), got), (HEADS,))
     own = lax.all_gather(full, "z", axis=0)
-    own_other = swap(lax.dynamic_index_in_dim(own, 2 * (1 - core) + head, 1, keepdims=False))
 
     along = [full] + [travel(full, s, 0) for s in (1, 2, 3)]
 
@@ -420,14 +422,16 @@
     do_far = turned_over(cotangent, q_far)
     sent = glue(pick, (selected, *along), ((2,) + HEADS,) * 3)
     got = [travel(sent[s - 1], s, 1) for s in (1, 2, 3)]
-    kept, send = glue(join, (after(selected, q_far, do_far), *along, *got), (PAIR, PAIR))
+    kept, send = glue(join, (after(selected, q_far), *along, *got), (PAIR, PAIR))
     same, cross = glue(arrange, (spot, kept, swap(send)), (PAIR, PAIR))
+    own_other = swap(lax.dynamic_index_in_dim(own, 2 * (1 - core) + head, 1, keepdims=False))
     pieces = [same] + [mirror(a, flip) for a, flip in ((same, 1), (cross, 2), (cross, 3))]
 
-    p, m, l, ot = call_own_forward(info, queries, q_far, own, own_other)
+    p, m, l, ot = call_own_forward(after(info, do_far), queries, q_far, own, own_other)
     out = call_picked(info, queries, q_far, cotangent, do_far, pieces, m, l, ot)
     o_near, o_far, dq, c, rd = out[:5]
-    last = call_own_backward(info, queries, q_far, cotangent, do_far, own, own_other, p, c, rd, dq)
+    last = call_own_backward(
+        info, queries, q_far, cotangent, do_far, own, own_other, p, c, rd, dq, o_far)
 
     def reduced(g, *others):
         arrived = [g[0]] + [mirror(g[flip], flip) for flip in (1, 2, 3)]
@@ -437,10 +441,10 @@
 
     (terms,) = glue(gather_heads, (spot, *reduced(out[5:9], last[0])), ((2,) + HEADS,))
     arrived = [terms] + [travel(terms, s, 1) for s in (1, 2, 3)]
-    o_far, dq_far = mirror(o_far, 3), mirror(last[1], 3)
     low, high = reduced([a[None] for a in last[2:6]])
-    sums = glue(collect, (after(selected, o_far, low), *arrived), (HEADS,) * 4)
-    total = after(sums[0], dq_far) + sum(travel(sums[s], 4 - s, 0) for s in (1, 2, 3))
+    back_far = mirror(after(last[1], low), 3)
+    sums = glue(collect, (after(selected, low), *arrived), (HEADS,) * 4)
+    total = after(sums[0], back_far) + sum(travel(sums[s], 4 - s, 0) for s in (1, 2, 3))
     total = total + jnp.where(
         core == 0, jnp.concatenate([low[0], high[0]], 0), jnp.concatenate([high[0], low[0]], 0)
     )
@@ -457,8 +461,8 @@
         return jnp.where(head == 0, jnp.concatenate([a, b], 1), jnp.concatenate([b, a], 1))
 
     return (
-        sides(o_near, o_far),
-        sides(last[0], dq_far),
+        sides(o_near, back_far[0]),
+        sides(last[0], back_far[1]),
         jnp.where(core == 0, keep, back),
         jnp.where(core == 0, back, keep),
     )

time: 239 us -> 230 us (0.962)
  waiting for transfers between devices: 85.8 us -> 78.4 us
  local copies, waits for them, and re-layouts: 5.59 us -> 8.84 us
    ppermute x13 -> x12, waiting for transfers between devices: 64.1 us -> 39.3 us  [mirror(): return lax.ppermute(array, 'z', [(i, i ^ flip) for i in range(4)])]
    ppermute x12, waiting for transfers between devices: 17.7 us -> 38 us  [travel(): return lax.ppermute(array, PLACE, pairs)]
    ppermute x13 -> x12, starting transfers between devices: 20.3 us -> 16.9 us  [mirror(): return lax.ppermute(array, 'z', [(i, i ^ flip) for i in range(4)])]
    ppermute x6, starting transfers between devices: 8.96 us -> 12 us  [swap(): return lax.ppermute(array, 'head', SWAP)]
    ppermute x6, waiting for transfers between devices: 4 us -> 1.1 us  [swap(): return lax.ppermute(array, 'head', SWAP)]
  transfers between devices with their start and end apart: 32 -> 31, of which waited for: 16 -> 16; matrix products, arithmetic and copies ran while one was open for 3% -> 4% of each run, Pallas kernels for 16% -> 16%
where the time goes in v11:
time: 230 us
  waiting for transfers between devices  78.4 us (34%)
  Pallas kernels  76.1 us (33%)
  starting transfers between devices  47.5 us (21%)
  between operations  14.2 us (6%)
  local copies, waits for them, and re-layouts  8.84 us (4%)
  other arithmetic  4.66 us (2%)
    ppermute x12, waiting for transfers between devices, mirror(): return lax.ppermute(array, 'z', [(i, i ^ flip) for i in range(4)])  39.3 us
    ppermute x12, waiting for transfers between devices, travel(): return lax.ppermute(array, PLACE, pairs)  38 us
    pallas_call x1, Pallas kernels, call_picked(): kernel(picked, [NEAR, FAR, NEAR, FAR] + [whole(PAIR)] * 4 + [tile(ROW), t...  36.3 us
    ppermute x12, starting transfers between devices, travel(): return lax.ppermute(array, PLACE, pairs)  18.5 us
    ppermute x12, starting transfers between devices, mirror(): return lax.ppermute(array, 'z', [(i, i ^ flip) for i in range(4)])  16.9 us
    pallas_call x1, Pallas kernels, call_own_backward(): kernel(own_backward, [NEAR, FAR, NEAR, FAR, whole(mine.shape), whole(othe...  15.2 us
    pallas_call x8, Pallas kernels, glue(): pl.pallas_call(body, out_shape=[jax.ShapeDtypeStruct(s, F32) for s in out...  13.5 us
    ppermute x6, starting transfers between devices, swap(): return lax.ppermute(array, 'head', SWAP)  12 us
  transfers between devices with their start and end apart: 31, of which 16 were waited for; matrix products, arithmetic and copies ran while one was open for 4% of the time, Pallas kernels for 16%

profile of v11, /device:TPU:1, one launch (start us, length us, event | category | flops | bytes accessed | tf_op | source)
XLA Modules:
  0.0 229.6 jit_solution(4224485812704446198)
XLA Ops:
  14.2 2.5 %collective-permute-start.4 = (f32[4,256,128]{2,1,0:T(8,128)}, f32[4,256,128]{2,1,0:T(8,128)S(1)}, u32[]{:S(2)}, u32[]{:S(2)}) collective-permute-start(f32[4,256,128]{2,1,0:T(8,128)} %assemble.1.refs_0_), channel_id=1, source_target_pairs={{0,64},{1,17},{8,72},{9,25},{16,80},{17,1},{24,88},{25,9},{32,96},... | collective-permute-start | bytes 1572872 | tf_op jit(solution)/shard_map/ppermute | solution.py:314
  17.9 4.8 %collective-permute-done.1.refs_1_ = f32[4,256,128]{2,1,0:T(8,128)S(1)} collective-permute-done((f32[4,256,128]{2,1,0:T(8,128)}, f32[4,256,128]{2,1,0:T(8,128)S(1)}, u32[]{:S(2)}, u32[]{:S(2)}) %collective-permute-start.1) | collective-permute-done | bytes 524320 | tf_op jit(solution)/shard_map/ppermute | solution.py:314
  22.6 6.7 %collective-permute-done.4.refs_2_ = f32[4,256,128]{2,1,0:T(8,128)S(1)} collective-permute-done((f32[4,256,128]{2,1,0:T(8,128)}, f32[4,256,128]{2,1,0:T(8,128)S(1)}, u32[]{:S(2)}, u32[]{:S(2)}) %collective-permute-start.4) | collective-permute-done | bytes 524320 | tf_op jit(solution)/shard_map/ppermute | solution.py:314
  29.3 3.2 %pick.1 = (f32[2,4,256,128]{3,2,1,0:T(8,128)}, f32[2,4,256,128]{3,2,1,0:T(8,128)}, f32[2,4,256,128]{3,2,1,0:T(8,128)}) custom-call(s32[16,3]{1,0:T(8,128)S(1)} %copy.12.table, f32[4,256,128]{2,1,0:T(8,128)} %assemble.1.refs_0_, f32[4,256,128]{2,1,0:T(8,128)S(1)} %collective-permute-done.1.refs_1_, f32[4,256,128]{2,1,0:T(8,128)S(1)} %collective-permute-done.4.refs_2_, ...), custom_call_target="tpu_custom_call" | custom-call | bytes 5242880 | tf_op jit(solution)/shard_map/pick/pallas_call | solution.py:291
  33.5 2.6 %collective-permute-start.7 = (f32[2,4,256,128]{3,2,1,0:T(8,128)}, f32[2,4,256,128]{3,2,1,0:T(8,128)}, u32[]{:S(2)}, u32[]{:S(2)}) collective-permute-start(f32[2,4,256,128]{3,2,1,0:T(8,128)} %get-tuple-element.50), channel_id=1, source_target_pairs={{0,16},{1,65},{8,24},{9,73},{16,0},{17,81},{24,8},{25,89},{32,48},... | collective-permute-start | bytes 3145736 | tf_op jit(solution)/shard_map/ppermute | solution.py:314
  39.1 3.8 %collective-permute-start.2 = (f32[256,512]{1,0:T(8,128)}, f32[256,512]{1,0:T(8,128)S(1)}, u32[]{:S(2)}, u32[]{:S(2)}) collective-permute-start(f32[256,512]{1,0:T(8,128)} %constant_dynamic-slice_fusion.1), channel_id=1, source_target_pairs={{0,6},{2,4},{4,2},{6,0},{1,7},{3,5},{5,3},{7,1},{8,14},{10,12},{12... | collective-permute-start | bytes 1572872 | tf_op jit(solution)/shard_map/ppermute | solution.py:317
  42.9 13.7 %collective-permute-done.2.qr_ref = f32[256,512]{1,0:T(8,128)S(1)} collective-permute-done((f32[256,512]{1,0:T(8,128)}, f32[256,512]{1,0:T(8,128)S(1)}, u32[]{:S(2)}, u32[]{:S(2)}) %collective-permute-start.2) | collective-permute-done | bytes 524320 | tf_op jit(solution)/shard_map/ppermute | solution.py:317
  60.2 2.7 %join.1 = (f32[2,2,256,128]{3,2,1,0:T(8,128)S(1)}, f32[2,2,256,128]{3,2,1,0:T(8,128)}) custom-call(s32[16,3]{1,0:T(8,128)S(1)} %copy.13.table, f32[4,256,128]{2,1,0:T(8,128)} %assemble.1.refs_0_, f32[4,256,128]{2,1,0:T(8,128)S(1)} %collective-permute-done.1.refs_1_, f32[4,256,128]{2,1,0:T(8,128)S(1)} %collective-permute-done.4.refs_2_, ...), custom_call_target="tpu_custom_call" | custom-call | bytes 6291456 | tf_op jit(solution)/shard_map/join/pallas_call | solution.py:291
  69.6 3.3 %collective-permute-start.11 = (f32[2,2,256,128]{3,2,1,0:T(8,128)S(1)}, f32[2,2,256,128]{3,2,1,0:T(8,128)S(1)}, u32[]{:S(2)}, u32[]{:S(2)}) collective-permute-start(f32[2,2,256,128]{3,2,1,0:T(8,128)S(1)} %get-tuple-element.55), channel_id=1, source_target_pairs={{0,4},{2,6},{4,0},{6,2},{1,5},{3,7},{5,1},{7,3},{8,12},{10,14},{12... | collective-permute-start | bytes 1572872 | tf_op jit(solution)/shard_map/ppermute | solution.py:317
  73.2 11.1 %own_forward.1 = (f32[4,1024,512]{2,1,0:T(8,128)}, f32[4,1,512]{2,1,0:T(1,128)}, f32[4,1,512]{2,1,0:T(1,128)}, f32[4,128,512]{2,1,0:T(8,128)}) custom-call(s32[5]{0:T(128)S(1)} %pad_add_fusion.info, f32[256,1024]{1,0:T(8,128)} %ql_ref.5, f32[256,512]{1,0:T(8,128)S(1)} %copy-done.5, f32[4,4,256,128]{3,2,1,0:T(8,128)} %bitcast.36, ...), custom_call_target="tpu_custom_call" | custom-call | flops 4294967296 | bytes 16777216 | tf_op jit(solution)/shard_map/own_forward/pallas_call | solution.py:252
  84.2 11.5 %collective-permute-done.11.s2 = f32[2,2,256,128]{3,2,1,0:T(8,128)S(1)} collective-permute-done((f32[2,2,256,128]{3,2,1,0:T(8,128)S(1)}, f32[2,2,256,128]{3,2,1,0:T(8,128)S(1)}, u32[]{:S(2)}, u32[]{:S(2)}) %collective-permute-start.11) | collective-permute-done | bytes 524320 | tf_op jit(solution)/shard_map/ppermute | solution.py:317
  97.9 36.3 %picked.1 = (f32[256,512]{1,0:T(8,128)}, f32[256,512]{1,0:T(8,128)}, f32[4,128,512]{2,1,0:T(8,128)}, f32[4,1,512]{2,1,0:T(1,128)}, f32[4,1,512]{2,1,0:T(1,128)},...) custom-call(s32[5]{0:T(128)S(1)} %pad_add_fusion.info, ...), custom_call_target="tpu_custom_call" | custom-call | flops 21474836480 | bytes 16777216 | tf_op jit(solution)/shard_map/picked/pallas_call | solution.py:262
  134.5 3.5 %collective-permute-start.19 = (f32[2,2,256,128]{3,2,1,0:T(8,128)}, f32[2,2,256,128]{3,2,1,0:T(8,128)S(1)}, u32[]{:S(2)}, u32[]{:S(2)}) collective-permute-start(f32[2,2,256,128]{3,2,1,0:T(8,128)} %get-tuple-element.77), channel_id=1, source_target_pairs={{0,4},{2,6},{4,0},{6,2},{1,5},{3,7},{5,1},{7,3},{8,12},{10,14},{12... | collective-permute-start | bytes 1572872 | tf_op jit(solution)/shard_map/ppermute | solution.py:317
  138.1 15.2 %own_backward.1 = (f32[256,512]{1,0:T(8,128)}, f32[2,256,512]{2,1,0:T(8,128)}, f32[2,256,128]{2,1,0:T(8,128)}, f32[2,256,128]{2,1,0:T(8,128)}, f32[2,256,128]{2,1,0:T(8,128)}, /*index=5*/f32[2,256,128]{2,1,0:T(8,128)}) custom-call(s32[5]{0:T(128)S(1)} %pad_add_fusion.info, f32[256,1024]{1,0:T(8,128)} %ql_ref.5, f32[256,512]{1,0:T(8,128)S(1)} %copy-done.5, ...), custom_call_target="tpu_custom_call" | custom-call | flops 6442450944 | bytes 16777216 | tf_op jit(solution)/shard_map/own_backward/pallas_call | solution.py:274
  153.4 5.9 %collective-permute-done.19.passed = f32[2,2,256,128]{3,2,1,0:T(8,128)S(1)} collective-permute-done((f32[2,2,256,128]{3,2,1,0:T(8,128)}, f32[2,2,256,128]{3,2,1,0:T(8,128)S(1)}, u32[]{:S(2)}, u32[]{:S(2)}) %collective-permute-start.19) | collective-permute-done | bytes 524320 | tf_op jit(solution)/shard_map/ppermute | solution.py:317
  159.9 3.2 %collective-permute-start.21 = (f32[2,2,256,128]{3,2,1,0:T(8,128)S(1)}, f32[2,2,256,128]{3,2,1,0:T(8,128)S(1)}, u32[]{:S(2)}, u32[]{:S(2)}) collective-permute-start(f32[2,2,256,128]{3,2,1,0:T(8,128)S(1)} %get-tuple-element.81), channel_id=1, source_target_pairs={{0,1},{1,0},{2,3},{3,2},{4,5},{5,4},{6,7},{7,6},{8,9},{9,8},{10,11... | collective-permute-start | bytes 1572872 | tf_op jit(solution)/shard_map/ppermute | solution.py:320
  163.5 3.5 %collective-permute-start.15 = (f32[1,2,256,128]{3,2,1,0:T(8,128)S(1)}, f32[1,2,256,128]{3,2,1,0:T(8,128)S(1)}, u32[]{:S(2)}, u32[]{:S(2)}) collective-permute-start(f32[1,2,256,128]{3,2,1,0:T(8,128)S(1)} %bitcast.38), channel_id=1, source_target_pairs={{0,4},{2,6},{4,0},{6,2},{1,5},{3,7},{5,1},{7,3},{8,12},{10,14},{12... | collective-permute-start | bytes 786440 | tf_op jit(solution)/shard_map/ppermute | solution.py:317
  174.2 4.5 %collective-permute-done.15.passed = f32[1,2,256,128]{3,2,1,0:T(8,128)S(1)} collective-permute-done((f32[1,2,256,128]{3,2,1,0:T(8,128)S(1)}, f32[1,2,256,128]{3,2,1,0:T(8,128)S(1)}, u32[]{:S(2)}, u32[]{:S(2)}) %collective-permute-start.15) | collective-permute-done | bytes 262176 | tf_op jit(solution)/shard_map/ppermute | solution.py:317
  180.4 2.5 %collective-permute-done.22.refs_1_ = f32[2,4,256,128]{3,2,1,0:T(8,128)S(1)} collective-permute-done((f32[2,4,256,128]{3,2,1,0:T(8,128)S(1)}, f32[2,4,256,128]{3,2,1,0:T(8,128)S(1)}, u32[]{:S(2)}, u32[]{:S(2)}) %collective-permute-start.22) | collective-permute-done | bytes 1048608 | tf_op jit(solution)/shard_map/ppermute | solution.py:314
  182.9 11.8 %collective-permute-done.23.refs_2_ = f32[2,4,256,128]{3,2,1,0:T(8,128)S(1)} collective-permute-done((f32[2,4,256,128]{3,2,1,0:T(8,128)S(1)}, f32[2,4,256,128]{3,2,1,0:T(8,128)S(1)}, u32[]{:S(2)}, u32[]{:S(2)}) %collective-permute-start.23) | collective-permute-done | bytes 1048608 | tf_op jit(solution)/shard_map/ppermute | solution.py:314
  194.8 3.2 %collect.1 = (f32[4,256,128]{2,1,0:T(8,128)S(1)}, f32[4,256,128]{2,1,0:T(8,128)}, f32[4,256,128]{2,1,0:T(8,128)}, f32[4,256,128]{2,1,0:T(8,128)}) custom-call(s32[16,3]{1,0:T(8,128)S(1)} %copy.14.table, f32[2,4,256,128]{3,2,1,0:T(8,128)S(1)} %gather_heads.1.refs_0_, f32[2,4,256,128]{3,2,1,0:T(8,128)S(1)} %collective-permute-done.22.refs_1_, ...), custom_call_target="tpu_custom_call" | custom-call | bytes 6291456 | tf_op jit(solution)/shard_map/collect/pallas_call | solution.py:291
  206.3 7.0 %collective-permute-done.25 = f32[4,256,128]{2,1,0:T(8,128)S(1)} collective-permute-done((f32[4,256,128]{2,1,0:T(8,128)}, f32[4,256,128]{2,1,0:T(8,128)S(1)}, u32[]{:S(2)}, u32[]{:S(2)}) %collective-permute-start.25) | collective-permute-done | bytes 524320 | tf_op jit(solution)/shard_map/ppermute | solution.py:314
  213.3 3.6 %collective-permute-done.27 = f32[4,256,128]{2,1,0:T(8,128)S(1)} collective-permute-done((f32[4,256,128]{2,1,0:T(8,128)}, f32[4,256,128]{2,1,0:T(8,128)S(1)}, u32[]{:S(2)}, u32[]{:S(2)}) %collective-permute-start.27) | collective-permute-done | bytes 524320 | tf_op jit(solution)/shard_map/ppermute | solution.py:314
  217.1 2.5 %collective-permute-start.29 = (f32[128,512]{1,0:T(8,128)S(1)}, f32[128,512]{1,0:T(8,128)S(1)}, u32[]{:S(2)}, u32[]{:S(2)}) collective-permute-start(f32[128,512]{1,0:T(8,128)S(1)} %pad_maximum_fusion.1), channel_id=1, source_target_pairs={{0,1},{1,0},{2,3},{3,2},{4,5},{5,4},{6,7},{7,6},{8,9},{9,8},{10,11... | collective-permute-start | bytes 786440 | tf_op jit(solution)/shard_map/ppermute | solution.py:320
  (97 shorter events, 47.0 us)
Async XLA Ops:
  7.2 58.1 %all-gather.3.cloned.1.call-start = ((), (), s32[]{:S(2)}) async-start(), calls=%async_computation | async-start | bytes 2621440 | tf_op jit(solution)/shard_map/all_gather | solution.py:414
  12.8 9.8 %collective-permute-start.1 = (f32[4,256,128]{2,1,0:T(8,128)}, f32[4,256,128]{2,1,0:T(8,128)S(1)}, u32[]{:S(2)}, u32[]{:S(2)}) collective-permute-start(f32[4,256,128]{2,1,0:T(8,128)} %assemble.1.refs_0_), channel_id=1, source_target_pairs={{0,32},{1,9},{8,40},{9,17},{16,48},{17,25},{24,56},{25,1},{32,64},... | collective-permute-start | bytes 1572872 | tf_op jit(solution)/shard_map/ppermute | solution.py:314
  14.2 15.1 %collective-permute-start.4 = (f32[4,256,128]{2,1,0:T(8,128)}, f32[4,256,128]{2,1,0:T(8,128)S(1)}, u32[]{:S(2)}, u32[]{:S(2)}) collective-permute-start(f32[4,256,128]{2,1,0:T(8,128)} %assemble.1.refs_0_), channel_id=1, source_target_pairs={{0,64},{1,17},{8,72},{9,25},{16,80},{17,1},{24,88},{25,9},{32,96},... | collective-permute-start | bytes 1572872 | tf_op jit(solution)/shard_map/ppermute | solution.py:314
  16.7 12.7 %collective-permute-start.5 = (f32[4,256,128]{2,1,0:T(8,128)}, f32[4,256,128]{2,1,0:T(8,128)S(1)}, u32[]{:S(2)}, u32[]{:S(2)}) collective-permute-start(f32[4,256,128]{2,1,0:T(8,128)} %assemble.1.refs_0_), channel_id=1, source_target_pairs={{0,96},{1,25},{8,104},{9,1},{16,112},{17,9},{24,120},{25,17},{32,0... | collective-permute-start | bytes 1572872 | tf_op jit(solution)/shard_map/ppermute | solution.py:314
  32.5 26.1 %collective-permute-start.6 = (f32[2,4,256,128]{3,2,1,0:T(8,128)}, f32[2,4,256,128]{3,2,1,0:T(8,128)S(1)}, u32[]{:S(2)}, u32[]{:S(2)}) collective-permute-start(f32[2,4,256,128]{3,2,1,0:T(8,128)} %get-tuple-element.49), channel_id=1, source_target_pairs={{0,8},{1,33},{8,16},{9,41},{16,24},{17,49},{24,0},{25,57},{32,40},... | collective-permute-start | bytes 3145736 | tf_op jit(solution)/shard_map/ppermute | solution.py:314
  33.5 26.6 %collective-permute-start.7 = (f32[2,4,256,128]{3,2,1,0:T(8,128)}, f32[2,4,256,128]{3,2,1,0:T(8,128)}, u32[]{:S(2)}, u32[]{:S(2)}) collective-permute-start(f32[2,4,256,128]{3,2,1,0:T(8,128)} %get-tuple-element.50), channel_id=1, source_target_pairs={{0,16},{1,65},{8,24},{9,73},{16,0},{17,81},{24,8},{25,89},{32,48},... | collective-permute-start | bytes 3145736 | tf_op jit(solution)/shard_map/ppermute | solution.py:314
  36.2 24.0 %collective-permute-start.8 = (f32[2,4,256,128]{3,2,1,0:T(8,128)}, f32[2,4,256,128]{3,2,1,0:T(8,128)}, u32[]{:S(2)}, u32[]{:S(2)}) collective-permute-start(f32[2,4,256,128]{3,2,1,0:T(8,128)} %get-tuple-element.51), channel_id=1, source_target_pairs={{0,24},{1,97},{8,0},{9,105},{16,8},{17,113},{24,16},{25,121},{32,5... | collective-permute-start | bytes 3145736 | tf_op jit(solution)/shard_map/ppermute | solution.py:314
  39.1 17.5 %collective-permute-start.2 = (f32[256,512]{1,0:T(8,128)}, f32[256,512]{1,0:T(8,128)S(1)}, u32[]{:S(2)}, u32[]{:S(2)}) collective-permute-start(f32[256,512]{1,0:T(8,128)} %constant_dynamic-slice_fusion.1), channel_id=1, source_target_pairs={{0,6},{2,4},{4,2},{6,0},{1,7},{3,5},{5,3},{7,1},{8,14},{10,12},{12... | collective-permute-start | bytes 1572872 | tf_op jit(solution)/shard_map/ppermute | solution.py:317
  58.6 14.5 %collective-permute-start.3 = (f32[256,512]{1,0:T(8,128)}, f32[256,512]{1,0:T(8,128)}, u32[]{:S(2)}, u32[]{:S(2)}) collective-permute-start(f32[256,512]{1,0:T(8,128)} %constant_dynamic-slice_fusion), channel_id=1, source_target_pairs={{0,6},{2,4},{4,2},{6,0},{1,7},{3,5},{5,3},{7,1},{8,14},{10,12},{12... | collective-permute-start | bytes 1572872 | tf_op jit(solution)/shard_map/ppermute | solution.py:317
  67.9 16.4 %collective-permute-start.10 = (f32[2,2,256,128]{3,2,1,0:T(8,128)S(1)}, f32[2,2,256,128]{3,2,1,0:T(8,128)S(1)}, u32[]{:S(2)}, u32[]{:S(2)}) collective-permute-start(f32[2,2,256,128]{3,2,1,0:T(8,128)S(1)} %get-tuple-element.54.s0), channel_id=1, source_target_pairs={{0,2},{2,0},{4,6},{6,4},{1,3},{3,1},{5,7},{7,5},{8,10},{10,8},{12,... | collective-permute-start | bytes 1572872 | tf_op jit(solution)/shard_map/ppermute | solution.py:317
  69.6 26.2 %collective-permute-start.11 = (f32[2,2,256,128]{3,2,1,0:T(8,128)S(1)}, f32[2,2,256,128]{3,2,1,0:T(8,128)S(1)}, u32[]{:S(2)}, u32[]{:S(2)}) collective-permute-start(f32[2,2,256,128]{3,2,1,0:T(8,128)S(1)} %get-tuple-element.55), channel_id=1, source_target_pairs={{0,4},{2,6},{4,0},{6,2},{1,5},{3,7},{5,1},{7,3},{8,12},{10,14},{12... | collective-permute-start | bytes 1572872 | tf_op jit(solution)/shard_map/ppermute | solution.py:317
  72.9 25.0 %collective-permute-start.12 = (f32[2,2,256,128]{3,2,1,0:T(8,128)S(1)}, f32[2,2,256,128]{3,2,1,0:T(8,128)}, u32[]{:S(2)}, u32[]{:S(2)}) collective-permute-start(f32[2,2,256,128]{3,2,1,0:T(8,128)S(1)} %get-tuple-element.55), channel_id=1, source_target_pairs={{0,6},{2,4},{4,2},{6,0},{1,7},{3,5},{5,3},{7,1},{8,14},{10,12},{12... | collective-permute-start | bytes 1572872 | tf_op jit(solution)/shard_map/ppermute | solution.py:317
  134.1 19.2 %collective-permute-start.20 = (f32[2,2,256,128]{3,2,1,0:T(8,128)}, f32[2,2,256,128]{3,2,1,0:T(8,128)S(1)}, u32[]{:S(2)}, u32[]{:S(2)}) collective-permute-start(f32[2,2,256,128]{3,2,1,0:T(8,128)} %get-tuple-element.78), channel_id=1, source_target_pairs={{0,6},{2,4},{4,2},{6,0},{1,7},{3,5},{5,3},{7,1},{8,14},{10,12},{12... | collective-permute-start | bytes 1572872 | tf_op jit(solution)/shard_map/ppermute | solution.py:317
  134.5 18.8 %collective-permute-start.18 = (f32[2,2,256,128]{3,2,1,0:T(8,128)}, f32[2,2,256,128]{3,2,1,0:T(8,128)S(1)}, u32[]{:S(2)}, u32[]{:S(2)}) collective-permute-start(f32[2,2,256,128]{3,2,1,0:T(8,128)} %get-tuple-element.76), channel_id=1, source_target_pairs={{0,2},{2,0},{4,6},{6,4},{1,3},{3,1},{5,7},{7,5},{8,10},{10,8},{12,... | collective-permute-start | bytes 1572872 | tf_op jit(solution)/shard_map/ppermute | solution.py:317
  134.5 24.8 %collective-permute-start.19 = (f32[2,2,256,128]{3,2,1,0:T(8,128)}, f32[2,2,256,128]{3,2,1,0:T(8,128)S(1)}, u32[]{:S(2)}, u32[]{:S(2)}) collective-permute-start(f32[2,2,256,128]{3,2,1,0:T(8,128)} %get-tuple-element.77), channel_id=1, source_target_pairs={{0,4},{2,6},{4,0},{6,2},{1,5},{3,7},{5,1},{7,3},{8,12},{10,14},{12... | collective-permute-start | bytes 1572872 | tf_op jit(solution)/shard_map/ppermute | solution.py:317
  163.5 10.8 %collective-permute-start.14 = (f32[1,2,256,128]{3,2,1,0:T(8,128)S(1)}, f32[1,2,256,128]{3,2,1,0:T(8,128)S(1)}, u32[]{:S(2)}, u32[]{:S(2)}) collective-permute-start(f32[1,2,256,128]{3,2,1,0:T(8,128)S(1)} %bitcast.39), channel_id=1, source_target_pairs={{0,2},{2,0},{4,6},{6,4},{1,3},{3,1},{5,7},{7,5},{8,10},{10,8},{12,... | collective-permute-start | bytes 786440 | tf_op jit(solution)/shard_map/ppermute | solution.py:317
  163.5 15.2 %collective-permute-start.15 = (f32[1,2,256,128]{3,2,1,0:T(8,128)S(1)}, f32[1,2,256,128]{3,2,1,0:T(8,128)S(1)}, u32[]{:S(2)}, u32[]{:S(2)}) collective-permute-start(f32[1,2,256,128]{3,2,1,0:T(8,128)S(1)} %bitcast.38), channel_id=1, source_target_pairs={{0,4},{2,6},{4,0},{6,2},{1,5},{3,7},{5,1},{7,3},{8,12},{10,14},{12... | collective-permute-start | bytes 786440 | tf_op jit(solution)/shard_map/ppermute | solution.py:317
  167.6 15.2 %collective-permute-start.22 = (f32[2,4,256,128]{3,2,1,0:T(8,128)S(1)}, f32[2,4,256,128]{3,2,1,0:T(8,128)S(1)}, u32[]{:S(2)}, u32[]{:S(2)}) collective-permute-start(f32[2,4,256,128]{3,2,1,0:T(8,128)S(1)} %gather_heads.1.refs_0_), channel_id=1, source_target_pairs={{0,8},{1,33},{8,16},{9,41},{16,24},{17,49},{24,0},{25,57},{32,40},... | collective-permute-start | bytes 3145736 | tf_op jit(solution)/shard_map/ppermute | solution.py:314
  169.1 25.5 %collective-permute-start.23 = (f32[2,4,256,128]{3,2,1,0:T(8,128)S(1)}, f32[2,4,256,128]{3,2,1,0:T(8,128)S(1)}, u32[]{:S(2)}, u32[]{:S(2)}) collective-permute-start(f32[2,4,256,128]{3,2,1,0:T(8,128)S(1)} %gather_heads.1.refs_0_), channel_id=1, source_target_pairs={{0,16},{1,65},{8,24},{9,73},{16,0},{17,81},{24,8},{25,89},{32,48},... | collective-permute-start | bytes 3145736 | tf_op jit(solution)/shard_map/ppermute | solution.py:314
  172.2 22.6 %collective-permute-start.24 = (f32[2,4,256,128]{3,2,1,0:T(8,128)S(1)}, f32[2,4,256,128]{3,2,1,0:T(8,128)}, u32[]{:S(2)}, u32[]{:S(2)}) collective-permute-start(f32[2,4,256,128]{3,2,1,0:T(8,128)S(1)} %gather_heads.1.refs_0_), channel_id=1, source_target_pairs={{0,24},{1,97},{8,0},{9,105},{16,8},{17,113},{24,16},{25,121},{32,5... | collective-permute-start | bytes 3145736 | tf_op jit(solution)/shard_map/ppermute | solution.py:314
  180.0 25.0 %collective-permute-start.17 = (f32[2,256,512]{2,1,0:T(8,128)}, f32[2,256,512]{2,1,0:T(8,128)}, u32[]{:S(2)}, u32[]{:S(2)}) collective-permute-start(f32[2,256,512]{2,1,0:T(8,128)} %get-tuple-element.72), channel_id=1, source_target_pairs={{0,6},{2,4},{4,2},{6,0},{1,7},{3,5},{5,3},{7,1},{8,14},{10,12},{12... | collective-permute-start | bytes 3145736 | tf_op jit(solution)/shard_map/ppermute | solution.py:317
  198.9 14.4 %collective-permute-start.25 = (f32[4,256,128]{2,1,0:T(8,128)}, f32[4,256,128]{2,1,0:T(8,128)S(1)}, u32[]{:S(2)}, u32[]{:S(2)}) collective-permute-start(f32[4,256,128]{2,1,0:T(8,128)} %get-tuple-element.84), channel_id=1, source_target_pairs={{0,96},{1,25},{8,104},{9,1},{16,112},{17,9},{24,120},{25,17},{32,0... | collective-permute-start | bytes 1572872 | tf_op jit(solution)/shard_map/ppermute | solution.py:314
  201.2 12.1 %collective-permute-start.26 = (f32[4,256,128]{2,1,0:T(8,128)}, f32[4,256,128]{2,1,0:T(8,128)S(1)}, u32[]{:S(2)}, u32[]{:S(2)}) collective-permute-start(f32[4,256,128]{2,1,0:T(8,128)} %get-tuple-element.85), channel_id=1, source_target_pairs={{0,64},{1,17},{8,72},{9,25},{16,80},{17,1},{24,88},{25,9},{32,96},... | collective-permute-start | bytes 1572872 | tf_op jit(solution)/shard_map/ppermute | solution.py:314
  202.3 14.5 %collective-permute-start.27 = (f32[4,256,128]{2,1,0:T(8,128)}, f32[4,256,128]{2,1,0:T(8,128)S(1)}, u32[]{:S(2)}, u32[]{:S(2)}) collective-permute-start(f32[4,256,128]{2,1,0:T(8,128)} %get-tuple-element.86), channel_id=1, source_target_pairs={{0,32},{1,9},{8,40},{9,17},{16,48},{17,25},{24,56},{25,1},{32,64},... | collective-permute-start | bytes 1572872 | tf_op jit(solution)/shard_map/ppermute | solution.py:314
  (22 other events, 174.8 us)
Sparse Core Ops, SparseCore 0:
  13.0 33.9 all-gather.2

commit v12 on v11

--- a/solution.py
+++ b/solution.py
@@ -285,12 +285,12 @@
 SWAP = [(0, 1), (1, 0)]
 PLACE = ("y", "x", "head")
 
-def glue(body, args, outs):
+def glue(body, args, outs, space=jax.ShapeDtypeStruct):
     spec = lambda shape: pl.BlockSpec(shape, lambda i: (0,) * len(shape))
     arrays = args[1:]
     return pl.pallas_call(
         body,
-        out_shape=[jax.ShapeDtypeStruct(s, F32) for s in outs],
+        out_shape=[space(s, F32) for s in outs],
         grid=(1,),
         in_specs=[pl.BlockSpec(memory_space=pltpu.SMEM)] + [spec(a.shape) for a in arrays],
         out_specs=[spec(s) for s in outs],
@@ -312,6 +312,11 @@
                     ty, tx = y, (x + step) % 4
                 pairs.append(((y * 4 + x) * 2 + core, (ty * 4 + tx) * 2 + core))
     return lax.ppermute(array, PLACE, pairs)
+
+def circle(arrays, stage, back=False):
+    step = (lambda s: 4 - s) if back else (lambda s: s)
+    two = travel(arrays[1], step(2), stage)
+    return [travel(arrays[0], step(1), stage), two, travel(arrays[2], step(3), stage)]
 
 def mirror(array, flip):
     return lax.ppermute(array, "z", [(i, i ^ flip) for i in range(4)])
@@ -413,7 +418,7 @@
     (full,) = glue(assemble, (spot, *in_hbm(keys, values), got), (HEADS,))
     own = lax.all_gather(full, "z", axis=0)
 
-    along = [full] + [travel(full, s, 0) for s in (1, 2, 3)]
+    along = [full] + circle([full] * 3, 0)
 
     def turned_over(array, *others):
         return mirror(lax.dynamic_slice_in_dim(after(array, *others), far * 4 * W, 4 * W, 1), 3)
@@ -421,7 +426,7 @@
     q_far = turned_over(queries, along[1])
     do_far = turned_over(cotangent, q_far)
     sent = glue(pick, (selected, *along), ((2,) + HEADS,) * 3)
-    got = [travel(sent[s - 1], s, 1) for s in (1, 2, 3)]
+    got = circle(sent, 1)
     kept, send = glue(join, (after(selected, q_far), *along, *got), (PAIR, PAIR))
     same, cross = glue(arrange, (spot, kept, swap(send)), (PAIR, PAIR))
     own_other = swap(lax.dynamic_index_in_dim(own, 2 * (1 - core) + head, 1, keepdims=False))
@@ -440,11 +445,16 @@
         return keep, swap(send)
 
     (terms,) = glue(gather_heads, (spot, *reduced(out[5:9], last[0])), ((2,) + HEADS,))
-    arrived = [terms] + [travel(terms, s, 1) for s in (1, 2, 3)]
+    arrived = [terms] + circle([terms] * 3, 1)
     low, high = reduced([a[None] for a in last[2:6]])
     back_far = mirror(after(last[1], low), 3)
-    sums = glue(collect, (after(selected, low), *arrived), (HEADS,) * 4)
-    total = after(sums[0], back_far) + sum(travel(sums[s], 4 - s, 0) for s in (1, 2, 3))
+    sums = glue(collect, (after(selected, low), *arrived), (HEADS,) * 4, pltpu.HBM)
+
+    def sides(a, b):
+        return jnp.where(head == 0, jnp.concatenate([a, b], 1), jnp.concatenate([b, a], 1))
+
+    wide = sides(o_near, back_far[0]), sides(last[0], back_far[1])
+    total = after(sums[0], *wide) + sum(circle(sums[1:], 0, True))
     total = total + jnp.where(
         core == 0, jnp.concatenate([low[0], high[0]], 0), jnp.concatenate([high[0], low[0]], 0)
     )
@@ -457,12 +467,8 @@
 
     keep, back = tokens(core), swap(tokens(1 - core))
 
-    def sides(a, b):
-        return jnp.where(head == 0, jnp.concatenate([a, b], 1), jnp.concatenate([b, a], 1))
-
     return (
-        sides(o_near, back_far[0]),
-        sides(last[0], back_far[1]),
+        *wide,
         jnp.where(core == 0, keep, back),
         jnp.where(core == 0, back, keep),
     )

time: 230 us -> 234 us (1.017)
  waiting for transfers between devices: 78.4 us -> 83.8 us
    ppermute x12, waiting for transfers between devices: 38 us -> 42 us  [travel(): return lax.ppermute(array, PLACE, pairs)]
where the time goes in v12:
time: 234 us; the launch traced here: 233 us
  waiting for transfers between devices  83.8 us (36%)
  Pallas kernels  76.3 us (33%)
  starting transfers between devices  46.2 us (20%)
  between operations  14.2 us (6%)
  local copies, waits for them, and re-layouts  8.08 us (3%)
  other arithmetic  4.69 us (2%)
    ppermute x12, waiting for transfers between devices, travel(): return lax.ppermute(array, PLACE, pairs)  42 us
    ppermute x12, waiting for transfers between devices, mirror(): return lax.ppermute(array, 'z', [(i, i ^ flip) for i in range(4)])  39.6 us
    pallas_call x1, Pallas kernels, call_picked(): kernel(picked, [NEAR, FAR, NEAR, FAR] + [whole(PAIR)] * 4 + [tile(ROW), t...  36.3 us
    ppermute x12, starting transfers between devices, travel(): return lax.ppermute(array, PLACE, pairs)  17.9 us
    ppermute x12, starting transfers between devices, mirror(): return lax.ppermute(array, 'z', [(i, i ^ flip) for i in range(4)])  17 us
    pallas_call x1, Pallas kernels, call_own_backward(): kernel(own_backward, [NEAR, FAR, NEAR, FAR, whole(mine.shape), whole(othe...  15.2 us
    pallas_call x8, Pallas kernels, glue(): pl.pallas_call(body, out_shape=[space(s, F32) for s in outs], grid=(1,),...  13.7 us
    ppermute x6, starting transfers between devices, swap(): return lax.ppermute(array, 'head', SWAP)  11.3 us
  transfers between devices with their start and end apart: 31, of which 16 were waited for; matrix products, arithmetic and copies ran while one was open for 4% of the time, Pallas kernels for 16%

profile of v12, /device:TPU:1, one launch (start us, length us, event | category | flops | bytes accessed | tf_op | source)
XLA Modules:
  0.0 233.3 jit_solution(7251218391640833130)
XLA Ops:
  14.2 2.5 %collective-permute-start.4 = (f32[4,256,128]{2,1,0:T(8,128)}, f32[4,256,128]{2,1,0:T(8,128)S(1)}, u32[]{:S(2)}, u32[]{:S(2)}) collective-permute-start(f32[4,256,128]{2,1,0:T(8,128)} %assemble.1.refs_0_), channel_id=1, source_target_pairs={{0,64},{1,17},{8,72},{9,25},{16,80},{17,1},{24,88},{25,9},{32,96},... | collective-permute-start | bytes 1572872 | tf_op jit(solution)/shard_map/ppermute | solution.py:314
  17.9 4.8 %collective-permute-done.1.refs_1_ = f32[4,256,128]{2,1,0:T(8,128)S(1)} collective-permute-done((f32[4,256,128]{2,1,0:T(8,128)}, f32[4,256,128]{2,1,0:T(8,128)S(1)}, u32[]{:S(2)}, u32[]{:S(2)}) %collective-permute-start.1) | collective-permute-done | bytes 524320 | tf_op jit(solution)/shard_map/ppermute | solution.py:314
  22.6 6.7 %collective-permute-done.4.refs_2_ = f32[4,256,128]{2,1,0:T(8,128)S(1)} collective-permute-done((f32[4,256,128]{2,1,0:T(8,128)}, f32[4,256,128]{2,1,0:T(8,128)S(1)}, u32[]{:S(2)}, u32[]{:S(2)}) %collective-permute-start.4) | collective-permute-done | bytes 524320 | tf_op jit(solution)/shard_map/ppermute | solution.py:314
  29.3 3.2 %pick.1 = (f32[2,4,256,128]{3,2,1,0:T(8,128)}, f32[2,4,256,128]{3,2,1,0:T(8,128)}, f32[2,4,256,128]{3,2,1,0:T(8,128)}) custom-call(s32[16,3]{1,0:T(8,128)S(1)} %copy.12.table, f32[4,256,128]{2,1,0:T(8,128)} %assemble.1.refs_0_, f32[4,256,128]{2,1,0:T(8,128)S(1)} %collective-permute-done.1.refs_1_, f32[4,256,128]{2,1,0:T(8,128)S(1)} %collective-permute-done.4.refs_2_, ...), custom_call_target="tpu_custom_call" | custom-call | bytes 5242880 | tf_op jit(solution)/shard_map/pick/pallas_call | solution.py:291
  33.5 2.6 %collective-permute-start.7 = (f32[2,4,256,128]{3,2,1,0:T(8,128)}, f32[2,4,256,128]{3,2,1,0:T(8,128)}, u32[]{:S(2)}, u32[]{:S(2)}) collective-permute-start(f32[2,4,256,128]{3,2,1,0:T(8,128)} %get-tuple-element.50), channel_id=1, source_target_pairs={{0,16},{1,65},{8,24},{9,73},{16,0},{17,81},{24,8},{25,89},{32,48},... | collective-permute-start | bytes 3145736 | tf_op jit(solution)/shard_map/ppermute | solution.py:314
  39.1 3.8 %collective-permute-start.2 = (f32[256,512]{1,0:T(8,128)}, f32[256,512]{1,0:T(8,128)S(1)}, u32[]{:S(2)}, u32[]{:S(2)}) collective-permute-start(f32[256,512]{1,0:T(8,128)} %constant_dynamic-slice_fusion.1), channel_id=1, source_target_pairs={{0,6},{2,4},{4,2},{6,0},{1,7},{3,5},{5,3},{7,1},{8,14},{10,12},{12... | collective-permute-start | bytes 1572872 | tf_op jit(solution)/shard_map/ppermute | solution.py:322
  42.9 13.7 %collective-permute-done.2.qr_ref = f32[256,512]{1,0:T(8,128)S(1)} collective-permute-done((f32[256,512]{1,0:T(8,128)}, f32[256,512]{1,0:T(8,128)S(1)}, u32[]{:S(2)}, u32[]{:S(2)}) %collective-permute-start.2) | collective-permute-done | bytes 524320 | tf_op jit(solution)/shard_map/ppermute | solution.py:322
  60.2 2.7 %join.1 = (f32[2,2,256,128]{3,2,1,0:T(8,128)S(1)}, f32[2,2,256,128]{3,2,1,0:T(8,128)}) custom-call(s32[16,3]{1,0:T(8,128)S(1)} %copy.13.table, f32[4,256,128]{2,1,0:T(8,128)} %assemble.1.refs_0_, f32[4,256,128]{2,1,0:T(8,128)S(1)} %collective-permute-done.1.refs_1_, f32[4,256,128]{2,1,0:T(8,128)S(1)} %collective-permute-done.4.refs_2_, ...), custom_call_target="tpu_custom_call" | custom-call | bytes 6291456 | tf_op jit(solution)/shard_map/join/pallas_call | solution.py:291
  69.6 3.3 %collective-permute-start.11 = (f32[2,2,256,128]{3,2,1,0:T(8,128)S(1)}, f32[2,2,256,128]{3,2,1,0:T(8,128)S(1)}, u32[]{:S(2)}, u32[]{:S(2)}) collective-permute-start(f32[2,2,256,128]{3,2,1,0:T(8,128)S(1)} %get-tuple-element.55), channel_id=1, source_target_pairs={{0,4},{2,6},{4,0},{6,2},{1,5},{3,7},{5,1},{7,3},{8,12},{10,14},{12... | collective-permute-start | bytes 1572872 | tf_op jit(solution)/shard_map/ppermute | solution.py:322
  73.1 11.1 %own_forward.1 = (f32[4,1024,512]{2,1,0:T(8,128)}, f32[4,1,512]{2,1,0:T(1,128)}, f32[4,1,512]{2,1,0:T(1,128)}, f32[4,128,512]{2,1,0:T(8,128)}) custom-call(s32[5]{0:T(128)S(1)} %pad_add_fusion.info, f32[256,1024]{1,0:T(8,128)} %ql_ref.5, f32[256,512]{1,0:T(8,128)S(1)} %copy-done.3, f32[4,4,256,128]{3,2,1,0:T(8,128)} %bitcast.36, ...), custom_call_target="tpu_custom_call" | custom-call | flops 4294967296 | bytes 16777216 | tf_op jit(solution)/shard_map/own_forward/pallas_call | solution.py:252
  84.2 11.5 %collective-permute-done.11.s2 = f32[2,2,256,128]{3,2,1,0:T(8,128)S(1)} collective-permute-done((f32[2,2,256,128]{3,2,1,0:T(8,128)S(1)}, f32[2,2,256,128]{3,2,1,0:T(8,128)S(1)}, u32[]{:S(2)}, u32[]{:S(2)}) %collective-permute-start.11) | collective-permute-done | bytes 524320 | tf_op jit(solution)/shard_map/ppermute | solution.py:322
  97.9 36.3 %picked.1 = (f32[256,512]{1,0:T(8,128)}, f32[256,512]{1,0:T(8,128)}, f32[4,128,512]{2,1,0:T(8,128)}, f32[4,1,512]{2,1,0:T(1,128)}, f32[4,1,512]{2,1,0:T(1,128)},...) custom-call(s32[5]{0:T(128)S(1)} %pad_add_fusion.info, ...), custom_call_target="tpu_custom_call" | custom-call | flops 21474836480 | bytes 16777216 | tf_op jit(solution)/shard_map/picked/pallas_call | solution.py:262
  134.5 3.5 %collective-permute-start.19 = (f32[2,2,256,128]{3,2,1,0:T(8,128)}, f32[2,2,256,128]{3,2,1,0:T(8,128)S(1)}, u32[]{:S(2)}, u32[]{:S(2)}) collective-permute-start(f32[2,2,256,128]{3,2,1,0:T(8,128)} %get-tuple-element.77), channel_id=1, source_target_pairs={{0,4},{2,6},{4,0},{6,2},{1,5},{3,7},{5,1},{7,3},{8,12},{10,14},{12... | collective-permute-start | bytes 1572872 | tf_op jit(solution)/shard_map/ppermute | solution.py:322
  138.1 15.2 %own_backward.1 = (f32[256,512]{1,0:T(8,128)}, f32[2,256,512]{2,1,0:T(8,128)}, f32[2,256,128]{2,1,0:T(8,128)}, f32[2,256,128]{2,1,0:T(8,128)}, f32[2,256,128]{2,1,0:T(8,128)}, /*index=5*/f32[2,256,128]{2,1,0:T(8,128)}) custom-call(s32[5]{0:T(128)S(1)} %pad_add_fusion.info, f32[256,1024]{1,0:T(8,128)} %ql_ref.5, f32[256,512]{1,0:T(8,128)S(1)} %copy-done.3, ...), custom_call_target="tpu_custom_call" | custom-call | flops 6442450944 | bytes 16777216 | tf_op jit(solution)/shard_map/own_backward/pallas_call | solution.py:274
  153.4 5.9 %collective-permute-done.19.passed = f32[2,2,256,128]{3,2,1,0:T(8,128)S(1)} collective-permute-done((f32[2,2,256,128]{3,2,1,0:T(8,128)}, f32[2,2,256,128]{3,2,1,0:T(8,128)S(1)}, u32[]{:S(2)}, u32[]{:S(2)}) %collective-permute-start.19) | collective-permute-done | bytes 524320 | tf_op jit(solution)/shard_map/ppermute | solution.py:322
  159.9 3.2 %collective-permute-start.21 = (f32[2,2,256,128]{3,2,1,0:T(8,128)S(1)}, f32[2,2,256,128]{3,2,1,0:T(8,128)S(1)}, u32[]{:S(2)}, u32[]{:S(2)}) collective-permute-start(f32[2,2,256,128]{3,2,1,0:T(8,128)S(1)} %get-tuple-element.81), channel_id=1, source_target_pairs={{0,1},{1,0},{2,3},{3,2},{4,5},{5,4},{6,7},{7,6},{8,9},{9,8},{10,11... | collective-permute-start | bytes 1572872 | tf_op jit(solution)/shard_map/ppermute | solution.py:325
  163.5 3.5 %collective-permute-start.15 = (f32[1,2,256,128]{3,2,1,0:T(8,128)S(1)}, f32[1,2,256,128]{3,2,1,0:T(8,128)S(1)}, u32[]{:S(2)}, u32[]{:S(2)}) collective-permute-start(f32[1,2,256,128]{3,2,1,0:T(8,128)S(1)} %bitcast.38), channel_id=1, source_target_pairs={{0,4},{2,6},{4,0},{6,2},{1,5},{3,7},{5,1},{7,3},{8,12},{10,14},{12... | collective-permute-start | bytes 786440 | tf_op jit(solution)/shard_map/ppermute | solution.py:322
  167.0 5.2 %collective-permute-done.16.passed2 = f32[1,2,256,128]{3,2,1,0:T(8,128)S(1)} collective-permute-done((f32[1,2,256,128]{3,2,1,0:T(8,128)S(1)}, f32[1,2,256,128]{3,2,1,0:T(8,128)S(1)}, u32[]{:S(2)}, u32[]{:S(2)}) %collective-permute-start.16) | collective-permute-done | bytes 262176 | tf_op jit(solution)/shard_map/ppermute | solution.py:322
  181.9 6.3 %collective-permute-done.22.refs_1_ = f32[2,4,256,128]{3,2,1,0:T(8,128)S(1)} collective-permute-done((f32[2,4,256,128]{3,2,1,0:T(8,128)S(1)}, f32[2,4,256,128]{3,2,1,0:T(8,128)S(1)}, u32[]{:S(2)}, u32[]{:S(2)}) %collective-permute-start.22) | collective-permute-done | bytes 1048608 | tf_op jit(solution)/shard_map/ppermute | solution.py:314
  188.2 11.6 %collective-permute-done.23.refs_2_ = f32[2,4,256,128]{3,2,1,0:T(8,128)S(1)} collective-permute-done((f32[2,4,256,128]{3,2,1,0:T(8,128)S(1)}, f32[2,4,256,128]{3,2,1,0:T(8,128)S(1)}, u32[]{:S(2)}, u32[]{:S(2)}) %collective-permute-start.23) | collective-permute-done | bytes 1048608 | tf_op jit(solution)/shard_map/ppermute | solution.py:314
  200.0 3.4 %collect.1 = (f32[4,256,128]{2,1,0:T(8,128)}, f32[4,256,128]{2,1,0:T(8,128)}, f32[4,256,128]{2,1,0:T(8,128)}, f32[4,256,128]{2,1,0:T(8,128)}) custom-call(s32[16,3]{1,0:T(8,128)S(1)} %copy.14.table, f32[2,4,256,128]{3,2,1,0:T(8,128)S(1)} %gather_heads.1.refs_0_, f32[2,4,256,128]{3,2,1,0:T(8,128)S(1)} %collective-permute-done.22.refs_1_, ...), custom_call_target="tpu_custom_call" | custom-call | bytes 6291456 | tf_op jit(solution)/shard_map/collect/pallas_call | solution.py:291
  210.5 7.3 %collective-permute-done.25 = f32[4,256,128]{2,1,0:T(8,128)S(1)} collective-permute-done((f32[4,256,128]{2,1,0:T(8,128)}, f32[4,256,128]{2,1,0:T(8,128)S(1)}, u32[]{:S(2)}, u32[]{:S(2)}) %collective-permute-start.25) | collective-permute-done | bytes 524320 | tf_op jit(solution)/shard_map/ppermute | solution.py:314
  217.8 3.6 %collective-permute-done.27 = f32[4,256,128]{2,1,0:T(8,128)S(1)} collective-permute-done((f32[4,256,128]{2,1,0:T(8,128)}, f32[4,256,128]{2,1,0:T(8,128)S(1)}, u32[]{:S(2)}, u32[]{:S(2)}) %collective-permute-start.27) | collective-permute-done | bytes 524320 | tf_op jit(solution)/shard_map/ppermute | solution.py:314
  221.7 2.7 %collective-permute-start.29 = (f32[128,512]{1,0:T(8,128)S(1)}, f32[128,512]{1,0:T(8,128)S(1)}, u32[]{:S(2)}, u32[]{:S(2)}) collective-permute-start(f32[128,512]{1,0:T(8,128)S(1)} %pad_maximum_fusion.1), channel_id=1, source_target_pairs={{0,1},{1,0},{2,3},{3,2},{4,5},{5,4},{6,7},{7,6},{8,9},{9,8},{10,11... | collective-permute-start | bytes 786440 | tf_op jit(solution)/shard_map/ppermute | solution.py:325
  (95 shorter events, 45.5 us)
Async XLA Ops:
  7.2 58.1 %all-gather.3.cloned.1.call-start = ((), (), s32[]{:S(2)}) async-start(), calls=%async_computation | async-start | bytes 2621440 | tf_op jit(solution)/shard_map/all_gather | solution.py:419
  14.2 15.1 %collective-permute-start.4 = (f32[4,256,128]{2,1,0:T(8,128)}, f32[4,256,128]{2,1,0:T(8,128)S(1)}, u32[]{:S(2)}, u32[]{:S(2)}) collective-permute-start(f32[4,256,128]{2,1,0:T(8,128)} %assemble.1.refs_0_), channel_id=1, source_target_pairs={{0,64},{1,17},{8,72},{9,25},{16,80},{17,1},{24,88},{25,9},{32,96},... | collective-permute-start | bytes 1572872 | tf_op jit(solution)/shard_map/ppermute | solution.py:314
  16.7 12.7 %collective-permute-start.5 = (f32[4,256,128]{2,1,0:T(8,128)}, f32[4,256,128]{2,1,0:T(8,128)S(1)}, u32[]{:S(2)}, u32[]{:S(2)}) collective-permute-start(f32[4,256,128]{2,1,0:T(8,128)} %assemble.1.refs_0_), channel_id=1, source_target_pairs={{0,96},{1,25},{8,104},{9,1},{16,112},{17,9},{24,120},{25,17},{32,0... | collective-permute-start | bytes 1572872 | tf_op jit(solution)/shard_map/ppermute | solution.py:314
  32.5 26.1 %collective-permute-start.6 = (f32[2,4,256,128]{3,2,1,0:T(8,128)}, f32[2,4,256,128]{3,2,1,0:T(8,128)S(1)}, u32[]{:S(2)}, u32[]{:S(2)}) collective-permute-start(f32[2,4,256,128]{3,2,1,0:T(8,128)} %get-tuple-element.49), channel_id=1, source_target_pairs={{0,8},{1,33},{8,16},{9,41},{16,24},{17,49},{24,0},{25,57},{32,40},... | collective-permute-start | bytes 3145736 | tf_op jit(solution)/shard_map/ppermute | solution.py:314
  33.5 26.6 %collective-permute-start.7 = (f32[2,4,256,128]{3,2,1,0:T(8,128)}, f32[2,4,256,128]{3,2,1,0:T(8,128)}, u32[]{:S(2)}, u32[]{:S(2)}) collective-permute-start(f32[2,4,256,128]{3,2,1,0:T(8,128)} %get-tuple-element.50), channel_id=1, source_target_pairs={{0,16},{1,65},{8,24},{9,73},{16,0},{17,81},{24,8},{25,89},{32,48},... | collective-permute-start | bytes 3145736 | tf_op jit(solution)/shard_map/ppermute | solution.py:314
  36.1 24.0 %collective-permute-start.8 = (f32[2,4,256,128]{3,2,1,0:T(8,128)}, f32[2,4,256,128]{3,2,1,0:T(8,128)}, u32[]{:S(2)}, u32[]{:S(2)}) collective-permute-start(f32[2,4,256,128]{3,2,1,0:T(8,128)} %get-tuple-element.51), channel_id=1, source_target_pairs={{0,24},{1,97},{8,0},{9,105},{16,8},{17,113},{24,16},{25,121},{32,5... | collective-permute-start | bytes 3145736 | tf_op jit(solution)/shard_map/ppermute | solution.py:314
  39.1 17.5 %collective-permute-start.2 = (f32[256,512]{1,0:T(8,128)}, f32[256,512]{1,0:T(8,128)S(1)}, u32[]{:S(2)}, u32[]{:S(2)}) collective-permute-start(f32[256,512]{1,0:T(8,128)} %constant_dynamic-slice_fusion.1), channel_id=1, source_target_pairs={{0,6},{2,4},{4,2},{6,0},{1,7},{3,5},{5,3},{7,1},{8,14},{10,12},{12... | collective-permute-start | bytes 1572872 | tf_op jit(solution)/shard_map/ppermute | solution.py:322
  58.6 14.5 %collective-permute-start.3 = (f32[256,512]{1,0:T(8,128)}, f32[256,512]{1,0:T(8,128)}, u32[]{:S(2)}, u32[]{:S(2)}) collective-permute-start(f32[256,512]{1,0:T(8,128)} %constant_dynamic-slice_fusion), channel_id=1, source_target_pairs={{0,6},{2,4},{4,2},{6,0},{1,7},{3,5},{5,3},{7,1},{8,14},{10,12},{12... | collective-permute-start | bytes 1572872 | tf_op jit(solution)/shard_map/ppermute | solution.py:322
  67.8 16.4 %collective-permute-start.10 = (f32[2,2,256,128]{3,2,1,0:T(8,128)S(1)}, f32[2,2,256,128]{3,2,1,0:T(8,128)S(1)}, u32[]{:S(2)}, u32[]{:S(2)}) collective-permute-start(f32[2,2,256,128]{3,2,1,0:T(8,128)S(1)} %get-tuple-element.54.s0), channel_id=1, source_target_pairs={{0,2},{2,0},{4,6},{6,4},{1,3},{3,1},{5,7},{7,5},{8,10},{10,8},{12,... | collective-permute-start | bytes 1572872 | tf_op jit(solution)/shard_map/ppermute | solution.py:322
  69.6 26.2 %collective-permute-start.11 = (f32[2,2,256,128]{3,2,1,0:T(8,128)S(1)}, f32[2,2,256,128]{3,2,1,0:T(8,128)S(1)}, u32[]{:S(2)}, u32[]{:S(2)}) collective-permute-start(f32[2,2,256,128]{3,2,1,0:T(8,128)S(1)} %get-tuple-element.55), channel_id=1, source_target_pairs={{0,4},{2,6},{4,0},{6,2},{1,5},{3,7},{5,1},{7,3},{8,12},{10,14},{12... | collective-permute-start | bytes 1572872 | tf_op jit(solution)/shard_map/ppermute | solution.py:322
  72.9 25.0 %collective-permute-start.12 = (f32[2,2,256,128]{3,2,1,0:T(8,128)S(1)}, f32[2,2,256,128]{3,2,1,0:T(8,128)}, u32[]{:S(2)}, u32[]{:S(2)}) collective-permute-start(f32[2,2,256,128]{3,2,1,0:T(8,128)S(1)} %get-tuple-element.55), channel_id=1, source_target_pairs={{0,6},{2,4},{4,2},{6,0},{1,7},{3,5},{5,3},{7,1},{8,14},{10,12},{12... | collective-permute-start | bytes 1572872 | tf_op jit(solution)/shard_map/ppermute | solution.py:322
  134.1 19.2 %collective-permute-start.20 = (f32[2,2,256,128]{3,2,1,0:T(8,128)}, f32[2,2,256,128]{3,2,1,0:T(8,128)S(1)}, u32[]{:S(2)}, u32[]{:S(2)}) collective-permute-start(f32[2,2,256,128]{3,2,1,0:T(8,128)} %get-tuple-element.78), channel_id=1, source_target_pairs={{0,6},{2,4},{4,2},{6,0},{1,7},{3,5},{5,3},{7,1},{8,14},{10,12},{12... | collective-permute-start | bytes 1572872 | tf_op jit(solution)/shard_map/ppermute | solution.py:322
  134.5 18.8 %collective-permute-start.18 = (f32[2,2,256,128]{3,2,1,0:T(8,128)}, f32[2,2,256,128]{3,2,1,0:T(8,128)S(1)}, u32[]{:S(2)}, u32[]{:S(2)}) collective-permute-start(f32[2,2,256,128]{3,2,1,0:T(8,128)} %get-tuple-element.76), channel_id=1, source_target_pairs={{0,2},{2,0},{4,6},{6,4},{1,3},{3,1},{5,7},{7,5},{8,10},{10,8},{12,... | collective-permute-start | bytes 1572872 | tf_op jit(solution)/shard_map/ppermute | solution.py:322
  134.5 24.7 %collective-permute-start.19 = (f32[2,2,256,128]{3,2,1,0:T(8,128)}, f32[2,2,256,128]{3,2,1,0:T(8,128)S(1)}, u32[]{:S(2)}, u32[]{:S(2)}) collective-permute-start(f32[2,2,256,128]{3,2,1,0:T(8,128)} %get-tuple-element.77), channel_id=1, source_target_pairs={{0,4},{2,6},{4,0},{6,2},{1,5},{3,7},{5,1},{7,3},{8,12},{10,14},{12... | collective-permute-start | bytes 1572872 | tf_op jit(solution)/shard_map/ppermute | solution.py:322
  159.9 12.3 %collective-permute-start.21 = (f32[2,2,256,128]{3,2,1,0:T(8,128)S(1)}, f32[2,2,256,128]{3,2,1,0:T(8,128)S(1)}, u32[]{:S(2)}, u32[]{:S(2)}) collective-permute-start(f32[2,2,256,128]{3,2,1,0:T(8,128)S(1)} %get-tuple-element.81), channel_id=1, source_target_pairs={{0,1},{1,0},{2,3},{3,2},{4,5},{5,4},{6,7},{7,6},{8,9},{9,8},{10,11... | collective-permute-start | bytes 1572872 | tf_op jit(solution)/shard_map/ppermute | solution.py:325
  163.5 14.1 %collective-permute-start.14 = (f32[1,2,256,128]{3,2,1,0:T(8,128)S(1)}, f32[1,2,256,128]{3,2,1,0:T(8,128)S(1)}, u32[]{:S(2)}, u32[]{:S(2)}) collective-permute-start(f32[1,2,256,128]{3,2,1,0:T(8,128)S(1)} %bitcast.39), channel_id=1, source_target_pairs={{0,2},{2,0},{4,6},{6,4},{1,3},{3,1},{5,7},{7,5},{8,10},{10,8},{12,... | collective-permute-start | bytes 786440 | tf_op jit(solution)/shard_map/ppermute | solution.py:322
  163.5 15.2 %collective-permute-start.15 = (f32[1,2,256,128]{3,2,1,0:T(8,128)S(1)}, f32[1,2,256,128]{3,2,1,0:T(8,128)S(1)}, u32[]{:S(2)}, u32[]{:S(2)}) collective-permute-start(f32[1,2,256,128]{3,2,1,0:T(8,128)S(1)} %bitcast.38), channel_id=1, source_target_pairs={{0,4},{2,6},{4,0},{6,2},{1,5},{3,7},{5,1},{7,3},{8,12},{10,14},{12... | collective-permute-start | bytes 786440 | tf_op jit(solution)/shard_map/ppermute | solution.py:322
  172.8 15.3 %collective-permute-start.22 = (f32[2,4,256,128]{3,2,1,0:T(8,128)S(1)}, f32[2,4,256,128]{3,2,1,0:T(8,128)S(1)}, u32[]{:S(2)}, u32[]{:S(2)}) collective-permute-start(f32[2,4,256,128]{3,2,1,0:T(8,128)S(1)} %gather_heads.1.refs_0_), channel_id=1, source_target_pairs={{0,8},{1,33},{8,16},{9,41},{16,24},{17,49},{24,0},{25,57},{32,40},... | collective-permute-start | bytes 3145736 | tf_op jit(solution)/shard_map/ppermute | solution.py:314
  174.3 25.5 %collective-permute-start.23 = (f32[2,4,256,128]{3,2,1,0:T(8,128)S(1)}, f32[2,4,256,128]{3,2,1,0:T(8,128)S(1)}, u32[]{:S(2)}, u32[]{:S(2)}) collective-permute-start(f32[2,4,256,128]{3,2,1,0:T(8,128)S(1)} %gather_heads.1.refs_0_), channel_id=1, source_target_pairs={{0,16},{1,65},{8,24},{9,73},{16,0},{17,81},{24,8},{25,89},{32,48},... | collective-permute-start | bytes 3145736 | tf_op jit(solution)/shard_map/ppermute | solution.py:314
  176.1 23.9 %collective-permute-start.24 = (f32[2,4,256,128]{3,2,1,0:T(8,128)S(1)}, f32[2,4,256,128]{3,2,1,0:T(8,128)}, u32[]{:S(2)}, u32[]{:S(2)}) collective-permute-start(f32[2,4,256,128]{3,2,1,0:T(8,128)S(1)} %gather_heads.1.refs_0_), channel_id=1, source_target_pairs={{0,24},{1,97},{8,0},{9,105},{16,8},{17,113},{24,16},{25,121},{32,5... | collective-permute-start | bytes 3145736 | tf_op jit(solution)/shard_map/ppermute | solution.py:314
  180.0 26.9 %collective-permute-start.17 = (f32[2,256,512]{2,1,0:T(8,128)}, f32[2,256,512]{2,1,0:T(8,128)}, u32[]{:S(2)}, u32[]{:S(2)}) collective-permute-start(f32[2,256,512]{2,1,0:T(8,128)} %get-tuple-element.72), channel_id=1, source_target_pairs={{0,6},{2,4},{4,2},{6,0},{1,7},{3,5},{5,3},{7,1},{8,14},{10,12},{12... | collective-permute-start | bytes 3145736 | tf_op jit(solution)/shard_map/ppermute | solution.py:322
  180.4 30.1 %collective-permute-start.28 = (f32[1,2,256,128]{3,2,1,0:T(8,128)}, f32[1,2,256,128]{3,2,1,0:T(8,128)S(1)}, u32[]{:S(2)}, u32[]{:S(2)}) collective-permute-start(f32[1,2,256,128]{3,2,1,0:T(8,128)} %copy-done.4), channel_id=1, source_target_pairs={{0,1},{1,0},{2,3},{3,2},{4,5},{5,4},{6,7},{7,6},{8,9},{9,8},{10,11... | collective-permute-start | bytes 786440 | tf_op jit(solution)/shard_map/ppermute | solution.py:325
  203.5 14.4 %collective-permute-start.25 = (f32[4,256,128]{2,1,0:T(8,128)}, f32[4,256,128]{2,1,0:T(8,128)S(1)}, u32[]{:S(2)}, u32[]{:S(2)}) collective-permute-start(f32[4,256,128]{2,1,0:T(8,128)} %get-tuple-element.84), channel_id=1, source_target_pairs={{0,96},{1,25},{8,104},{9,1},{16,112},{17,9},{24,120},{25,17},{32,0... | collective-permute-start | bytes 1572872 | tf_op jit(solution)/shard_map/ppermute | solution.py:314
  206.8 14.6 %collective-permute-start.27 = (f32[4,256,128]{2,1,0:T(8,128)}, f32[4,256,128]{2,1,0:T(8,128)S(1)}, u32[]{:S(2)}, u32[]{:S(2)}) collective-permute-start(f32[4,256,128]{2,1,0:T(8,128)} %get-tuple-element.86), channel_id=1, source_target_pairs={{0,32},{1,9},{8,40},{9,17},{16,48},{17,25},{24,56},{25,1},{32,64},... | collective-permute-start | bytes 1572872 | tf_op jit(solution)/shard_map/ppermute | solution.py:314
  (21 other events, 180.1 us)
Sparse Core Ops, SparseCore 0:
  12.9 33.9 all-gather.2

commit v13 on v12

--- a/solution.py
+++ b/solution.py
@@ -446,7 +446,7 @@
 
     (terms,) = glue(gather_heads, (spot, *reduced(out[5:9], last[0])), ((2,) + HEADS,))
     arrived = [terms] + circle([terms] * 3, 1)
-    low, high = reduced([a[None] for a in last[2:6]])
+    low, high = reduced([after(a, terms)[None] for a in last[2:6]])
     back_far = mirror(after(last[1], low), 3)
     sums = glue(collect, (after(selected, low), *arrived), (HEADS,) * 4, pltpu.HBM)
 

time: 234 us -> 230 us (0.983)
  waiting for transfers between devices: 83.8 us -> 78.7 us
    ppermute x12, waiting for transfers between devices: 42 us -> 31.3 us  [travel(): return lax.ppermute(array, PLACE, pairs)]
    ppermute x12, waiting for transfers between devices: 39.6 us -> 43.5 us  [mirror(): return lax.ppermute(array, 'z', [(i, i ^ flip) for i in range(4)])]
  transfers between devices with their start and end apart: 31 -> 31, of which waited for: 16 -> 17; matrix products, arithmetic and copies ran while one was open for 4% -> 4% of each run, Pallas kernels for 16% -> 16%
where the time goes in v13:
time: 230 us; the launch traced here: 229 us
  waiting for transfers between devices  78.7 us (34%)
  Pallas kernels  76 us (33%)
  starting transfers between devices  48.1 us (21%)
  between operations  14.2 us (6%)
  local copies, waits for them, and re-layouts  8.04 us (3%)
  other arithmetic  4.04 us (2%)
    ppermute x12, waiting for transfers between devices, mirror(): return lax.ppermute(array, 'z', [(i, i ^ flip) for i in range(4)])  43.5 us
    pallas_call x1, Pallas kernels, call_picked(): kernel(picked, [NEAR, FAR, NEAR, FAR] + [whole(PAIR)] * 4 + [tile(ROW), t...  36.3 us
    ppermute x12, waiting for transfers between devices, travel(): return lax.ppermute(array, PLACE, pairs)  31.3 us
    ppermute x12, starting transfers between devices, travel(): return lax.ppermute(array, PLACE, pairs)  18.5 us
    ppermute x12, starting transfers between devices, mirror(): return lax.ppermute(array, 'z', [(i, i ^ flip) for i in range(4)])  16.3 us
    pallas_call x1, Pallas kernels, call_own_backward(): kernel(own_backward, [NEAR, FAR, NEAR, FAR, whole(mine.shape), whole(othe...  15.2 us
    pallas_call x8, Pallas kernels, glue(): pl.pallas_call(body, out_shape=[space(s, F32) for s in outs], grid=(1,),...  13.5 us
    ppermute x6, starting transfers between devices, swap(): return lax.ppermute(array, 'head', SWAP)  13.3 us
  transfers between devices with their start and end apart: 31, of which 17 were waited for; matrix products, arithmetic and copies ran while one was open for 4% of the time, Pallas kernels for 16%

profile of v13, /device:TPU:1, one launch (start us, length us, event | category | flops | bytes accessed | tf_op | source)
XLA Modules:
  0.0 229.1 jit_solution(1981754252266230645)
XLA Ops:
  14.2 2.5 %collective-permute-start.4 = (f32[4,256,128]{2,1,0:T(8,128)}, f32[4,256,128]{2,1,0:T(8,128)S(1)}, u32[]{:S(2)}, u32[]{:S(2)}) collective-permute-start(f32[4,256,128]{2,1,0:T(8,128)} %assemble.1.refs_0_), channel_id=1, source_target_pairs={{0,64},{1,17},{8,72},{9,25},{16,80},{17,1},{24,88},{25,9},{32,96},... | collective-permute-start | bytes 1572872 | tf_op jit(solution)/shard_map/ppermute | solution.py:314
  17.9 4.8 %collective-permute-done.1.refs_1_ = f32[4,256,128]{2,1,0:T(8,128)S(1)} collective-permute-done((f32[4,256,128]{2,1,0:T(8,128)}, f32[4,256,128]{2,1,0:T(8,128)S(1)}, u32[]{:S(2)}, u32[]{:S(2)}) %collective-permute-start.1) | collective-permute-done | bytes 524320 | tf_op jit(solution)/shard_map/ppermute | solution.py:314
  22.6 6.7 %collective-permute-done.4.refs_2_ = f32[4,256,128]{2,1,0:T(8,128)S(1)} collective-permute-done((f32[4,256,128]{2,1,0:T(8,128)}, f32[4,256,128]{2,1,0:T(8,128)S(1)}, u32[]{:S(2)}, u32[]{:S(2)}) %collective-permute-start.4) | collective-permute-done | bytes 524320 | tf_op jit(solution)/shard_map/ppermute | solution.py:314
  29.3 3.2 %pick.1 = (f32[2,4,256,128]{3,2,1,0:T(8,128)}, f32[2,4,256,128]{3,2,1,0:T(8,128)}, f32[2,4,256,128]{3,2,1,0:T(8,128)}) custom-call(s32[16,3]{1,0:T(8,128)S(1)} %copy.12.table, f32[4,256,128]{2,1,0:T(8,128)} %assemble.1.refs_0_, f32[4,256,128]{2,1,0:T(8,128)S(1)} %collective-permute-done.1.refs_1_, f32[4,256,128]{2,1,0:T(8,128)S(1)} %collective-permute-done.4.refs_2_, ...), custom_call_target="tpu_custom_call" | custom-call | bytes 5242880 | tf_op jit(solution)/shard_map/pick/pallas_call | solution.py:291
  33.5 2.6 %collective-permute-start.7 = (f32[2,4,256,128]{3,2,1,0:T(8,128)}, f32[2,4,256,128]{3,2,1,0:T(8,128)}, u32[]{:S(2)}, u32[]{:S(2)}) collective-permute-start(f32[2,4,256,128]{3,2,1,0:T(8,128)} %get-tuple-element.54), channel_id=1, source_target_pairs={{0,16},{1,65},{8,24},{9,73},{16,0},{17,81},{24,8},{25,89},{32,48},... | collective-permute-start | bytes 3145736 | tf_op jit(solution)/shard_map/ppermute | solution.py:314
  39.1 3.8 %collective-permute-start.2 = (f32[256,512]{1,0:T(8,128)}, f32[256,512]{1,0:T(8,128)S(1)}, u32[]{:S(2)}, u32[]{:S(2)}) collective-permute-start(f32[256,512]{1,0:T(8,128)} %constant_dynamic-slice_fusion.1), channel_id=1, source_target_pairs={{0,6},{2,4},{4,2},{6,0},{1,7},{3,5},{5,3},{7,1},{8,14},{10,12},{12... | collective-permute-start | bytes 1572872 | tf_op jit(solution)/shard_map/ppermute | solution.py:322
  42.9 13.7 %collective-permute-done.2.qr_ref = f32[256,512]{1,0:T(8,128)S(1)} collective-permute-done((f32[256,512]{1,0:T(8,128)}, f32[256,512]{1,0:T(8,128)S(1)}, u32[]{:S(2)}, u32[]{:S(2)}) %collective-permute-start.2) | collective-permute-done | bytes 524320 | tf_op jit(solution)/shard_map/ppermute | solution.py:322
  60.2 2.7 %join.1 = (f32[2,2,256,128]{3,2,1,0:T(8,128)S(1)}, f32[2,2,256,128]{3,2,1,0:T(8,128)}) custom-call(s32[16,3]{1,0:T(8,128)S(1)} %copy.13.table, f32[4,256,128]{2,1,0:T(8,128)} %assemble.1.refs_0_, f32[4,256,128]{2,1,0:T(8,128)S(1)} %collective-permute-done.1.refs_1_, f32[4,256,128]{2,1,0:T(8,128)S(1)} %collective-permute-done.4.refs_2_, ...), custom_call_target="tpu_custom_call" | custom-call | bytes 6291456 | tf_op jit(solution)/shard_map/join/pallas_call | solution.py:291
  62.9 2.3 %collective-permute-start.9 = (f32[2,2,256,128]{3,2,1,0:T(8,128)}, f32[2,2,256,128]{3,2,1,0:T(8,128)S(1)}, u32[]{:S(2)}, u32[]{:S(2)}) collective-permute-start(f32[2,2,256,128]{3,2,1,0:T(8,128)} %get-tuple-element.57), channel_id=1, source_target_pairs={{0,1},{1,0},{2,3},{3,2},{4,5},{5,4},{6,7},{7,6},{8,9},{9,8},{10,11... | collective-permute-start | bytes 1572872 | tf_op jit(solution)/shard_map/ppermute | solution.py:325
  69.6 3.3 %collective-permute-start.11 = (f32[2,2,256,128]{3,2,1,0:T(8,128)S(1)}, f32[2,2,256,128]{3,2,1,0:T(8,128)S(1)}, u32[]{:S(2)}, u32[]{:S(2)}) collective-permute-start(f32[2,2,256,128]{3,2,1,0:T(8,128)S(1)} %get-tuple-element.59), channel_id=1, source_target_pairs={{0,4},{2,6},{4,0},{6,2},{1,5},{3,7},{5,1},{7,3},{8,12},{10,14},{12... | collective-permute-start | bytes 1572872 | tf_op jit(solution)/shard_map/ppermute | solution.py:322
  73.2 11.1 %own_forward.1 = (f32[4,1024,512]{2,1,0:T(8,128)}, f32[4,1,512]{2,1,0:T(1,128)}, f32[4,1,512]{2,1,0:T(1,128)}, f32[4,128,512]{2,1,0:T(8,128)}) custom-call(s32[5]{0:T(128)S(1)} %pad_add_fusion.info, f32[256,1024]{1,0:T(8,128)} %ql_ref.5, f32[256,512]{1,0:T(8,128)S(1)} %copy-done.3, f32[4,4,256,128]{3,2,1,0:T(8,128)} %bitcast.36, ...), custom_call_target="tpu_custom_call" | custom-call | flops 4294967296 | bytes 16777216 | tf_op jit(solution)/shard_map/own_forward/pallas_call | solution.py:252
  84.2 11.5 %collective-permute-done.11.s2 = f32[2,2,256,128]{3,2,1,0:T(8,128)S(1)} collective-permute-done((f32[2,2,256,128]{3,2,1,0:T(8,128)S(1)}, f32[2,2,256,128]{3,2,1,0:T(8,128)S(1)}, u32[]{:S(2)}, u32[]{:S(2)}) %collective-permute-start.11) | collective-permute-done | bytes 524320 | tf_op jit(solution)/shard_map/ppermute | solution.py:322
  97.9 36.3 %picked.1 = (f32[256,512]{1,0:T(8,128)}, f32[256,512]{1,0:T(8,128)}, f32[4,128,512]{2,1,0:T(8,128)}, f32[4,1,512]{2,1,0:T(1,128)}, f32[4,1,512]{2,1,0:T(1,128)},...) custom-call(s32[5]{0:T(128)S(1)} %pad_add_fusion.info, ...), custom_call_target="tpu_custom_call" | custom-call | flops 21474836480 | bytes 16777216 | tf_op jit(solution)/shard_map/picked/pallas_call | solution.py:262
  134.5 3.5 %collective-permute-start.15 = (f32[2,2,256,128]{3,2,1,0:T(8,128)}, f32[2,2,256,128]{3,2,1,0:T(8,128)S(1)}, u32[]{:S(2)}, u32[]{:S(2)}) collective-permute-start(f32[2,2,256,128]{3,2,1,0:T(8,128)} %get-tuple-element.74), channel_id=1, source_target_pairs={{0,4},{2,6},{4,0},{6,2},{1,5},{3,7},{5,1},{7,3},{8,12},{10,14},{12... | collective-permute-start | bytes 1572872 | tf_op jit(solution)/shard_map/ppermute | solution.py:322
  138.1 15.2 %own_backward.1 = (f32[256,512]{1,0:T(8,128)}, f32[2,256,512]{2,1,0:T(8,128)}, f32[2,256,128]{2,1,0:T(8,128)}, f32[2,256,128]{2,1,0:T(8,128)}, f32[2,256,128]{2,1,0:T(8,128)}, /*index=5*/f32[2,256,128]{2,1,0:T(8,128)}) custom-call(s32[5]{0:T(128)S(1)} %pad_add_fusion.info, f32[256,1024]{1,0:T(8,128)} %ql_ref.5, f32[256,512]{1,0:T(8,128)S(1)} %copy-done.3, ...), custom_call_target="tpu_custom_call" | custom-call | flops 6442450944 | bytes 16777216 | tf_op jit(solution)/shard_map/own_backward/pallas_call | solution.py:274
  153.3 5.9 %collective-permute-done.15.passed = f32[2,2,256,128]{3,2,1,0:T(8,128)S(1)} collective-permute-done((f32[2,2,256,128]{3,2,1,0:T(8,128)}, f32[2,2,256,128]{3,2,1,0:T(8,128)S(1)}, u32[]{:S(2)}, u32[]{:S(2)}) %collective-permute-start.15) | collective-permute-done | bytes 524320 | tf_op jit(solution)/shard_map/ppermute | solution.py:322
  160.0 3.2 %collective-permute-start.17 = (f32[2,2,256,128]{3,2,1,0:T(8,128)S(1)}, f32[2,2,256,128]{3,2,1,0:T(8,128)S(1)}, u32[]{:S(2)}, u32[]{:S(2)}) collective-permute-start(f32[2,2,256,128]{3,2,1,0:T(8,128)S(1)} %get-tuple-element.79), channel_id=1, source_target_pairs={{0,1},{1,0},{2,3},{3,2},{4,5},{5,4},{6,7},{7,6},{8,9},{9,8},{10,11... | collective-permute-start | bytes 1572872 | tf_op jit(solution)/shard_map/ppermute | solution.py:325
  171.9 8.0 %collective-permute-done.20.passed2 = f32[1,2,256,128]{3,2,1,0:T(8,128)S(1)} collective-permute-done((f32[1,2,256,128]{3,2,1,0:T(8,128)S(1)}, f32[1,2,256,128]{3,2,1,0:T(8,128)S(1)}, u32[]{:S(2)}, u32[]{:S(2)}) %collective-permute-start.20) | collective-permute-done | bytes 262176 | tf_op jit(solution)/shard_map/ppermute | solution.py:322
  183.8 11.8 %collective-permute-done.23.refs_2_ = f32[2,4,256,128]{3,2,1,0:T(8,128)S(1)} collective-permute-done((f32[2,4,256,128]{3,2,1,0:T(8,128)S(1)}, f32[2,4,256,128]{3,2,1,0:T(8,128)S(1)}, u32[]{:S(2)}, u32[]{:S(2)}) %collective-permute-start.23) | collective-permute-done | bytes 1048608 | tf_op jit(solution)/shard_map/ppermute | solution.py:314
  195.7 3.2 %collect.1 = (f32[4,256,128]{2,1,0:T(8,128)}, f32[4,256,128]{2,1,0:T(8,128)}, f32[4,256,128]{2,1,0:T(8,128)}, f32[4,256,128]{2,1,0:T(8,128)}) custom-call(s32[16,3]{1,0:T(8,128)S(1)} %copy.14.table, f32[2,4,256,128]{3,2,1,0:T(8,128)S(1)} %gather_heads.1.refs_0_, f32[2,4,256,128]{3,2,1,0:T(8,128)S(1)} %collective-permute-done.22.refs_1_, ...), custom_call_target="tpu_custom_call" | custom-call | bytes 6291456 | tf_op jit(solution)/shard_map/collect/pallas_call | solution.py:291
  202.6 2.9 %collective-permute-start.28 = (f32[1,2,256,128]{3,2,1,0:T(8,128)}, f32[1,2,256,128]{3,2,1,0:T(8,128)S(1)}, u32[]{:S(2)}, u32[]{:S(2)}) collective-permute-start(f32[1,2,256,128]{3,2,1,0:T(8,128)} %copy-done.4), channel_id=1, source_target_pairs={{0,1},{1,0},{2,3},{3,2},{4,5},{5,4},{6,7},{7,6},{8,9},{9,8},{10,11... | collective-permute-start | bytes 786440 | tf_op jit(solution)/shard_map/ppermute | solution.py:325
  210.8 2.5 %collective-permute-done.25 = f32[4,256,128]{2,1,0:T(8,128)S(1)} collective-permute-done((f32[4,256,128]{2,1,0:T(8,128)}, f32[4,256,128]{2,1,0:T(8,128)S(1)}, u32[]{:S(2)}, u32[]{:S(2)}) %collective-permute-start.25) | collective-permute-done | bytes 524320 | tf_op jit(solution)/shard_map/ppermute | solution.py:314
  213.3 3.6 %collective-permute-done.27 = f32[4,256,128]{2,1,0:T(8,128)S(1)} collective-permute-done((f32[4,256,128]{2,1,0:T(8,128)}, f32[4,256,128]{2,1,0:T(8,128)S(1)}, u32[]{:S(2)}, u32[]{:S(2)}) %collective-permute-start.27) | collective-permute-done | bytes 524320 | tf_op jit(solution)/shard_map/ppermute | solution.py:314
  217.1 3.2 %collective-permute-start.29 = (f32[128,512]{1,0:T(8,128)S(1)}, f32[128,512]{1,0:T(8,128)S(1)}, u32[]{:S(2)}, u32[]{:S(2)}) collective-permute-start(f32[128,512]{1,0:T(8,128)S(1)} %pad_maximum_fusion.1), channel_id=1, source_target_pairs={{0,1},{1,0},{2,3},{3,2},{4,5},{5,4},{6,7},{7,6},{8,9},{9,8},{10,11... | collective-permute-start | bytes 786440 | tf_op jit(solution)/shard_map/ppermute | solution.py:325
  (94 shorter events, 47.4 us)
Async XLA Ops:
  7.2 58.1 %all-gather.3.cloned.1.call-start = ((), (), s32[]{:S(2)}) async-start(), calls=%async_computation | async-start | bytes 2621440 | tf_op jit(solution)/shard_map/all_gather | solution.py:419
  14.2 15.1 %collective-permute-start.4 = (f32[4,256,128]{2,1,0:T(8,128)}, f32[4,256,128]{2,1,0:T(8,128)S(1)}, u32[]{:S(2)}, u32[]{:S(2)}) collective-permute-start(f32[4,256,128]{2,1,0:T(8,128)} %assemble.1.refs_0_), channel_id=1, source_target_pairs={{0,64},{1,17},{8,72},{9,25},{16,80},{17,1},{24,88},{25,9},{32,96},... | collective-permute-start | bytes 1572872 | tf_op jit(solution)/shard_map/ppermute | solution.py:314
  16.7 12.7 %collective-permute-start.5 = (f32[4,256,128]{2,1,0:T(8,128)}, f32[4,256,128]{2,1,0:T(8,128)S(1)}, u32[]{:S(2)}, u32[]{:S(2)}) collective-permute-start(f32[4,256,128]{2,1,0:T(8,128)} %assemble.1.refs_0_), channel_id=1, source_target_pairs={{0,96},{1,25},{8,104},{9,1},{16,112},{17,9},{24,120},{25,17},{32,0... | collective-permute-start | bytes 1572872 | tf_op jit(solution)/shard_map/ppermute | solution.py:314
  32.5 26.1 %collective-permute-start.6 = (f32[2,4,256,128]{3,2,1,0:T(8,128)}, f32[2,4,256,128]{3,2,1,0:T(8,128)S(1)}, u32[]{:S(2)}, u32[]{:S(2)}) collective-permute-start(f32[2,4,256,128]{3,2,1,0:T(8,128)} %get-tuple-element.53), channel_id=1, source_target_pairs={{0,8},{1,33},{8,16},{9,41},{16,24},{17,49},{24,0},{25,57},{32,40},... | collective-permute-start | bytes 3145736 | tf_op jit(solution)/shard_map/ppermute | solution.py:314
  33.5 26.6 %collective-permute-start.7 = (f32[2,4,256,128]{3,2,1,0:T(8,128)}, f32[2,4,256,128]{3,2,1,0:T(8,128)}, u32[]{:S(2)}, u32[]{:S(2)}) collective-permute-start(f32[2,4,256,128]{3,2,1,0:T(8,128)} %get-tuple-element.54), channel_id=1, source_target_pairs={{0,16},{1,65},{8,24},{9,73},{16,0},{17,81},{24,8},{25,89},{32,48},... | collective-permute-start | bytes 3145736 | tf_op jit(solution)/shard_map/ppermute | solution.py:314
  36.2 24.0 %collective-permute-start.8 = (f32[2,4,256,128]{3,2,1,0:T(8,128)}, f32[2,4,256,128]{3,2,1,0:T(8,128)}, u32[]{:S(2)}, u32[]{:S(2)}) collective-permute-start(f32[2,4,256,128]{3,2,1,0:T(8,128)} %get-tuple-element.55), channel_id=1, source_target_pairs={{0,24},{1,97},{8,0},{9,105},{16,8},{17,113},{24,16},{25,121},{32,5... | collective-permute-start | bytes 3145736 | tf_op jit(solution)/shard_map/ppermute | solution.py:314
  39.1 17.5 %collective-permute-start.2 = (f32[256,512]{1,0:T(8,128)}, f32[256,512]{1,0:T(8,128)S(1)}, u32[]{:S(2)}, u32[]{:S(2)}) collective-permute-start(f32[256,512]{1,0:T(8,128)} %constant_dynamic-slice_fusion.1), channel_id=1, source_target_pairs={{0,6},{2,4},{4,2},{6,0},{1,7},{3,5},{5,3},{7,1},{8,14},{10,12},{12... | collective-permute-start | bytes 1572872 | tf_op jit(solution)/shard_map/ppermute | solution.py:322
  58.6 14.5 %collective-permute-start.3 = (f32[256,512]{1,0:T(8,128)}, f32[256,512]{1,0:T(8,128)}, u32[]{:S(2)}, u32[]{:S(2)}) collective-permute-start(f32[256,512]{1,0:T(8,128)} %constant_dynamic-slice_fusion), channel_id=1, source_target_pairs={{0,6},{2,4},{4,2},{6,0},{1,7},{3,5},{5,3},{7,1},{8,14},{10,12},{12... | collective-permute-start | bytes 1572872 | tf_op jit(solution)/shard_map/ppermute | solution.py:322
  67.9 16.4 %collective-permute-start.10 = (f32[2,2,256,128]{3,2,1,0:T(8,128)S(1)}, f32[2,2,256,128]{3,2,1,0:T(8,128)S(1)}, u32[]{:S(2)}, u32[]{:S(2)}) collective-permute-start(f32[2,2,256,128]{3,2,1,0:T(8,128)S(1)} %get-tuple-element.58.s0), channel_id=1, source_target_pairs={{0,2},{2,0},{4,6},{6,4},{1,3},{3,1},{5,7},{7,5},{8,10},{10,8},{12,... | collective-permute-start | bytes 1572872 | tf_op jit(solution)/shard_map/ppermute | solution.py:322
  69.6 26.2 %collective-permute-start.11 = (f32[2,2,256,128]{3,2,1,0:T(8,128)S(1)}, f32[2,2,256,128]{3,2,1,0:T(8,128)S(1)}, u32[]{:S(2)}, u32[]{:S(2)}) collective-permute-start(f32[2,2,256,128]{3,2,1,0:T(8,128)S(1)} %get-tuple-element.59), channel_id=1, source_target_pairs={{0,4},{2,6},{4,0},{6,2},{1,5},{3,7},{5,1},{7,3},{8,12},{10,14},{12... | collective-permute-start | bytes 1572872 | tf_op jit(solution)/shard_map/ppermute | solution.py:322
  72.9 25.0 %collective-permute-start.12 = (f32[2,2,256,128]{3,2,1,0:T(8,128)S(1)}, f32[2,2,256,128]{3,2,1,0:T(8,128)}, u32[]{:S(2)}, u32[]{:S(2)}) collective-permute-start(f32[2,2,256,128]{3,2,1,0:T(8,128)S(1)} %get-tuple-element.59), channel_id=1, source_target_pairs={{0,6},{2,4},{4,2},{6,0},{1,7},{3,5},{5,3},{7,1},{8,14},{10,12},{12... | collective-permute-start | bytes 1572872 | tf_op jit(solution)/shard_map/ppermute | solution.py:322
  134.1 19.2 %collective-permute-start.16 = (f32[2,2,256,128]{3,2,1,0:T(8,128)}, f32[2,2,256,128]{3,2,1,0:T(8,128)S(1)}, u32[]{:S(2)}, u32[]{:S(2)}) collective-permute-start(f32[2,2,256,128]{3,2,1,0:T(8,128)} %get-tuple-element.75), channel_id=1, source_target_pairs={{0,6},{2,4},{4,2},{6,0},{1,7},{3,5},{5,3},{7,1},{8,14},{10,12},{12... | collective-permute-start | bytes 1572872 | tf_op jit(solution)/shard_map/ppermute | solution.py:322
  134.5 18.8 %collective-permute-start.14 = (f32[2,2,256,128]{3,2,1,0:T(8,128)}, f32[2,2,256,128]{3,2,1,0:T(8,128)S(1)}, u32[]{:S(2)}, u32[]{:S(2)}) collective-permute-start(f32[2,2,256,128]{3,2,1,0:T(8,128)} %get-tuple-element.73), channel_id=1, source_target_pairs={{0,2},{2,0},{4,6},{6,4},{1,3},{3,1},{5,7},{7,5},{8,10},{10,8},{12,... | collective-permute-start | bytes 1572872 | tf_op jit(solution)/shard_map/ppermute | solution.py:322
  134.5 24.8 %collective-permute-start.15 = (f32[2,2,256,128]{3,2,1,0:T(8,128)}, f32[2,2,256,128]{3,2,1,0:T(8,128)S(1)}, u32[]{:S(2)}, u32[]{:S(2)}) collective-permute-start(f32[2,2,256,128]{3,2,1,0:T(8,128)} %get-tuple-element.74), channel_id=1, source_target_pairs={{0,4},{2,6},{4,0},{6,2},{1,5},{3,7},{5,1},{7,3},{8,12},{10,14},{12... | collective-permute-start | bytes 1572872 | tf_op jit(solution)/shard_map/ppermute | solution.py:322
  165.3 14.5 %collective-permute-start.20 = (f32[1,2,256,128]{3,2,1,0:T(8,128)S(1)}, f32[1,2,256,128]{3,2,1,0:T(8,128)S(1)}, u32[]{:S(2)}, u32[]{:S(2)}) collective-permute-start(f32[1,2,256,128]{3,2,1,0:T(8,128)S(1)} %bitcast.40), channel_id=1, source_target_pairs={{0,6},{2,4},{4,2},{6,0},{1,7},{3,5},{5,3},{7,1},{8,14},{10,12},{12... | collective-permute-start | bytes 786440 | tf_op jit(solution)/shard_map/ppermute | solution.py:322
  165.7 16.2 %collective-permute-start.19 = (f32[1,2,256,128]{3,2,1,0:T(8,128)S(1)}, f32[1,2,256,128]{3,2,1,0:T(8,128)S(1)}, u32[]{:S(2)}, u32[]{:S(2)}) collective-permute-start(f32[1,2,256,128]{3,2,1,0:T(8,128)S(1)} %bitcast.39), channel_id=1, source_target_pairs={{0,4},{2,6},{4,0},{6,2},{1,5},{3,7},{5,1},{7,3},{8,12},{10,14},{12... | collective-permute-start | bytes 786440 | tf_op jit(solution)/shard_map/ppermute | solution.py:322
  166.6 15.3 %collective-permute-start.18 = (f32[1,2,256,128]{3,2,1,0:T(8,128)S(1)}, f32[1,2,256,128]{3,2,1,0:T(8,128)S(1)}, u32[]{:S(2)}, u32[]{:S(2)}) collective-permute-start(f32[1,2,256,128]{3,2,1,0:T(8,128)S(1)} %bitcast.38), channel_id=1, source_target_pairs={{0,2},{2,0},{4,6},{6,4},{1,3},{3,1},{5,7},{7,5},{8,10},{10,8},{12,... | collective-permute-start | bytes 786440 | tf_op jit(solution)/shard_map/ppermute | solution.py:322
  168.7 15.2 %collective-permute-start.22 = (f32[2,4,256,128]{3,2,1,0:T(8,128)S(1)}, f32[2,4,256,128]{3,2,1,0:T(8,128)S(1)}, u32[]{:S(2)}, u32[]{:S(2)}) collective-permute-start(f32[2,4,256,128]{3,2,1,0:T(8,128)S(1)} %gather_heads.1.refs_0_), channel_id=1, source_target_pairs={{0,8},{1,33},{8,16},{9,41},{16,24},{17,49},{24,0},{25,57},{32,40},... | collective-permute-start | bytes 3145736 | tf_op jit(solution)/shard_map/ppermute | solution.py:314
  170.0 25.5 %collective-permute-start.23 = (f32[2,4,256,128]{3,2,1,0:T(8,128)S(1)}, f32[2,4,256,128]{3,2,1,0:T(8,128)S(1)}, u32[]{:S(2)}, u32[]{:S(2)}) collective-permute-start(f32[2,4,256,128]{3,2,1,0:T(8,128)S(1)} %gather_heads.1.refs_0_), channel_id=1, source_target_pairs={{0,16},{1,65},{8,24},{9,73},{16,0},{17,81},{24,8},{25,89},{32,48},... | collective-permute-start | bytes 3145736 | tf_op jit(solution)/shard_map/ppermute | solution.py:314
  179.9 15.9 %collective-permute-start.24 = (f32[2,4,256,128]{3,2,1,0:T(8,128)S(1)}, f32[2,4,256,128]{3,2,1,0:T(8,128)}, u32[]{:S(2)}, u32[]{:S(2)}) collective-permute-start(f32[2,4,256,128]{3,2,1,0:T(8,128)S(1)} %gather_heads.1.refs_0_), channel_id=1, source_target_pairs={{0,24},{1,97},{8,0},{9,105},{16,8},{17,113},{24,16},{25,121},{32,5... | collective-permute-start | bytes 3145736 | tf_op jit(solution)/shard_map/ppermute | solution.py:314
  183.2 24.6 %collective-permute-start.21 = (f32[2,256,512]{2,1,0:T(8,128)}, f32[2,256,512]{2,1,0:T(8,128)}, u32[]{:S(2)}, u32[]{:S(2)}) collective-permute-start(f32[2,256,512]{2,1,0:T(8,128)} %get-tuple-element.88), channel_id=1, source_target_pairs={{0,6},{2,4},{4,2},{6,0},{1,7},{3,5},{5,3},{7,1},{8,14},{10,12},{12... | collective-permute-start | bytes 3145736 | tf_op jit(solution)/shard_map/ppermute | solution.py:322
  198.9 14.3 %collective-permute-start.25 = (f32[4,256,128]{2,1,0:T(8,128)}, f32[4,256,128]{2,1,0:T(8,128)S(1)}, u32[]{:S(2)}, u32[]{:S(2)}) collective-permute-start(f32[4,256,128]{2,1,0:T(8,128)} %get-tuple-element.92), channel_id=1, source_target_pairs={{0,96},{1,25},{8,104},{9,1},{16,112},{17,9},{24,120},{25,17},{32,0... | collective-permute-start | bytes 1572872 | tf_op jit(solution)/shard_map/ppermute | solution.py:314
  201.2 12.1 %collective-permute-start.26 = (f32[4,256,128]{2,1,0:T(8,128)}, f32[4,256,128]{2,1,0:T(8,128)S(1)}, u32[]{:S(2)}, u32[]{:S(2)}) collective-permute-start(f32[4,256,128]{2,1,0:T(8,128)} %get-tuple-element.93), channel_id=1, source_target_pairs={{0,64},{1,17},{8,72},{9,25},{16,80},{17,1},{24,88},{25,9},{32,96},... | collective-permute-start | bytes 1572872 | tf_op jit(solution)/shard_map/ppermute | solution.py:314
  202.4 14.5 %collective-permute-start.27 = (f32[4,256,128]{2,1,0:T(8,128)}, f32[4,256,128]{2,1,0:T(8,128)S(1)}, u32[]{:S(2)}, u32[]{:S(2)}) collective-permute-start(f32[4,256,128]{2,1,0:T(8,128)} %get-tuple-element.94), channel_id=1, source_target_pairs={{0,32},{1,9},{8,40},{9,17},{16,48},{17,25},{24,56},{25,1},{32,64},... | collective-permute-start | bytes 1572872 | tf_op jit(solution)/shard_map/ppermute | solution.py:314
  (21 other events, 172.6 us)
Sparse Core Ops, SparseCore 0:
  13.0 33.9 all-gather.2
